TPU v7x, 256 devices: a whole 4x4x8 slice. The times are simulated.
256 devices in a mesh: seq: 64 (over z_hi, y, x, core), chan: 4 (over z_lo).
Axes of the slice: x: 4, y: 4, z: 8 (z_hi: 2, z_lo: 4; z = z_hi * 4 + z_lo), core: 2. Of those that a mesh axis runs over, the one named last changes fastest.
Arguments:
- layer_input: bfloat16 [8192, 4096], P('seq', 'chan'), may hold values from -16 to 16
- gate_query: bfloat16 [8192, 4096], P('seq', 'chan'), may hold values from -6 to 6
- gate_key: bfloat16 [8192, 4096], P('seq', 'chan'), may hold values from -6 to 6
- value_proj: bfloat16 [8192, 4096], P('seq', 'chan'), may hold values from -6 to 6
- grad_out: bfloat16 [8192, 4096], P('seq', 'chan'), may hold values from -6 to 6
- filter_taps: bfloat16 [8192, 4096], P('seq', 'chan'), may hold values from -1.1 to 1.1
Outputs:
- grad_query: bfloat16 [8192, 4096], P('seq', 'chan')
- grad_key: bfloat16 [8192, 4096], P('seq', 'chan')
- grad_value: bfloat16 [8192, 4096], P('seq', 'chan')
- grad_filter: bfloat16 [8192, 4096], P('seq', 'chan')
- grad_weight: float32 [4096, 4096], P('seq', 'chan')
All inputs are finite; a program needn't handle non-finite values.
Results may differ from a plain program's by a relative error of at most 0.0067.
Values may be sent and summed in bfloat16 or wider, within the bound.
No kernel may reach another device: no remote copies, remote signals or barrier semaphores. Data moves between devices by JAX's collectives and lax.ppermute only.
A program may use at most 128 MiB of HBM per device.

v0:
```python
import math

import jax
import jax.numpy as jnp
from jax import lax
from jax.sharding import PartitionSpec as P

FULL_PRECISION = lax.Precision.HIGHEST


def angle_table(first, second, period):
    product = first[:, None] * second[None, :] % period
    return product.astype(jnp.float32) * (2.0 * math.pi / period)


def mixed_sum(matrix, operand, form):
    return jnp.einsum(form, matrix, operand, precision=FULL_PRECISION)


def outer_forward(signal, first_cos, first_sin, twist_cos, twist_sin):
    widened = signal.astype(jnp.float32)
    real_part = mixed_sum(first_cos, widened, "ka,ajc->kjc")
    other_part = -mixed_sum(first_sin, widened, "ka,ajc->kjc")
    cosine = twist_cos[:, :, None]
    sine = twist_sin[:, :, None]
    turned_real = real_part * cosine + other_part * sine
    turned_other = other_part * cosine - real_part * sine
    return (turned_real.astype(jnp.bfloat16), turned_other.astype(jnp.bfloat16))


def inner_forward(real_in, other_in, cosine, sine):
    real_wide = real_in.astype(jnp.float32)
    other_wide = other_in.astype(jnp.float32)
    real_out = mixed_sum(cosine, real_wide, "mj,rjc->rmc") + mixed_sum(
        sine, other_wide, "mj,rjc->rmc"
    )
    other_out = mixed_sum(cosine, other_wide, "mj,rjc->rmc") - mixed_sum(
        sine, real_wide, "mj,rjc->rmc"
    )
    return (real_out, other_out)


def inner_inverse(spectrum, cosine, sine, twist_cos, twist_sin):
    real_in, other_in = spectrum
    real_mid = mixed_sum(cosine, real_in, "jm,rmc->rjc") - mixed_sum(sine, other_in, "jm,rmc->rjc")
    other_mid = mixed_sum(cosine, other_in, "jm,rmc->rjc") + mixed_sum(sine, real_in, "jm,rmc->rjc")
    turn_cos = twist_cos[:, :, None]
    turn_sin = twist_sin[:, :, None]
    real_out = real_mid * turn_cos - other_mid * turn_sin
    other_out = real_mid * turn_sin + other_mid * turn_cos
    return (real_out.astype(jnp.bfloat16), other_out.astype(jnp.bfloat16))


def outer_inverse(real_in, other_in, cosine, sine, factor):
    total = mixed_sum(cosine, real_in.astype(jnp.float32), "ak,kjc->ajc") - mixed_sum(
        sine, other_in.astype(jnp.float32), "ak,kjc->ajc"
    )
    return (total * factor).astype(jnp.bfloat16)


def spectral_products(mixed_spec, taps_spec, gated_spec):
    mixed_real, mixed_other = mixed_spec
    taps_real, taps_other = taps_spec
    gated_real, gated_other = gated_spec
    forward_pair = (
        mixed_real * taps_real - mixed_other * taps_other,
        mixed_real * taps_other + mixed_other * taps_real,
    )
    backward_pair = (
        gated_real * taps_real + gated_other * taps_other,
        gated_other * taps_real - gated_real * taps_other,
    )
    filter_pair = (
        gated_real * mixed_real + gated_other * mixed_other,
        gated_other * mixed_real - gated_real * mixed_other,
    )
    return (forward_pair, backward_pair, filter_pair)


def shards(layer_input, gate_query, gate_key, value_proj, grad_out, filter_taps):
    rows = gate_query.shape[0]
    width = gate_query.shape[1]
    half = width // 2
    blocks = lax.axis_size("seq")
    share = rows // blocks
    length = rows * blocks
    period = 2 * length
    index = lax.axis_index("seq")
    outer_count = 2 * blocks
    block_ids = jnp.arange(blocks, dtype=jnp.int32)
    freq_ids = jnp.arange(outer_count, dtype=jnp.int32)
    row_ids = jnp.arange(rows, dtype=jnp.int32)
    first_angle = angle_table(freq_ids, block_ids, outer_count)
    first_cos = jnp.cos(first_angle)
    first_sin = jnp.sin(first_angle)
    local_rows = index * share + jnp.arange(share, dtype=jnp.int32)
    twist_angle = angle_table(freq_ids, local_rows, period)
    twist_cos = jnp.cos(twist_angle)
    twist_sin = jnp.sin(twist_angle)
    inner_angle = angle_table(row_ids, row_ids, rows)
    inner_cos = jnp.cos(inner_angle)
    inner_sin = jnp.sin(inner_angle)
    held_freq = index * 2 + jnp.arange(2, dtype=jnp.int32)
    back_angle = angle_table(held_freq, row_ids, period)
    back_cos = jnp.cos(back_angle)
    back_sin = jnp.sin(back_angle)
    last_angle = angle_table(block_ids, freq_ids, outer_count)
    last_cos = jnp.cos(last_angle)
    last_sin = jnp.sin(last_angle)
    scale_root = 1.0 / math.sqrt(length)
    last_scale = 1.0 / period
    mixed = (gate_key.astype(jnp.float32) * value_proj.astype(jnp.float32)).astype(jnp.bfloat16)
    gated = (grad_out.astype(jnp.float32) * gate_query.astype(jnp.float32)).astype(jnp.bfloat16)
    features = lax.all_gather(layer_input, "chan", axis=1, tiled=True)
    conv_parts = []
    back_parts = []
    filter_parts = []
    value_parts = []
    for section in range(2):
        offset = section * half
        mixed_part = mixed[:, offset : offset + half]
        taps_part = filter_taps[:, offset : offset + half]
        gated_part = gated[:, offset : offset + half]
        spread = (
            lax.all_to_all(mixed_part[None], "seq", split_axis=1, concat_axis=0, tiled=True),
            lax.all_to_all(taps_part[None], "seq", split_axis=1, concat_axis=0, tiled=True),
            lax.all_to_all(gated_part[None], "seq", split_axis=1, concat_axis=0, tiled=True),
        )
        turned = []
        for signal in spread:
            turned.extend(outer_forward(signal, first_cos, first_sin, twist_cos, twist_sin))
        freq = (
            lax.all_to_all(turned[0], "seq", split_axis=0, concat_axis=1, tiled=True),
            lax.all_to_all(turned[1], "seq", split_axis=0, concat_axis=1, tiled=True),
            lax.all_to_all(turned[2], "seq", split_axis=0, concat_axis=1, tiled=True),
            lax.all_to_all(turned[3], "seq", split_axis=0, concat_axis=1, tiled=True),
            lax.all_to_all(turned[4], "seq", split_axis=0, concat_axis=1, tiled=True),
            lax.all_to_all(turned[5], "seq", split_axis=0, concat_axis=1, tiled=True),
        )
        mixed_spec = inner_forward(freq[0], freq[1], inner_cos, inner_sin)
        taps_spec = inner_forward(freq[2], freq[3], inner_cos, inner_sin)
        gated_spec = inner_forward(freq[4], freq[5], inner_cos, inner_sin)
        pairs = spectral_products(mixed_spec, taps_spec, gated_spec)
        rowed = []
        for spectrum in pairs:
            rowed.extend(inner_inverse(spectrum, inner_cos, inner_sin, back_cos, back_sin))
        returned = (
            lax.all_to_all(rowed[0], "seq", split_axis=1, concat_axis=0, tiled=True),
            lax.all_to_all(rowed[1], "seq", split_axis=1, concat_axis=0, tiled=True),
            lax.all_to_all(rowed[2], "seq", split_axis=1, concat_axis=0, tiled=True),
            lax.all_to_all(rowed[3], "seq", split_axis=1, concat_axis=0, tiled=True),
            lax.all_to_all(rowed[4], "seq", split_axis=1, concat_axis=0, tiled=True),
            lax.all_to_all(rowed[5], "seq", split_axis=1, concat_axis=0, tiled=True),
        )
        conv_block = outer_inverse(returned[0], returned[1], last_cos, last_sin, last_scale)
        back_block = outer_inverse(returned[2], returned[3], last_cos, last_sin, last_scale)
        filter_block = outer_inverse(
            returned[4], returned[5], last_cos, last_sin, last_scale * scale_root
        )
        restored = (
            lax.all_to_all(conv_block, "seq", split_axis=0, concat_axis=1, tiled=True),
            lax.all_to_all(back_block, "seq", split_axis=0, concat_axis=1, tiled=True),
            lax.all_to_all(filter_block, "seq", split_axis=0, concat_axis=1, tiled=True),
        )
        conv_part = restored[0][0]
        back_part = restored[1][0]
        value_part = (
            back_part.astype(jnp.float32) * gate_key[:, offset : offset + half].astype(jnp.float32)
        ).astype(jnp.bfloat16)
        conv_parts.append(conv_part)
        back_parts.append(back_part)
        filter_parts.append(restored[2][0])
        value_parts.append(value_part)
    conv_out = jnp.concatenate(conv_parts, axis=1)
    back_grad = jnp.concatenate(back_parts, axis=1)
    grad_filter = jnp.concatenate(filter_parts, axis=1)
    grad_value = jnp.concatenate(value_parts, axis=1)
    grad_query = (grad_out.astype(jnp.float32) * conv_out.astype(jnp.float32)).astype(jnp.bfloat16)
    grad_key = (back_grad.astype(jnp.float32) * value_proj.astype(jnp.float32)).astype(jnp.bfloat16)
    product = lax.dot_general(
        features, grad_value, (((0,), (0,)), ((), ())), preferred_element_type=jnp.float32
    )
    grad_weight = lax.psum_scatter(product * scale_root, "seq", scatter_dimension=0, tiled=True)
    return (grad_query, grad_key, grad_value, grad_filter, grad_weight)


def solution(mesh):
    placed = (
        P("seq", "chan"),
        P("seq", "chan"),
        P("seq", "chan"),
        P("seq", "chan"),
        P("seq", "chan"),
        P("seq", "chan"),
    )
    return jax.shard_map(
        shards,
        mesh=mesh,
        in_specs=placed,
        out_specs=(
            P("seq", "chan"),
            P("seq", "chan"),
            P("seq", "chan"),
            P("seq", "chan"),
            P("seq", "chan"),
        ),
        check_vma=False,
    )
```

profile of v0, /device:TPU:32, one launch (start us, length us, event | category | flops | bytes accessed | tf_op | source)
XLA Modules:
  0.0 1052.8 jit_solution(3475811893956550262)
XLA Ops:
  11.0 13.7 %all-to-all-start.12 = ((bf16[64,2,512]{2,1,0:T(2,128)(2,1)}), bf16[64,2,512]{2,1,0:T(2,128)(2,1)S(1)}, u32[]{:S(2)}, u32[]{:S(2)}) async-start(bf16[64,2,512]{2,1,0:T(2,128)(2,1)} %reshape.180), calls=%async_computation.12 | async-start | bytes 262144 | tf_op jit(solution)/shard_map/all_to_all | solution.py:126
  38.7 12.8 %all-to-all-start.3 = ((bf16[64,2,512]{2,1,0:T(2,128)(2,1)}), bf16[64,2,512]{2,1,0:T(2,128)(2,1)S(1)}, u32[]{:S(2)}, u32[]{:S(2)}) async-start(bf16[64,2,512]{2,1,0:T(2,128)(2,1)} %reshape.184), calls=%async_computation.3 | async-start | bytes 262144 | tf_op jit(solution)/shard_map/all_to_all | solution.py:126
  53.6 11.7 %all-to-all-done.3 = bf16[64,2,512]{2,1,0:T(2,128)(2,1)S(1)} async-done(((bf16[64,2,512]{2,1,0:T(2,128)(2,1)}), bf16[64,2,512]{2,1,0:T(2,128)(2,1)S(1)}, u32[]{:S(2)}, u32[]{:S(2)}) %all-to-all-start.3) | async-done | bytes 131104 | tf_op jit(solution)/shard_map/all_to_all | solution.py:126
  72.1 11.1 %all-to-all-done.9 = bf16[64,2,512]{2,1,0:T(2,128)(2,1)S(1)} async-done(((bf16[64,2,512]{2,1,0:T(2,128)(2,1)}), bf16[64,2,512]{2,1,0:T(2,128)(2,1)S(1)}, u32[]{:S(2)}, u32[]{:S(2)}) %all-to-all-start.9) | async-done | bytes 131104 | tf_op jit(solution)/shard_map/all_to_all | solution.py:125
  89.9 10.9 %all-to-all-done = bf16[64,2,512]{2,1,0:T(2,128)(2,1)S(1)} async-done(((bf16[64,2,512]{2,1,0:T(2,128)(2,1)}), bf16[64,2,512]{2,1,0:T(2,128)(2,1)S(1)}, u32[]{:S(2)}, u32[]{:S(2)}) %all-to-all-start) | async-done | bytes 131104 | tf_op jit(solution)/shard_map/all_to_all | solution.py:125
  109.9 8.8 all-to-all-done.24
  130.2 6.4 all-to-all-done.18
  143.5 6.5 all-to-all-start.20
  151.9 13.4 %all-to-all-done.20 = bf16[128,2,512]{2,1,0:T(2,128)(2,1)S(1)} async-done(((bf16[128,2,512]{2,1,0:T(2,128)(2,1)}), bf16[128,2,512]{2,1,0:T(2,128)(2,1)S(1)}, u32[]{:S(2)}, u32[]{:S(2)}) %all-to-all-start.20) | async-done | bytes 262176 | tf_op jit(solution)/shard_map/all_to_all | solution.py:138
  171.9 13.8 %all-to-all-done.19 = bf16[128,2,512]{2,1,0:T(2,128)(2,1)S(1)} async-done(((bf16[128,2,512]{2,1,0:T(2,128)(2,1)}), bf16[128,2,512]{2,1,0:T(2,128)(2,1)S(1)}, u32[]{:S(2)}, u32[]{:S(2)}) %all-to-all-start.19) | async-done | bytes 262176 | tf_op jit(solution)/shard_map/all_to_all | solution.py:137
  192.2 13.8 %all-to-all-done.4 = bf16[128,2,512]{2,1,0:T(2,128)(2,1)S(1)} async-done(((bf16[128,2,512]{2,1,0:T(2,128)(2,1)}), bf16[128,2,512]{2,1,0:T(2,128)(2,1)S(1)}, u32[]{:S(2)}, u32[]{:S(2)}) %all-to-all-start.4) | async-done | bytes 262176 | tf_op jit(solution)/shard_map/all_to_all | solution.py:135
  212.5 13.8 %all-to-all-done.5 = bf16[128,2,512]{2,1,0:T(2,128)(2,1)S(1)} async-done(((bf16[128,2,512]{2,1,0:T(2,128)(2,1)}), bf16[128,2,512]{2,1,0:T(2,128)(2,1)S(1)}, u32[]{:S(2)}, u32[]{:S(2)}) %all-to-all-start.5) | async-done | bytes 262176 | tf_op jit(solution)/shard_map/all_to_all | solution.py:136
  232.9 13.8 %all-to-all-done.11 = bf16[128,2,512]{2,1,0:T(2,128)(2,1)S(1)} async-done(((bf16[128,2,512]{2,1,0:T(2,128)(2,1)}), bf16[128,2,512]{2,1,0:T(2,128)(2,1)S(1)}, u32[]{:S(2)}, u32[]{:S(2)}) %all-to-all-start.11) | async-done | bytes 262176 | tf_op jit(solution)/shard_map/all_to_all | solution.py:134
  253.4 13.6 %all-to-all-done.10 = bf16[128,2,512]{2,1,0:T(2,128)(2,1)S(1)} async-done(((bf16[128,2,512]{2,1,0:T(2,128)(2,1)}), bf16[128,2,512]{2,1,0:T(2,128)(2,1)S(1)}, u32[]{:S(2)}, u32[]{:S(2)}) %all-to-all-start.10) | async-done | bytes 262176 | tf_op jit(solution)/shard_map/all_to_all | solution.py:133
  273.5 13.8 %all-to-all-done.13 = bf16[128,2,512]{2,1,0:T(2,128)(2,1)S(1)} async-done(((bf16[128,2,512]{2,1,0:T(2,128)(2,1)}), bf16[128,2,512]{2,1,0:T(2,128)(2,1)S(1)}, u32[]{:S(2)}, u32[]{:S(2)}) %all-to-all-start.13) | async-done | bytes 262176 | tf_op jit(solution)/shard_map/all_to_all | solution.py:135
  293.9 13.8 %all-to-all-done.14 = bf16[128,2,512]{2,1,0:T(2,128)(2,1)S(1)} async-done(((bf16[128,2,512]{2,1,0:T(2,128)(2,1)}), bf16[128,2,512]{2,1,0:T(2,128)(2,1)S(1)}, u32[]{:S(2)}, u32[]{:S(2)}) %all-to-all-start.14) | async-done | bytes 262176 | tf_op jit(solution)/shard_map/all_to_all | solution.py:136
  314.2 13.8 %all-to-all-done.25 = bf16[128,2,512]{2,1,0:T(2,128)(2,1)S(1)} async-done(((bf16[128,2,512]{2,1,0:T(2,128)(2,1)}), bf16[128,2,512]{2,1,0:T(2,128)(2,1)S(1)}, u32[]{:S(2)}, u32[]{:S(2)}) %all-to-all-start.25) | async-done | bytes 262176 | tf_op jit(solution)/shard_map/all_to_all | solution.py:137
  334.5 13.8 %all-to-all-done.26 = bf16[128,2,512]{2,1,0:T(2,128)(2,1)S(1)} async-done(((bf16[128,2,512]{2,1,0:T(2,128)(2,1)}), bf16[128,2,512]{2,1,0:T(2,128)(2,1)S(1)}, u32[]{:S(2)}, u32[]{:S(2)}) %all-to-all-start.26) | async-done | bytes 262176 | tf_op jit(solution)/shard_map/all_to_all | solution.py:138
  353.9 14.7 %all-to-all-done.2 = bf16[128,2,512]{2,1,0:T(2,128)(2,1)S(1)} async-done(((bf16[128,2,512]{2,1,0:T(2,128)(2,1)}), bf16[128,2,512]{2,1,0:T(2,128)(2,1)S(1)}, u32[]{:S(2)}, u32[]{:S(2)}) %all-to-all-start.2) | async-done | bytes 262176 | tf_op jit(solution)/shard_map/all_to_all | solution.py:134
  430.1 8.8 all-to-all-start.21
  439.9 14.8 %all-to-all-done.21 = bf16[2,128,512]{2,0,1:T(2,128)(2,1)S(1)} async-done(((bf16[2,128,512]{2,0,1:T(2,128)(2,1)}), bf16[2,128,512]{2,0,1:T(2,128)(2,1)S(1)}, u32[]{:S(2)}, u32[]{:S(2)}) %all-to-all-start.21) | async-done | bytes 262176 | tf_op jit(solution)/shard_map/all_to_all | solution.py:150
  460.2 14.8 %all-to-all-done.22 = bf16[2,128,512]{2,0,1:T(2,128)(2,1)S(1)} async-done(((bf16[2,128,512]{2,0,1:T(2,128)(2,1)}), bf16[2,128,512]{2,0,1:T(2,128)(2,1)S(1)}, u32[]{:S(2)}, u32[]{:S(2)}) %all-to-all-start.22) | async-done | bytes 262176 | tf_op jit(solution)/shard_map/all_to_all | solution.py:151
  480.5 14.8 %all-to-all-done.27 = bf16[2,128,512]{2,0,1:T(2,128)(2,1)S(1)} async-done(((bf16[2,128,512]{2,0,1:T(2,128)(2,1)}), bf16[2,128,512]{2,0,1:T(2,128)(2,1)S(1)}, u32[]{:S(2)}, u32[]{:S(2)}) %all-to-all-start.27) | async-done | bytes 262176 | tf_op jit(solution)/shard_map/all_to_all | solution.py:150
  506.5 9.2 all-to-all-done.28
  522.4 14.1 %all-to-all-done.23 = bf16[64,2,512]{2,1,0:T(2,128)(2,1)S(1)} async-done(((bf16[64,2,512]{2,1,0:T(2,128)(2,1)}), bf16[64,2,512]{2,1,0:T(2,128)(2,1)S(1)}, u32[]{:S(2)}, u32[]{:S(2)}) %all-to-all-start.23) | async-done | bytes 131104 | tf_op jit(solution)/shard_map/all_to_all | solution.py:162
  541.8 12.2 %all-to-all-done.29 = bf16[64,2,512]{2,1,0:T(2,128)(2,1)S(1)} async-done(((bf16[64,2,512]{2,1,0:T(2,128)(2,1)}), bf16[64,2,512]{2,1,0:T(2,128)(2,1)S(1)}, u32[]{:S(2)}, u32[]{:S(2)}) %all-to-all-start.29) | async-done | bytes 131104 | tf_op jit(solution)/shard_map/all_to_all | solution.py:162
  554.3 9.4 multiply_bitcast_fusion
  563.7 17.5 %copy.307 = f32[4096,1024]{1,0:T(8,128)} copy(f32[4096,1024]{0,1:T(8,128)} %multiply_bitcast_fusion) | data formatting | bytes 33554432
  587.6 14.3 %all-to-all-done.31 = bf16[2,128,512]{2,0,1:T(2,128)(2,1)S(1)} async-done(((bf16[2,128,512]{2,0,1:T(2,128)(2,1)}), bf16[2,128,512]{2,0,1:T(2,128)(2,1)S(1)}, u32[]{:S(2)}, u32[]{:S(2)}) %all-to-all-start.31) | async-done | bytes 262176 | tf_op jit(solution)/shard_map/all_to_all | solution.py:153
  601.9 6.3 all-to-all-start.30
  609.0 12.7 %all-to-all-done.30 = bf16[2,128,512]{2,0,1:T(2,128)(2,1)S(1)} async-done(((bf16[2,128,512]{2,0,1:T(2,128)(2,1)}), bf16[2,128,512]{2,0,1:T(2,128)(2,1)S(1)}, u32[]{:S(2)}, u32[]{:S(2)}) %all-to-all-start.30) | async-done | bytes 262176 | tf_op jit(solution)/shard_map/all_to_all | solution.py:152
  627.9 14.9 %all-to-all-done.6 = bf16[2,128,512]{2,0,1:T(2,128)(2,1)S(1)} async-done(((bf16[2,128,512]{2,0,1:T(2,128)(2,1)}), bf16[2,128,512]{2,0,1:T(2,128)(2,1)S(1)}, u32[]{:S(2)}, u32[]{:S(2)}) %all-to-all-start.6) | async-done | bytes 262176 | tf_op jit(solution)/shard_map/all_to_all | solution.py:148
  642.8 5.6 all-to-all-start.7
  649.3 15.2 %all-to-all-done.7 = bf16[2,128,512]{2,0,1:T(2,128)(2,1)S(1)} async-done(((bf16[2,128,512]{2,0,1:T(2,128)(2,1)}), bf16[2,128,512]{2,0,1:T(2,128)(2,1)S(1)}, u32[]{:S(2)}, u32[]{:S(2)}) %all-to-all-start.7) | async-done | bytes 262176 | tf_op jit(solution)/shard_map/all_to_all | solution.py:149
  664.5 5.9 all-to-all-start.15
  671.3 15.9 %all-to-all-done.15 = bf16[2,128,512]{2,0,1:T(2,128)(2,1)S(1)} async-done(((bf16[2,128,512]{2,0,1:T(2,128)(2,1)}), bf16[2,128,512]{2,0,1:T(2,128)(2,1)S(1)}, u32[]{:S(2)}, u32[]{:S(2)}) %all-to-all-start.15) | async-done | bytes 262176 | tf_op jit(solution)/shard_map/all_to_all | solution.py:148
  687.1 6.3 all-to-all-start.16
  694.3 13.7 %all-to-all-done.16 = bf16[2,128,512]{2,0,1:T(2,128)(2,1)S(1)} async-done(((bf16[2,128,512]{2,0,1:T(2,128)(2,1)}), bf16[2,128,512]{2,0,1:T(2,128)(2,1)S(1)}, u32[]{:S(2)}, u32[]{:S(2)}) %all-to-all-start.16) | async-done | bytes 262176 | tf_op jit(solution)/shard_map/all_to_all | solution.py:149
  714.3 15.5 %all-to-all-done.33 = bf16[2,128,512]{2,0,1:T(2,128)(2,1)S(1)} async-done(((bf16[2,128,512]{2,0,1:T(2,128)(2,1)}), bf16[2,128,512]{2,0,1:T(2,128)(2,1)S(1)}, u32[]{:S(2)}, u32[]{:S(2)}) %all-to-all-start.33) | async-done | bytes 262176 | tf_op jit(solution)/shard_map/all_to_all | solution.py:152
  729.8 5.6 all-to-all-start.34
  737.9 11.7 %all-to-all-done.34 = bf16[2,128,512]{2,0,1:T(2,128)(2,1)S(1)} async-done(((bf16[2,128,512]{2,0,1:T(2,128)(2,1)}), bf16[2,128,512]{2,0,1:T(2,128)(2,1)S(1)}, u32[]{:S(2)}, u32[]{:S(2)}) %all-to-all-start.34) | async-done | bytes 262176 | tf_op jit(solution)/shard_map/all_to_all | solution.py:153
  749.6 5.9 all-to-all-start.32
  757.7 12.0 %all-to-all-done.32 = bf16[64,2,512]{2,1,0:T(2,128)(2,1)S(1)} async-done(((bf16[64,2,512]{2,1,0:T(2,128)(2,1)}), bf16[64,2,512]{2,1,0:T(2,128)(2,1)S(1)}, u32[]{:S(2)}, u32[]{:S(2)}) %all-to-all-start.32) | async-done | bytes 131104 | tf_op jit(solution)/shard_map/all_to_all | solution.py:163
  776.6 11.6 %all-to-all-done.8 = bf16[64,2,512]{2,1,0:T(2,128)(2,1)S(1)} async-done(((bf16[64,2,512]{2,1,0:T(2,128)(2,1)}), bf16[64,2,512]{2,1,0:T(2,128)(2,1)S(1)}, u32[]{:S(2)}, u32[]{:S(2)}) %all-to-all-start.8) | async-done | bytes 131104 | tf_op jit(solution)/shard_map/all_to_all | solution.py:161
  794.8 10.5 all-to-all-done.17
  805.2 5.7 all-to-all-start.35
  811.1 14.8 %all-to-all-done.35 = bf16[64,2,512]{2,1,0:T(2,128)(2,1)S(1)} async-done(((bf16[64,2,512]{2,1,0:T(2,128)(2,1)}), bf16[64,2,512]{2,1,0:T(2,128)(2,1)S(1)}, u32[]{:S(2)}, u32[]{:S(2)}) %all-to-all-start.35) | async-done | bytes 131104 | tf_op jit(solution)/shard_map/all_to_all | solution.py:163
  828.3 217.3 %reduce-scatter.4.cloned.1.call-done = f32[64,1024]{1,0:T(8,128)} async-done(((f32[4096,1024]{1,0:T(8,128)}), f32[64,1024]{1,0:T(8,128)}) %reduce-scatter.4.cloned.1.call-update) | async-done | bytes 262160
  (246 shorter events, 266.1 us)
Async XLA Ops:
  11.0 27.7 %all-to-all-start.12 = ((bf16[64,2,512]{2,1,0:T(2,128)(2,1)}), bf16[64,2,512]{2,1,0:T(2,128)(2,1)S(1)}, u32[]{:S(2)}, u32[]{:S(2)}) async-start(bf16[64,2,512]{2,1,0:T(2,128)(2,1)} %reshape.180), calls=%async_computation.12 | async-start | bytes 262144 | tf_op jit(solution)/shard_map/all_to_all | solution.py:126
  38.7 26.5 %all-to-all-start.3 = ((bf16[64,2,512]{2,1,0:T(2,128)(2,1)}), bf16[64,2,512]{2,1,0:T(2,128)(2,1)S(1)}, u32[]{:S(2)}, u32[]{:S(2)}) async-start(bf16[64,2,512]{2,1,0:T(2,128)(2,1)} %reshape.184), calls=%async_computation.3 | async-start | bytes 262144 | tf_op jit(solution)/shard_map/all_to_all | solution.py:126
  65.3 18.0 %all-to-all-start.9 = ((bf16[64,2,512]{2,1,0:T(2,128)(2,1)}), bf16[64,2,512]{2,1,0:T(2,128)(2,1)S(1)}, u32[]{:S(2)}, u32[]{:S(2)}) async-start(bf16[64,2,512]{2,1,0:T(2,128)(2,1)} %reshape.178), calls=%async_computation.9 | async-start | bytes 262144 | tf_op jit(solution)/shard_map/all_to_all | solution.py:125
  83.3 17.6 %all-to-all-start = ((bf16[64,2,512]{2,1,0:T(2,128)(2,1)}), bf16[64,2,512]{2,1,0:T(2,128)(2,1)S(1)}, u32[]{:S(2)}, u32[]{:S(2)}) async-start(bf16[64,2,512]{2,1,0:T(2,128)(2,1)} %reshape.182), calls=%async_computation | async-start | bytes 262144 | tf_op jit(solution)/shard_map/all_to_all | solution.py:125
  100.9 17.8 %all-to-all-start.24 = ((bf16[64,2,512]{2,1,0:T(2,128)(2,1)}), bf16[64,2,512]{2,1,0:T(2,128)(2,1)}, u32[]{:S(2)}, u32[]{:S(2)}) async-start(bf16[64,2,512]{2,1,0:T(2,128)(2,1)} %reshape.186), calls=%async_computation.24 | async-start | bytes 262144 | tf_op jit(solution)/shard_map/all_to_all | solution.py:127
  118.7 17.9 %all-to-all-start.18 = ((bf16[64,2,512]{2,1,0:T(2,128)(2,1)}), bf16[64,2,512]{2,1,0:T(2,128)(2,1)S(1)}, u32[]{:S(2)}, u32[]{:S(2)}) async-start(bf16[64,2,512]{2,1,0:T(2,128)(2,1)} %reshape.188), calls=%async_computation.18 | async-start | bytes 262144 | tf_op jit(solution)/shard_map/all_to_all | solution.py:127
  143.5 21.9 %all-to-all-start.20 = ((bf16[128,2,512]{2,1,0:T(2,128)(2,1)}), bf16[128,2,512]{2,1,0:T(2,128)(2,1)S(1)}, u32[]{:S(2)}, u32[]{:S(2)}) async-start(bf16[128,2,512]{2,1,0:T(2,128)(2,1)} %copy.270), calls=%async_computation.20 | async-start | bytes 524288 | tf_op jit(solution)/shard_map/all_to_all | solution.py:138
  165.3 20.3 %all-to-all-start.19 = ((bf16[128,2,512]{2,1,0:T(2,128)(2,1)}), bf16[128,2,512]{2,1,0:T(2,128)(2,1)S(1)}, u32[]{:S(2)}, u32[]{:S(2)}) async-start(bf16[128,2,512]{2,1,0:T(2,128)(2,1)} %copy.267), calls=%async_computation.19 | async-start | bytes 524288 | tf_op jit(solution)/shard_map/all_to_all | solution.py:137
  185.7 20.3 %all-to-all-start.4 = ((bf16[128,2,512]{2,1,0:T(2,128)(2,1)}), bf16[128,2,512]{2,1,0:T(2,128)(2,1)S(1)}, u32[]{:S(2)}, u32[]{:S(2)}) async-start(bf16[128,2,512]{2,1,0:T(2,128)(2,1)} %copy.222), calls=%async_computation.4 | async-start | bytes 524288 | tf_op jit(solution)/shard_map/all_to_all | solution.py:135
  206.0 20.3 %all-to-all-start.5 = ((bf16[128,2,512]{2,1,0:T(2,128)(2,1)}), bf16[128,2,512]{2,1,0:T(2,128)(2,1)S(1)}, u32[]{:S(2)}, u32[]{:S(2)}) async-start(bf16[128,2,512]{2,1,0:T(2,128)(2,1)} %copy.225), calls=%async_computation.5 | async-start | bytes 524288 | tf_op jit(solution)/shard_map/all_to_all | solution.py:136
  226.3 20.3 %all-to-all-start.11 = ((bf16[128,2,512]{2,1,0:T(2,128)(2,1)}), bf16[128,2,512]{2,1,0:T(2,128)(2,1)S(1)}, u32[]{:S(2)}, u32[]{:S(2)}) async-start(bf16[128,2,512]{2,1,0:T(2,128)(2,1)} %copy.243), calls=%async_computation.11 | async-start | bytes 524288 | tf_op jit(solution)/shard_map/all_to_all | solution.py:134
  246.7 20.3 %all-to-all-start.10 = ((bf16[128,2,512]{2,1,0:T(2,128)(2,1)}), bf16[128,2,512]{2,1,0:T(2,128)(2,1)S(1)}, u32[]{:S(2)}, u32[]{:S(2)}) async-start(bf16[128,2,512]{2,1,0:T(2,128)(2,1)} %copy.240), calls=%async_computation.10 | async-start | bytes 524288 | tf_op jit(solution)/shard_map/all_to_all | solution.py:133
  267.0 20.3 %all-to-all-start.13 = ((bf16[128,2,512]{2,1,0:T(2,128)(2,1)}), bf16[128,2,512]{2,1,0:T(2,128)(2,1)S(1)}, u32[]{:S(2)}, u32[]{:S(2)}) async-start(bf16[128,2,512]{2,1,0:T(2,128)(2,1)} %copy.249), calls=%async_computation.13 | async-start | bytes 524288 | tf_op jit(solution)/shard_map/all_to_all | solution.py:135
  287.3 20.3 %all-to-all-start.14 = ((bf16[128,2,512]{2,1,0:T(2,128)(2,1)}), bf16[128,2,512]{2,1,0:T(2,128)(2,1)S(1)}, u32[]{:S(2)}, u32[]{:S(2)}) async-start(bf16[128,2,512]{2,1,0:T(2,128)(2,1)} %copy.252), calls=%async_computation.14 | async-start | bytes 524288 | tf_op jit(solution)/shard_map/all_to_all | solution.py:136
  307.7 20.3 %all-to-all-start.25 = ((bf16[128,2,512]{2,1,0:T(2,128)(2,1)}), bf16[128,2,512]{2,1,0:T(2,128)(2,1)S(1)}, u32[]{:S(2)}, u32[]{:S(2)}) async-start(bf16[128,2,512]{2,1,0:T(2,128)(2,1)} %copy.283), calls=%async_computation.25 | async-start | bytes 524288 | tf_op jit(solution)/shard_map/all_to_all | solution.py:137
  328.0 20.3 %all-to-all-start.26 = ((bf16[128,2,512]{2,1,0:T(2,128)(2,1)}), bf16[128,2,512]{2,1,0:T(2,128)(2,1)S(1)}, u32[]{:S(2)}, u32[]{:S(2)}) async-start(bf16[128,2,512]{2,1,0:T(2,128)(2,1)} %copy.286), calls=%async_computation.26 | async-start | bytes 524288 | tf_op jit(solution)/shard_map/all_to_all | solution.py:138
  348.3 20.3 %all-to-all-start.2 = ((bf16[128,2,512]{2,1,0:T(2,128)(2,1)}), bf16[128,2,512]{2,1,0:T(2,128)(2,1)S(1)}, u32[]{:S(2)}, u32[]{:S(2)}) async-start(bf16[128,2,512]{2,1,0:T(2,128)(2,1)} %copy.216), calls=%async_computation.2 | async-start | bytes 524288 | tf_op jit(solution)/shard_map/all_to_all | solution.py:134
  368.7 20.3 %all-to-all-start.1 = ((bf16[128,2,512]{2,1,0:T(2,128)(2,1)}), bf16[128,2,512]{2,1,0:T(2,128)(2,1)S(1)}, u32[]{:S(2)}, u32[]{:S(2)}) async-start(bf16[128,2,512]{2,1,0:T(2,128)(2,1)} %copy.213), calls=%async_computation.1 | async-start | bytes 524288 | tf_op jit(solution)/shard_map/all_to_all | solution.py:133
  419.8 134.3 %copy-start.1 = (bf16[128,1024]{1,0:T(8,128)(2,1)S(1)}, bf16[128,1024]{1,0:T(8,128)(2,1)}, u32[]{:S(2)}) copy-start(bf16[128,1024]{1,0:T(8,128)(2,1)} %param.8) | copy-start | bytes 786436
  430.1 24.5 %all-to-all-start.21 = ((bf16[2,128,512]{2,0,1:T(2,128)(2,1)}), bf16[2,128,512]{2,0,1:T(2,128)(2,1)S(1)}, u32[]{:S(2)}, u32[]{:S(2)}) async-start(bf16[2,128,512]{2,0,1:T(2,128)(2,1)} %copy.275), calls=%async_computation.21 | async-start | bytes 524288 | tf_op jit(solution)/shard_map/all_to_all | solution.py:150
  454.7 20.3 %all-to-all-start.22 = ((bf16[2,128,512]{2,0,1:T(2,128)(2,1)}), bf16[2,128,512]{2,0,1:T(2,128)(2,1)S(1)}, u32[]{:S(2)}, u32[]{:S(2)}) async-start(bf16[2,128,512]{2,0,1:T(2,128)(2,1)} %copy.277), calls=%async_computation.22 | async-start | bytes 524288 | tf_op jit(solution)/shard_map/all_to_all | solution.py:151
  475.0 20.3 %all-to-all-start.27 = ((bf16[2,128,512]{2,0,1:T(2,128)(2,1)}), bf16[2,128,512]{2,0,1:T(2,128)(2,1)S(1)}, u32[]{:S(2)}, u32[]{:S(2)}) async-start(bf16[2,128,512]{2,0,1:T(2,128)(2,1)} %copy.291), calls=%async_computation.27 | async-start | bytes 524288 | tf_op jit(solution)/shard_map/all_to_all | solution.py:150
  495.4 20.3 %all-to-all-start.28 = ((bf16[2,128,512]{2,0,1:T(2,128)(2,1)}), bf16[2,128,512]{2,0,1:T(2,128)(2,1)S(1)}, u32[]{:S(2)}, u32[]{:S(2)}) async-start(bf16[2,128,512]{2,0,1:T(2,128)(2,1)} %copy.293), calls=%async_computation.28 | async-start | bytes 524288 | tf_op jit(solution)/shard_map/all_to_all | solution.py:151
  500.0 54.3 %all-gather.2.cloned.1.call-start = ((), (), s32[]{:S(2)}) async-start(), calls=%async_computation.37 | async-start | bytes 1310720 | tf_op jit(solution)/shard_map/all_gather | solution.py:114
  515.7 20.7 %all-to-all-start.23 = ((bf16[64,2,512]{2,1,0:T(2,128)(2,1)}), bf16[64,2,512]{2,1,0:T(2,128)(2,1)S(1)}, u32[]{:S(2)}, u32[]{:S(2)}) async-start(bf16[64,2,512]{2,1,0:T(2,128)(2,1)} %copy.279), calls=%async_computation.23 | async-start | bytes 262144 | tf_op jit(solution)/shard_map/all_to_all | solution.py:162
  536.4 17.6 %all-to-all-start.29 = ((bf16[64,2,512]{2,1,0:T(2,128)(2,1)}), bf16[64,2,512]{2,1,0:T(2,128)(2,1)S(1)}, u32[]{:S(2)}, u32[]{:S(2)}) async-start(bf16[64,2,512]{2,1,0:T(2,128)(2,1)} %copy.295), calls=%async_computation.29 | async-start | bytes 262144 | tf_op jit(solution)/shard_map/all_to_all | solution.py:162
  541.7 503.9 %reduce-scatter.4.cloned.1.call-start = ((), (), s32[]{:S(2)}) async-start(), calls=%async_computation.38 | async-start | bytes 17039360
  554.2 26.9 %copy-start = (bf16[128,1024]{1,0:T(8,128)(2,1)}, bf16[128,1024]{1,0:T(8,128)(2,1)S(1)}, u32[]{:S(2)}) copy-start(bf16[128,1024]{1,0:T(8,128)(2,1)S(1)} %pad_maximum_fusion) | copy-start | bytes 786436
  581.2 245.6 %copy-start.2 = (bf16[128,1024]{1,0:T(8,128)(2,1)S(1)}, bf16[128,1024]{1,0:T(8,128)(2,1)}, u32[]{:S(2)}) copy-start(bf16[128,1024]{1,0:T(8,128)(2,1)} %param.9) | copy-start | bytes 786436
  581.2 246.4 %copy-start.3 = (bf16[128,1024]{1,0:T(8,128)(2,1)S(1)}, bf16[128,1024]{1,0:T(8,128)(2,1)}, u32[]{:S(2)}) copy-start(bf16[128,1024]{1,0:T(8,128)(2,1)} %param.10) | copy-start | bytes 786436
  582.1 19.8 %all-to-all-start.31 = ((bf16[2,128,512]{2,0,1:T(2,128)(2,1)}), bf16[2,128,512]{2,0,1:T(2,128)(2,1)S(1)}, u32[]{:S(2)}, u32[]{:S(2)}) async-start(bf16[2,128,512]{2,0,1:T(2,128)(2,1)} %copy.298), calls=%async_computation.31 | async-start | bytes 524288 | tf_op jit(solution)/shard_map/all_to_all | solution.py:153
  601.9 19.9 %all-to-all-start.30 = ((bf16[2,128,512]{2,0,1:T(2,128)(2,1)}), bf16[2,128,512]{2,0,1:T(2,128)(2,1)S(1)}, u32[]{:S(2)}, u32[]{:S(2)}) async-start(bf16[2,128,512]{2,0,1:T(2,128)(2,1)} %copy.296), calls=%async_computation.30 | async-start | bytes 524288 | tf_op jit(solution)/shard_map/all_to_all | solution.py:152
  621.7 21.1 %all-to-all-start.6 = ((bf16[2,128,512]{2,0,1:T(2,128)(2,1)}), bf16[2,128,512]{2,0,1:T(2,128)(2,1)S(1)}, u32[]{:S(2)}, u32[]{:S(2)}) async-start(bf16[2,128,512]{2,0,1:T(2,128)(2,1)} %copy.232), calls=%async_computation.6 | async-start | bytes 524288 | tf_op jit(solution)/shard_map/all_to_all | solution.py:148
  642.8 21.7 %all-to-all-start.7 = ((bf16[2,128,512]{2,0,1:T(2,128)(2,1)}), bf16[2,128,512]{2,0,1:T(2,128)(2,1)S(1)}, u32[]{:S(2)}, u32[]{:S(2)}) async-start(bf16[2,128,512]{2,0,1:T(2,128)(2,1)} %copy.234), calls=%async_computation.7 | async-start | bytes 524288 | tf_op jit(solution)/shard_map/all_to_all | solution.py:149
  664.5 22.6 %all-to-all-start.15 = ((bf16[2,128,512]{2,0,1:T(2,128)(2,1)}), bf16[2,128,512]{2,0,1:T(2,128)(2,1)S(1)}, u32[]{:S(2)}, u32[]{:S(2)}) async-start(bf16[2,128,512]{2,0,1:T(2,128)(2,1)} %copy.259), calls=%async_computation.15 | async-start | bytes 524288 | tf_op jit(solution)/shard_map/all_to_all | solution.py:148
  687.1 20.9 %all-to-all-start.16 = ((bf16[2,128,512]{2,0,1:T(2,128)(2,1)}), bf16[2,128,512]{2,0,1:T(2,128)(2,1)S(1)}, u32[]{:S(2)}, u32[]{:S(2)}) async-start(bf16[2,128,512]{2,0,1:T(2,128)(2,1)} %copy.261), calls=%async_computation.16 | async-start | bytes 524288 | tf_op jit(solution)/shard_map/all_to_all | solution.py:149
  708.0 21.8 %all-to-all-start.33 = ((bf16[2,128,512]{2,0,1:T(2,128)(2,1)}), bf16[2,128,512]{2,0,1:T(2,128)(2,1)S(1)}, u32[]{:S(2)}, u32[]{:S(2)}) async-start(bf16[2,128,512]{2,0,1:T(2,128)(2,1)} %copy.301), calls=%async_computation.33 | async-start | bytes 524288 | tf_op jit(solution)/shard_map/all_to_all | solution.py:152
  729.8 19.7 %all-to-all-start.34 = ((bf16[2,128,512]{2,0,1:T(2,128)(2,1)}), bf16[2,128,512]{2,0,1:T(2,128)(2,1)S(1)}, u32[]{:S(2)}, u32[]{:S(2)}) async-start(bf16[2,128,512]{2,0,1:T(2,128)(2,1)} %copy.303), calls=%async_computation.34 | async-start | bytes 524288 | tf_op jit(solution)/shard_map/all_to_all | solution.py:153
  749.6 20.1 %all-to-all-start.32 = ((bf16[64,2,512]{2,1,0:T(2,128)(2,1)}), bf16[64,2,512]{2,1,0:T(2,128)(2,1)S(1)}, u32[]{:S(2)}, u32[]{:S(2)}) async-start(bf16[64,2,512]{2,1,0:T(2,128)(2,1)} %copy.300), calls=%async_computation.32 | async-start | bytes 262144 | tf_op jit(solution)/shard_map/all_to_all | solution.py:163
  769.7 18.6 %all-to-all-start.8 = ((bf16[64,2,512]{2,1,0:T(2,128)(2,1)}), bf16[64,2,512]{2,1,0:T(2,128)(2,1)S(1)}, u32[]{:S(2)}, u32[]{:S(2)}) async-start(bf16[64,2,512]{2,1,0:T(2,128)(2,1)} %copy.236), calls=%async_computation.8 | async-start | bytes 262144 | tf_op jit(solution)/shard_map/all_to_all | solution.py:161
  788.3 17.0 %all-to-all-start.17 = ((bf16[64,2,512]{2,1,0:T(2,128)(2,1)}), bf16[64,2,512]{2,1,0:T(2,128)(2,1)S(1)}, u32[]{:S(2)}, u32[]{:S(2)}) async-start(bf16[64,2,512]{2,1,0:T(2,128)(2,1)} %copy.263), calls=%async_computation.17 | async-start | bytes 262144 | tf_op jit(solution)/shard_map/all_to_all | solution.py:161
  805.2 20.7 %all-to-all-start.35 = ((bf16[64,2,512]{2,1,0:T(2,128)(2,1)}), bf16[64,2,512]{2,1,0:T(2,128)(2,1)S(1)}, u32[]{:S(2)}, u32[]{:S(2)}) async-start(bf16[64,2,512]{2,1,0:T(2,128)(2,1)} %copy.305), calls=%async_computation.35 | async-start | bytes 262144 | tf_op jit(solution)/shard_map/all_to_all | solution.py:163
Sparse Core Ops, SparseCore 0:
  502.6 35.6 all-gather.1
  581.3 464.2 reduce-scatter.3
where the time goes:
time: 1060 us; the launch traced here: 1050 us
  waiting for transfers between devices  666 us (63%)
  starting transfers between devices  203 us (19%)
  local copies, waits for them, and re-layouts  89.6 us (8%)
  matrix products  65.5 us (6%)
  between operations  15.8 us (1%)
  other arithmetic  13.2 us (1%)
    unnamed x3, waiting for transfers between devices  218 us
    dot_general x72, matrix products, mixed_sum(): return jnp.einsum(form, matrix, operand, precision=FULL_PRECISION)  56.1 us
    all_to_all x2, waiting for transfers between devices, shards(): lax.all_to_all(rowed[0], 'seq', split_axis=1, concat_axis=0, tiled=True)  30.8 us
    all_to_all x2, waiting for transfers between devices, shards(): lax.all_to_all(rowed[2], 'seq', split_axis=1, concat_axis=0, tiled=True)  29.6 us
    all_to_all x2, waiting for transfers between devices, shards(): lax.all_to_all(rowed[1], 'seq', split_axis=1, concat_axis=0, tiled=True)  28.9 us
    all_to_all x2, waiting for transfers between devices, shards(): lax.all_to_all(turned[1], 'seq', split_axis=0, concat_axis=1, tiled=True)  28.5 us
    all_to_all x2, waiting for transfers between devices, shards(): lax.all_to_all(rowed[4], 'seq', split_axis=1, concat_axis=0, tiled=True)  28.2 us
    all_to_all x2, waiting for transfers between devices, shards(): lax.all_to_all(turned[4], 'seq', split_axis=0, concat_axis=1, tiled=True)  27.6 us
  transfers between devices with their start and end apart: 38, of which 36 were waited for; matrix products, arithmetic and copies ran while one was open for 8% of the time, Pallas kernels for 0%

commit v1 on v0

v1 whole, which is shorter than its diff:
```python
import math

import numpy as np

import jax
import jax.numpy as jnp
from jax import lax
from jax.experimental import pallas as pl
from jax.experimental.pallas import tpu as pltpu
from jax.sharding import PartitionSpec as P

BLOCKS = 64
ROWS = 128
CHANNELS = 16
LANES = 3 * CHANNELS
PERIOD = 2 * BLOCKS * ROWS
LAST_SCALE = 1.0 / PERIOD
ROOT_SCALE = 1.0 / math.sqrt(BLOCKS * ROWS)
NEAR = [[8 * g + i for i in range(8)] for g in range(8)]
FAR = [[g + 8 * i for i in range(8)] for g in range(8)]


def split_table(table):
    high = table.astype(jnp.bfloat16)
    low = (table - high.astype(np.float64)).astype(jnp.bfloat16)
    return high, low


def make_tables():
    freq = np.arange(2 * BLOCKS)
    block = np.arange(BLOCKS)
    row = np.arange(ROWS)
    outer = 2.0 * math.pi * (freq[:, None] * block[None, :] % (2 * BLOCKS)) / (2 * BLOCKS)
    first = np.concatenate([np.cos(outer), -np.sin(outer)], axis=0)
    first = np.concatenate(split_table(first), axis=1)
    last = np.concatenate([np.cos(outer).T, -np.sin(outer).T], axis=1)
    last = np.concatenate(split_table(last), axis=0)
    twist = 2.0 * math.pi * (freq[:, None] * row[None, :] % PERIOD) / PERIOD
    inner = 2.0 * math.pi * (row[:, None] * row[None, :] % ROWS) / ROWS
    cosine, sine = np.cos(inner), np.sin(inner)
    ahead = np.block([[cosine, -sine], [sine, cosine]])
    return (
        first,
        np.cos(twist).astype(np.float32),
        np.sin(twist).astype(np.float32),
        *split_table(ahead),
        *split_table(ahead.T),
        last,
    )


def product(left, right):
    return lax.dot_general(left, right, (((1,), (0,)), ((), ())), preferred_element_type=jnp.float32)


def gather_body(key_ref, value_ref, grad_ref, query_ref, taps_ref, input_ref, sent_ref, features_ref):
    for part in range(8):
        cols = pl.ds(part * 128, 128)
        mixed = key_ref[:, cols].astype(jnp.float32) * value_ref[:, cols].astype(jnp.float32)
        gated = grad_ref[:, cols].astype(jnp.float32) * query_ref[:, cols].astype(jnp.float32)
        for place, signal in enumerate((mixed, taps_ref[:, cols].astype(jnp.float32), gated)):
            turned = signal.T.astype(jnp.bfloat16)
            sent_ref[pl.ds(part * 8, 8), pl.ds(place * 16, 16), :] = turned.reshape(8, 16, 128)
    for near in range(8):
        features_ref[near] = jnp.concatenate(
            [input_ref[:, near * 64 : near * 64 + 64], input_ref[:, 512 + near * 64 : 576 + near * 64]],
            axis=1,
        )


def gather_signals(gate_key, value_proj, grad_out, gate_query, filter_taps, layer_input):
    return pl.pallas_call(
        gather_body,
        out_shape=(
            jax.ShapeDtypeStruct((BLOCKS, LANES, ROWS), jnp.bfloat16),
            jax.ShapeDtypeStruct((8, ROWS, 128), jnp.bfloat16),
        ),
        name="gather_signals",
    )(gate_key, value_proj, grad_out, gate_query, filter_taps, layer_input)


UNROLL = 2


def convolve_body(
    signals_ref, first_ref, cos_ref, sin_ref, ahead_ref, ahead_low_ref, back_ref, back_low_ref, last_ref,
    out_ref, wide_in, wide_out,
):
    wide_in[...] = signals_ref[...].astype(jnp.float32).reshape(BLOCKS * LANES, ROWS)
    first = first_ref[...]
    cosine = cos_ref[...]
    sine = sin_ref[...]

    def channel(place):
        rows = jnp.concatenate(
            [wide_in[pl.ds(place + CHANNELS * s, BLOCKS, stride=LANES), :] for s in range(3)], axis=1
        ).astype(jnp.bfloat16)
        outer = product(first, jnp.concatenate([rows, rows], axis=0))
        turned = []
        for s in range(3):
            real_part = outer[:128, s * 128 : s * 128 + 128]
            other_part = outer[128:, s * 128 : s * 128 + 128]
            turned_real = (real_part * cosine + other_part * sine).astype(jnp.bfloat16)
            turned_other = (other_part * cosine - real_part * sine).astype(jnp.bfloat16)
            turned.append(jnp.concatenate([turned_real, turned_other], axis=1))
        turned = jnp.concatenate(turned, axis=0)
        spectra = product(turned, ahead_ref[...]) + product(turned, ahead_low_ref[...])
        mixed_real, mixed_other = spectra[:128, :128], spectra[:128, 128:]
        taps_real, taps_other = spectra[128:256, :128], spectra[128:256, 128:]
        gated_real, gated_other = spectra[256:, :128], spectra[256:, 128:]
        pairs = jnp.concatenate(
            [
                jnp.concatenate(pair, axis=1)
                for pair in (
                    (
                        mixed_real * taps_real - mixed_other * taps_other,
                        mixed_real * taps_other + mixed_other * taps_real,
                    ),
                    (
                        gated_real * taps_real + gated_other * taps_other,
                        gated_other * taps_real - gated_real * taps_other,
                    ),
                    (
                        gated_real * mixed_real + gated_other * mixed_other,
                        gated_other * mixed_real - gated_real * mixed_other,
                    ),
                )
            ],
            axis=0,
        )
        high = pairs.astype(jnp.bfloat16)
        low = (pairs - high.astype(jnp.float32)).astype(jnp.bfloat16)
        rowed = (
            product(high, back_ref[...]) + product(low, back_ref[...]) + product(high, back_low_ref[...])
        )
        bent = []
        for s in range(3):
            real_part = rowed[s * 128 : s * 128 + 128, :128]
            other_part = rowed[s * 128 : s * 128 + 128, 128:]
            bent_real = (real_part * cosine - other_part * sine).astype(jnp.bfloat16)
            bent_other = (real_part * sine + other_part * cosine).astype(jnp.bfloat16)
            bent.append(jnp.concatenate([bent_real, bent_other], axis=0))
        total = product(last_ref[...], jnp.concatenate(bent, axis=1))
        total = total[:BLOCKS] + total[BLOCKS:]
        for s in range(3):
            factor = LAST_SCALE * (ROOT_SCALE if s == 2 else 1.0)
            wide_out[pl.ds(place + CHANNELS * s, BLOCKS, stride=LANES), :] = (
                total[:, s * 128 : s * 128 + 128] * factor
            )

    def step(index, carry):
        for inside in range(UNROLL):
            channel(index * UNROLL + inside)
        return carry

    lax.fori_loop(0, CHANNELS // UNROLL, step, 0)
    out_ref[...] = wide_out[...].reshape(BLOCKS, LANES, ROWS).astype(jnp.bfloat16)


def convolve(signals, tables):
    return pl.pallas_call(
        convolve_body,
        out_shape=jax.ShapeDtypeStruct((BLOCKS, LANES, ROWS), jnp.bfloat16),
        scratch_shapes=[
            pltpu.VMEM((BLOCKS * LANES, ROWS), jnp.float32),
            pltpu.VMEM((BLOCKS * LANES, ROWS), jnp.float32),
        ],
        name="convolve",
    )(signals, *tables)


def finish_body(back_ref, grad_ref, value_ref, key_ref, query_out, key_out, value_out, filter_out):
    for part in range(8):
        cols = pl.ds(part * 128, 128)

        def turned(place):
            block = back_ref[pl.ds(part * 8, 8), pl.ds(place * 16, 16), :]
            return block.reshape(128, 128).astype(jnp.float32).T

        back = turned(1)
        query_out[:, cols] = (grad_ref[:, cols].astype(jnp.float32) * turned(0)).astype(jnp.bfloat16)
        key_out[:, cols] = (back * value_ref[:, cols].astype(jnp.float32)).astype(jnp.bfloat16)
        value_out[:, cols] = (back * key_ref[:, cols].astype(jnp.float32)).astype(jnp.bfloat16)
        filter_out[:, cols] = turned(2).astype(jnp.bfloat16)


def finish(returned, grad_out, value_proj, gate_key):
    shape = jax.ShapeDtypeStruct(grad_out.shape, jnp.bfloat16)
    return pl.pallas_call(finish_body, out_shape=(shape,) * 4, name="finish")(
        returned, grad_out, value_proj, gate_key
    )


def exchange(array, groups=None):
    return lax.all_to_all(
        array, "seq", split_axis=0, concat_axis=0, tiled=True, axis_index_groups=groups
    )


def shards(layer_input, gate_query, gate_key, value_proj, grad_out, filter_taps):
    tables = [jnp.asarray(table) for table in make_tables()]
    sent, features = gather_signals(
        gate_key, value_proj, grad_out, gate_query, filter_taps, layer_input
    )
    features = exchange(features, NEAR).reshape(8 * ROWS, 128)
    features = lax.all_gather(features, "chan", axis=0)
    results = exchange(convolve(exchange(sent), tables))
    grad_query, grad_key, grad_value, grad_filter = finish(results, grad_out, value_proj, gate_key)
    columns = lax.all_gather(grad_value, "seq", axis=0, tiled=True, axis_index_groups=NEAR)
    partial = jnp.einsum("cpf,pn->cfn", features, columns, preferred_element_type=jnp.float32)
    partial = partial.astype(jnp.bfloat16).reshape(8, 64, partial.shape[-1])
    grad_weight = jnp.sum(exchange(partial, FAR).astype(jnp.float32), axis=0) * ROOT_SCALE
    return (grad_query, grad_key, grad_value, grad_filter, grad_weight)


def solution(mesh):
    placed = P("seq", "chan")
    return jax.shard_map(
        shards,
        mesh=mesh,
        in_specs=(placed,) * 6,
        out_specs=(placed,) * 5,
        check_vma=False,
    )
```

time: 1060 us -> 186 us (0.18)
  waiting for transfers between devices: 666 us -> 50.2 us
  starting transfers between devices: 203 us -> 11.9 us
  local copies, waits for them, and re-layouts: 89.6 us -> 0.9 us
  blocking collectives: 0 us -> 81.2 us
  matrix products: 65.5 us -> 3.18 us
  Pallas kernels: 0 us -> 23.5 us
  other arithmetic: 13.2 us -> 0.9 us
    all_to_all x36 -> x1, waiting for transfers between devices: 448 us -> 26.8 us  [exchange(): lax.all_to_all(array, 'seq', split_axis=0, concat_axis=0, tiled=True, axi...]
    unnamed x3 -> x2, waiting for transfers between devices: 218 us -> 0.7 us
    all_to_all x36 -> x1, starting transfers between devices: 203 us -> 11.8 us  [exchange(): lax.all_to_all(array, 'seq', split_axis=0, concat_axis=0, tiled=True, axi...]
    all_to_all x0 -> x3, blocking collectives: none -> 81.2 us  [exchange(): lax.all_to_all(array, 'seq', split_axis=0, concat_axis=0, tiled=True, axi...]
    dot_general x73 -> x1, matrix products: 65.5 us -> 3.18 us  [shards(): jnp.einsum('cpf,pn->cfn', features, columns, preferred_element_type=jnp.f...]
    convert_element_type x30 -> x0, local copies, waits for them, and re-layouts: 36.5 us -> none  [the longest x12 21.2 us: outer_forward(): return (turned_real.astype(jnp.bfloat16), turned_other.astype(jnp.bfloat16))]
    all_to_all x60 -> x0, local copies, waits for them, and re-layouts: 26.4 us -> none  [the longest x4 3.15 us: shards(): lax.all_to_all(gated_part[None], 'seq', split_axis=1, concat_axis=0, tile...]
    pallas_call x0 -> x3, Pallas kernels: none -> 23.5 us  [the longest x1 18.2 us: convolve(): pl.pallas_call(convolve_body, out_shape=jax.ShapeDtypeStruct((BLOCKS, LAN...]
  transfers between devices with their start and end apart: 38 -> 3, of which waited for: 36 -> 2; matrix products, arithmetic and copies ran while one was open for 8% -> 0% of each run, Pallas kernels for 0% -> 11%
where the time goes in v1:
time: 186 us
  blocking collectives  81.2 us (44%)
  waiting for transfers between devices  50.2 us (27%)
  Pallas kernels  23.5 us (13%)
  between operations  14.1 us (8%)
  starting transfers between devices  11.9 us (6%)
  matrix products  3.18 us (2%)
    all_to_all x3, blocking collectives, exchange(): lax.all_to_all(array, 'seq', split_axis=0, concat_axis=0, tiled=True, axi...  81.2 us
    all_to_all x1, waiting for transfers between devices, exchange(): lax.all_to_all(array, 'seq', split_axis=0, concat_axis=0, tiled=True, axi...  26.8 us
    all_gather x1, waiting for transfers between devices, shards(): lax.all_gather(grad_value, 'seq', axis=0, tiled=True, axis_index_groups=N...  22.7 us
    pallas_call x1, Pallas kernels, convolve(): pl.pallas_call(convolve_body, out_shape=jax.ShapeDtypeStruct((BLOCKS, LAN...  18.2 us
    all_to_all x1, starting transfers between devices, exchange(): lax.all_to_all(array, 'seq', split_axis=0, concat_axis=0, tiled=True, axi...  11.8 us
  transfers between devices with their start and end apart: 3, of which 2 were waited for; matrix products, arithmetic and copies ran while one was open for 0% of the time, Pallas kernels for 11%

profile of v1, /device:TPU:32, one launch (start us, length us, event | category | flops | bytes accessed | tf_op | source)
XLA Modules:
  0.0 185.9 jit_solution(11855696337596494604)
XLA Ops:
  7.2 2.6 %gather_signals.1 = (bf16[64,48,128]{2,1,0:T(8,128)(2,1)}, bf16[8,128,128]{2,1,0:T(8,128)(2,1)}) custom-call(bf16[128,1024]{1,0:T(8,128)(2,1)} %key_ref.3, bf16[128,1024]{1,0:T(8,128)(2,1)} %value_ref.3, bf16[128,1024]{1,0:T(8,128)(2,1)} %grad_ref.3, bf16[128,1024]{1,0:T(8,128)(2,1)} %query_ref.1, bf16[128,1024]{1,0:T(8,128)(2,1)} %taps_ref.1, ...), custom_call_target="tpu_custom_call" | custom-call | tf_op jit(solution)/shard_map/gather_signals/pallas_call | solution.py:72
  9.8 11.9 %all_to_all.20 = bf16[8,128,128]{2,1,0:T(8,128)(2,1)} all-to-all(bf16[8,128,128]{2,1,0:T(8,128)(2,1)} %get-tuple-element.16), channel_id=1, replica_groups={{0,4,8,12,16,20,24,28},{32,36,40,44,48,52,56,60},{64,68,72,76,80,84,88,..., dimensions={0} | all-to-all | bytes 524288 | tf_op jit(solution)/shard_map/all_to_all | solution.py:195
  21.7 11.8 %all-to-all-start = ((bf16[64,48,128]{2,1,0:T(8,128)(2,1)}), bf16[64,48,128]{2,1,0:T(8,128)(2,1)S(1)}, u32[]{:S(2)}, u32[]{:S(2)}) async-start(bf16[64,48,128]{2,1,0:T(8,128)(2,1)} %get-tuple-element.11), calls=%async_computation | async-start | bytes 1572864 | tf_op jit(solution)/shard_map/all_to_all | solution.py:195
  33.5 0.0 all-gather.3.cloned.1.call-start
  33.6 0.7 all-gather.3.cloned.1.call-update
  34.2 0.0 all-gather.5.cloned.1.call-start
  34.3 26.8 %all-to-all-done.signals_ref = bf16[64,48,128]{2,1,0:T(8,128)(2,1)S(1)} async-done(((bf16[64,48,128]{2,1,0:T(8,128)(2,1)}), bf16[64,48,128]{2,1,0:T(8,128)(2,1)S(1)}, u32[]{:S(2)}, u32[]{:S(2)}) %all-to-all-start) | async-done | bytes 786464 | tf_op jit(solution)/shard_map/all_to_all | solution.py:195
  61.1 0.0 copy-start
  61.1 0.9 copy-done
  62.0 18.2 %convolve.1 = bf16[64,48,128]{2,1,0:T(8,128)(2,1)} custom-call(bf16[64,48,128]{2,1,0:T(8,128)(2,1)} %copy-done, bf16[256,128]{1,0:T(8,128)(2,1)} %constant.20.clone.first_ref, f32[128,128]{1,0:T(8,128)} %constant.21.clone.cos_ref, f32[128,128]{1,0:T(8,128)} %constant.22.clone.sin_ref, bf16[256,256]{1,0:T(8,128)(2,1)} %constant.23.clone.ahead_ref, ...), custom_call_target="tpu_custom_call" | custom-call | tf_op jit(solution)/shard_map/convolve/pallas_call | solution.py:161
  80.2 30.1 %all_to_all.21.back_ref = bf16[64,48,128]{2,1,0:T(8,128)(2,1)} all-to-all(bf16[64,48,128]{2,1,0:T(8,128)(2,1)} %convolve.1), channel_id=1, replica_groups=mesh['seq'=64,'chan'=4] {'seq'}, dimensions={0} | all-to-all | bytes 1572864 | tf_op jit(solution)/shard_map/all_to_all | solution.py:195
  110.3 2.6 %finish.1 = (bf16[128,1024]{1,0:T(8,128)(2,1)}, bf16[128,1024]{1,0:T(8,128)(2,1)}, bf16[128,1024]{1,0:T(8,128)(2,1)}, bf16[128,1024]{1,0:T(8,128)(2,1)}) custom-call(bf16[64,48,128]{2,1,0:T(8,128)(2,1)} %all_to_all.21.back_ref, bf16[128,1024]{1,0:T(8,128)(2,1)} %grad_ref.3, bf16[128,1024]{1,0:T(8,128)(2,1)} %value_ref.3, bf16[128,1024]{1,0:T(8,128)(2,1)} %key_ref.3), custom_call_target="tpu_custom_call" | custom-call | tf_op jit(solution)/shard_map/finish/pallas_call | solution.py:189
  113.0 0.0 all-gather.5.cloned.1.call-update
  113.0 0.0 all-gather.3.cloned.1.call-done
  113.0 22.7 %all-gather.5.cloned.1.call-done = bf16[1024,1024]{1,0:T(8,128)(2,1)} async-done(((bf16[128,1024]{1,0:T(8,128)(2,1)}), bf16[1024,1024]{1,0:T(8,128)(2,1)}) %all-gather.5.cloned.1.call-update) | async-done | bytes 2097168 | tf_op jit(solution)/shard_map/all_gather | solution.py:209
  135.7 3.2 %fusion.2 = bf16[4,128,1024]{2,1,0:T(8,128)(2,1)S(1)} fusion(bf16[4,1024,128]{2,1,0:T(8,128)(2,1)} %all-gather.3.cloned.1.call-done, bf16[1024,1024]{1,0:T(8,128)(2,1)} %all-gather.5.cloned.1.call-done), kind=kOutput, calls=%fused_computation.3 | convolution fusion | flops 1074266112 | bytes 4194304 | tf_op jit(solution)/shard_map/cpf,pn->cfn/dot_general | solution.py:210
  138.9 39.2 %all_to_all.22 = bf16[8,64,1024]{2,1,0:T(8,128)(2,1)S(1)} all-to-all(bf16[8,64,1024]{2,1,0:T(8,128)(2,1)S(1)} %bitcast.8), channel_id=1, replica_groups={{0,32,64,96,128,160,192,224},{4,36,68,100,132,164,196,228},{8,40,72,104..., dimensions={0} | all-to-all | bytes 2097152 | tf_op jit(solution)/shard_map/all_to_all | solution.py:195
  178.1 0.2 convert_reduce_fusion
  178.3 0.7 broadcast_multiply_fusion
Async XLA Ops:
  21.7 39.4 %all-to-all-start = ((bf16[64,48,128]{2,1,0:T(8,128)(2,1)}), bf16[64,48,128]{2,1,0:T(8,128)(2,1)S(1)}, u32[]{:S(2)}, u32[]{:S(2)}) async-start(bf16[64,48,128]{2,1,0:T(8,128)(2,1)} %get-tuple-element.11), calls=%async_computation | async-start | bytes 1572864 | tf_op jit(solution)/shard_map/all_to_all | solution.py:195
  33.5 79.5 %all-gather.3.cloned.1.call-start = ((), (), s32[]{:S(2)}) async-start(), calls=%async_computation.4 | async-start | bytes 1310720 | tf_op jit(solution)/shard_map/all_gather | solution.py:206
  34.2 101.5 %all-gather.5.cloned.1.call-start = ((), (), s32[]{:S(2)}) async-start(), calls=%async_computation.5 | async-start | bytes 2359296 | tf_op jit(solution)/shard_map/all_gather | solution.py:209
  61.1 0.9 copy-start
Sparse Core Ops, SparseCore 0:
  36.1 37.6 all-gather.2
  113.1 22.5 all-gather.4

commit v2 on v1

--- a/solution.py
+++ b/solution.py
@@ -8,6 +8,7 @@
 from jax.experimental import pallas as pl
 from jax.experimental.pallas import tpu as pltpu
 from jax.sharding import PartitionSpec as P
+
 
 BLOCKS = 64
 ROWS = 128
@@ -16,8 +17,33 @@
 PERIOD = 2 * BLOCKS * ROWS
 LAST_SCALE = 1.0 / PERIOD
 ROOT_SCALE = 1.0 / math.sqrt(BLOCKS * ROWS)
-NEAR = [[8 * g + i for i in range(8)] for g in range(8)]
-FAR = [[g + 8 * i for i in range(8)] for g in range(8)]
+SENT = 4 * CHANNELS
+PLANES = [[32 * z + i for i in range(32)] for z in range(2)]
+
+
+def along_x(shift):
+    return [(s, s // 8 * 8 + (s // 2 + shift) % 4 * 2 + s % 2) for s in range(64)]
+
+
+def across(flip):
+    pairs = []
+    for s in range(64):
+        place = (s // 8 % 4 * 2 + s % 2) ^ flip
+        pairs.append((s, s // 32 * 32 + place // 2 * 8 + s // 2 % 4 * 2 + place % 2))
+    return pairs
+
+
+def along_z(shift):
+    pairs = []
+    for flat in range(256):
+        s, c = divmod(flat, 4)
+        place = (s // 32 * 4 + c + shift) % 8
+        pairs.append((flat, (place // 4 * 32 + s % 32) * 4 + place % 4))
+    return pairs
+
+
+def opposite():
+    return [(s, (s + 32) % 64) for s in range(64)]
 
 
 def split_table(table):
@@ -53,30 +79,43 @@
     return lax.dot_general(left, right, (((1,), (0,)), ((), ())), preferred_element_type=jnp.float32)
 
 
-def gather_body(key_ref, value_ref, grad_ref, query_ref, taps_ref, input_ref, sent_ref, features_ref):
+def gather_body(key_ref, value_ref, grad_ref, query_ref, taps_ref, sent_ref):
     for part in range(8):
         cols = pl.ds(part * 128, 128)
-        mixed = key_ref[:, cols].astype(jnp.float32) * value_ref[:, cols].astype(jnp.float32)
+        key = key_ref[:, cols].astype(jnp.float32)
+        mixed = key * value_ref[:, cols].astype(jnp.float32)
         gated = grad_ref[:, cols].astype(jnp.float32) * query_ref[:, cols].astype(jnp.float32)
-        for place, signal in enumerate((mixed, taps_ref[:, cols].astype(jnp.float32), gated)):
+        for place, signal in enumerate((mixed, taps_ref[:, cols].astype(jnp.float32), gated, key)):
             turned = signal.T.astype(jnp.bfloat16)
             sent_ref[pl.ds(part * 8, 8), pl.ds(place * 16, 16), :] = turned.reshape(8, 16, 128)
-    for near in range(8):
-        features_ref[near] = jnp.concatenate(
-            [input_ref[:, near * 64 : near * 64 + 64], input_ref[:, 512 + near * 64 : 576 + near * 64]],
-            axis=1,
-        )
-
-
-def gather_signals(gate_key, value_proj, grad_out, gate_query, filter_taps, layer_input):
+
+
+def gather_signals(gate_key, value_proj, grad_out, gate_query, filter_taps):
     return pl.pallas_call(
         gather_body,
-        out_shape=(
-            jax.ShapeDtypeStruct((BLOCKS, LANES, ROWS), jnp.bfloat16),
-            jax.ShapeDtypeStruct((8, ROWS, 128), jnp.bfloat16),
-        ),
+        out_shape=jax.ShapeDtypeStruct((BLOCKS, SENT, ROWS), jnp.bfloat16),
         name="gather_signals",
-    )(gate_key, value_proj, grad_out, gate_query, filter_taps, layer_input)
+    )(gate_key, value_proj, grad_out, gate_query, filter_taps)
+
+
+def features_body(where_ref, input_ref, *outs):
+    for shift, out_ref in enumerate(outs):
+        start = (where_ref[0] + shift) % 4 * 128
+        for side in range(2):
+            block = input_ref[:, pl.ds(pl.multiple_of(side * 512 + start, 128), 128)]
+            out_ref[side * 128 : side * 128 + 128, :] = block.astype(jnp.float32).T.astype(jnp.bfloat16)
+
+
+def split_features(where, layer_input):
+    return pl.pallas_call(
+        features_body,
+        out_shape=(jax.ShapeDtypeStruct((256, ROWS), jnp.bfloat16),) * 4,
+        in_specs=[
+            pl.BlockSpec(memory_space=pltpu.SMEM),
+            pl.BlockSpec(memory_space=pltpu.VMEM),
+        ],
+        name="split_features",
+    )(where, layer_input)
 
 
 UNROLL = 2
@@ -84,16 +123,16 @@
 
 def convolve_body(
     signals_ref, first_ref, cos_ref, sin_ref, ahead_ref, ahead_low_ref, back_ref, back_low_ref, last_ref,
-    out_ref, wide_in, wide_out,
+    out_ref, value_ref, wide_in, wide_out, wide_value,
 ):
-    wide_in[...] = signals_ref[...].astype(jnp.float32).reshape(BLOCKS * LANES, ROWS)
+    wide_in[...] = signals_ref[...].astype(jnp.float32).reshape(BLOCKS * SENT, ROWS)
     first = first_ref[...]
     cosine = cos_ref[...]
     sine = sin_ref[...]
 
     def channel(place):
         rows = jnp.concatenate(
-            [wide_in[pl.ds(place + CHANNELS * s, BLOCKS, stride=LANES), :] for s in range(3)], axis=1
+            [wide_in[pl.ds(place + CHANNELS * s, BLOCKS, stride=SENT), :] for s in range(3)], axis=1
         ).astype(jnp.bfloat16)
         outer = product(first, jnp.concatenate([rows, rows], axis=0))
         turned = []
@@ -147,6 +186,9 @@
             wide_out[pl.ds(place + CHANNELS * s, BLOCKS, stride=LANES), :] = (
                 total[:, s * 128 : s * 128 + 128] * factor
             )
+        back = (total[:, 128:256] * LAST_SCALE).astype(jnp.bfloat16).astype(jnp.float32)
+        key = wide_in[pl.ds(place + CHANNELS * 3, BLOCKS, stride=SENT), :]
+        wide_value[pl.ds(place, BLOCKS, stride=CHANNELS), :] = back * key
 
     def step(index, carry):
         for inside in range(UNROLL):
@@ -155,15 +197,24 @@
 
     lax.fori_loop(0, CHANNELS // UNROLL, step, 0)
     out_ref[...] = wide_out[...].reshape(BLOCKS, LANES, ROWS).astype(jnp.bfloat16)
+    for block in range(BLOCKS):
+        tile = wide_value[block * CHANNELS : block * CHANNELS + CHANNELS, :].astype(jnp.bfloat16)
+        z, y, x, core = block // 32, block // 8 % 4, block // 2 % 4, block % 2
+        for target in range(4):
+            value_ref[y * 8 + target * 2 + core, z * 4 + x] = tile
 
 
 def convolve(signals, tables):
     return pl.pallas_call(
         convolve_body,
-        out_shape=jax.ShapeDtypeStruct((BLOCKS, LANES, ROWS), jnp.bfloat16),
+        out_shape=(
+            jax.ShapeDtypeStruct((BLOCKS, LANES, ROWS), jnp.bfloat16),
+            jax.ShapeDtypeStruct((32, 8, CHANNELS, ROWS), jnp.bfloat16),
+        ),
         scratch_shapes=[
+            pltpu.VMEM((BLOCKS * SENT, ROWS), jnp.float32),
             pltpu.VMEM((BLOCKS * LANES, ROWS), jnp.float32),
-            pltpu.VMEM((BLOCKS * LANES, ROWS), jnp.float32),
+            pltpu.VMEM((BLOCKS * CHANNELS, ROWS), jnp.float32),
         ],
         name="convolve",
     )(signals, *tables)
@@ -191,25 +242,103 @@
     )
 
 
+def weight_body(where_ref, value_ref, *refs):
+    features, outs, (aligned, pieces) = refs[:8], refs[8:16], refs[16:]
+    x, ring, place = where_ref[0], where_ref[1], where_ref[2]
+    for z in range(2):
+        for back in range(4):
+            block = value_ref[:, z * 4 + (x - back + 4) % 4]
+            aligned[z, :, back * 128 : back * 128 + 128] = block.reshape(512, ROWS)
+    for apart in range(4):
+        total = None
+        for half in range(2):
+            source = (ring - apart - 4 * half + 8) % 8
+            rows = features[apart + 4 * half]
+            rows = jnp.concatenate([rows[back] for back in range(4)], axis=1)
+            term = lax.dot_general(
+                rows, aligned[source // 4], (((1,), (1,)), ((), ())), preferred_element_type=jnp.float32
+            )
+            total = term if total is None else total + term
+        group = (ring - apart + 8) % 4
+        for side in range(2):
+            for core in range(2):
+                target = ((group % 2) * 2 + side) * 2 + core
+                start = side * 128 + core * 64
+                pieces[target * 2 + group // 2] = total[start : start + 64].astype(jnp.bfloat16)
+    for flip, out_ref in enumerate(outs):
+        out_ref[...] = pieces[pl.ds((place ^ flip) * 2, 2)]
+
+
+def weight_parts(where, value, features):
+    return pl.pallas_call(
+        weight_body,
+        out_shape=(jax.ShapeDtypeStruct((2, 64, 512), jnp.bfloat16),) * 8,
+        in_specs=[pl.BlockSpec(memory_space=pltpu.SMEM)] + [pl.BlockSpec(memory_space=pltpu.VMEM)] * 9,
+        scratch_shapes=[
+            pltpu.VMEM((2, 512, 512), jnp.bfloat16),
+            pltpu.VMEM((16, 64, 512), jnp.bfloat16),
+        ],
+        name="weight_parts",
+    )(where, value, *features)
+
+
+def total_body(where_ref, *refs):
+    parts, (kept_ref, sent_ref) = refs[:8], refs[8:]
+    z = where_ref[3]
+    for out_ref, place in ((kept_ref, z), (sent_ref, 1 - z)):
+        total = parts[0][place].astype(jnp.float32)
+        for part in parts[1:]:
+            total = total + part[place].astype(jnp.float32)
+        out_ref[...] = total * ROOT_SCALE
+
+
+def weight_total(where, parts):
+    return pl.pallas_call(
+        total_body,
+        out_shape=(jax.ShapeDtypeStruct((64, 512), jnp.float32),) * 2,
+        in_specs=[pl.BlockSpec(memory_space=pltpu.SMEM)] + [pl.BlockSpec(memory_space=pltpu.VMEM)] * 8,
+        name="weight_total",
+    )(where, *parts)
+
+
 def exchange(array, groups=None):
     return lax.all_to_all(
         array, "seq", split_axis=0, concat_axis=0, tiled=True, axis_index_groups=groups
     )
 
 
+def ring_step(array, shift):
+    return lax.ppermute(array, ("seq", "chan"), along_z(shift))
+
+
 def shards(layer_input, gate_query, gate_key, value_proj, grad_out, filter_taps):
     tables = [jnp.asarray(table) for table in make_tables()]
-    sent, features = gather_signals(
-        gate_key, value_proj, grad_out, gate_query, filter_taps, layer_input
-    )
-    features = exchange(features, NEAR).reshape(8 * ROWS, 128)
-    features = lax.all_gather(features, "chan", axis=0)
-    results = exchange(convolve(exchange(sent), tables))
-    grad_query, grad_key, grad_value, grad_filter = finish(results, grad_out, value_proj, gate_key)
-    columns = lax.all_gather(grad_value, "seq", axis=0, tiled=True, axis_index_groups=NEAR)
-    partial = jnp.einsum("cpf,pn->cfn", features, columns, preferred_element_type=jnp.float32)
-    partial = partial.astype(jnp.bfloat16).reshape(8, 64, partial.shape[-1])
-    grad_weight = jnp.sum(exchange(partial, FAR).astype(jnp.float32), axis=0) * ROOT_SCALE
+    index = lax.axis_index("seq")
+    z, y, x, core = index // 32, index // 8 % 4, index // 2 % 4, index % 2
+    where = jnp.stack([x, z * 4 + lax.axis_index("chan"), y * 2 + core, z]).astype(jnp.int32)
+    pieces = split_features(where, layer_input)
+    own = [lax.ppermute(pieces[n], "seq", along_x(n)) for n in range(1, 4)]
+    own = jnp.stack([pieces[0]] + own)
+    sent = gather_signals(gate_key, value_proj, grad_out, gate_query, filter_taps)
+    up, down = ring_step(own, 1), ring_step(own, -1)
+    signals = exchange(sent)
+    up2, down2 = ring_step(up, 1), ring_step(down, -1)
+    results, value = convolve(signals, tables)
+    up3, down3, far = ring_step(up2, 1), ring_step(down2, -1), ring_step(up2, 2)
+    value = exchange(value, PLANES)
+    parts = weight_parts(where, value, (own, up, up2, up3, far, down3, down2, down))
+    parts = [parts[0]] + [lax.ppermute(parts[n], "seq", across(n)) for n in range(1, 8)]
+    results = exchange(results)
+    kept, sent = weight_total(where, parts)
+    received = lax.ppermute(sent, "seq", opposite())
+    grad_query, grad_key, grad_value, grad_filter = finish(
+        results, grad_out, value_proj, gate_key
+    )
+    grad_weight = jnp.where(
+        z == 0,
+        jnp.concatenate([kept, received], axis=1),
+        jnp.concatenate([received, kept], axis=1),
+    )
     return (grad_query, grad_key, grad_value, grad_filter, grad_weight)
 
 

time: 186 us -> 199 us (1.070)
  the two profiles are of different devices: /device:TPU:32 before, /device:TPU:1 now
where the time goes in v2:
time: 199 us; the launch traced here: 198 us
  waiting for transfers between devices  68.7 us (35%)
  starting transfers between devices  51.9 us (26%)
  blocking collectives  39 us (20%)
  Pallas kernels  32.5 us (16%)
  other arithmetic  3.25 us (2%)
  local copies, waits for them, and re-layouts  2.27 us (1%)
    all_to_all x1, blocking collectives, exchange(): lax.all_to_all(array, 'seq', split_axis=0, concat_axis=0, tiled=True, axi...  39 us
    ppermute x7, waiting for transfers between devices, ring_step(): return lax.ppermute(array, ('seq', 'chan'), along_z(shift))  26.9 us
    pallas_call x1, Pallas kernels, convolve(): pl.pallas_call(convolve_body, out_shape=(jax.ShapeDtypeStruct((BLOCKS, LA...  19 us
    all_to_all x2, waiting for transfers between devices, exchange(): lax.all_to_all(array, 'seq', split_axis=0, concat_axis=0, tiled=True, axi...  17 us
    all_to_all x2, starting transfers between devices, exchange(): lax.all_to_all(array, 'seq', split_axis=0, concat_axis=0, tiled=True, axi...  16.6 us
    ppermute x7, starting transfers between devices, ring_step(): return lax.ppermute(array, ('seq', 'chan'), along_z(shift))  15.7 us
    ppermute x7, starting transfers between devices, shards(): lax.ppermute(parts[n], 'seq', across(n))  11.3 us
    ppermute x7, waiting for transfers between devices, shards(): lax.ppermute(parts[n], 'seq', across(n))  11 us
  transfers between devices with their start and end apart: 20, of which 13 were waited for; matrix products, arithmetic and copies ran while one was open for 2% of the time, Pallas kernels for 4%

profile of v2, /device:TPU:1, one launch (start us, length us, event | category | flops | bytes accessed | tf_op | source)
XLA Modules:
  0.0 198.3 jit_solution(13492407606450103626)
XLA Ops:
  0.6 2.6 %gather_signals.1 = bf16[64,64,128]{2,1,0:T(8,128)(2,1)} custom-call(bf16[128,1024]{1,0:T(8,128)(2,1)} %key_ref.3, bf16[128,1024]{1,0:T(8,128)(2,1)} %value_ref.3, bf16[128,1024]{1,0:T(8,128)(2,1)} %grad_ref.3, bf16[128,1024]{1,0:T(8,128)(2,1)} %query_ref.1, bf16[128,1024]{1,0:T(8,128)(2,1)} %taps_ref.1), custom_call_target="tpu_custom_call" | custom-call | tf_op jit(solution)/shard_map/gather_signals/pallas_call | solution.py:94
  3.3 39.0 %all_to_all.15.signals_ref = bf16[64,64,128]{2,1,0:T(8,128)(2,1)} all-to-all(bf16[64,64,128]{2,1,0:T(8,128)(2,1)} %gather_signals.1), channel_id=1, replica_groups=mesh['seq'=64,'chan'=4] {'seq'}, dimensions={0} | all-to-all | bytes 2097152 | tf_op jit(solution)/shard_map/all_to_all | solution.py:305
  42.2 19.0 %convolve.1 = (bf16[64,48,128]{2,1,0:T(8,128)(2,1)}, bf16[32,8,16,128]{3,2,1,0:T(8,128)(2,1)}) custom-call(bf16[64,64,128]{2,1,0:T(8,128)(2,1)} %all_to_all.15.signals_ref, bf16[256,128]{1,0:T(8,128)(2,1)} %constant.85.clone.first_ref, f32[128,128]{1,0:T(8,128)} %constant.86.clone.cos_ref, f32[128,128]{1,0:T(8,128)} %constant.87.clone.sin_ref, ...), custom_call_target="tpu_custom_call" | custom-call | tf_op jit(solution)/shard_map/convolve/pallas_call | solution.py:208
  61.3 12.1 %all-to-all-start.2 = ((bf16[32,8,16,128]{3,2,1,0:T(8,128)(2,1)}), bf16[32,8,16,128]{3,2,1,0:T(8,128)(2,1)S(1)}, u32[]{:S(2)}, u32[]{:S(2)}) async-start(bf16[32,8,16,128]{3,2,1,0:T(8,128)(2,1)} %get-tuple-element.30), calls=%async_computation.2 | async-start | bytes 2097152 | tf_op jit(solution)/shard_map/all_to_all | solution.py:305
  73.5 17.0 %all-to-all-done.2.value_ref = bf16[32,8,16,128]{3,2,1,0:T(8,128)(2,1)S(1)} async-done(((bf16[32,8,16,128]{3,2,1,0:T(8,128)(2,1)}), bf16[32,8,16,128]{3,2,1,0:T(8,128)(2,1)S(1)}, u32[]{:S(2)}, u32[]{:S(2)}) %all-to-all-start.2) | async-done | bytes 1048608 | tf_op jit(solution)/shard_map/all_to_all | solution.py:305
  90.5 4.5 %all-to-all-start.1 = ((bf16[64,48,128]{2,1,0:T(8,128)(2,1)}), bf16[64,48,128]{2,1,0:T(8,128)(2,1)S(1)}, u32[]{:S(2)}, u32[]{:S(2)}) async-start(bf16[64,48,128]{2,1,0:T(8,128)(2,1)} %get-tuple-element.25), calls=%async_computation.1 | async-start | bytes 1572864 | tf_op jit(solution)/shard_map/all_to_all | solution.py:305
  94.9 0.7 pad_add_fusion.where_ref
  95.6 1.8 split_features.1
  97.4 1.4 collective-permute-start
  98.7 2.4 %collective-permute-start.1 = (bf16[256,128]{1,0:T(8,128)(2,1)}, bf16[256,128]{1,0:T(8,128)(2,1)S(1)}, u32[]{:S(2)}, u32[]{:S(2)}) collective-permute-start(bf16[256,128]{1,0:T(8,128)(2,1)} %get-tuple-element.33), channel_id=1, source_target_pairs={{0,16},{4,20},{8,24},{12,28},{16,0},{20,4},{24,8},{28,12},{32,48},... | collective-permute-start | bytes 196616 | tf_op jit(solution)/shard_map/ppermute | solution.py:320
  101.2 1.2 collective-permute-start.2
  102.3 1.7 collective-permute-done
  104.0 3.3 %collective-permute-done.1 = bf16[256,128]{1,0:T(8,128)(2,1)S(1)} collective-permute-done((bf16[256,128]{1,0:T(8,128)(2,1)}, bf16[256,128]{1,0:T(8,128)(2,1)S(1)}, u32[]{:S(2)}, u32[]{:S(2)}) %collective-permute-start.1) | collective-permute-done | bytes 65568 | tf_op jit(solution)/shard_map/ppermute | solution.py:320
  107.3 0.0 collective-permute-done.2
  107.3 0.9 pad_maximum_fusion.refs_0_
  108.2 0.0 copy-start.2
  108.2 6.6 %collective-permute-start.7 = (bf16[4,256,128]{2,1,0:T(8,128)(2,1)S(1)}, bf16[4,256,128]{2,1,0:T(8,128)(2,1)S(1)}, u32[]{:S(2)}, u32[]{:S(2)}) collective-permute-start(bf16[4,256,128]{2,1,0:T(8,128)(2,1)S(1)} %pad_maximum_fusion.refs_0_), channel_id=1, source_target_pairs={{0,131},{1,0},{2,1},{3,2},{4,135},{5,4},{6,5},{7,6},{8,139},{9,8},... | collective-permute-start | bytes 786440 | tf_op jit(solution)/shard_map/ppermute | solution.py:311
  114.8 5.2 %collective-permute-done.7.refs_7_ = bf16[4,256,128]{2,1,0:T(8,128)(2,1)S(1)} collective-permute-done((bf16[4,256,128]{2,1,0:T(8,128)(2,1)S(1)}, bf16[4,256,128]{2,1,0:T(8,128)(2,1)S(1)}, u32[]{:S(2)}, u32[]{:S(2)}) %collective-permute-start.7) | collective-permute-done | bytes 262176 | tf_op jit(solution)/shard_map/ppermute | solution.py:311
  120.1 3.2 %collective-permute-start.8 = (bf16[4,256,128]{2,1,0:T(8,128)(2,1)S(1)}, bf16[4,256,128]{2,1,0:T(8,128)(2,1)S(1)}, u32[]{:S(2)}, u32[]{:S(2)}) collective-permute-start(bf16[4,256,128]{2,1,0:T(8,128)(2,1)S(1)} %collective-permute-done.7.refs_7_), channel_id=1, source_target_pairs={{0,131},{1,0},{2,1},{3,2},{4,135},{5,4},{6,5},{7,6},{8,139},{9,8},... | collective-permute-start | bytes 786440 | tf_op jit(solution)/shard_map/ppermute | solution.py:311
  123.3 1.5 collective-permute-start.4
  124.8 5.4 %collective-permute-done.8.refs_6_ = bf16[4,256,128]{2,1,0:T(8,128)(2,1)S(1)} collective-permute-done((bf16[4,256,128]{2,1,0:T(8,128)(2,1)S(1)}, bf16[4,256,128]{2,1,0:T(8,128)(2,1)S(1)}, u32[]{:S(2)}, u32[]{:S(2)}) %collective-permute-start.8) | collective-permute-done | bytes 262176 | tf_op jit(solution)/shard_map/ppermute | solution.py:311
  130.3 0.7 collective-permute-start.9
  131.0 1.8 collective-permute-start.6
  132.7 1.9 collective-permute-start.5
  134.6 2.1 %collective-permute-done.9.refs_5_ = bf16[4,256,128]{2,1,0:T(8,128)(2,1)S(1)} collective-permute-done((bf16[4,256,128]{2,1,0:T(8,128)(2,1)S(1)}, bf16[4,256,128]{2,1,0:T(8,128)(2,1)S(1)}, u32[]{:S(2)}, u32[]{:S(2)}) %collective-permute-start.9) | collective-permute-done | bytes 262176 | tf_op jit(solution)/shard_map/ppermute | solution.py:311
  136.7 9.0 %collective-permute-done.6.refs_4_ = bf16[4,256,128]{2,1,0:T(8,128)(2,1)S(1)} collective-permute-done((bf16[4,256,128]{2,1,0:T(8,128)(2,1)S(1)}, bf16[4,256,128]{2,1,0:T(8,128)(2,1)S(1)}, u32[]{:S(2)}, u32[]{:S(2)}) %collective-permute-start.6) | collective-permute-done | bytes 262176 | tf_op jit(solution)/shard_map/ppermute | solution.py:311
  145.7 5.1 %collective-permute-done.5.refs_3_ = bf16[4,256,128]{2,1,0:T(8,128)(2,1)S(1)} collective-permute-done((bf16[4,256,128]{2,1,0:T(8,128)(2,1)S(1)}, bf16[4,256,128]{2,1,0:T(8,128)(2,1)S(1)}, u32[]{:S(2)}, u32[]{:S(2)}) %collective-permute-start.5) | collective-permute-done | bytes 262176 | tf_op jit(solution)/shard_map/ppermute | solution.py:311
  150.8 0.0 copy-start.9
  150.8 0.7 copy-done.9
  151.5 4.3 %weight_parts.1 = (bf16[2,64,512]{2,1,0:T(8,128)(2,1)}, bf16[2,64,512]{2,1,0:T(8,128)(2,1)}, bf16[2,64,512]{2,1,0:T(8,128)(2,1)}, bf16[2,64,512]{2,1,0:T(8,128)(...) custom-call(s32[4]{0:T(128)} %pad_add_fusion.where_ref, ...), custom_call_target="tpu_custom_call" | custom-call | tf_op jit(solution)/shard_map/weight_parts/pallas_call | solution.py:273
  155.8 2.2 %collective-permute-start.10 = (bf16[2,64,512]{2,1,0:T(8,128)(2,1)}, bf16[2,64,512]{2,1,0:T(8,128)(2,1)S(1)}, u32[]{:S(2)}, u32[]{:S(2)}) collective-permute-start(bf16[2,64,512]{2,1,0:T(8,128)(2,1)} %get-tuple-element.36), channel_id=1, source_target_pairs={{0,4},{4,0},{8,12},{12,8},{16,20},{20,16},{24,28},{28,24},{32,36},... | collective-permute-start | bytes 393224 | tf_op jit(solution)/shard_map/ppermute | solution.py:330
  158.1 1.4 collective-permute-start.11
  159.5 0.3 collective-permute-start.12
  159.8 2.8 %collective-permute-start.13 = (bf16[2,64,512]{2,1,0:T(8,128)(2,1)}, bf16[2,64,512]{2,1,0:T(8,128)(2,1)S(1)}, u32[]{:S(2)}, u32[]{:S(2)}) collective-permute-start(bf16[2,64,512]{2,1,0:T(8,128)(2,1)} %get-tuple-element.39), channel_id=1, source_target_pairs={{0,64},{4,68},{8,72},{12,76},{16,80},{20,84},{24,88},{28,92},{32,9... | collective-permute-start | bytes 393224 | tf_op jit(solution)/shard_map/ppermute | solution.py:330
  162.5 0.5 collective-permute-start.14
  163.1 2.5 %collective-permute-start.15 = (bf16[2,64,512]{2,1,0:T(8,128)(2,1)}, bf16[2,64,512]{2,1,0:T(8,128)(2,1)S(1)}, u32[]{:S(2)}, u32[]{:S(2)}) collective-permute-start(bf16[2,64,512]{2,1,0:T(8,128)(2,1)} %get-tuple-element.41), channel_id=1, source_target_pairs={{0,96},{4,100},{8,104},{12,108},{16,112},{20,116},{24,120},{28,124... | collective-permute-start | bytes 393224 | tf_op jit(solution)/shard_map/ppermute | solution.py:330
  165.6 1.6 collective-permute-start.16
  167.1 4.0 %collective-permute-done.13.refs_4_ = bf16[2,64,512]{2,1,0:T(8,128)(2,1)S(1)} collective-permute-done((bf16[2,64,512]{2,1,0:T(8,128)(2,1)}, bf16[2,64,512]{2,1,0:T(8,128)(2,1)S(1)}, u32[]{:S(2)}, u32[]{:S(2)}) %collective-permute-start.13) | collective-permute-done | bytes 131104 | tf_op jit(solution)/shard_map/ppermute | solution.py:330
  171.1 3.1 %collective-permute-done.14.refs_5_ = bf16[2,64,512]{2,1,0:T(8,128)(2,1)S(1)} collective-permute-done((bf16[2,64,512]{2,1,0:T(8,128)(2,1)}, bf16[2,64,512]{2,1,0:T(8,128)(2,1)S(1)}, u32[]{:S(2)}, u32[]{:S(2)}) %collective-permute-start.14) | collective-permute-done | bytes 131104 | tf_op jit(solution)/shard_map/ppermute | solution.py:330
  174.2 0.8 collective-permute-done.15.refs_6_
  175.1 3.1 %collective-permute-done.16.refs_7_ = bf16[2,64,512]{2,1,0:T(8,128)(2,1)S(1)} collective-permute-done((bf16[2,64,512]{2,1,0:T(8,128)(2,1)}, bf16[2,64,512]{2,1,0:T(8,128)(2,1)S(1)}, u32[]{:S(2)}, u32[]{:S(2)}) %collective-permute-start.16) | collective-permute-done | bytes 131104 | tf_op jit(solution)/shard_map/ppermute | solution.py:330
  178.2 0.6 copy-done.16
  178.8 2.1 %weight_total.1 = (f32[64,512]{1,0:T(8,128)}, f32[64,512]{1,0:T(8,128)}) custom-call(s32[4]{0:T(128)} %pad_add_fusion.where_ref, bf16[2,64,512]{2,1,0:T(8,128)(2,1)} %get-tuple-element.35.refs_0_, bf16[2,64,512]{2,1,0:T(8,128)(2,1)} %copy-done.10, bf16[2,64,512]{2,1,0:T(8,128)(2,1)} %copy-done.11, bf16[2,64,512]{2,1,0:T(8,128)(2,1)} %copy-done.12, ...), custom_call_target="tpu_custom_call" | custom-call | tf_op jit(solution)/shard_map/weight_total/pallas_call | solution.py:296
  180.9 3.3 %collective-permute-start.17 = (f32[64,512]{1,0:T(8,128)}, f32[64,512]{1,0:T(8,128)S(1)}, u32[]{:S(2)}, u32[]{:S(2)}) collective-permute-start(f32[64,512]{1,0:T(8,128)} %get-tuple-element.44), channel_id=1, source_target_pairs={{0,128},{4,132},{8,136},{12,140},{16,144},{20,148},{24,152},{28,15... | collective-permute-start | bytes 393224 | tf_op jit(solution)/shard_map/ppermute | solution.py:333
  184.2 8.9 %collective-permute-done.17 = f32[64,512]{1,0:T(8,128)S(1)} collective-permute-done((f32[64,512]{1,0:T(8,128)}, f32[64,512]{1,0:T(8,128)S(1)}, u32[]{:S(2)}, u32[]{:S(2)}) %collective-permute-start.17) | collective-permute-done | bytes 131104 | tf_op jit(solution)/shard_map/ppermute | solution.py:333
  193.1 1.7 maximum_select_fusion
  194.8 0.9 copy-done.1
  195.7 2.6 %finish.1 = (bf16[128,1024]{1,0:T(8,128)(2,1)}, bf16[128,1024]{1,0:T(8,128)(2,1)}, bf16[128,1024]{1,0:T(8,128)(2,1)}, bf16[128,1024]{1,0:T(8,128)(2,1)}) custom-call(bf16[64,48,128]{2,1,0:T(8,128)(2,1)} %copy-done.1, bf16[128,1024]{1,0:T(8,128)(2,1)} %grad_ref.3, bf16[128,1024]{1,0:T(8,128)(2,1)} %value_ref.3, bf16[128,1024]{1,0:T(8,128)(2,1)} %key_ref.3), custom_call_target="tpu_custom_call" | custom-call | tf_op jit(solution)/shard_map/finish/pallas_call | solution.py:240
  (36 shorter events, 0.1 us)
Async XLA Ops:
  61.3 29.2 %all-to-all-start.2 = ((bf16[32,8,16,128]{3,2,1,0:T(8,128)(2,1)}), bf16[32,8,16,128]{3,2,1,0:T(8,128)(2,1)S(1)}, u32[]{:S(2)}, u32[]{:S(2)}) async-start(bf16[32,8,16,128]{3,2,1,0:T(8,128)(2,1)} %get-tuple-element.30), calls=%async_computation.2 | async-start | bytes 2097152 | tf_op jit(solution)/shard_map/all_to_all | solution.py:305
  90.5 17.7 %copy-start = (bf16[32,8,16,128]{3,2,1,0:T(8,128)(2,1)}, bf16[32,8,16,128]{3,2,1,0:T(8,128)(2,1)S(1)}, u32[]{:S(2)}) copy-start(bf16[32,8,16,128]{3,2,1,0:T(8,128)(2,1)S(1)} %all-to-all-done.2.value_ref) | copy-start | bytes 3145732
  90.5 104.3 %all-to-all-start.1 = ((bf16[64,48,128]{2,1,0:T(8,128)(2,1)}), bf16[64,48,128]{2,1,0:T(8,128)(2,1)S(1)}, u32[]{:S(2)}, u32[]{:S(2)}) async-start(bf16[64,48,128]{2,1,0:T(8,128)(2,1)} %get-tuple-element.25), calls=%async_computation.1 | async-start | bytes 1572864 | tf_op jit(solution)/shard_map/all_to_all | solution.py:305
  97.4 6.6 %collective-permute-start = (bf16[256,128]{1,0:T(8,128)(2,1)}, bf16[256,128]{1,0:T(8,128)(2,1)S(1)}, u32[]{:S(2)}, u32[]{:S(2)}) collective-permute-start(bf16[256,128]{1,0:T(8,128)(2,1)} %get-tuple-element.32), channel_id=1, source_target_pairs={{0,8},{4,12},{8,16},{12,20},{16,24},{20,28},{24,0},{28,4},{32,40},... | collective-permute-start | bytes 196616 | tf_op jit(solution)/shard_map/ppermute | solution.py:320
  98.7 8.5 %collective-permute-start.1 = (bf16[256,128]{1,0:T(8,128)(2,1)}, bf16[256,128]{1,0:T(8,128)(2,1)S(1)}, u32[]{:S(2)}, u32[]{:S(2)}) collective-permute-start(bf16[256,128]{1,0:T(8,128)(2,1)} %get-tuple-element.33), channel_id=1, source_target_pairs={{0,16},{4,20},{8,24},{12,28},{16,0},{20,4},{24,8},{28,12},{32,48},... | collective-permute-start | bytes 196616 | tf_op jit(solution)/shard_map/ppermute | solution.py:320
  101.2 6.1 %collective-permute-start.2 = (bf16[256,128]{1,0:T(8,128)(2,1)}, bf16[256,128]{1,0:T(8,128)(2,1)S(1)}, u32[]{:S(2)}, u32[]{:S(2)}) collective-permute-start(bf16[256,128]{1,0:T(8,128)(2,1)} %get-tuple-element.34), channel_id=1, source_target_pairs={{0,24},{4,28},{8,0},{12,4},{16,8},{20,12},{24,16},{28,20},{32,56},... | collective-permute-start | bytes 196616 | tf_op jit(solution)/shard_map/ppermute | solution.py:320
  108.2 42.6 %copy-start.2 = (bf16[4,256,128]{2,1,0:T(8,128)(2,1)}, bf16[4,256,128]{2,1,0:T(8,128)(2,1)S(1)}, u32[]{:S(2)}) copy-start(bf16[4,256,128]{2,1,0:T(8,128)(2,1)S(1)} %pad_maximum_fusion.refs_0_) | copy-start | bytes 786436
  108.2 11.9 %collective-permute-start.7 = (bf16[4,256,128]{2,1,0:T(8,128)(2,1)S(1)}, bf16[4,256,128]{2,1,0:T(8,128)(2,1)S(1)}, u32[]{:S(2)}, u32[]{:S(2)}) collective-permute-start(bf16[4,256,128]{2,1,0:T(8,128)(2,1)S(1)} %pad_maximum_fusion.refs_0_), channel_id=1, source_target_pairs={{0,131},{1,0},{2,1},{3,2},{4,135},{5,4},{6,5},{7,6},{8,139},{9,8},... | collective-permute-start | bytes 786440 | tf_op jit(solution)/shard_map/ppermute | solution.py:311
  114.8 8.5 %collective-permute-start.3 = (bf16[4,256,128]{2,1,0:T(8,128)(2,1)S(1)}, bf16[4,256,128]{2,1,0:T(8,128)(2,1)S(1)}, u32[]{:S(2)}, u32[]{:S(2)}) collective-permute-start(bf16[4,256,128]{2,1,0:T(8,128)(2,1)S(1)} %pad_maximum_fusion.refs_0_), channel_id=1, source_target_pairs={{0,1},{1,2},{2,3},{3,128},{4,5},{5,6},{6,7},{7,132},{8,9},{9,10},{... | collective-permute-start | bytes 786440 | tf_op jit(solution)/shard_map/ppermute | solution.py:311
  120.1 30.7 %copy-start.3 = (bf16[4,256,128]{2,1,0:T(8,128)(2,1)}, bf16[4,256,128]{2,1,0:T(8,128)(2,1)S(1)}, u32[]{:S(2)}) copy-start(bf16[4,256,128]{2,1,0:T(8,128)(2,1)S(1)} %collective-permute-done.7.refs_7_) | copy-start | bytes 786436
  120.1 10.2 %collective-permute-start.8 = (bf16[4,256,128]{2,1,0:T(8,128)(2,1)S(1)}, bf16[4,256,128]{2,1,0:T(8,128)(2,1)S(1)}, u32[]{:S(2)}, u32[]{:S(2)}) collective-permute-start(bf16[4,256,128]{2,1,0:T(8,128)(2,1)S(1)} %collective-permute-done.7.refs_7_), channel_id=1, source_target_pairs={{0,131},{1,0},{2,1},{3,2},{4,135},{5,4},{6,5},{7,6},{8,139},{9,8},... | collective-permute-start | bytes 786440 | tf_op jit(solution)/shard_map/ppermute | solution.py:311
  123.3 27.5 %copy-start.4 = (bf16[4,256,128]{2,1,0:T(8,128)(2,1)}, bf16[4,256,128]{2,1,0:T(8,128)(2,1)S(1)}, u32[]{:S(2)}) copy-start(bf16[4,256,128]{2,1,0:T(8,128)(2,1)S(1)} %collective-permute-done.3.refs_1_) | copy-start | bytes 786436
  123.3 7.6 %collective-permute-start.4 = (bf16[4,256,128]{2,1,0:T(8,128)(2,1)S(1)}, bf16[4,256,128]{2,1,0:T(8,128)(2,1)S(1)}, u32[]{:S(2)}, u32[]{:S(2)}) collective-permute-start(bf16[4,256,128]{2,1,0:T(8,128)(2,1)S(1)} %collective-permute-done.3.refs_1_), channel_id=1, source_target_pairs={{0,1},{1,2},{2,3},{3,128},{4,5},{5,6},{6,7},{7,132},{8,9},{9,10},{... | collective-permute-start | bytes 786440 | tf_op jit(solution)/shard_map/ppermute | solution.py:311
  130.3 20.5 %copy-start.5 = (bf16[4,256,128]{2,1,0:T(8,128)(2,1)}, bf16[4,256,128]{2,1,0:T(8,128)(2,1)S(1)}, u32[]{:S(2)}) copy-start(bf16[4,256,128]{2,1,0:T(8,128)(2,1)S(1)} %collective-permute-done.8.refs_6_) | copy-start | bytes 786436
  130.3 6.4 %collective-permute-start.9 = (bf16[4,256,128]{2,1,0:T(8,128)(2,1)S(1)}, bf16[4,256,128]{2,1,0:T(8,128)(2,1)S(1)}, u32[]{:S(2)}, u32[]{:S(2)}) collective-permute-start(bf16[4,256,128]{2,1,0:T(8,128)(2,1)S(1)} %collective-permute-done.8.refs_6_), channel_id=1, source_target_pairs={{0,131},{1,0},{2,1},{3,2},{4,135},{5,4},{6,5},{7,6},{8,139},{9,8},... | collective-permute-start | bytes 786440 | tf_op jit(solution)/shard_map/ppermute | solution.py:311
  131.0 19.8 %copy-start.6 = (bf16[4,256,128]{2,1,0:T(8,128)(2,1)}, bf16[4,256,128]{2,1,0:T(8,128)(2,1)S(1)}, u32[]{:S(2)}) copy-start(bf16[4,256,128]{2,1,0:T(8,128)(2,1)S(1)} %collective-permute-done.4.refs_2_) | copy-start | bytes 786436
  131.0 14.7 %collective-permute-start.6 = (bf16[4,256,128]{2,1,0:T(8,128)(2,1)S(1)}, bf16[4,256,128]{2,1,0:T(8,128)(2,1)S(1)}, u32[]{:S(2)}, u32[]{:S(2)}) collective-permute-start(bf16[4,256,128]{2,1,0:T(8,128)(2,1)S(1)} %collective-permute-done.4.refs_2_), channel_id=1, source_target_pairs={{0,2},{1,3},{2,128},{3,129},{4,6},{5,7},{6,132},{7,133},{8,10},{9,... | collective-permute-start | bytes 786440 | tf_op jit(solution)/shard_map/ppermute | solution.py:311
  132.7 18.1 %collective-permute-start.5 = (bf16[4,256,128]{2,1,0:T(8,128)(2,1)S(1)}, bf16[4,256,128]{2,1,0:T(8,128)(2,1)S(1)}, u32[]{:S(2)}, u32[]{:S(2)}) collective-permute-start(bf16[4,256,128]{2,1,0:T(8,128)(2,1)S(1)} %collective-permute-done.4.refs_2_), channel_id=1, source_target_pairs={{0,1},{1,2},{2,3},{3,128},{4,5},{5,6},{6,7},{7,132},{8,9},{9,10},{... | collective-permute-start | bytes 786440 | tf_op jit(solution)/shard_map/ppermute | solution.py:311
  136.7 14.1 %copy-start.7 = (bf16[4,256,128]{2,1,0:T(8,128)(2,1)}, bf16[4,256,128]{2,1,0:T(8,128)(2,1)S(1)}, u32[]{:S(2)}) copy-start(bf16[4,256,128]{2,1,0:T(8,128)(2,1)S(1)} %collective-permute-done.9.refs_5_) | copy-start | bytes 786436
  145.7 5.1 %copy-start.8 = (bf16[4,256,128]{2,1,0:T(8,128)(2,1)}, bf16[4,256,128]{2,1,0:T(8,128)(2,1)S(1)}, u32[]{:S(2)}) copy-start(bf16[4,256,128]{2,1,0:T(8,128)(2,1)S(1)} %collective-permute-done.6.refs_4_) | copy-start | bytes 786436
  150.8 0.7 copy-start.9
  155.8 7.2 %collective-permute-start.10 = (bf16[2,64,512]{2,1,0:T(8,128)(2,1)}, bf16[2,64,512]{2,1,0:T(8,128)(2,1)S(1)}, u32[]{:S(2)}, u32[]{:S(2)}) collective-permute-start(bf16[2,64,512]{2,1,0:T(8,128)(2,1)} %get-tuple-element.36), channel_id=1, source_target_pairs={{0,4},{4,0},{8,12},{12,8},{16,20},{20,16},{24,28},{28,24},{32,36},... | collective-permute-start | bytes 393224 | tf_op jit(solution)/shard_map/ppermute | solution.py:330
  158.1 7.5 %collective-permute-start.11 = (bf16[2,64,512]{2,1,0:T(8,128)(2,1)}, bf16[2,64,512]{2,1,0:T(8,128)(2,1)S(1)}, u32[]{:S(2)}, u32[]{:S(2)}) collective-permute-start(bf16[2,64,512]{2,1,0:T(8,128)(2,1)} %get-tuple-element.37), channel_id=1, source_target_pairs={{0,32},{4,36},{8,40},{12,44},{16,48},{20,52},{24,56},{28,60},{32,0... | collective-permute-start | bytes 393224 | tf_op jit(solution)/shard_map/ppermute | solution.py:330
  159.5 7.6 %collective-permute-start.12 = (bf16[2,64,512]{2,1,0:T(8,128)(2,1)}, bf16[2,64,512]{2,1,0:T(8,128)(2,1)S(1)}, u32[]{:S(2)}, u32[]{:S(2)}) collective-permute-start(bf16[2,64,512]{2,1,0:T(8,128)(2,1)} %get-tuple-element.38), channel_id=1, source_target_pairs={{0,36},{4,32},{8,44},{12,40},{16,52},{20,48},{24,60},{28,56},{32,4... | collective-permute-start | bytes 393224 | tf_op jit(solution)/shard_map/ppermute | solution.py:330
  159.8 11.3 %collective-permute-start.13 = (bf16[2,64,512]{2,1,0:T(8,128)(2,1)}, bf16[2,64,512]{2,1,0:T(8,128)(2,1)S(1)}, u32[]{:S(2)}, u32[]{:S(2)}) collective-permute-start(bf16[2,64,512]{2,1,0:T(8,128)(2,1)} %get-tuple-element.39), channel_id=1, source_target_pairs={{0,64},{4,68},{8,72},{12,76},{16,80},{20,84},{24,88},{28,92},{32,9... | collective-permute-start | bytes 393224 | tf_op jit(solution)/shard_map/ppermute | solution.py:330
  162.5 11.7 %collective-permute-start.14 = (bf16[2,64,512]{2,1,0:T(8,128)(2,1)}, bf16[2,64,512]{2,1,0:T(8,128)(2,1)S(1)}, u32[]{:S(2)}, u32[]{:S(2)}) collective-permute-start(bf16[2,64,512]{2,1,0:T(8,128)(2,1)} %get-tuple-element.40), channel_id=1, source_target_pairs={{0,68},{4,64},{8,76},{12,72},{16,84},{20,80},{24,92},{28,88},{32,1... | collective-permute-start | bytes 393224 | tf_op jit(solution)/shard_map/ppermute | solution.py:330
  163.1 15.1 %copy-start.10 = (bf16[2,64,512]{2,1,0:T(8,128)(2,1)}, bf16[2,64,512]{2,1,0:T(8,128)(2,1)S(1)}, u32[]{:S(2)}) copy-start(bf16[2,64,512]{2,1,0:T(8,128)(2,1)S(1)} %collective-permute-done.10.refs_1_) | copy-start | bytes 393220
  163.1 12.0 %collective-permute-start.15 = (bf16[2,64,512]{2,1,0:T(8,128)(2,1)}, bf16[2,64,512]{2,1,0:T(8,128)(2,1)S(1)}, u32[]{:S(2)}, u32[]{:S(2)}) collective-permute-start(bf16[2,64,512]{2,1,0:T(8,128)(2,1)} %get-tuple-element.41), channel_id=1, source_target_pairs={{0,96},{4,100},{8,104},{12,108},{16,112},{20,116},{24,120},{28,124... | collective-permute-start | bytes 393224 | tf_op jit(solution)/shard_map/ppermute | solution.py:330
  165.6 12.6 %copy-start.11 = (bf16[2,64,512]{2,1,0:T(8,128)(2,1)}, bf16[2,64,512]{2,1,0:T(8,128)(2,1)S(1)}, u32[]{:S(2)}) copy-start(bf16[2,64,512]{2,1,0:T(8,128)(2,1)S(1)} %collective-permute-done.11.refs_2_) | copy-start | bytes 393220
  165.6 12.6 %collective-permute-start.16 = (bf16[2,64,512]{2,1,0:T(8,128)(2,1)}, bf16[2,64,512]{2,1,0:T(8,128)(2,1)S(1)}, u32[]{:S(2)}, u32[]{:S(2)}) collective-permute-start(bf16[2,64,512]{2,1,0:T(8,128)(2,1)} %get-tuple-element.42), channel_id=1, source_target_pairs={{0,100},{4,96},{8,108},{12,104},{16,116},{20,112},{24,124},{28,120... | collective-permute-start | bytes 393224 | tf_op jit(solution)/shard_map/ppermute | solution.py:330
  167.1 11.0 %copy-start.12 = (bf16[2,64,512]{2,1,0:T(8,128)(2,1)}, bf16[2,64,512]{2,1,0:T(8,128)(2,1)S(1)}, u32[]{:S(2)}) copy-start(bf16[2,64,512]{2,1,0:T(8,128)(2,1)S(1)} %collective-permute-done.12.refs_3_) | copy-start | bytes 393220
  171.1 7.0 %copy-start.13 = (bf16[2,64,512]{2,1,0:T(8,128)(2,1)}, bf16[2,64,512]{2,1,0:T(8,128)(2,1)S(1)}, u32[]{:S(2)}) copy-start(bf16[2,64,512]{2,1,0:T(8,128)(2,1)S(1)} %collective-permute-done.13.refs_4_) | copy-start | bytes 393220
  174.2 3.9 %copy-start.14 = (bf16[2,64,512]{2,1,0:T(8,128)(2,1)}, bf16[2,64,512]{2,1,0:T(8,128)(2,1)S(1)}, u32[]{:S(2)}) copy-start(bf16[2,64,512]{2,1,0:T(8,128)(2,1)S(1)} %collective-permute-done.14.refs_5_) | copy-start | bytes 393220
  175.1 3.1 %copy-start.15 = (bf16[2,64,512]{2,1,0:T(8,128)(2,1)}, bf16[2,64,512]{2,1,0:T(8,128)(2,1)S(1)}, u32[]{:S(2)}) copy-start(bf16[2,64,512]{2,1,0:T(8,128)(2,1)S(1)} %collective-permute-done.15.refs_6_) | copy-start | bytes 393220
  178.1 0.7 copy-start.16
  180.9 12.2 %collective-permute-start.17 = (f32[64,512]{1,0:T(8,128)}, f32[64,512]{1,0:T(8,128)S(1)}, u32[]{:S(2)}, u32[]{:S(2)}) collective-permute-start(f32[64,512]{1,0:T(8,128)} %get-tuple-element.44), channel_id=1, source_target_pairs={{0,128},{4,132},{8,136},{12,140},{16,144},{20,148},{24,152},{28,15... | collective-permute-start | bytes 393224 | tf_op jit(solution)/shard_map/ppermute | solution.py:333
  194.8 0.9 copy-start.1

commit v3 on v2

--- a/solution.py
+++ b/solution.py
@@ -16,6 +16,7 @@
 LANES = 3 * CHANNELS
 PERIOD = 2 * BLOCKS * ROWS
 LAST_SCALE = 1.0 / PERIOD
+KEPT = 72
 ROOT_SCALE = 1.0 / math.sqrt(BLOCKS * ROWS)
 SENT = 4 * CHANNELS
 PLANES = [[32 * z + i for i in range(32)] for z in range(2)]
@@ -53,24 +54,26 @@
 
 
 def make_tables():
-    freq = np.arange(2 * BLOCKS)
+    freq = np.arange(KEPT)
     block = np.arange(BLOCKS)
     row = np.arange(ROWS)
     outer = 2.0 * math.pi * (freq[:, None] * block[None, :] % (2 * BLOCKS)) / (2 * BLOCKS)
     first = np.concatenate([np.cos(outer), -np.sin(outer)], axis=0)
     first = np.concatenate(split_table(first), axis=1)
-    last = np.concatenate([np.cos(outer).T, -np.sin(outer).T], axis=1)
+    weight = np.where((freq == 0) | (freq == BLOCKS), 1.0, np.where(freq < BLOCKS, 2.0, 0.0))
+    last = np.concatenate([np.cos(outer).T * weight, -np.sin(outer).T * weight], axis=1)
     last = np.concatenate(split_table(last), axis=0)
     twist = 2.0 * math.pi * (freq[:, None] * row[None, :] % PERIOD) / PERIOD
     inner = 2.0 * math.pi * (row[:, None] * row[None, :] % ROWS) / ROWS
     cosine, sine = np.cos(inner), np.sin(inner)
     ahead = np.block([[cosine, -sine], [sine, cosine]])
+    back_high, back_low = split_table(ahead.T)
     return (
         first,
         np.cos(twist).astype(np.float32),
         np.sin(twist).astype(np.float32),
-        *split_table(ahead),
-        *split_table(ahead.T),
+        np.concatenate(split_table(ahead), axis=0),
+        np.concatenate([back_high, back_high, back_low], axis=0),
         last,
     )
 
@@ -122,77 +125,91 @@
 
 
 def convolve_body(
-    signals_ref, first_ref, cos_ref, sin_ref, ahead_ref, ahead_low_ref, back_ref, back_low_ref, last_ref,
+    signals_ref, first_ref, cos_ref, sin_ref, ahead_ref, back_ref, last_ref,
     out_ref, value_ref, wide_in, wide_out, wide_value,
 ):
     wide_in[...] = signals_ref[...].astype(jnp.float32).reshape(BLOCKS * SENT, ROWS)
-    first = first_ref[...]
-    cosine = cos_ref[...]
-    sine = sin_ref[...]
-
-    def channel(place):
+
+    def step(index, carry):
+        cosine = cos_ref[...]
+        sine = sin_ref[...]
+        places = [index * UNROLL + inside for inside in range(UNROLL)]
+        number = 3 * UNROLL
         rows = jnp.concatenate(
-            [wide_in[pl.ds(place + CHANNELS * s, BLOCKS, stride=SENT), :] for s in range(3)], axis=1
+            [
+                wide_in[pl.ds(place + CHANNELS * s, BLOCKS, stride=SENT), :]
+                for place in places
+                for s in range(3)
+            ],
+            axis=1,
         ).astype(jnp.bfloat16)
-        outer = product(first, jnp.concatenate([rows, rows], axis=0))
+        outer = product(first_ref[...], jnp.concatenate([rows, rows], axis=0))
         turned = []
-        for s in range(3):
-            real_part = outer[:128, s * 128 : s * 128 + 128]
-            other_part = outer[128:, s * 128 : s * 128 + 128]
-            turned_real = (real_part * cosine + other_part * sine).astype(jnp.bfloat16)
-            turned_other = (other_part * cosine - real_part * sine).astype(jnp.bfloat16)
-            turned.append(jnp.concatenate([turned_real, turned_other], axis=1))
-        turned = jnp.concatenate(turned, axis=0)
-        spectra = product(turned, ahead_ref[...]) + product(turned, ahead_low_ref[...])
-        mixed_real, mixed_other = spectra[:128, :128], spectra[:128, 128:]
-        taps_real, taps_other = spectra[128:256, :128], spectra[128:256, 128:]
-        gated_real, gated_other = spectra[256:, :128], spectra[256:, 128:]
-        pairs = jnp.concatenate(
-            [
-                jnp.concatenate(pair, axis=1)
-                for pair in (
-                    (
-                        mixed_real * taps_real - mixed_other * taps_other,
-                        mixed_real * taps_other + mixed_other * taps_real,
-                    ),
-                    (
-                        gated_real * taps_real + gated_other * taps_other,
-                        gated_other * taps_real - gated_real * taps_other,
-                    ),
-                    (
-                        gated_real * mixed_real + gated_other * mixed_other,
-                        gated_other * mixed_real - gated_real * mixed_other,
-                    ),
+        for n in range(number):
+            real_part = outer[:KEPT, n * 128 : n * 128 + 128]
+            other_part = outer[KEPT:, n * 128 : n * 128 + 128]
+            turned.append(
+                jnp.concatenate(
+                    [
+                        real_part * cosine + other_part * sine,
+                        other_part * cosine - real_part * sine,
+                    ],
+                    axis=1,
                 )
-            ],
-            axis=0,
-        )
+            )
+        turned = jnp.concatenate(turned, axis=0).astype(jnp.bfloat16)
+        spectra = product(jnp.concatenate([turned, turned], axis=1), ahead_ref[...])
+        pairs = []
+        for n in range(UNROLL):
+            parts = [
+                (spectra[start : start + KEPT, :128], spectra[start : start + KEPT, 128:])
+                for start in range(3 * n * KEPT, (3 * n + 3) * KEPT, KEPT)
+            ]
+            (mixed_real, mixed_other), (taps_real, taps_other), (gated_real, gated_other) = parts
+            for pair in (
+                (
+                    mixed_real * taps_real - mixed_other * taps_other,
+                    mixed_real * taps_other + mixed_other * taps_real,
+                ),
+                (
+                    gated_real * taps_real + gated_other * taps_other,
+                    gated_other * taps_real - gated_real * taps_other,
+                ),
+                (
+                    gated_real * mixed_real + gated_other * mixed_other,
+                    gated_other * mixed_real - gated_real * mixed_other,
+                ),
+            ):
+                pairs.append(jnp.concatenate(pair, axis=1))
+        pairs = jnp.concatenate(pairs, axis=0)
         high = pairs.astype(jnp.bfloat16)
         low = (pairs - high.astype(jnp.float32)).astype(jnp.bfloat16)
-        rowed = (
-            product(high, back_ref[...]) + product(low, back_ref[...]) + product(high, back_low_ref[...])
-        )
+        rowed = product(jnp.concatenate([high, low, high], axis=1), back_ref[...])
         bent = []
-        for s in range(3):
-            real_part = rowed[s * 128 : s * 128 + 128, :128]
-            other_part = rowed[s * 128 : s * 128 + 128, 128:]
-            bent_real = (real_part * cosine - other_part * sine).astype(jnp.bfloat16)
-            bent_other = (real_part * sine + other_part * cosine).astype(jnp.bfloat16)
-            bent.append(jnp.concatenate([bent_real, bent_other], axis=0))
-        total = product(last_ref[...], jnp.concatenate(bent, axis=1))
+        for n in range(number):
+            real_part = rowed[n * KEPT : n * KEPT + KEPT, :128]
+            other_part = rowed[n * KEPT : n * KEPT + KEPT, 128:]
+            bent.append(
+                jnp.concatenate(
+                    [
+                        real_part * cosine - other_part * sine,
+                        real_part * sine + other_part * cosine,
+                    ],
+                    axis=0,
+                )
+            )
+        total = product(last_ref[...], jnp.concatenate(bent, axis=1).astype(jnp.bfloat16))
         total = total[:BLOCKS] + total[BLOCKS:]
-        for s in range(3):
+        for n in range(number):
+            s, place = n % 3, places[n // 3]
             factor = LAST_SCALE * (ROOT_SCALE if s == 2 else 1.0)
-            wide_out[pl.ds(place + CHANNELS * s, BLOCKS, stride=LANES), :] = (
-                total[:, s * 128 : s * 128 + 128] * factor
-            )
-        back = (total[:, 128:256] * LAST_SCALE).astype(jnp.bfloat16).astype(jnp.float32)
-        key = wide_in[pl.ds(place + CHANNELS * 3, BLOCKS, stride=SENT), :]
-        wide_value[pl.ds(place, BLOCKS, stride=CHANNELS), :] = back * key
-
-    def step(index, carry):
-        for inside in range(UNROLL):
-            channel(index * UNROLL + inside)
+            result = total[:, n * 128 : n * 128 + 128] * factor
+            wide_out[pl.ds(place + CHANNELS * s, BLOCKS, stride=LANES), :] = result
+            if s == 1:
+                key = wide_in[pl.ds(place + CHANNELS * 3, BLOCKS, stride=SENT), :]
+                wide_value[pl.ds(place, BLOCKS, stride=CHANNELS), :] = (
+                    result.astype(jnp.bfloat16).astype(jnp.float32) * key
+                )
         return carry
 
     lax.fori_loop(0, CHANNELS // UNROLL, step, 0)
@@ -331,9 +348,7 @@
     results = exchange(results)
     kept, sent = weight_total(where, parts)
     received = lax.ppermute(sent, "seq", opposite())
-    grad_query, grad_key, grad_value, grad_filter = finish(
-        results, grad_out, value_proj, gate_key
-    )
+    grad_query, grad_key, grad_value, grad_filter = finish(results, grad_out, value_proj, gate_key)
     grad_weight = jnp.where(
         z == 0,
         jnp.concatenate([kept, received], axis=1),

time: 199 us -> 192 us (0.965)
  Pallas kernels: 32.5 us -> 25.3 us
    pallas_call x1, Pallas kernels: 19 us -> 11.9 us  [convolve(): pl.pallas_call(convolve_body, out_shape=(jax.ShapeDtypeStruct((BLOCKS, LA...]
where the time goes in v3:
time: 192 us; the launch traced here: 191 us
  waiting for transfers between devices  68.6 us (36%)
  starting transfers between devices  51.9 us (27%)
  blocking collectives  39 us (20%)
  Pallas kernels  25.3 us (13%)
  other arithmetic  3.25 us (2%)
  local copies, waits for them, and re-layouts  2.27 us (1%)
    all_to_all x1, blocking collectives, exchange(): lax.all_to_all(array, 'seq', split_axis=0, concat_axis=0, tiled=True, axi...  39 us
    ppermute x7, waiting for transfers between devices, ring_step(): return lax.ppermute(array, ('seq', 'chan'), along_z(shift))  26.8 us
    all_to_all x2, waiting for transfers between devices, exchange(): lax.all_to_all(array, 'seq', split_axis=0, concat_axis=0, tiled=True, axi...  17 us
    all_to_all x2, starting transfers between devices, exchange(): lax.all_to_all(array, 'seq', split_axis=0, concat_axis=0, tiled=True, axi...  16.6 us
    ppermute x7, starting transfers between devices, ring_step(): return lax.ppermute(array, ('seq', 'chan'), along_z(shift))  15.7 us
    pallas_call x1, Pallas kernels, convolve(): pl.pallas_call(convolve_body, out_shape=(jax.ShapeDtypeStruct((BLOCKS, LA...  11.9 us
    ppermute x7, starting transfers between devices, shards(): lax.ppermute(parts[n], 'seq', across(n))  11.3 us
    ppermute x7, waiting for transfers between devices, shards(): lax.ppermute(parts[n], 'seq', across(n))  11 us
  transfers between devices with their start and end apart: 20, of which 13 were waited for; matrix products, arithmetic and copies ran while one was open for 2% of the time, Pallas kernels for 4%

profile of v3, /device:TPU:1, one launch (start us, length us, event | category | flops | bytes accessed | tf_op | source)
XLA Modules:
  0.0 191.2 jit_solution(286649103451315599)
XLA Ops:
  0.6 2.6 %gather_signals.1 = bf16[64,64,128]{2,1,0:T(8,128)(2,1)} custom-call(bf16[128,1024]{1,0:T(8,128)(2,1)} %key_ref.3, bf16[128,1024]{1,0:T(8,128)(2,1)} %value_ref.3, bf16[128,1024]{1,0:T(8,128)(2,1)} %grad_ref.3, bf16[128,1024]{1,0:T(8,128)(2,1)} %query_ref.1, bf16[128,1024]{1,0:T(8,128)(2,1)} %taps_ref.1), custom_call_target="tpu_custom_call" | custom-call | tf_op jit(solution)/shard_map/gather_signals/pallas_call | solution.py:97
  3.3 39.0 %all_to_all.15.signals_ref = bf16[64,64,128]{2,1,0:T(8,128)(2,1)} all-to-all(bf16[64,64,128]{2,1,0:T(8,128)(2,1)} %gather_signals.1), channel_id=1, replica_groups=mesh['seq'=64,'chan'=4] {'seq'}, dimensions={0} | all-to-all | bytes 2097152 | tf_op jit(solution)/shard_map/all_to_all | solution.py:322
  42.2 11.9 %convolve.1 = (bf16[64,48,128]{2,1,0:T(8,128)(2,1)}, bf16[32,8,16,128]{3,2,1,0:T(8,128)(2,1)}) custom-call(bf16[64,64,128]{2,1,0:T(8,128)(2,1)} %all_to_all.15.signals_ref, bf16[144,128]{1,0:T(8,128)(2,1)} %constant.81.clone.first_ref, f32[72,128]{1,0:T(8,128)} %constant.82.clone.cos_ref, f32[72,128]{1,0:T(8,128)} %constant.83.clone.sin_ref, ...), custom_call_target="tpu_custom_call" | custom-call | tf_op jit(solution)/shard_map/convolve/pallas_call | solution.py:225
  54.2 12.1 %all-to-all-start.2 = ((bf16[32,8,16,128]{3,2,1,0:T(8,128)(2,1)}), bf16[32,8,16,128]{3,2,1,0:T(8,128)(2,1)S(1)}, u32[]{:S(2)}, u32[]{:S(2)}) async-start(bf16[32,8,16,128]{3,2,1,0:T(8,128)(2,1)} %get-tuple-element.30), calls=%async_computation.2 | async-start | bytes 2097152 | tf_op jit(solution)/shard_map/all_to_all | solution.py:322
  66.4 17.0 %all-to-all-done.2.value_ref = bf16[32,8,16,128]{3,2,1,0:T(8,128)(2,1)S(1)} async-done(((bf16[32,8,16,128]{3,2,1,0:T(8,128)(2,1)}), bf16[32,8,16,128]{3,2,1,0:T(8,128)(2,1)S(1)}, u32[]{:S(2)}, u32[]{:S(2)}) %all-to-all-start.2) | async-done | bytes 1048608 | tf_op jit(solution)/shard_map/all_to_all | solution.py:322
  83.3 4.5 %all-to-all-start.1 = ((bf16[64,48,128]{2,1,0:T(8,128)(2,1)}), bf16[64,48,128]{2,1,0:T(8,128)(2,1)S(1)}, u32[]{:S(2)}, u32[]{:S(2)}) async-start(bf16[64,48,128]{2,1,0:T(8,128)(2,1)} %get-tuple-element.25), calls=%async_computation.1 | async-start | bytes 1572864 | tf_op jit(solution)/shard_map/all_to_all | solution.py:322
  87.8 0.7 pad_add_fusion.where_ref
  88.5 1.8 split_features.1
  90.3 1.4 collective-permute-start
  91.6 2.4 %collective-permute-start.1 = (bf16[256,128]{1,0:T(8,128)(2,1)}, bf16[256,128]{1,0:T(8,128)(2,1)S(1)}, u32[]{:S(2)}, u32[]{:S(2)}) collective-permute-start(bf16[256,128]{1,0:T(8,128)(2,1)} %get-tuple-element.33), channel_id=1, source_target_pairs={{0,16},{4,20},{8,24},{12,28},{16,0},{20,4},{24,8},{28,12},{32,48},... | collective-permute-start | bytes 196616 | tf_op jit(solution)/shard_map/ppermute | solution.py:337
  94.0 1.2 collective-permute-start.2
  95.2 1.7 collective-permute-done
  96.9 3.3 %collective-permute-done.1 = bf16[256,128]{1,0:T(8,128)(2,1)S(1)} collective-permute-done((bf16[256,128]{1,0:T(8,128)(2,1)}, bf16[256,128]{1,0:T(8,128)(2,1)S(1)}, u32[]{:S(2)}, u32[]{:S(2)}) %collective-permute-start.1) | collective-permute-done | bytes 65568 | tf_op jit(solution)/shard_map/ppermute | solution.py:337
  100.2 0.0 collective-permute-done.2
  100.2 0.9 pad_maximum_fusion.refs_0_
  101.0 0.0 copy-start.2
  101.1 6.6 %collective-permute-start.7 = (bf16[4,256,128]{2,1,0:T(8,128)(2,1)S(1)}, bf16[4,256,128]{2,1,0:T(8,128)(2,1)S(1)}, u32[]{:S(2)}, u32[]{:S(2)}) collective-permute-start(bf16[4,256,128]{2,1,0:T(8,128)(2,1)S(1)} %pad_maximum_fusion.refs_0_), channel_id=1, source_target_pairs={{0,131},{1,0},{2,1},{3,2},{4,135},{5,4},{6,5},{7,6},{8,139},{9,8},... | collective-permute-start | bytes 786440 | tf_op jit(solution)/shard_map/ppermute | solution.py:328
  107.7 5.2 %collective-permute-done.7.refs_7_ = bf16[4,256,128]{2,1,0:T(8,128)(2,1)S(1)} collective-permute-done((bf16[4,256,128]{2,1,0:T(8,128)(2,1)S(1)}, bf16[4,256,128]{2,1,0:T(8,128)(2,1)S(1)}, u32[]{:S(2)}, u32[]{:S(2)}) %collective-permute-start.7) | collective-permute-done | bytes 262176 | tf_op jit(solution)/shard_map/ppermute | solution.py:328
  112.9 3.2 %collective-permute-start.8 = (bf16[4,256,128]{2,1,0:T(8,128)(2,1)S(1)}, bf16[4,256,128]{2,1,0:T(8,128)(2,1)S(1)}, u32[]{:S(2)}, u32[]{:S(2)}) collective-permute-start(bf16[4,256,128]{2,1,0:T(8,128)(2,1)S(1)} %collective-permute-done.7.refs_7_), channel_id=1, source_target_pairs={{0,131},{1,0},{2,1},{3,2},{4,135},{5,4},{6,5},{7,6},{8,139},{9,8},... | collective-permute-start | bytes 786440 | tf_op jit(solution)/shard_map/ppermute | solution.py:328
  116.2 1.5 collective-permute-start.4
  117.7 5.4 %collective-permute-done.8.refs_6_ = bf16[4,256,128]{2,1,0:T(8,128)(2,1)S(1)} collective-permute-done((bf16[4,256,128]{2,1,0:T(8,128)(2,1)S(1)}, bf16[4,256,128]{2,1,0:T(8,128)(2,1)S(1)}, u32[]{:S(2)}, u32[]{:S(2)}) %collective-permute-start.8) | collective-permute-done | bytes 262176 | tf_op jit(solution)/shard_map/ppermute | solution.py:328
  123.1 0.7 collective-permute-start.9
  123.8 1.8 collective-permute-start.6
  125.6 1.9 collective-permute-start.5
  127.5 2.1 %collective-permute-done.9.refs_5_ = bf16[4,256,128]{2,1,0:T(8,128)(2,1)S(1)} collective-permute-done((bf16[4,256,128]{2,1,0:T(8,128)(2,1)S(1)}, bf16[4,256,128]{2,1,0:T(8,128)(2,1)S(1)}, u32[]{:S(2)}, u32[]{:S(2)}) %collective-permute-start.9) | collective-permute-done | bytes 262176 | tf_op jit(solution)/shard_map/ppermute | solution.py:328
  129.5 9.0 %collective-permute-done.6.refs_4_ = bf16[4,256,128]{2,1,0:T(8,128)(2,1)S(1)} collective-permute-done((bf16[4,256,128]{2,1,0:T(8,128)(2,1)S(1)}, bf16[4,256,128]{2,1,0:T(8,128)(2,1)S(1)}, u32[]{:S(2)}, u32[]{:S(2)}) %collective-permute-start.6) | collective-permute-done | bytes 262176 | tf_op jit(solution)/shard_map/ppermute | solution.py:328
  138.6 5.1 %collective-permute-done.5.refs_3_ = bf16[4,256,128]{2,1,0:T(8,128)(2,1)S(1)} collective-permute-done((bf16[4,256,128]{2,1,0:T(8,128)(2,1)S(1)}, bf16[4,256,128]{2,1,0:T(8,128)(2,1)S(1)}, u32[]{:S(2)}, u32[]{:S(2)}) %collective-permute-start.5) | collective-permute-done | bytes 262176 | tf_op jit(solution)/shard_map/ppermute | solution.py:328
  143.7 0.0 copy-start.9
  143.7 0.7 copy-done.9
  144.4 4.3 %weight_parts.1 = (bf16[2,64,512]{2,1,0:T(8,128)(2,1)}, bf16[2,64,512]{2,1,0:T(8,128)(2,1)}, bf16[2,64,512]{2,1,0:T(8,128)(2,1)}, bf16[2,64,512]{2,1,0:T(8,128)(...) custom-call(s32[4]{0:T(128)} %pad_add_fusion.where_ref, ...), custom_call_target="tpu_custom_call" | custom-call | tf_op jit(solution)/shard_map/weight_parts/pallas_call | solution.py:290
  148.7 2.2 %collective-permute-start.10 = (bf16[2,64,512]{2,1,0:T(8,128)(2,1)}, bf16[2,64,512]{2,1,0:T(8,128)(2,1)S(1)}, u32[]{:S(2)}, u32[]{:S(2)}) collective-permute-start(bf16[2,64,512]{2,1,0:T(8,128)(2,1)} %get-tuple-element.36), channel_id=1, source_target_pairs={{0,4},{4,0},{8,12},{12,8},{16,20},{20,16},{24,28},{28,24},{32,36},... | collective-permute-start | bytes 393224 | tf_op jit(solution)/shard_map/ppermute | solution.py:347
  151.0 1.4 collective-permute-start.11
  152.4 0.3 collective-permute-start.12
  152.7 2.8 %collective-permute-start.13 = (bf16[2,64,512]{2,1,0:T(8,128)(2,1)}, bf16[2,64,512]{2,1,0:T(8,128)(2,1)S(1)}, u32[]{:S(2)}, u32[]{:S(2)}) collective-permute-start(bf16[2,64,512]{2,1,0:T(8,128)(2,1)} %get-tuple-element.39), channel_id=1, source_target_pairs={{0,64},{4,68},{8,72},{12,76},{16,80},{20,84},{24,88},{28,92},{32,9... | collective-permute-start | bytes 393224 | tf_op jit(solution)/shard_map/ppermute | solution.py:347
  155.4 0.5 collective-permute-start.14
  156.0 2.5 %collective-permute-start.15 = (bf16[2,64,512]{2,1,0:T(8,128)(2,1)}, bf16[2,64,512]{2,1,0:T(8,128)(2,1)S(1)}, u32[]{:S(2)}, u32[]{:S(2)}) collective-permute-start(bf16[2,64,512]{2,1,0:T(8,128)(2,1)} %get-tuple-element.41), channel_id=1, source_target_pairs={{0,96},{4,100},{8,104},{12,108},{16,112},{20,116},{24,120},{28,124... | collective-permute-start | bytes 393224 | tf_op jit(solution)/shard_map/ppermute | solution.py:347
  158.4 1.6 collective-permute-start.16
  160.0 4.0 %collective-permute-done.13.refs_4_ = bf16[2,64,512]{2,1,0:T(8,128)(2,1)S(1)} collective-permute-done((bf16[2,64,512]{2,1,0:T(8,128)(2,1)}, bf16[2,64,512]{2,1,0:T(8,128)(2,1)S(1)}, u32[]{:S(2)}, u32[]{:S(2)}) %collective-permute-start.13) | collective-permute-done | bytes 131104 | tf_op jit(solution)/shard_map/ppermute | solution.py:347
  164.0 3.1 %collective-permute-done.14.refs_5_ = bf16[2,64,512]{2,1,0:T(8,128)(2,1)S(1)} collective-permute-done((bf16[2,64,512]{2,1,0:T(8,128)(2,1)}, bf16[2,64,512]{2,1,0:T(8,128)(2,1)S(1)}, u32[]{:S(2)}, u32[]{:S(2)}) %collective-permute-start.14) | collective-permute-done | bytes 131104 | tf_op jit(solution)/shard_map/ppermute | solution.py:347
  167.1 0.8 collective-permute-done.15.refs_6_
  168.0 3.1 %collective-permute-done.16.refs_7_ = bf16[2,64,512]{2,1,0:T(8,128)(2,1)S(1)} collective-permute-done((bf16[2,64,512]{2,1,0:T(8,128)(2,1)}, bf16[2,64,512]{2,1,0:T(8,128)(2,1)S(1)}, u32[]{:S(2)}, u32[]{:S(2)}) %collective-permute-start.16) | collective-permute-done | bytes 131104 | tf_op jit(solution)/shard_map/ppermute | solution.py:347
  171.1 0.6 copy-done.16
  171.7 2.1 %weight_total.1 = (f32[64,512]{1,0:T(8,128)}, f32[64,512]{1,0:T(8,128)}) custom-call(s32[4]{0:T(128)} %pad_add_fusion.where_ref, bf16[2,64,512]{2,1,0:T(8,128)(2,1)} %get-tuple-element.35.refs_0_, bf16[2,64,512]{2,1,0:T(8,128)(2,1)} %copy-done.10, bf16[2,64,512]{2,1,0:T(8,128)(2,1)} %copy-done.11, bf16[2,64,512]{2,1,0:T(8,128)(2,1)} %copy-done.12, ...), custom_call_target="tpu_custom_call" | custom-call | tf_op jit(solution)/shard_map/weight_total/pallas_call | solution.py:313
  173.8 3.3 %collective-permute-start.17 = (f32[64,512]{1,0:T(8,128)}, f32[64,512]{1,0:T(8,128)S(1)}, u32[]{:S(2)}, u32[]{:S(2)}) collective-permute-start(f32[64,512]{1,0:T(8,128)} %get-tuple-element.44), channel_id=1, source_target_pairs={{0,128},{4,132},{8,136},{12,140},{16,144},{20,148},{24,152},{28,15... | collective-permute-start | bytes 393224 | tf_op jit(solution)/shard_map/ppermute | solution.py:350
  177.1 8.9 %collective-permute-done.17 = f32[64,512]{1,0:T(8,128)S(1)} collective-permute-done((f32[64,512]{1,0:T(8,128)}, f32[64,512]{1,0:T(8,128)S(1)}, u32[]{:S(2)}, u32[]{:S(2)}) %collective-permute-start.17) | collective-permute-done | bytes 131104 | tf_op jit(solution)/shard_map/ppermute | solution.py:350
  186.0 1.7 maximum_select_fusion
  187.7 0.9 copy-done.1
  188.6 2.6 %finish.1 = (bf16[128,1024]{1,0:T(8,128)(2,1)}, bf16[128,1024]{1,0:T(8,128)(2,1)}, bf16[128,1024]{1,0:T(8,128)(2,1)}, bf16[128,1024]{1,0:T(8,128)(2,1)}) custom-call(bf16[64,48,128]{2,1,0:T(8,128)(2,1)} %copy-done.1, bf16[128,1024]{1,0:T(8,128)(2,1)} %grad_ref.3, bf16[128,1024]{1,0:T(8,128)(2,1)} %value_ref.3, bf16[128,1024]{1,0:T(8,128)(2,1)} %key_ref.3), custom_call_target="tpu_custom_call" | custom-call | tf_op jit(solution)/shard_map/finish/pallas_call | solution.py:257
  (36 shorter events, 0.1 us)
Async XLA Ops:
  54.2 29.2 %all-to-all-start.2 = ((bf16[32,8,16,128]{3,2,1,0:T(8,128)(2,1)}), bf16[32,8,16,128]{3,2,1,0:T(8,128)(2,1)S(1)}, u32[]{:S(2)}, u32[]{:S(2)}) async-start(bf16[32,8,16,128]{3,2,1,0:T(8,128)(2,1)} %get-tuple-element.30), calls=%async_computation.2 | async-start | bytes 2097152 | tf_op jit(solution)/shard_map/all_to_all | solution.py:322
  83.3 17.7 %copy-start = (bf16[32,8,16,128]{3,2,1,0:T(8,128)(2,1)}, bf16[32,8,16,128]{3,2,1,0:T(8,128)(2,1)S(1)}, u32[]{:S(2)}) copy-start(bf16[32,8,16,128]{3,2,1,0:T(8,128)(2,1)S(1)} %all-to-all-done.2.value_ref) | copy-start | bytes 3145732
  83.3 104.3 %all-to-all-start.1 = ((bf16[64,48,128]{2,1,0:T(8,128)(2,1)}), bf16[64,48,128]{2,1,0:T(8,128)(2,1)S(1)}, u32[]{:S(2)}, u32[]{:S(2)}) async-start(bf16[64,48,128]{2,1,0:T(8,128)(2,1)} %get-tuple-element.25), calls=%async_computation.1 | async-start | bytes 1572864 | tf_op jit(solution)/shard_map/all_to_all | solution.py:322
  90.3 6.6 %collective-permute-start = (bf16[256,128]{1,0:T(8,128)(2,1)}, bf16[256,128]{1,0:T(8,128)(2,1)S(1)}, u32[]{:S(2)}, u32[]{:S(2)}) collective-permute-start(bf16[256,128]{1,0:T(8,128)(2,1)} %get-tuple-element.32), channel_id=1, source_target_pairs={{0,8},{4,12},{8,16},{12,20},{16,24},{20,28},{24,0},{28,4},{32,40},... | collective-permute-start | bytes 196616 | tf_op jit(solution)/shard_map/ppermute | solution.py:337
  91.6 8.5 %collective-permute-start.1 = (bf16[256,128]{1,0:T(8,128)(2,1)}, bf16[256,128]{1,0:T(8,128)(2,1)S(1)}, u32[]{:S(2)}, u32[]{:S(2)}) collective-permute-start(bf16[256,128]{1,0:T(8,128)(2,1)} %get-tuple-element.33), channel_id=1, source_target_pairs={{0,16},{4,20},{8,24},{12,28},{16,0},{20,4},{24,8},{28,12},{32,48},... | collective-permute-start | bytes 196616 | tf_op jit(solution)/shard_map/ppermute | solution.py:337
  94.0 6.1 %collective-permute-start.2 = (bf16[256,128]{1,0:T(8,128)(2,1)}, bf16[256,128]{1,0:T(8,128)(2,1)S(1)}, u32[]{:S(2)}, u32[]{:S(2)}) collective-permute-start(bf16[256,128]{1,0:T(8,128)(2,1)} %get-tuple-element.34), channel_id=1, source_target_pairs={{0,24},{4,28},{8,0},{12,4},{16,8},{20,12},{24,16},{28,20},{32,56},... | collective-permute-start | bytes 196616 | tf_op jit(solution)/shard_map/ppermute | solution.py:337
  101.0 42.6 %copy-start.2 = (bf16[4,256,128]{2,1,0:T(8,128)(2,1)}, bf16[4,256,128]{2,1,0:T(8,128)(2,1)S(1)}, u32[]{:S(2)}) copy-start(bf16[4,256,128]{2,1,0:T(8,128)(2,1)S(1)} %pad_maximum_fusion.refs_0_) | copy-start | bytes 786436
  101.1 11.9 %collective-permute-start.7 = (bf16[4,256,128]{2,1,0:T(8,128)(2,1)S(1)}, bf16[4,256,128]{2,1,0:T(8,128)(2,1)S(1)}, u32[]{:S(2)}, u32[]{:S(2)}) collective-permute-start(bf16[4,256,128]{2,1,0:T(8,128)(2,1)S(1)} %pad_maximum_fusion.refs_0_), channel_id=1, source_target_pairs={{0,131},{1,0},{2,1},{3,2},{4,135},{5,4},{6,5},{7,6},{8,139},{9,8},... | collective-permute-start | bytes 786440 | tf_op jit(solution)/shard_map/ppermute | solution.py:328
  107.7 8.5 %collective-permute-start.3 = (bf16[4,256,128]{2,1,0:T(8,128)(2,1)S(1)}, bf16[4,256,128]{2,1,0:T(8,128)(2,1)S(1)}, u32[]{:S(2)}, u32[]{:S(2)}) collective-permute-start(bf16[4,256,128]{2,1,0:T(8,128)(2,1)S(1)} %pad_maximum_fusion.refs_0_), channel_id=1, source_target_pairs={{0,1},{1,2},{2,3},{3,128},{4,5},{5,6},{6,7},{7,132},{8,9},{9,10},{... | collective-permute-start | bytes 786440 | tf_op jit(solution)/shard_map/ppermute | solution.py:328
  112.9 30.7 %copy-start.3 = (bf16[4,256,128]{2,1,0:T(8,128)(2,1)}, bf16[4,256,128]{2,1,0:T(8,128)(2,1)S(1)}, u32[]{:S(2)}) copy-start(bf16[4,256,128]{2,1,0:T(8,128)(2,1)S(1)} %collective-permute-done.7.refs_7_) | copy-start | bytes 786436
  112.9 10.2 %collective-permute-start.8 = (bf16[4,256,128]{2,1,0:T(8,128)(2,1)S(1)}, bf16[4,256,128]{2,1,0:T(8,128)(2,1)S(1)}, u32[]{:S(2)}, u32[]{:S(2)}) collective-permute-start(bf16[4,256,128]{2,1,0:T(8,128)(2,1)S(1)} %collective-permute-done.7.refs_7_), channel_id=1, source_target_pairs={{0,131},{1,0},{2,1},{3,2},{4,135},{5,4},{6,5},{7,6},{8,139},{9,8},... | collective-permute-start | bytes 786440 | tf_op jit(solution)/shard_map/ppermute | solution.py:328
  116.2 27.5 %copy-start.4 = (bf16[4,256,128]{2,1,0:T(8,128)(2,1)}, bf16[4,256,128]{2,1,0:T(8,128)(2,1)S(1)}, u32[]{:S(2)}) copy-start(bf16[4,256,128]{2,1,0:T(8,128)(2,1)S(1)} %collective-permute-done.3.refs_1_) | copy-start | bytes 786436
  116.2 7.6 %collective-permute-start.4 = (bf16[4,256,128]{2,1,0:T(8,128)(2,1)S(1)}, bf16[4,256,128]{2,1,0:T(8,128)(2,1)S(1)}, u32[]{:S(2)}, u32[]{:S(2)}) collective-permute-start(bf16[4,256,128]{2,1,0:T(8,128)(2,1)S(1)} %collective-permute-done.3.refs_1_), channel_id=1, source_target_pairs={{0,1},{1,2},{2,3},{3,128},{4,5},{5,6},{6,7},{7,132},{8,9},{9,10},{... | collective-permute-start | bytes 786440 | tf_op jit(solution)/shard_map/ppermute | solution.py:328
  123.1 20.5 %copy-start.5 = (bf16[4,256,128]{2,1,0:T(8,128)(2,1)}, bf16[4,256,128]{2,1,0:T(8,128)(2,1)S(1)}, u32[]{:S(2)}) copy-start(bf16[4,256,128]{2,1,0:T(8,128)(2,1)S(1)} %collective-permute-done.8.refs_6_) | copy-start | bytes 786436
  123.1 6.4 %collective-permute-start.9 = (bf16[4,256,128]{2,1,0:T(8,128)(2,1)S(1)}, bf16[4,256,128]{2,1,0:T(8,128)(2,1)S(1)}, u32[]{:S(2)}, u32[]{:S(2)}) collective-permute-start(bf16[4,256,128]{2,1,0:T(8,128)(2,1)S(1)} %collective-permute-done.8.refs_6_), channel_id=1, source_target_pairs={{0,131},{1,0},{2,1},{3,2},{4,135},{5,4},{6,5},{7,6},{8,139},{9,8},... | collective-permute-start | bytes 786440 | tf_op jit(solution)/shard_map/ppermute | solution.py:328
  123.8 19.8 %copy-start.6 = (bf16[4,256,128]{2,1,0:T(8,128)(2,1)}, bf16[4,256,128]{2,1,0:T(8,128)(2,1)S(1)}, u32[]{:S(2)}) copy-start(bf16[4,256,128]{2,1,0:T(8,128)(2,1)S(1)} %collective-permute-done.4.refs_2_) | copy-start | bytes 786436
  123.8 14.7 %collective-permute-start.6 = (bf16[4,256,128]{2,1,0:T(8,128)(2,1)S(1)}, bf16[4,256,128]{2,1,0:T(8,128)(2,1)S(1)}, u32[]{:S(2)}, u32[]{:S(2)}) collective-permute-start(bf16[4,256,128]{2,1,0:T(8,128)(2,1)S(1)} %collective-permute-done.4.refs_2_), channel_id=1, source_target_pairs={{0,2},{1,3},{2,128},{3,129},{4,6},{5,7},{6,132},{7,133},{8,10},{9,... | collective-permute-start | bytes 786440 | tf_op jit(solution)/shard_map/ppermute | solution.py:328
  125.6 18.1 %collective-permute-start.5 = (bf16[4,256,128]{2,1,0:T(8,128)(2,1)S(1)}, bf16[4,256,128]{2,1,0:T(8,128)(2,1)S(1)}, u32[]{:S(2)}, u32[]{:S(2)}) collective-permute-start(bf16[4,256,128]{2,1,0:T(8,128)(2,1)S(1)} %collective-permute-done.4.refs_2_), channel_id=1, source_target_pairs={{0,1},{1,2},{2,3},{3,128},{4,5},{5,6},{6,7},{7,132},{8,9},{9,10},{... | collective-permute-start | bytes 786440 | tf_op jit(solution)/shard_map/ppermute | solution.py:328
  129.5 14.2 %copy-start.7 = (bf16[4,256,128]{2,1,0:T(8,128)(2,1)}, bf16[4,256,128]{2,1,0:T(8,128)(2,1)S(1)}, u32[]{:S(2)}) copy-start(bf16[4,256,128]{2,1,0:T(8,128)(2,1)S(1)} %collective-permute-done.9.refs_5_) | copy-start | bytes 786436
  138.6 5.1 %copy-start.8 = (bf16[4,256,128]{2,1,0:T(8,128)(2,1)}, bf16[4,256,128]{2,1,0:T(8,128)(2,1)S(1)}, u32[]{:S(2)}) copy-start(bf16[4,256,128]{2,1,0:T(8,128)(2,1)S(1)} %collective-permute-done.6.refs_4_) | copy-start | bytes 786436
  143.7 0.7 copy-start.9
  148.7 7.2 %collective-permute-start.10 = (bf16[2,64,512]{2,1,0:T(8,128)(2,1)}, bf16[2,64,512]{2,1,0:T(8,128)(2,1)S(1)}, u32[]{:S(2)}, u32[]{:S(2)}) collective-permute-start(bf16[2,64,512]{2,1,0:T(8,128)(2,1)} %get-tuple-element.36), channel_id=1, source_target_pairs={{0,4},{4,0},{8,12},{12,8},{16,20},{20,16},{24,28},{28,24},{32,36},... | collective-permute-start | bytes 393224 | tf_op jit(solution)/shard_map/ppermute | solution.py:347
  151.0 7.5 %collective-permute-start.11 = (bf16[2,64,512]{2,1,0:T(8,128)(2,1)}, bf16[2,64,512]{2,1,0:T(8,128)(2,1)S(1)}, u32[]{:S(2)}, u32[]{:S(2)}) collective-permute-start(bf16[2,64,512]{2,1,0:T(8,128)(2,1)} %get-tuple-element.37), channel_id=1, source_target_pairs={{0,32},{4,36},{8,40},{12,44},{16,48},{20,52},{24,56},{28,60},{32,0... | collective-permute-start | bytes 393224 | tf_op jit(solution)/shard_map/ppermute | solution.py:347
  152.4 7.6 %collective-permute-start.12 = (bf16[2,64,512]{2,1,0:T(8,128)(2,1)}, bf16[2,64,512]{2,1,0:T(8,128)(2,1)S(1)}, u32[]{:S(2)}, u32[]{:S(2)}) collective-permute-start(bf16[2,64,512]{2,1,0:T(8,128)(2,1)} %get-tuple-element.38), channel_id=1, source_target_pairs={{0,36},{4,32},{8,44},{12,40},{16,52},{20,48},{24,60},{28,56},{32,4... | collective-permute-start | bytes 393224 | tf_op jit(solution)/shard_map/ppermute | solution.py:347
  152.7 11.3 %collective-permute-start.13 = (bf16[2,64,512]{2,1,0:T(8,128)(2,1)}, bf16[2,64,512]{2,1,0:T(8,128)(2,1)S(1)}, u32[]{:S(2)}, u32[]{:S(2)}) collective-permute-start(bf16[2,64,512]{2,1,0:T(8,128)(2,1)} %get-tuple-element.39), channel_id=1, source_target_pairs={{0,64},{4,68},{8,72},{12,76},{16,80},{20,84},{24,88},{28,92},{32,9... | collective-permute-start | bytes 393224 | tf_op jit(solution)/shard_map/ppermute | solution.py:347
  155.4 11.7 %collective-permute-start.14 = (bf16[2,64,512]{2,1,0:T(8,128)(2,1)}, bf16[2,64,512]{2,1,0:T(8,128)(2,1)S(1)}, u32[]{:S(2)}, u32[]{:S(2)}) collective-permute-start(bf16[2,64,512]{2,1,0:T(8,128)(2,1)} %get-tuple-element.40), channel_id=1, source_target_pairs={{0,68},{4,64},{8,76},{12,72},{16,84},{20,80},{24,92},{28,88},{32,1... | collective-permute-start | bytes 393224 | tf_op jit(solution)/shard_map/ppermute | solution.py:347
  156.0 15.1 %copy-start.10 = (bf16[2,64,512]{2,1,0:T(8,128)(2,1)}, bf16[2,64,512]{2,1,0:T(8,128)(2,1)S(1)}, u32[]{:S(2)}) copy-start(bf16[2,64,512]{2,1,0:T(8,128)(2,1)S(1)} %collective-permute-done.10.refs_1_) | copy-start | bytes 393220
  156.0 12.0 %collective-permute-start.15 = (bf16[2,64,512]{2,1,0:T(8,128)(2,1)}, bf16[2,64,512]{2,1,0:T(8,128)(2,1)S(1)}, u32[]{:S(2)}, u32[]{:S(2)}) collective-permute-start(bf16[2,64,512]{2,1,0:T(8,128)(2,1)} %get-tuple-element.41), channel_id=1, source_target_pairs={{0,96},{4,100},{8,104},{12,108},{16,112},{20,116},{24,120},{28,124... | collective-permute-start | bytes 393224 | tf_op jit(solution)/shard_map/ppermute | solution.py:347
  158.4 12.6 %copy-start.11 = (bf16[2,64,512]{2,1,0:T(8,128)(2,1)}, bf16[2,64,512]{2,1,0:T(8,128)(2,1)S(1)}, u32[]{:S(2)}) copy-start(bf16[2,64,512]{2,1,0:T(8,128)(2,1)S(1)} %collective-permute-done.11.refs_2_) | copy-start | bytes 393220
  158.4 12.6 %collective-permute-start.16 = (bf16[2,64,512]{2,1,0:T(8,128)(2,1)}, bf16[2,64,512]{2,1,0:T(8,128)(2,1)S(1)}, u32[]{:S(2)}, u32[]{:S(2)}) collective-permute-start(bf16[2,64,512]{2,1,0:T(8,128)(2,1)} %get-tuple-element.42), channel_id=1, source_target_pairs={{0,100},{4,96},{8,108},{12,104},{16,116},{20,112},{24,124},{28,120... | collective-permute-start | bytes 393224 | tf_op jit(solution)/shard_map/ppermute | solution.py:347
  160.0 11.0 %copy-start.12 = (bf16[2,64,512]{2,1,0:T(8,128)(2,1)}, bf16[2,64,512]{2,1,0:T(8,128)(2,1)S(1)}, u32[]{:S(2)}) copy-start(bf16[2,64,512]{2,1,0:T(8,128)(2,1)S(1)} %collective-permute-done.12.refs_3_) | copy-start | bytes 393220
  164.0 7.1 %copy-start.13 = (bf16[2,64,512]{2,1,0:T(8,128)(2,1)}, bf16[2,64,512]{2,1,0:T(8,128)(2,1)S(1)}, u32[]{:S(2)}) copy-start(bf16[2,64,512]{2,1,0:T(8,128)(2,1)S(1)} %collective-permute-done.13.refs_4_) | copy-start | bytes 393220
  167.1 3.9 %copy-start.14 = (bf16[2,64,512]{2,1,0:T(8,128)(2,1)}, bf16[2,64,512]{2,1,0:T(8,128)(2,1)S(1)}, u32[]{:S(2)}) copy-start(bf16[2,64,512]{2,1,0:T(8,128)(2,1)S(1)} %collective-permute-done.14.refs_5_) | copy-start | bytes 393220
  168.0 3.1 %copy-start.15 = (bf16[2,64,512]{2,1,0:T(8,128)(2,1)}, bf16[2,64,512]{2,1,0:T(8,128)(2,1)S(1)}, u32[]{:S(2)}) copy-start(bf16[2,64,512]{2,1,0:T(8,128)(2,1)S(1)} %collective-permute-done.15.refs_6_) | copy-start | bytes 393220
  171.0 0.7 copy-start.16
  173.8 12.2 %collective-permute-start.17 = (f32[64,512]{1,0:T(8,128)}, f32[64,512]{1,0:T(8,128)S(1)}, u32[]{:S(2)}, u32[]{:S(2)}) collective-permute-start(f32[64,512]{1,0:T(8,128)} %get-tuple-element.44), channel_id=1, source_target_pairs={{0,128},{4,132},{8,136},{12,140},{16,144},{20,148},{24,152},{28,15... | collective-permute-start | bytes 393224 | tf_op jit(solution)/shard_map/ppermute | solution.py:350
  187.7 0.9 copy-start.1

commit v4 on v3

--- a/solution.py
+++ b/solution.py
@@ -17,6 +17,7 @@
 PERIOD = 2 * BLOCKS * ROWS
 LAST_SCALE = 1.0 / PERIOD
 KEPT = 72
+VMEM_GRANT = 12 << 20
 ROOT_SCALE = 1.0 / math.sqrt(BLOCKS * ROWS)
 SENT = 4 * CHANNELS
 PLANES = [[32 * z + i for i in range(32)] for z in range(2)]
@@ -67,13 +68,12 @@
     inner = 2.0 * math.pi * (row[:, None] * row[None, :] % ROWS) / ROWS
     cosine, sine = np.cos(inner), np.sin(inner)
     ahead = np.block([[cosine, -sine], [sine, cosine]])
-    back_high, back_low = split_table(ahead.T)
     return (
         first,
         np.cos(twist).astype(np.float32),
         np.sin(twist).astype(np.float32),
         np.concatenate(split_table(ahead), axis=0),
-        np.concatenate([back_high, back_high, back_low], axis=0),
+        np.concatenate(split_table(ahead.T), axis=0),
         last,
     )
 
@@ -98,6 +98,7 @@
         gather_body,
         out_shape=jax.ShapeDtypeStruct((BLOCKS, SENT, ROWS), jnp.bfloat16),
         name="gather_signals",
+        compiler_params=pltpu.CompilerParams(vmem_limit_bytes=VMEM_GRANT),
     )(gate_key, value_proj, grad_out, gate_query, filter_taps)
 
 
@@ -118,15 +119,35 @@
             pl.BlockSpec(memory_space=pltpu.VMEM),
         ],
         name="split_features",
+        compiler_params=pltpu.CompilerParams(vmem_limit_bytes=VMEM_GRANT),
     )(where, layer_input)
 
 
-UNROLL = 2
+UNROLL = 4
+
+
+def invert(pairs, number, cosine, sine, back_ref, last_ref):
+    rowed = product(jnp.concatenate([pairs, pairs], axis=1), back_ref[...])
+    bent = []
+    for n in range(number):
+        real_part = rowed[n * KEPT : n * KEPT + KEPT, :128]
+        other_part = rowed[n * KEPT : n * KEPT + KEPT, 128:]
+        bent.append(
+            jnp.concatenate(
+                [
+                    real_part * cosine - other_part * sine,
+                    real_part * sine + other_part * cosine,
+                ],
+                axis=0,
+            )
+        )
+    total = product(last_ref[...], jnp.concatenate(bent, axis=1).astype(jnp.bfloat16))
+    return total[:BLOCKS] + total[BLOCKS:]
 
 
 def convolve_body(
     signals_ref, first_ref, cos_ref, sin_ref, ahead_ref, back_ref, last_ref,
-    out_ref, value_ref, wide_in, wide_out, wide_value,
+    out_ref, value_ref, rest_ref, wide_in, wide_out, wide_value,
 ):
     wide_in[...] = signals_ref[...].astype(jnp.float32).reshape(BLOCKS * SENT, ROWS)
 
@@ -134,7 +155,6 @@
         cosine = cos_ref[...]
         sine = sin_ref[...]
         places = [index * UNROLL + inside for inside in range(UNROLL)]
-        number = 3 * UNROLL
         rows = jnp.concatenate(
             [
                 wide_in[pl.ds(place + CHANNELS * s, BLOCKS, stride=SENT), :]
@@ -145,7 +165,7 @@
         ).astype(jnp.bfloat16)
         outer = product(first_ref[...], jnp.concatenate([rows, rows], axis=0))
         turned = []
-        for n in range(number):
+        for n in range(3 * UNROLL):
             real_part = outer[:KEPT, n * 128 : n * 128 + 128]
             other_part = outer[KEPT:, n * 128 : n * 128 + 128]
             turned.append(
@@ -159,61 +179,54 @@
             )
         turned = jnp.concatenate(turned, axis=0).astype(jnp.bfloat16)
         spectra = product(jnp.concatenate([turned, turned], axis=1), ahead_ref[...])
-        pairs = []
+        firsts, rest = [], []
         for n in range(UNROLL):
             parts = [
                 (spectra[start : start + KEPT, :128], spectra[start : start + KEPT, 128:])
                 for start in range(3 * n * KEPT, (3 * n + 3) * KEPT, KEPT)
             ]
             (mixed_real, mixed_other), (taps_real, taps_other), (gated_real, gated_other) = parts
-            for pair in (
-                (
-                    mixed_real * taps_real - mixed_other * taps_other,
-                    mixed_real * taps_other + mixed_other * taps_real,
-                ),
-                (
-                    gated_real * taps_real + gated_other * taps_other,
-                    gated_other * taps_real - gated_real * taps_other,
-                ),
-                (
-                    gated_real * mixed_real + gated_other * mixed_other,
-                    gated_other * mixed_real - gated_real * mixed_other,
-                ),
-            ):
-                pairs.append(jnp.concatenate(pair, axis=1))
-        pairs = jnp.concatenate(pairs, axis=0)
-        high = pairs.astype(jnp.bfloat16)
-        low = (pairs - high.astype(jnp.float32)).astype(jnp.bfloat16)
-        rowed = product(jnp.concatenate([high, low, high], axis=1), back_ref[...])
-        bent = []
-        for n in range(number):
-            real_part = rowed[n * KEPT : n * KEPT + KEPT, :128]
-            other_part = rowed[n * KEPT : n * KEPT + KEPT, 128:]
-            bent.append(
+            firsts.append(
                 jnp.concatenate(
                     [
-                        real_part * cosine - other_part * sine,
-                        real_part * sine + other_part * cosine,
+                        gated_real * taps_real + gated_other * taps_other,
+                        gated_other * taps_real - gated_real * taps_other,
                     ],
-                    axis=0,
+                    axis=1,
                 )
             )
-        total = product(last_ref[...], jnp.concatenate(bent, axis=1).astype(jnp.bfloat16))
-        total = total[:BLOCKS] + total[BLOCKS:]
-        for n in range(number):
-            s, place = n % 3, places[n // 3]
-            factor = LAST_SCALE * (ROOT_SCALE if s == 2 else 1.0)
-            result = total[:, n * 128 : n * 128 + 128] * factor
-            wide_out[pl.ds(place + CHANNELS * s, BLOCKS, stride=LANES), :] = result
-            if s == 1:
-                key = wide_in[pl.ds(place + CHANNELS * 3, BLOCKS, stride=SENT), :]
-                wide_value[pl.ds(place, BLOCKS, stride=CHANNELS), :] = (
-                    result.astype(jnp.bfloat16).astype(jnp.float32) * key
+            rest.append(
+                jnp.concatenate(
+                    [
+                        mixed_real * taps_real - mixed_other * taps_other,
+                        mixed_real * taps_other + mixed_other * taps_real,
+                    ],
+                    axis=1,
                 )
+            )
+            rest.append(
+                jnp.concatenate(
+                    [
+                        gated_real * mixed_real + gated_other * mixed_other,
+                        gated_other * mixed_real - gated_real * mixed_other,
+                    ],
+                    axis=1,
+                )
+            )
+        rest_ref[index] = jnp.concatenate(rest, axis=0).astype(jnp.bfloat16)
+        firsts = jnp.concatenate(firsts, axis=0).astype(jnp.bfloat16)
+        total = invert(firsts, UNROLL, cosine, sine, back_ref, last_ref)
+        for n, place in enumerate(places):
+            result = total[:, n * 128 : n * 128 + 128] * LAST_SCALE
+            wide_out[pl.ds(place, BLOCKS, stride=CHANNELS), :] = result
+            key = wide_in[pl.ds(place + CHANNELS * 3, BLOCKS, stride=SENT), :]
+            wide_value[pl.ds(place, BLOCKS, stride=CHANNELS), :] = (
+                result.astype(jnp.bfloat16).astype(jnp.float32) * key
+            )
         return carry
 
     lax.fori_loop(0, CHANNELS // UNROLL, step, 0)
-    out_ref[...] = wide_out[...].reshape(BLOCKS, LANES, ROWS).astype(jnp.bfloat16)
+    out_ref[...] = wide_out[...].reshape(BLOCKS, CHANNELS, ROWS).astype(jnp.bfloat16)
     for block in range(BLOCKS):
         tile = wide_value[block * CHANNELS : block * CHANNELS + CHANNELS, :].astype(jnp.bfloat16)
         z, y, x, core = block // 32, block // 8 % 4, block // 2 % 4, block % 2
@@ -225,16 +238,48 @@
     return pl.pallas_call(
         convolve_body,
         out_shape=(
-            jax.ShapeDtypeStruct((BLOCKS, LANES, ROWS), jnp.bfloat16),
+            jax.ShapeDtypeStruct((BLOCKS, CHANNELS, ROWS), jnp.bfloat16),
             jax.ShapeDtypeStruct((32, 8, CHANNELS, ROWS), jnp.bfloat16),
+            jax.ShapeDtypeStruct((CHANNELS // UNROLL, 2 * UNROLL * KEPT, 256), jnp.bfloat16),
         ),
         scratch_shapes=[
             pltpu.VMEM((BLOCKS * SENT, ROWS), jnp.float32),
-            pltpu.VMEM((BLOCKS * LANES, ROWS), jnp.float32),
+            pltpu.VMEM((BLOCKS * CHANNELS, ROWS), jnp.float32),
             pltpu.VMEM((BLOCKS * CHANNELS, ROWS), jnp.float32),
         ],
         name="convolve",
+        compiler_params=pltpu.CompilerParams(vmem_limit_bytes=VMEM_GRANT),
     )(signals, *tables)
+
+
+def complete_body(back_grad_ref, rest_ref, cos_ref, sin_ref, back_ref, last_ref, out_ref, wide_out):
+    def step(index, carry):
+        cosine = cos_ref[...]
+        sine = sin_ref[...]
+        total = invert(rest_ref[index], 2 * UNROLL, cosine, sine, back_ref, last_ref)
+        for n in range(2 * UNROLL):
+            place = index * UNROLL + n // 2
+            factor = LAST_SCALE * (ROOT_SCALE if n % 2 else 1.0)
+            wide_out[pl.ds(place + CHANNELS * (n % 2), BLOCKS, stride=2 * CHANNELS), :] = (
+                total[:, n * 128 : n * 128 + 128] * factor
+            )
+        return carry
+
+    lax.fori_loop(0, CHANNELS // UNROLL, step, 0)
+    wide = wide_out[...].reshape(BLOCKS, 2 * CHANNELS, ROWS).astype(jnp.bfloat16)
+    out_ref[:, : 2 * CHANNELS, :] = wide
+    out_ref[:, 2 * CHANNELS :, :] = back_grad_ref[...]
+
+
+def complete(back_grad, rest, tables):
+    _, cosine, sine, _, back, last = tables
+    return pl.pallas_call(
+        complete_body,
+        out_shape=jax.ShapeDtypeStruct((BLOCKS, LANES, ROWS), jnp.bfloat16),
+        scratch_shapes=[pltpu.VMEM((BLOCKS * 2 * CHANNELS, ROWS), jnp.float32)],
+        name="complete",
+        compiler_params=pltpu.CompilerParams(vmem_limit_bytes=VMEM_GRANT),
+    )(back_grad, rest, cosine, sine, back, last)
 
 
 def finish_body(back_ref, grad_ref, value_ref, key_ref, query_out, key_out, value_out, filter_out):
@@ -245,22 +290,22 @@
             block = back_ref[pl.ds(part * 8, 8), pl.ds(place * 16, 16), :]
             return block.reshape(128, 128).astype(jnp.float32).T
 
-        back = turned(1)
+        back = turned(2)
         query_out[:, cols] = (grad_ref[:, cols].astype(jnp.float32) * turned(0)).astype(jnp.bfloat16)
         key_out[:, cols] = (back * value_ref[:, cols].astype(jnp.float32)).astype(jnp.bfloat16)
         value_out[:, cols] = (back * key_ref[:, cols].astype(jnp.float32)).astype(jnp.bfloat16)
-        filter_out[:, cols] = turned(2).astype(jnp.bfloat16)
+        filter_out[:, cols] = turned(1).astype(jnp.bfloat16)
 
 
 def finish(returned, grad_out, value_proj, gate_key):
     shape = jax.ShapeDtypeStruct(grad_out.shape, jnp.bfloat16)
-    return pl.pallas_call(finish_body, out_shape=(shape,) * 4, name="finish")(
+    return pl.pallas_call(finish_body, out_shape=(shape,) * 4, name="finish", compiler_params=pltpu.CompilerParams(vmem_limit_bytes=VMEM_GRANT))(
         returned, grad_out, value_proj, gate_key
     )
 
 
 def weight_body(where_ref, value_ref, *refs):
-    features, outs, (aligned, pieces) = refs[:8], refs[8:16], refs[16:]
+    features, (kept_ref, sent_ref, aligned, pieces) = refs[:8], refs[8:]
     x, ring, place = where_ref[0], where_ref[1], where_ref[2]
     for z in range(2):
         for back in range(4):
@@ -282,25 +327,44 @@
                 target = ((group % 2) * 2 + side) * 2 + core
                 start = side * 128 + core * 64
                 pieces[target * 2 + group // 2] = total[start : start + 64].astype(jnp.bfloat16)
-    for flip, out_ref in enumerate(outs):
-        out_ref[...] = pieces[pl.ds((place ^ flip) * 2, 2)]
+    side, core = place // 2, place % 2
+    for flip in range(4):
+        target = (side ^ flip) * 2
+        kept_ref[flip] = pieces[pl.ds((target + core) * 2, 2)]
+        sent_ref[flip] = pieces[pl.ds((target + 1 - core) * 2, 2)]
 
 
 def weight_parts(where, value, features):
     return pl.pallas_call(
         weight_body,
-        out_shape=(jax.ShapeDtypeStruct((2, 64, 512), jnp.bfloat16),) * 8,
+        out_shape=(jax.ShapeDtypeStruct((4, 2, 64, 512), jnp.bfloat16),) * 2,
         in_specs=[pl.BlockSpec(memory_space=pltpu.SMEM)] + [pl.BlockSpec(memory_space=pltpu.VMEM)] * 9,
         scratch_shapes=[
             pltpu.VMEM((2, 512, 512), jnp.bfloat16),
             pltpu.VMEM((16, 64, 512), jnp.bfloat16),
         ],
         name="weight_parts",
+        compiler_params=pltpu.CompilerParams(vmem_limit_bytes=VMEM_GRANT),
     )(where, value, *features)
 
 
+def join_body(kept_ref, received_ref, *outs):
+    for flip, out_ref in enumerate(outs):
+        total = kept_ref[flip].astype(jnp.float32) + received_ref[flip].astype(jnp.float32)
+        out_ref[...] = total.astype(jnp.bfloat16)
+
+
+def join_cores(kept, received):
+    return pl.pallas_call(
+        join_body,
+        out_shape=(jax.ShapeDtypeStruct((2, 64, 512), jnp.bfloat16),) * 4,
+        name="join_cores",
+        compiler_params=pltpu.CompilerParams(vmem_limit_bytes=VMEM_GRANT),
+    )(kept, received)
+
+
 def total_body(where_ref, *refs):
-    parts, (kept_ref, sent_ref) = refs[:8], refs[8:]
+    parts, (kept_ref, sent_ref) = refs[:4], refs[4:]
     z = where_ref[3]
     for out_ref, place in ((kept_ref, z), (sent_ref, 1 - z)):
         total = parts[0][place].astype(jnp.float32)
@@ -313,8 +377,9 @@
     return pl.pallas_call(
         total_body,
         out_shape=(jax.ShapeDtypeStruct((64, 512), jnp.float32),) * 2,
-        in_specs=[pl.BlockSpec(memory_space=pltpu.SMEM)] + [pl.BlockSpec(memory_space=pltpu.VMEM)] * 8,
+        in_specs=[pl.BlockSpec(memory_space=pltpu.SMEM)] + [pl.BlockSpec(memory_space=pltpu.VMEM)] * 4,
         name="weight_total",
+        compiler_params=pltpu.CompilerParams(vmem_limit_bytes=VMEM_GRANT),
     )(where, *parts)
 
 
@@ -340,12 +405,15 @@
     up, down = ring_step(own, 1), ring_step(own, -1)
     signals = exchange(sent)
     up2, down2 = ring_step(up, 1), ring_step(down, -1)
-    results, value = convolve(signals, tables)
+    back_grad, value, rest = convolve(signals, tables)
     up3, down3, far = ring_step(up2, 1), ring_step(down2, -1), ring_step(up2, 2)
     value = exchange(value, PLANES)
-    parts = weight_parts(where, value, (own, up, up2, up3, far, down3, down2, down))
-    parts = [parts[0]] + [lax.ppermute(parts[n], "seq", across(n)) for n in range(1, 8)]
+    results = complete(back_grad, rest, tables)
+    kept, sent = weight_parts(where, value, (own, up, up2, up3, far, down3, down2, down))
+    received = lax.ppermute(sent, "seq", across(1))
     results = exchange(results)
+    parts = join_cores(kept, received)
+    parts = [parts[0]] + [lax.ppermute(parts[n], "seq", across(2 * n)) for n in range(1, 4)]
     kept, sent = weight_total(where, parts)
     received = lax.ppermute(sent, "seq", opposite())
     grad_query, grad_key, grad_value, grad_filter = finish(results, grad_out, value_proj, gate_key)

time: 192 us -> 171 us (0.89)
  the two profiles are of different devices: /device:TPU:1 before, /device:TPU:32 now
where the time goes in v4:
time: 171 us
  waiting for transfers between devices  72.8 us (43%)
  blocking collectives  45.2 us (26%)
  starting transfers between devices  29.5 us (17%)
  Pallas kernels  14.4 us (8%)
  local copies, waits for them, and re-layouts  7.18 us (4%)
    all_to_all x1, blocking collectives, exchange(): lax.all_to_all(array, 'seq', split_axis=0, concat_axis=0, tiled=True, axi...  45.2 us
    ppermute x7, waiting for transfers between devices, ring_step(): return lax.ppermute(array, ('seq', 'chan'), along_z(shift))  42.9 us
    ppermute x3, waiting for transfers between devices, shards(): own = [lax.ppermute(pieces[n], 'seq', along_x(n)) for n in range(1, 4)]  12.5 us
    all_to_all x2, starting transfers between devices, exchange(): lax.all_to_all(array, 'seq', split_axis=0, concat_axis=0, tiled=True, axi...  11.1 us
    ppermute x7, starting transfers between devices, ring_step(): return lax.ppermute(array, ('seq', 'chan'), along_z(shift))  8.31 us
    ppermute x3, waiting for transfers between devices, shards(): lax.ppermute(parts[n], 'seq', across(2 * n))  8.25 us
    ppermute x1, waiting for transfers between devices, shards(): received = lax.ppermute(sent, 'seq', opposite())  7.23 us
    unnamed x36, local copies, waits for them, and re-layouts  7.18 us
  transfers between devices with their start and end apart: 17, of which 11 were waited for; matrix products, arithmetic and copies ran while one was open for 0% of the time, Pallas kernels for 5%

profile of v4, /device:TPU:32, one launch (start us, length us, event | category | flops | bytes accessed | tf_op | source)
XLA Modules:
  0.0 170.8 jit_solution(15769790044413322966)
XLA Ops:
  0.6 0.9 copy-done
  1.6 0.9 copy-done.2
  2.5 0.9 copy-done.4
  3.5 0.9 copy-done.7
  4.4 0.9 copy-done.8
  5.4 0.4 gather_signals.1
  5.8 0.0 copy-start.6
  5.9 45.2 %all_to_all.15.signals_ref = bf16[64,64,128]{2,1,0:T(8,128)(2,1)S(1)} all-to-all(bf16[64,64,128]{2,1,0:T(8,128)(2,1)S(1)} %gather_signals.1), channel_id=1, replica_groups=mesh['seq'=64,'chan'=4] {'seq'}, dimensions={0} | all-to-all | bytes 2097152 | tf_op jit(solution)/shard_map/all_to_all | solution.py:387
  51.1 5.9 %convolve.1 = (bf16[64,16,128]{2,1,0:T(8,128)(2,1)S(1)}, bf16[32,8,16,128]{3,2,1,0:T(8,128)(2,1)}, bf16[4,576,256]{2,1,0:T(8,128)(2,1)S(1)}) custom-call(bf16[64,64,128]{2,1,0:T(8,128)(2,1)S(1)} %all_to_all.15.signals_ref, bf16[144,128]{1,0:T(8,128)(2,1)S(1)} %copy-done.17, f32[72,128]{1,0:T(8,128)S(1)} %copy-done.13, f32[72,128]{1,0:T(8,128)S(1)} %copy-done.15, ...), custom_call_target="tpu_custom_call" | custom-call | tf_op jit(solution)/shard_map/convolve/pallas_call | solution.py:238
  57.0 4.9 %all-to-all-start.2 = ((bf16[32,8,16,128]{3,2,1,0:T(8,128)(2,1)}), bf16[32,8,16,128]{3,2,1,0:T(8,128)(2,1)S(1)}, u32[]{:S(2)}, u32[]{:S(2)}) async-start(bf16[32,8,16,128]{3,2,1,0:T(8,128)(2,1)} %get-tuple-element.30), calls=%async_computation.2 | async-start | bytes 2097152 | tf_op jit(solution)/shard_map/all_to_all | solution.py:387
  61.9 0.1 pad_add_fusion.where_ref
  62.0 0.7 split_features.1
  62.7 3.1 %collective-permute-start.2 = (bf16[256,128]{1,0:T(8,128)(2,1)S(1)}, bf16[256,128]{1,0:T(8,128)(2,1)S(1)}, u32[]{:S(2)}, u32[]{:S(2)}) collective-permute-start(bf16[256,128]{1,0:T(8,128)(2,1)S(1)} %get-tuple-element.34), channel_id=1, source_target_pairs={{0,24},{4,28},{8,0},{12,4},{16,8},{20,12},{24,16},{28,20},{32,56},... | collective-permute-start | bytes 196616 | tf_op jit(solution)/shard_map/ppermute | solution.py:402
  65.8 0.9 collective-permute-start.1
  66.7 0.9 collective-permute-start
  67.5 10.4 %collective-permute-done.2 = bf16[256,128]{1,0:T(8,128)(2,1)S(1)} collective-permute-done((bf16[256,128]{1,0:T(8,128)(2,1)S(1)}, bf16[256,128]{1,0:T(8,128)(2,1)S(1)}, u32[]{:S(2)}, u32[]{:S(2)}) %collective-permute-start.2) | collective-permute-done | bytes 65568 | tf_op jit(solution)/shard_map/ppermute | solution.py:402
  77.9 1.6 collective-permute-done.1
  79.5 0.5 collective-permute-done
  80.0 1.1 collective-permute-start.3
  81.1 1.0 collective-permute-start.7
  82.1 0.8 copy-done.12
  83.0 0.8 copy-done.14
  83.7 0.8 copy-done.16
  84.5 3.3 %complete.1 = bf16[64,48,128]{2,1,0:T(8,128)(2,1)} custom-call(bf16[64,16,128]{2,1,0:T(8,128)(2,1)S(1)} %get-tuple-element.24.back_grad_ref, bf16[4,576,256]{2,1,0:T(8,128)(2,1)S(1)} %get-tuple-element.25.rest_ref, f32[72,128]{1,0:T(8,128)S(1)} %copy-done.14, f32[72,128]{1,0:T(8,128)S(1)} %copy-done.16, bf16[512,256]{1,0:T(8,128)(2,1)S(1)} %copy-done.6, ...), custom_call_target="tpu_custom_call" | custom-call | tf_op jit(solution)/shard_map/complete/pallas_call | solution.py:276
  87.8 6.2 %all-to-all-start.1 = ((bf16[64,48,128]{2,1,0:T(8,128)(2,1)}), bf16[64,48,128]{2,1,0:T(8,128)(2,1)S(1)}, u32[]{:S(2)}, u32[]{:S(2)}) async-start(bf16[64,48,128]{2,1,0:T(8,128)(2,1)} %complete.1), calls=%async_computation.1 | async-start | bytes 1572864 | tf_op jit(solution)/shard_map/all_to_all | solution.py:387
  94.1 1.1 collective-permute-start.4
  95.1 1.0 collective-permute-start.8
  96.2 23.0 %collective-permute-done.4.refs_2_ = bf16[4,256,128]{2,1,0:T(8,128)(2,1)S(1)} collective-permute-done((bf16[4,256,128]{2,1,0:T(8,128)(2,1)S(1)}, bf16[4,256,128]{2,1,0:T(8,128)(2,1)S(1)}, u32[]{:S(2)}, u32[]{:S(2)}) %collective-permute-start.4) | collective-permute-done | bytes 262176 | tf_op jit(solution)/shard_map/ppermute | solution.py:393
  119.2 1.1 collective-permute-start.5
  120.3 2.1 %collective-permute-start.6 = (bf16[4,256,128]{2,1,0:T(8,128)(2,1)S(1)}, bf16[4,256,128]{2,1,0:T(8,128)(2,1)S(1)}, u32[]{:S(2)}, u32[]{:S(2)}) collective-permute-start(bf16[4,256,128]{2,1,0:T(8,128)(2,1)S(1)} %collective-permute-done.4.refs_2_), channel_id=1, source_target_pairs={{0,2},{1,3},{2,128},{3,129},{4,6},{5,7},{6,132},{7,133},{8,10},{9,... | collective-permute-start | bytes 786440 | tf_op jit(solution)/shard_map/ppermute | solution.py:393
  122.4 0.9 collective-permute-start.9
  123.3 6.9 %collective-permute-done.5.refs_3_ = bf16[4,256,128]{2,1,0:T(8,128)(2,1)S(1)} collective-permute-done((bf16[4,256,128]{2,1,0:T(8,128)(2,1)S(1)}, bf16[4,256,128]{2,1,0:T(8,128)(2,1)S(1)}, u32[]{:S(2)}, u32[]{:S(2)}) %collective-permute-start.5) | collective-permute-done | bytes 262176 | tf_op jit(solution)/shard_map/ppermute | solution.py:393
  130.2 13.0 %collective-permute-done.6.refs_4_ = bf16[4,256,128]{2,1,0:T(8,128)(2,1)S(1)} collective-permute-done((bf16[4,256,128]{2,1,0:T(8,128)(2,1)S(1)}, bf16[4,256,128]{2,1,0:T(8,128)(2,1)S(1)}, u32[]{:S(2)}, u32[]{:S(2)}) %collective-permute-start.6) | collective-permute-done | bytes 262176 | tf_op jit(solution)/shard_map/ppermute | solution.py:393
  143.2 2.1 %weight_parts.1 = (bf16[4,2,64,512]{3,2,1,0:T(8,128)(2,1)S(1)}, bf16[4,2,64,512]{3,2,1,0:T(8,128)(2,1)S(1)}) custom-call(s32[4]{0:T(128)S(1)} %pad_add_fusion.where_ref, bf16[32,8,16,128]{3,2,1,0:T(8,128)(2,1)S(1)} %all-to-all-done.2.value_ref, bf16[4,256,128]{2,1,0:T(8,128)(2,1)S(1)} %pad_maximum_fusion.refs_0_, ...), custom_call_target="tpu_custom_call" | custom-call | tf_op jit(solution)/shard_map/weight_parts/pallas_call | solution.py:338
  145.3 0.1 collective-permute-start.10
  145.4 1.9 %collective-permute-done.10.received_ref = bf16[4,2,64,512]{3,2,1,0:T(8,128)(2,1)S(1)} collective-permute-done((bf16[4,2,64,512]{3,2,1,0:T(8,128)(2,1)S(1)}, bf16[4,2,64,512]{3,2,1,0:T(8,128)(2,1)S(1)}, u32[]{:S(2)}, u32[]{:S(2)}) %collective-permute-start.10) | collective-permute-done | bytes 524320 | tf_op jit(solution)/shard_map/ppermute | solution.py:413
  147.3 0.1 join_cores.1
  147.4 1.6 collective-permute-start.11
  149.0 2.8 %collective-permute-start.12 = (bf16[2,64,512]{2,1,0:T(8,128)(2,1)S(1)}, bf16[2,64,512]{2,1,0:T(8,128)(2,1)S(1)}, u32[]{:S(2)}, u32[]{:S(2)}) collective-permute-start(bf16[2,64,512]{2,1,0:T(8,128)(2,1)S(1)} %get-tuple-element.39), channel_id=1, source_target_pairs={{0,64},{4,68},{8,72},{12,76},{16,80},{20,84},{24,88},{28,92},{32,9... | collective-permute-start | bytes 393224 | tf_op jit(solution)/shard_map/ppermute | solution.py:416
  151.8 0.4 collective-permute-start.13
  152.2 1.4 collective-permute-done.11.refs_1_
  153.7 4.6 %collective-permute-done.12.refs_2_ = bf16[2,64,512]{2,1,0:T(8,128)(2,1)S(1)} collective-permute-done((bf16[2,64,512]{2,1,0:T(8,128)(2,1)S(1)}, bf16[2,64,512]{2,1,0:T(8,128)(2,1)S(1)}, u32[]{:S(2)}, u32[]{:S(2)}) %collective-permute-start.12) | collective-permute-done | bytes 131104 | tf_op jit(solution)/shard_map/ppermute | solution.py:416
  158.2 2.2 %collective-permute-done.13.refs_3_ = bf16[2,64,512]{2,1,0:T(8,128)(2,1)S(1)} collective-permute-done((bf16[2,64,512]{2,1,0:T(8,128)(2,1)S(1)}, bf16[2,64,512]{2,1,0:T(8,128)(2,1)S(1)}, u32[]{:S(2)}, u32[]{:S(2)}) %collective-permute-start.13) | collective-permute-done | bytes 131104 | tf_op jit(solution)/shard_map/ppermute | solution.py:416
  160.5 0.6 weight_total.1
  161.1 0.4 collective-permute-start.14
  161.5 1.3 finish.1
  162.8 7.2 %collective-permute-done.14 = f32[64,512]{1,0:T(8,128)S(1)} collective-permute-done((f32[64,512]{1,0:T(8,128)S(1)}, f32[64,512]{1,0:T(8,128)S(1)}, u32[]{:S(2)}, u32[]{:S(2)}) %collective-permute-start.14) | collective-permute-done | bytes 131104 | tf_op jit(solution)/shard_map/ppermute | solution.py:418
  170.1 0.7 maximum_select_fusion
  (34 shorter events, 0.1 us)
Async XLA Ops:
  0.6 1.0 copy-start
  1.6 0.9 copy-start.2
  2.5 0.9 copy-start.4
  3.5 0.9 copy-start.7
  4.4 0.9 copy-start.8
  5.8 45.3 %copy-start.6 = (bf16[512,256]{1,0:T(8,128)(2,1)S(1)}, bf16[512,256]{1,0:T(8,128)(2,1)}, u32[]{:S(2)}) copy-start(bf16[512,256]{1,0:T(8,128)(2,1)} %constant.85.clone.back_ref) | copy-start | bytes 786436
  5.8 45.3 %copy-start.10 = (bf16[512,256]{1,0:T(8,128)(2,1)S(1)}, bf16[512,256]{1,0:T(8,128)(2,1)}, u32[]{:S(2)}) copy-start(bf16[512,256]{1,0:T(8,128)(2,1)} %constant.84.clone.ahead_ref) | copy-start | bytes 786436
  5.8 45.3 %copy-start.11 = (bf16[128,144]{1,0:T(8,128)(2,1)S(1)}, bf16[128,144]{1,0:T(8,128)(2,1)}, u32[]{:S(2)}) copy-start(bf16[128,144]{1,0:T(8,128)(2,1)} %constant.86.clone.last_ref) | copy-start | bytes 110596
  5.8 45.3 %copy-start.13 = (f32[72,128]{1,0:T(8,128)S(1)}, f32[72,128]{1,0:T(8,128)}, u32[]{:S(2)}) copy-start(f32[72,128]{1,0:T(8,128)} %constant.82.clone.cos_ref) | copy-start | bytes 110596
  5.8 45.3 %copy-start.15 = (f32[72,128]{1,0:T(8,128)S(1)}, f32[72,128]{1,0:T(8,128)}, u32[]{:S(2)}) copy-start(f32[72,128]{1,0:T(8,128)} %constant.83.clone.sin_ref) | copy-start | bytes 110596
  5.8 45.2 %copy-start.17 = (bf16[144,128]{1,0:T(8,128)(2,1)S(1)}, bf16[144,128]{1,0:T(8,128)(2,1)}, u32[]{:S(2)}) copy-start(bf16[144,128]{1,0:T(8,128)(2,1)} %constant.81.clone.first_ref) | copy-start | bytes 110596
  57.0 5.0 %copy-start.9 = (bf16[128,1024]{1,0:T(8,128)(2,1)S(1)}, bf16[128,1024]{1,0:T(8,128)(2,1)}, u32[]{:S(2)}) copy-start(bf16[128,1024]{1,0:T(8,128)(2,1)} %input_ref.1) | copy-start | bytes 786436
  57.0 30.9 %all-to-all-start.2 = ((bf16[32,8,16,128]{3,2,1,0:T(8,128)(2,1)}), bf16[32,8,16,128]{3,2,1,0:T(8,128)(2,1)S(1)}, u32[]{:S(2)}, u32[]{:S(2)}) async-start(bf16[32,8,16,128]{3,2,1,0:T(8,128)(2,1)} %get-tuple-element.30), calls=%async_computation.2 | async-start | bytes 2097152 | tf_op jit(solution)/shard_map/all_to_all | solution.py:387
  62.7 15.2 %collective-permute-start.2 = (bf16[256,128]{1,0:T(8,128)(2,1)S(1)}, bf16[256,128]{1,0:T(8,128)(2,1)S(1)}, u32[]{:S(2)}, u32[]{:S(2)}) collective-permute-start(bf16[256,128]{1,0:T(8,128)(2,1)S(1)} %get-tuple-element.34), channel_id=1, source_target_pairs={{0,24},{4,28},{8,0},{12,4},{16,8},{20,12},{24,16},{28,20},{32,56},... | collective-permute-start | bytes 196616 | tf_op jit(solution)/shard_map/ppermute | solution.py:402
  65.8 13.7 %collective-permute-start.1 = (bf16[256,128]{1,0:T(8,128)(2,1)S(1)}, bf16[256,128]{1,0:T(8,128)(2,1)S(1)}, u32[]{:S(2)}, u32[]{:S(2)}) collective-permute-start(bf16[256,128]{1,0:T(8,128)(2,1)S(1)} %get-tuple-element.33), channel_id=1, source_target_pairs={{0,16},{4,20},{8,24},{12,28},{16,0},{20,4},{24,8},{28,12},{32,48},... | collective-permute-start | bytes 196616 | tf_op jit(solution)/shard_map/ppermute | solution.py:402
  66.7 13.3 %collective-permute-start = (bf16[256,128]{1,0:T(8,128)(2,1)S(1)}, bf16[256,128]{1,0:T(8,128)(2,1)S(1)}, u32[]{:S(2)}, u32[]{:S(2)}) collective-permute-start(bf16[256,128]{1,0:T(8,128)(2,1)S(1)} %get-tuple-element.32), channel_id=1, source_target_pairs={{0,8},{4,12},{8,16},{12,20},{16,24},{20,28},{24,0},{28,4},{32,40},... | collective-permute-start | bytes 196616 | tf_op jit(solution)/shard_map/ppermute | solution.py:402
  80.0 14.0 %collective-permute-start.3 = (bf16[4,256,128]{2,1,0:T(8,128)(2,1)S(1)}, bf16[4,256,128]{2,1,0:T(8,128)(2,1)S(1)}, u32[]{:S(2)}, u32[]{:S(2)}) collective-permute-start(bf16[4,256,128]{2,1,0:T(8,128)(2,1)S(1)} %pad_maximum_fusion.refs_0_), channel_id=1, source_target_pairs={{0,1},{1,2},{2,3},{3,128},{4,5},{5,6},{6,7},{7,132},{8,9},{9,10},{... | collective-permute-start | bytes 786440 | tf_op jit(solution)/shard_map/ppermute | solution.py:393
  81.1 14.0 %collective-permute-start.7 = (bf16[4,256,128]{2,1,0:T(8,128)(2,1)S(1)}, bf16[4,256,128]{2,1,0:T(8,128)(2,1)S(1)}, u32[]{:S(2)}, u32[]{:S(2)}) collective-permute-start(bf16[4,256,128]{2,1,0:T(8,128)(2,1)S(1)} %pad_maximum_fusion.refs_0_), channel_id=1, source_target_pairs={{0,131},{1,0},{2,1},{3,2},{4,135},{5,4},{6,5},{7,6},{8,139},{9,8},... | collective-permute-start | bytes 786440 | tf_op jit(solution)/shard_map/ppermute | solution.py:393
  82.1 0.8 copy-start.12
  83.0 0.8 copy-start.14
  83.7 0.8 copy-start.16
  87.8 73.7 %all-to-all-start.1 = ((bf16[64,48,128]{2,1,0:T(8,128)(2,1)}), bf16[64,48,128]{2,1,0:T(8,128)(2,1)S(1)}, u32[]{:S(2)}, u32[]{:S(2)}) async-start(bf16[64,48,128]{2,1,0:T(8,128)(2,1)} %complete.1), calls=%async_computation.1 | async-start | bytes 1572864 | tf_op jit(solution)/shard_map/all_to_all | solution.py:387
  94.1 25.1 %collective-permute-start.4 = (bf16[4,256,128]{2,1,0:T(8,128)(2,1)S(1)}, bf16[4,256,128]{2,1,0:T(8,128)(2,1)S(1)}, u32[]{:S(2)}, u32[]{:S(2)}) collective-permute-start(bf16[4,256,128]{2,1,0:T(8,128)(2,1)S(1)} %collective-permute-done.3.refs_1_), channel_id=1, source_target_pairs={{0,1},{1,2},{2,3},{3,128},{4,5},{5,6},{6,7},{7,132},{8,9},{9,10},{... | collective-permute-start | bytes 786440 | tf_op jit(solution)/shard_map/ppermute | solution.py:393
  95.1 27.3 %collective-permute-start.8 = (bf16[4,256,128]{2,1,0:T(8,128)(2,1)S(1)}, bf16[4,256,128]{2,1,0:T(8,128)(2,1)S(1)}, u32[]{:S(2)}, u32[]{:S(2)}) collective-permute-start(bf16[4,256,128]{2,1,0:T(8,128)(2,1)S(1)} %collective-permute-done.7.refs_7_), channel_id=1, source_target_pairs={{0,131},{1,0},{2,1},{3,2},{4,135},{5,4},{6,5},{7,6},{8,139},{9,8},... | collective-permute-start | bytes 786440 | tf_op jit(solution)/shard_map/ppermute | solution.py:393
  119.2 11.0 %collective-permute-start.5 = (bf16[4,256,128]{2,1,0:T(8,128)(2,1)S(1)}, bf16[4,256,128]{2,1,0:T(8,128)(2,1)S(1)}, u32[]{:S(2)}, u32[]{:S(2)}) collective-permute-start(bf16[4,256,128]{2,1,0:T(8,128)(2,1)S(1)} %collective-permute-done.4.refs_2_), channel_id=1, source_target_pairs={{0,1},{1,2},{2,3},{3,128},{4,5},{5,6},{6,7},{7,132},{8,9},{9,10},{... | collective-permute-start | bytes 786440 | tf_op jit(solution)/shard_map/ppermute | solution.py:393
  120.3 22.9 %collective-permute-start.6 = (bf16[4,256,128]{2,1,0:T(8,128)(2,1)S(1)}, bf16[4,256,128]{2,1,0:T(8,128)(2,1)S(1)}, u32[]{:S(2)}, u32[]{:S(2)}) collective-permute-start(bf16[4,256,128]{2,1,0:T(8,128)(2,1)S(1)} %collective-permute-done.4.refs_2_), channel_id=1, source_target_pairs={{0,2},{1,3},{2,128},{3,129},{4,6},{5,7},{6,132},{7,133},{8,10},{9,... | collective-permute-start | bytes 786440 | tf_op jit(solution)/shard_map/ppermute | solution.py:393
  122.4 20.8 %collective-permute-start.9 = (bf16[4,256,128]{2,1,0:T(8,128)(2,1)S(1)}, bf16[4,256,128]{2,1,0:T(8,128)(2,1)S(1)}, u32[]{:S(2)}, u32[]{:S(2)}) collective-permute-start(bf16[4,256,128]{2,1,0:T(8,128)(2,1)S(1)} %collective-permute-done.8.refs_6_), channel_id=1, source_target_pairs={{0,131},{1,0},{2,1},{3,2},{4,135},{5,4},{6,5},{7,6},{8,139},{9,8},... | collective-permute-start | bytes 786440 | tf_op jit(solution)/shard_map/ppermute | solution.py:393
  145.3 16.2 %copy-start.1 = (bf16[128,1024]{1,0:T(8,128)(2,1)S(1)}, bf16[128,1024]{1,0:T(8,128)(2,1)}, u32[]{:S(2)}) copy-start(bf16[128,1024]{1,0:T(8,128)(2,1)} %key_ref.3) | copy-start | bytes 786436
  145.3 16.2 %copy-start.3 = (bf16[128,1024]{1,0:T(8,128)(2,1)S(1)}, bf16[128,1024]{1,0:T(8,128)(2,1)}, u32[]{:S(2)}) copy-start(bf16[128,1024]{1,0:T(8,128)(2,1)} %value_ref.3) | copy-start | bytes 786436
  145.3 16.2 %copy-start.5 = (bf16[128,1024]{1,0:T(8,128)(2,1)S(1)}, bf16[128,1024]{1,0:T(8,128)(2,1)}, u32[]{:S(2)}) copy-start(bf16[128,1024]{1,0:T(8,128)(2,1)} %grad_ref.3) | copy-start | bytes 786436
  145.3 2.0 %collective-permute-start.10 = (bf16[4,2,64,512]{3,2,1,0:T(8,128)(2,1)S(1)}, bf16[4,2,64,512]{3,2,1,0:T(8,128)(2,1)S(1)}, u32[]{:S(2)}, u32[]{:S(2)}) collective-permute-start(bf16[4,2,64,512]{3,2,1,0:T(8,128)(2,1)S(1)} %get-tuple-element.36), channel_id=1, source_target_pairs={{0,4},{4,0},{8,12},{12,8},{16,20},{20,16},{24,28},{28,24},{32,36},... | collective-permute-start | bytes 1572872 | tf_op jit(solution)/shard_map/ppermute | solution.py:413
  147.4 6.2 %collective-permute-start.11 = (bf16[2,64,512]{2,1,0:T(8,128)(2,1)S(1)}, bf16[2,64,512]{2,1,0:T(8,128)(2,1)S(1)}, u32[]{:S(2)}, u32[]{:S(2)}) collective-permute-start(bf16[2,64,512]{2,1,0:T(8,128)(2,1)S(1)} %get-tuple-element.38), channel_id=1, source_target_pairs={{0,32},{4,36},{8,40},{12,44},{16,48},{20,52},{24,56},{28,60},{32,0... | collective-permute-start | bytes 393224 | tf_op jit(solution)/shard_map/ppermute | solution.py:416
  149.0 9.2 %collective-permute-start.12 = (bf16[2,64,512]{2,1,0:T(8,128)(2,1)S(1)}, bf16[2,64,512]{2,1,0:T(8,128)(2,1)S(1)}, u32[]{:S(2)}, u32[]{:S(2)}) collective-permute-start(bf16[2,64,512]{2,1,0:T(8,128)(2,1)S(1)} %get-tuple-element.39), channel_id=1, source_target_pairs={{0,64},{4,68},{8,72},{12,76},{16,80},{20,84},{24,88},{28,92},{32,9... | collective-permute-start | bytes 393224 | tf_op jit(solution)/shard_map/ppermute | solution.py:416
  151.8 8.6 %collective-permute-start.13 = (bf16[2,64,512]{2,1,0:T(8,128)(2,1)S(1)}, bf16[2,64,512]{2,1,0:T(8,128)(2,1)S(1)}, u32[]{:S(2)}, u32[]{:S(2)}) collective-permute-start(bf16[2,64,512]{2,1,0:T(8,128)(2,1)S(1)} %get-tuple-element.40), channel_id=1, source_target_pairs={{0,96},{4,100},{8,104},{12,108},{16,112},{20,116},{24,120},{28,124... | collective-permute-start | bytes 393224 | tf_op jit(solution)/shard_map/ppermute | solution.py:416
  161.1 9.0 %collective-permute-start.14 = (f32[64,512]{1,0:T(8,128)S(1)}, f32[64,512]{1,0:T(8,128)S(1)}, u32[]{:S(2)}, u32[]{:S(2)}) collective-permute-start(f32[64,512]{1,0:T(8,128)S(1)} %get-tuple-element.42), channel_id=1, source_target_pairs={{0,128},{4,132},{8,136},{12,140},{16,144},{20,148},{24,152},{28,15... | collective-permute-start | bytes 393224 | tf_op jit(solution)/shard_map/ppermute | solution.py:418

commit v5 on v4

--- a/solution.py
+++ b/solution.py
@@ -20,7 +20,6 @@
 VMEM_GRANT = 12 << 20
 ROOT_SCALE = 1.0 / math.sqrt(BLOCKS * ROWS)
 SENT = 4 * CHANNELS
-PLANES = [[32 * z + i for i in range(32)] for z in range(2)]
 
 
 def along_x(shift):
@@ -82,8 +81,12 @@
     return lax.dot_general(left, right, (((1,), (0,)), ((), ())), preferred_element_type=jnp.float32)
 
 
+WHOLE_GRANT = 60 << 20
+STEPS = 4
+
+
 def gather_body(key_ref, value_ref, grad_ref, query_ref, taps_ref, sent_ref):
-    for part in range(8):
+    for part in range(8 // STEPS):
         cols = pl.ds(part * 128, 128)
         key = key_ref[:, cols].astype(jnp.float32)
         mixed = key * value_ref[:, cols].astype(jnp.float32)
@@ -96,10 +99,28 @@
 def gather_signals(gate_key, value_proj, grad_out, gate_query, filter_taps):
     return pl.pallas_call(
         gather_body,
+        grid=(STEPS,),
         out_shape=jax.ShapeDtypeStruct((BLOCKS, SENT, ROWS), jnp.bfloat16),
+        in_specs=[pl.BlockSpec((ROWS, 1024 // STEPS), lambda i: (0, i))] * 5,
+        out_specs=pl.BlockSpec((BLOCKS // STEPS, SENT, ROWS), lambda i: (i, 0, 0)),
         name="gather_signals",
-        compiler_params=pltpu.CompilerParams(vmem_limit_bytes=VMEM_GRANT),
+        compiler_params=pltpu.CompilerParams(vmem_limit_bytes=WHOLE_GRANT),
     )(gate_key, value_proj, grad_out, gate_query, filter_taps)
+
+
+def stage_body(*refs):
+    half = len(refs) // 2
+    for source, target in zip(refs[:half], refs[half:]):
+        target[...] = source[...]
+
+
+def stage(arrays):
+    return pl.pallas_call(
+        stage_body,
+        out_shape=tuple(jax.ShapeDtypeStruct(array.shape, array.dtype) for array in arrays),
+        name="stage",
+        compiler_params=pltpu.CompilerParams(vmem_limit_bytes=VMEM_GRANT),
+    )(*arrays)
 
 
 def features_body(where_ref, input_ref, *outs):
@@ -146,9 +167,10 @@
 
 
 def convolve_body(
-    signals_ref, first_ref, cos_ref, sin_ref, ahead_ref, back_ref, last_ref,
-    out_ref, value_ref, rest_ref, wide_in, wide_out, wide_value,
+    where_ref, signals_ref, first_ref, cos_ref, sin_ref, ahead_ref, back_ref, last_ref,
+    out_ref, rest_ref, *refs,
 ):
+    pieces, (wide_in, wide_out, wide_value, sorted_value) = refs[:8], refs[8:]
     wide_in[...] = signals_ref[...].astype(jnp.float32).reshape(BLOCKS * SENT, ROWS)
 
     def step(index, carry):
@@ -230,26 +252,29 @@
     for block in range(BLOCKS):
         tile = wide_value[block * CHANNELS : block * CHANNELS + CHANNELS, :].astype(jnp.bfloat16)
         z, y, x, core = block // 32, block // 8 % 4, block // 2 % 4, block % 2
-        for target in range(4):
-            value_ref[y * 8 + target * 2 + core, z * 4 + x] = tile
-
-
-def convolve(signals, tables):
+        sorted_value[y * 2 + core, z * 4 + x] = tile
+    for flip, piece in enumerate(pieces):
+        piece[...] = sorted_value[where_ref[2] ^ flip]
+
+
+def convolve(where, signals, tables):
     return pl.pallas_call(
         convolve_body,
         out_shape=(
             jax.ShapeDtypeStruct((BLOCKS, CHANNELS, ROWS), jnp.bfloat16),
-            jax.ShapeDtypeStruct((32, 8, CHANNELS, ROWS), jnp.bfloat16),
             jax.ShapeDtypeStruct((CHANNELS // UNROLL, 2 * UNROLL * KEPT, 256), jnp.bfloat16),
-        ),
+        )
+        + (jax.ShapeDtypeStruct((8, CHANNELS, ROWS), jnp.bfloat16),) * 8,
+        in_specs=[pl.BlockSpec(memory_space=pltpu.SMEM)] + [pl.BlockSpec(memory_space=pltpu.VMEM)] * 7,
         scratch_shapes=[
             pltpu.VMEM((BLOCKS * SENT, ROWS), jnp.float32),
             pltpu.VMEM((BLOCKS * CHANNELS, ROWS), jnp.float32),
             pltpu.VMEM((BLOCKS * CHANNELS, ROWS), jnp.float32),
+            pltpu.VMEM((8, 8, CHANNELS, ROWS), jnp.bfloat16),
         ],
         name="convolve",
         compiler_params=pltpu.CompilerParams(vmem_limit_bytes=VMEM_GRANT),
-    )(signals, *tables)
+    )(where, signals, *tables)
 
 
 def complete_body(back_grad_ref, rest_ref, cos_ref, sin_ref, back_ref, last_ref, out_ref, wide_out):
@@ -304,13 +329,34 @@
     )
 
 
-def weight_body(where_ref, value_ref, *refs):
-    features, (kept_ref, sent_ref, aligned, pieces) = refs[:8], refs[8:]
+def bundle_body(*refs):
+    for n, piece in enumerate(refs[:8]):
+        refs[8][n] = piece[...]
+
+
+def bundle(pieces):
+    return pl.pallas_call(
+        bundle_body,
+        out_shape=jax.ShapeDtypeStruct((8, 8, CHANNELS, ROWS), jnp.bfloat16),
+        name="bundle",
+        compiler_params=pltpu.CompilerParams(vmem_limit_bytes=VMEM_GRANT),
+    )(*pieces)
+
+
+def weight_body(where_ref, *refs):
+    values, features = refs[:4], refs[4:12]
+    kept_ref, sent_ref, aligned, pieces = refs[12:]
     x, ring, place = where_ref[0], where_ref[1], where_ref[2]
-    for z in range(2):
-        for back in range(4):
-            block = value_ref[:, z * 4 + (x - back + 4) % 4]
-            aligned[z, :, back * 128 : back * 128 + 128] = block.reshape(512, ROWS)
+    for apart, value_ref in enumerate(values):
+        column = (x - apart + 4) % 4
+        for flip in range(8):
+            origin = place ^ flip
+            origin = origin // 2 * 8 + column * 2 + origin % 2
+            for z in range(2):
+                for back in range(4):
+                    aligned[z, origin, :, back * 128 : back * 128 + 128] = value_ref[
+                        flip, z * 4 + (x - back + 4) % 4
+                    ]
     for apart in range(4):
         total = None
         for half in range(2):
@@ -318,7 +364,10 @@
             rows = features[apart + 4 * half]
             rows = jnp.concatenate([rows[back] for back in range(4)], axis=1)
             term = lax.dot_general(
-                rows, aligned[source // 4], (((1,), (1,)), ((), ())), preferred_element_type=jnp.float32
+                rows,
+                aligned[source // 4].reshape(512, 512),
+                (((1,), (1,)), ((), ())),
+                preferred_element_type=jnp.float32,
             )
             total = term if total is None else total + term
         group = (ring - apart + 8) % 4
@@ -334,18 +383,19 @@
         sent_ref[flip] = pieces[pl.ds((target + 1 - core) * 2, 2)]
 
 
-def weight_parts(where, value, features):
+def weight_parts(where, values, features):
     return pl.pallas_call(
         weight_body,
         out_shape=(jax.ShapeDtypeStruct((4, 2, 64, 512), jnp.bfloat16),) * 2,
-        in_specs=[pl.BlockSpec(memory_space=pltpu.SMEM)] + [pl.BlockSpec(memory_space=pltpu.VMEM)] * 9,
+        in_specs=[pl.BlockSpec(memory_space=pltpu.SMEM)]
+        + [pl.BlockSpec(memory_space=pltpu.VMEM)] * 12,
         scratch_shapes=[
-            pltpu.VMEM((2, 512, 512), jnp.bfloat16),
+            pltpu.VMEM((2, 32, CHANNELS, 512), jnp.bfloat16),
             pltpu.VMEM((16, 64, 512), jnp.bfloat16),
         ],
         name="weight_parts",
         compiler_params=pltpu.CompilerParams(vmem_limit_bytes=VMEM_GRANT),
-    )(where, value, *features)
+    )(where, *values, *features)
 
 
 def join_body(kept_ref, received_ref, *outs):
@@ -370,23 +420,24 @@
         total = parts[0][place].astype(jnp.float32)
         for part in parts[1:]:
             total = total + part[place].astype(jnp.float32)
-        out_ref[...] = total * ROOT_SCALE
+        out_ref[...] = (total * ROOT_SCALE).astype(out_ref.dtype)
 
 
 def weight_total(where, parts):
     return pl.pallas_call(
         total_body,
-        out_shape=(jax.ShapeDtypeStruct((64, 512), jnp.float32),) * 2,
+        out_shape=(
+            jax.ShapeDtypeStruct((64, 512), jnp.float32),
+            jax.ShapeDtypeStruct((64, 512), jnp.bfloat16),
+        ),
         in_specs=[pl.BlockSpec(memory_space=pltpu.SMEM)] + [pl.BlockSpec(memory_space=pltpu.VMEM)] * 4,
         name="weight_total",
         compiler_params=pltpu.CompilerParams(vmem_limit_bytes=VMEM_GRANT),
     )(where, *parts)
 
 
-def exchange(array, groups=None):
-    return lax.all_to_all(
-        array, "seq", split_axis=0, concat_axis=0, tiled=True, axis_index_groups=groups
-    )
+def exchange(array):
+    return lax.all_to_all(array, "seq", split_axis=0, concat_axis=0, tiled=True)
 
 
 def ring_step(array, shift):
@@ -403,19 +454,22 @@
     own = jnp.stack([pieces[0]] + own)
     sent = gather_signals(gate_key, value_proj, grad_out, gate_query, filter_taps)
     up, down = ring_step(own, 1), ring_step(own, -1)
+    tables = stage(tables)
     signals = exchange(sent)
     up2, down2 = ring_step(up, 1), ring_step(down, -1)
-    back_grad, value, rest = convolve(signals, tables)
+    back_grad, rest, *pieces = convolve(where, signals, tables)
+    pieces = pieces[:1] + [lax.ppermute(pieces[n], "seq", across(n)) for n in range(1, 8)]
     up3, down3, far = ring_step(up2, 1), ring_step(down2, -1), ring_step(up2, 2)
-    value = exchange(value, PLANES)
     results = complete(back_grad, rest, tables)
-    kept, sent = weight_parts(where, value, (own, up, up2, up3, far, down3, down2, down))
+    value = bundle(pieces)
+    values = [value] + [lax.ppermute(value, "seq", along_x(n)) for n in range(1, 4)]
+    results = exchange(results)
+    kept, sent = weight_parts(where, values, (own, up, up2, up3, far, down3, down2, down))
     received = lax.ppermute(sent, "seq", across(1))
-    results = exchange(results)
     parts = join_cores(kept, received)
     parts = [parts[0]] + [lax.ppermute(parts[n], "seq", across(2 * n)) for n in range(1, 4)]
     kept, sent = weight_total(where, parts)
-    received = lax.ppermute(sent, "seq", opposite())
+    received = lax.ppermute(sent, "seq", opposite()).astype(jnp.float32)
     grad_query, grad_key, grad_value, grad_filter = finish(results, grad_out, value_proj, gate_key)
     grad_weight = jnp.where(
         z == 0,

time: 171 us -> 151 us (0.88)
  blocking collectives: 45.2 us -> 0 us
  starting transfers between devices: 29.5 us -> 61.7 us
  local copies, waits for them, and re-layouts: 7.18 us -> 0.06 us
  waiting for transfers between devices: 72.8 us -> 69.2 us
  Pallas kernels: 14.4 us -> 17.4 us
    all_to_all x1 -> x0, blocking collectives: 45.2 us -> none  [exchange(): lax.all_to_all(array, 'seq', split_axis=0, concat_axis=0, tiled=True, axi...]
    ppermute x1 -> x11, starting transfers between devices: 0.4 us -> 16.4 us  [the longest x7 8.09 us: shards(): lax.ppermute(pieces[n], 'seq', across(n))]
    all_to_all x2, starting transfers between devices: 11.1 us -> 25.2 us  [exchange(): return lax.all_to_all(array, 'seq', split_axis=0, concat_axis=0, tiled=True)]
    unnamed x36 -> x20, local copies, waits for them, and re-layouts: 7.18 us -> 0.06 us
    ppermute x3, waiting for transfers between devices: 12.5 us -> 7.12 us  [shards(): own = [lax.ppermute(pieces[n], 'seq', along_x(n)) for n in range(1, 4)]]
    pallas_call x1 -> x3, Pallas kernels: 0.39 us -> 3.73 us  [the longest x1 3.66 us: gather_signals(): pl.pallas_call(gather_body, grid=(STEPS,), out_shape=jax.ShapeDtypeStruct...]
    ppermute x1 -> x11, waiting for transfers between devices: 7.23 us -> 10.4 us  [the longest x1 5.64 us: shards(): received = lax.ppermute(sent, 'seq', opposite()).astype(jnp.float32)]
    ppermute x7, starting transfers between devices: 8.31 us -> 10.6 us  [ring_step(): return lax.ppermute(array, ('seq', 'chan'), along_z(shift))]
  transfers between devices with their start and end apart: 17 -> 27, of which waited for: 11 -> 13; matrix products, arithmetic and copies ran while one was open for 0% -> 1% of each run, Pallas kernels for 5% -> 8%
where the time goes in v5:
time: 151 us; the launch traced here: 150 us
  waiting for transfers between devices  69.2 us (46%)
  starting transfers between devices  61.7 us (41%)
  Pallas kernels  17.4 us (12%)
    ppermute x7, waiting for transfers between devices, ring_step(): return lax.ppermute(array, ('seq', 'chan'), along_z(shift))  41.7 us
    all_to_all x2, starting transfers between devices, exchange(): return lax.all_to_all(array, 'seq', split_axis=0, concat_axis=0, tiled=True)  25.2 us
    ppermute x7, starting transfers between devices, ring_step(): return lax.ppermute(array, ('seq', 'chan'), along_z(shift))  10.6 us
    ppermute x7, starting transfers between devices, shards(): lax.ppermute(pieces[n], 'seq', across(n))  8.09 us
    ppermute x3, waiting for transfers between devices, shards(): lax.ppermute(parts[n], 'seq', across(2 * n))  7.65 us
    ppermute x3, waiting for transfers between devices, shards(): own = [lax.ppermute(pieces[n], 'seq', along_x(n)) for n in range(1, 4)]  7.12 us
    ppermute x3, starting transfers between devices, shards(): lax.ppermute(value, 'seq', along_x(n))  5.7 us
    ppermute x1, waiting for transfers between devices, shards(): received = lax.ppermute(sent, 'seq', opposite()).astype(jnp.float32)  5.64 us
  transfers between devices with their start and end apart: 27, of which 13 were waited for; matrix products, arithmetic and copies ran while one was open for 1% of the time, Pallas kernels for 8%

profile of v5, /device:TPU:32, one launch (start us, length us, event | category | flops | bytes accessed | tf_op | source)
XLA Modules:
  0.0 150.1 jit_solution(10270820866269549205)
XLA Ops:
  0.6 3.7 %gather_signals.1 = bf16[64,64,128]{2,1,0:T(8,128)(2,1)} custom-call(bf16[128,1024]{1,0:T(8,128)(2,1)} %key_ref.3, bf16[128,1024]{1,0:T(8,128)(2,1)} %value_ref.3, bf16[128,1024]{1,0:T(8,128)(2,1)} %grad_ref.3, bf16[128,1024]{1,0:T(8,128)(2,1)} %query_ref.1, bf16[128,1024]{1,0:T(8,128)(2,1)} %taps_ref.1), custom_call_target="tpu_custom_call" | custom-call | tf_op jit(solution)/shard_map/gather_signals/pallas_call | solution.py:100
  4.4 13.8 %all-to-all-start = ((bf16[64,64,128]{2,1,0:T(8,128)(2,1)}), bf16[64,64,128]{2,1,0:T(8,128)(2,1)S(1)}, u32[]{:S(2)}, u32[]{:S(2)}) async-start(bf16[64,64,128]{2,1,0:T(8,128)(2,1)} %gather_signals.1), calls=%async_computation | async-start | bytes 2097152 | tf_op jit(solution)/shard_map/all_to_all | solution.py:440
  18.2 0.1 pad_add_fusion.where_ref
  18.3 0.7 split_features.1
  19.0 2.9 %collective-permute-start.12 = (bf16[256,128]{1,0:T(8,128)(2,1)S(1)}, bf16[256,128]{1,0:T(8,128)(2,1)S(1)}, u32[]{:S(2)}, u32[]{:S(2)}) collective-permute-start(bf16[256,128]{1,0:T(8,128)(2,1)S(1)} %get-tuple-element.60), channel_id=1, source_target_pairs={{0,24},{4,28},{8,0},{12,4},{16,8},{20,12},{24,16},{28,20},{32,56},... | collective-permute-start | bytes 196616 | tf_op jit(solution)/shard_map/ppermute | solution.py:453
  21.9 0.9 collective-permute-start.11
  22.7 0.9 collective-permute-start.10
  23.6 5.2 %collective-permute-done.12 = bf16[256,128]{1,0:T(8,128)(2,1)S(1)} collective-permute-done((bf16[256,128]{1,0:T(8,128)(2,1)S(1)}, bf16[256,128]{1,0:T(8,128)(2,1)S(1)}, u32[]{:S(2)}, u32[]{:S(2)}) %collective-permute-start.12) | collective-permute-done | bytes 65568 | tf_op jit(solution)/shard_map/ppermute | solution.py:453
  28.8 1.6 %collective-permute-done.11 = bf16[256,128]{1,0:T(8,128)(2,1)S(1)} collective-permute-done((bf16[256,128]{1,0:T(8,128)(2,1)S(1)}, bf16[256,128]{1,0:T(8,128)(2,1)S(1)}, u32[]{:S(2)}, u32[]{:S(2)}) %collective-permute-start.11) | collective-permute-done | bytes 65568 | tf_op jit(solution)/shard_map/ppermute | solution.py:453
  30.3 0.4 collective-permute-done.10
  30.8 1.1 collective-permute-start.13
  31.9 2.3 %collective-permute-start.17 = (bf16[4,256,128]{2,1,0:T(8,128)(2,1)S(1)}, bf16[4,256,128]{2,1,0:T(8,128)(2,1)S(1)}, u32[]{:S(2)}, u32[]{:S(2)}) collective-permute-start(bf16[4,256,128]{2,1,0:T(8,128)(2,1)S(1)} %pad_maximum_fusion.refs_4_), channel_id=1, source_target_pairs={{0,131},{1,0},{2,1},{3,2},{4,135},{5,4},{6,5},{7,6},{8,139},{9,8},... | collective-permute-start | bytes 786440 | tf_op jit(solution)/shard_map/ppermute | solution.py:444
  34.1 14.5 %collective-permute-done.13.refs_5_ = bf16[4,256,128]{2,1,0:T(8,128)(2,1)S(1)} collective-permute-done((bf16[4,256,128]{2,1,0:T(8,128)(2,1)S(1)}, bf16[4,256,128]{2,1,0:T(8,128)(2,1)S(1)}, u32[]{:S(2)}, u32[]{:S(2)}) %collective-permute-start.13) | collective-permute-done | bytes 262176 | tf_op jit(solution)/shard_map/ppermute | solution.py:444
  48.7 1.0 collective-permute-start.14
  49.6 0.1 stage.1
  49.7 0.4 all-to-all-done.signals_ref
  50.1 5.4 %convolve.1 = (bf16[64,16,128]{2,1,0:T(8,128)(2,1)S(1)}, bf16[4,576,256]{2,1,0:T(8,128)(2,1)S(1)}, bf16[8,16,128]{2,1,0:T(8,128)(2,1)S(1)}, bf16[8,16,128]{2,1,0...) custom-call(s32[4]{0:T(128)S(1)} %pad_add_fusion.where_ref, ...), custom_call_target="tpu_custom_call" | custom-call | tf_op jit(solution)/shard_map/convolve/pallas_call | solution.py:261
  55.6 3.4 %complete.1 = bf16[64,48,128]{2,1,0:T(8,128)(2,1)} custom-call(bf16[64,16,128]{2,1,0:T(8,128)(2,1)S(1)} %get-tuple-element.43.back_grad_ref, bf16[4,576,256]{2,1,0:T(8,128)(2,1)S(1)} %get-tuple-element.44.rest_ref, f32[72,128]{1,0:T(8,128)S(1)} %get-tuple-element.38.cos_ref, f32[72,128]{1,0:T(8,128)S(1)} %get-tuple-element.39.sin_ref, ...), custom_call_target="tpu_custom_call" | custom-call | tf_op jit(solution)/shard_map/complete/pallas_call | solution.py:301
  58.9 11.4 %all-to-all-start.1 = ((bf16[64,48,128]{2,1,0:T(8,128)(2,1)}), bf16[64,48,128]{2,1,0:T(8,128)(2,1)S(1)}, u32[]{:S(2)}, u32[]{:S(2)}) async-start(bf16[64,48,128]{2,1,0:T(8,128)(2,1)} %complete.1), calls=%async_computation.1 | async-start | bytes 1572864 | tf_op jit(solution)/shard_map/all_to_all | solution.py:440
  70.4 0.6 collective-permute-start.18
  71.0 1.5 collective-permute-start.15
  72.5 1.6 %collective-permute-start.1 = (bf16[8,16,128]{2,1,0:T(8,128)(2,1)S(1)}, bf16[8,16,128]{2,1,0:T(8,128)(2,1)S(1)}, u32[]{:S(2)}, u32[]{:S(2)}) collective-permute-start(bf16[8,16,128]{2,1,0:T(8,128)(2,1)S(1)} %get-tuple-element.51), channel_id=1, source_target_pairs={{0,32},{4,36},{8,40},{12,44},{16,48},{20,52},{24,56},{28,60},{32,0... | collective-permute-start | bytes 98312 | tf_op jit(solution)/shard_map/ppermute | solution.py:461
  74.1 0.3 collective-permute-start.2
  74.3 21.2 %collective-permute-done.18.refs_10_ = bf16[4,256,128]{2,1,0:T(8,128)(2,1)S(1)} collective-permute-done((bf16[4,256,128]{2,1,0:T(8,128)(2,1)S(1)}, bf16[4,256,128]{2,1,0:T(8,128)(2,1)S(1)}, u32[]{:S(2)}, u32[]{:S(2)}) %collective-permute-start.18) | collective-permute-done | bytes 262176 | tf_op jit(solution)/shard_map/ppermute | solution.py:444
  95.6 3.1 %collective-permute-start.3 = (bf16[8,16,128]{2,1,0:T(8,128)(2,1)S(1)}, bf16[8,16,128]{2,1,0:T(8,128)(2,1)S(1)}, u32[]{:S(2)}, u32[]{:S(2)}) collective-permute-start(bf16[8,16,128]{2,1,0:T(8,128)(2,1)S(1)} %get-tuple-element.53), channel_id=1, source_target_pairs={{0,64},{4,68},{8,72},{12,76},{16,80},{20,84},{24,88},{28,92},{32,9... | collective-permute-start | bytes 98312 | tf_op jit(solution)/shard_map/ppermute | solution.py:461
  98.7 1.9 %collective-permute-start.5 = (bf16[8,16,128]{2,1,0:T(8,128)(2,1)S(1)}, bf16[8,16,128]{2,1,0:T(8,128)(2,1)S(1)}, u32[]{:S(2)}, u32[]{:S(2)}) collective-permute-start(bf16[8,16,128]{2,1,0:T(8,128)(2,1)S(1)} %get-tuple-element.55), channel_id=1, source_target_pairs={{0,96},{4,100},{8,104},{12,108},{16,112},{20,116},{24,120},{28,124... | collective-permute-start | bytes 98312 | tf_op jit(solution)/shard_map/ppermute | solution.py:461
  100.6 1.2 collective-permute-start.6
  101.8 4.2 %collective-permute-start.16 = (bf16[4,256,128]{2,1,0:T(8,128)(2,1)S(1)}, bf16[4,256,128]{2,1,0:T(8,128)(2,1)S(1)}, u32[]{:S(2)}, u32[]{:S(2)}) collective-permute-start(bf16[4,256,128]{2,1,0:T(8,128)(2,1)S(1)} %collective-permute-done.14.refs_6_), channel_id=1, source_target_pairs={{0,2},{1,3},{2,128},{3,129},{4,6},{5,7},{6,132},{7,133},{8,10},{9,... | collective-permute-start | bytes 786440 | tf_op jit(solution)/shard_map/ppermute | solution.py:444
  106.1 1.6 %collective-permute-start.7 = (bf16[8,8,16,128]{3,2,1,0:T(8,128)(2,1)S(1)}, bf16[8,8,16,128]{3,2,1,0:T(8,128)(2,1)S(1)}, u32[]{:S(2)}, u32[]{:S(2)}) collective-permute-start(bf16[8,8,16,128]{3,2,1,0:T(8,128)(2,1)S(1)} %bundle.1.refs_0_), channel_id=1, source_target_pairs={{0,8},{4,12},{8,16},{12,20},{16,24},{20,28},{24,0},{28,4},{32,40},... | collective-permute-start | bytes 786440 | tf_op jit(solution)/shard_map/ppermute | solution.py:465
  107.6 2.7 %collective-permute-start.8 = (bf16[8,8,16,128]{3,2,1,0:T(8,128)(2,1)S(1)}, bf16[8,8,16,128]{3,2,1,0:T(8,128)(2,1)S(1)}, u32[]{:S(2)}, u32[]{:S(2)}) collective-permute-start(bf16[8,8,16,128]{3,2,1,0:T(8,128)(2,1)S(1)} %bundle.1.refs_0_), channel_id=1, source_target_pairs={{0,16},{4,20},{8,24},{12,28},{16,0},{20,4},{24,8},{28,12},{32,48},... | collective-permute-start | bytes 786440 | tf_op jit(solution)/shard_map/ppermute | solution.py:465
  110.3 1.4 collective-permute-start.9
  111.8 6.0 %collective-permute-done.16.refs_8_ = bf16[4,256,128]{2,1,0:T(8,128)(2,1)S(1)} collective-permute-done((bf16[4,256,128]{2,1,0:T(8,128)(2,1)S(1)}, bf16[4,256,128]{2,1,0:T(8,128)(2,1)S(1)}, u32[]{:S(2)}, u32[]{:S(2)}) %collective-permute-start.16) | collective-permute-done | bytes 262176 | tf_op jit(solution)/shard_map/ppermute | solution.py:444
  117.7 4.7 %collective-permute-done.8.refs_2_ = bf16[8,8,16,128]{3,2,1,0:T(8,128)(2,1)S(1)} collective-permute-done((bf16[8,8,16,128]{3,2,1,0:T(8,128)(2,1)S(1)}, bf16[8,8,16,128]{3,2,1,0:T(8,128)(2,1)S(1)}, u32[]{:S(2)}, u32[]{:S(2)}) %collective-permute-start.8) | collective-permute-done | bytes 262176 | tf_op jit(solution)/shard_map/ppermute | solution.py:465
  122.5 2.1 %weight_parts.1 = (bf16[4,2,64,512]{3,2,1,0:T(8,128)(2,1)S(1)}, bf16[4,2,64,512]{3,2,1,0:T(8,128)(2,1)S(1)}) custom-call(s32[4]{0:T(128)S(1)} %pad_add_fusion.where_ref, bf16[8,8,16,128]{3,2,1,0:T(8,128)(2,1)S(1)} %bundle.1.refs_0_, bf16[8,8,16,128]{3,2,1,0:T(8,128)(2,1)S(1)} %collective-permute-done.7.refs_1_, ...), custom_call_target="tpu_custom_call" | custom-call | tf_op jit(solution)/shard_map/weight_parts/pallas_call | solution.py:387
  124.6 0.1 collective-permute-start.20
  124.7 1.9 %collective-permute-done.20.received_ref = bf16[4,2,64,512]{3,2,1,0:T(8,128)(2,1)S(1)} collective-permute-done((bf16[4,2,64,512]{3,2,1,0:T(8,128)(2,1)S(1)}, bf16[4,2,64,512]{3,2,1,0:T(8,128)(2,1)S(1)}, u32[]{:S(2)}, u32[]{:S(2)}) %collective-permute-start.20) | collective-permute-done | bytes 524320 | tf_op jit(solution)/shard_map/ppermute | solution.py:468
  126.6 0.1 join_cores.1
  126.8 0.1 collective-permute-start.21
  126.9 3.7 %collective-permute-start.22 = (bf16[2,64,512]{2,1,0:T(8,128)(2,1)S(1)}, bf16[2,64,512]{2,1,0:T(8,128)(2,1)S(1)}, u32[]{:S(2)}, u32[]{:S(2)}) collective-permute-start(bf16[2,64,512]{2,1,0:T(8,128)(2,1)S(1)} %get-tuple-element.65), channel_id=1, source_target_pairs={{0,64},{4,68},{8,72},{12,76},{16,80},{20,84},{24,88},{28,92},{32,9... | collective-permute-start | bytes 393224 | tf_op jit(solution)/shard_map/ppermute | solution.py:470
  130.5 1.0 collective-permute-start.23
  131.5 1.7 %collective-permute-done.21.refs_1_ = bf16[2,64,512]{2,1,0:T(8,128)(2,1)S(1)} collective-permute-done((bf16[2,64,512]{2,1,0:T(8,128)(2,1)S(1)}, bf16[2,64,512]{2,1,0:T(8,128)(2,1)S(1)}, u32[]{:S(2)}, u32[]{:S(2)}) %collective-permute-start.21) | collective-permute-done | bytes 131104 | tf_op jit(solution)/shard_map/ppermute | solution.py:470
  133.2 3.8 %collective-permute-done.22.refs_2_ = bf16[2,64,512]{2,1,0:T(8,128)(2,1)S(1)} collective-permute-done((bf16[2,64,512]{2,1,0:T(8,128)(2,1)S(1)}, bf16[2,64,512]{2,1,0:T(8,128)(2,1)S(1)}, u32[]{:S(2)}, u32[]{:S(2)}) %collective-permute-start.22) | collective-permute-done | bytes 131104 | tf_op jit(solution)/shard_map/ppermute | solution.py:470
  137.0 2.2 %collective-permute-done.23.refs_3_ = bf16[2,64,512]{2,1,0:T(8,128)(2,1)S(1)} collective-permute-done((bf16[2,64,512]{2,1,0:T(8,128)(2,1)S(1)}, bf16[2,64,512]{2,1,0:T(8,128)(2,1)S(1)}, u32[]{:S(2)}, u32[]{:S(2)}) %collective-permute-start.23) | collective-permute-done | bytes 131104 | tf_op jit(solution)/shard_map/ppermute | solution.py:470
  139.2 0.6 weight_total.1
  139.8 2.6 %collective-permute-start.24 = (bf16[64,512]{1,0:T(8,128)(2,1)S(1)}, bf16[64,512]{1,0:T(8,128)(2,1)S(1)}, u32[]{:S(2)}, u32[]{:S(2)}) collective-permute-start(bf16[64,512]{1,0:T(8,128)(2,1)S(1)} %get-tuple-element.68), channel_id=1, source_target_pairs={{0,128},{4,132},{8,136},{12,140},{16,144},{20,148},{24,152},{28,15... | collective-permute-start | bytes 196616 | tf_op jit(solution)/shard_map/ppermute | solution.py:472
  142.4 5.6 %collective-permute-done.24 = bf16[64,512]{1,0:T(8,128)(2,1)S(1)} collective-permute-done((bf16[64,512]{1,0:T(8,128)(2,1)S(1)}, bf16[64,512]{1,0:T(8,128)(2,1)S(1)}, u32[]{:S(2)}, u32[]{:S(2)}) %collective-permute-start.24) | collective-permute-done | bytes 65568 | tf_op jit(solution)/shard_map/ppermute | solution.py:472
  148.1 0.7 maximum_select_fusion
  148.8 1.3 finish.1
  (40 shorter events, 0.2 us)
Async XLA Ops:
  4.3 14.0 %copy-start.3 = (bf16[128,1024]{1,0:T(8,128)(2,1)S(1)}, bf16[128,1024]{1,0:T(8,128)(2,1)}, u32[]{:S(2)}) copy-start(bf16[128,1024]{1,0:T(8,128)(2,1)} %input_ref.1) | copy-start | bytes 786436
  4.3 45.3 %copy-start.4 = (bf16[512,256]{1,0:T(8,128)(2,1)S(1)}, bf16[512,256]{1,0:T(8,128)(2,1)}, u32[]{:S(2)}) copy-start(bf16[512,256]{1,0:T(8,128)(2,1)} %constant.84.clone.refs_3_) | copy-start | bytes 786436
  4.3 45.3 %copy-start.5 = (bf16[512,256]{1,0:T(8,128)(2,1)S(1)}, bf16[512,256]{1,0:T(8,128)(2,1)}, u32[]{:S(2)}) copy-start(bf16[512,256]{1,0:T(8,128)(2,1)} %constant.85.clone.refs_4_) | copy-start | bytes 786436
  4.3 45.3 %copy-start.6 = (bf16[128,144]{1,0:T(8,128)(2,1)S(1)}, bf16[128,144]{1,0:T(8,128)(2,1)}, u32[]{:S(2)}) copy-start(bf16[128,144]{1,0:T(8,128)(2,1)} %constant.86.clone.refs_5_) | copy-start | bytes 110596
  4.3 45.3 %copy-start.7 = (bf16[144,128]{1,0:T(8,128)(2,1)S(1)}, bf16[144,128]{1,0:T(8,128)(2,1)}, u32[]{:S(2)}) copy-start(bf16[144,128]{1,0:T(8,128)(2,1)} %constant.81.clone.refs_0_) | copy-start | bytes 110596
  4.3 45.3 %copy-start.8 = (f32[72,128]{1,0:T(8,128)S(1)}, f32[72,128]{1,0:T(8,128)}, u32[]{:S(2)}) copy-start(f32[72,128]{1,0:T(8,128)} %constant.82.clone.refs_1_) | copy-start | bytes 110596
  4.3 45.3 %copy-start.9 = (f32[72,128]{1,0:T(8,128)S(1)}, f32[72,128]{1,0:T(8,128)}, u32[]{:S(2)}) copy-start(f32[72,128]{1,0:T(8,128)} %constant.83.clone.refs_2_) | copy-start | bytes 110596
  4.4 45.8 %all-to-all-start = ((bf16[64,64,128]{2,1,0:T(8,128)(2,1)}), bf16[64,64,128]{2,1,0:T(8,128)(2,1)S(1)}, u32[]{:S(2)}, u32[]{:S(2)}) async-start(bf16[64,64,128]{2,1,0:T(8,128)(2,1)} %gather_signals.1), calls=%async_computation | async-start | bytes 2097152 | tf_op jit(solution)/shard_map/all_to_all | solution.py:440
  19.0 9.7 %collective-permute-start.12 = (bf16[256,128]{1,0:T(8,128)(2,1)S(1)}, bf16[256,128]{1,0:T(8,128)(2,1)S(1)}, u32[]{:S(2)}, u32[]{:S(2)}) collective-permute-start(bf16[256,128]{1,0:T(8,128)(2,1)S(1)} %get-tuple-element.60), channel_id=1, source_target_pairs={{0,24},{4,28},{8,0},{12,4},{16,8},{20,12},{24,16},{28,20},{32,56},... | collective-permute-start | bytes 196616 | tf_op jit(solution)/shard_map/ppermute | solution.py:453
  21.9 8.4 %collective-permute-start.11 = (bf16[256,128]{1,0:T(8,128)(2,1)S(1)}, bf16[256,128]{1,0:T(8,128)(2,1)S(1)}, u32[]{:S(2)}, u32[]{:S(2)}) collective-permute-start(bf16[256,128]{1,0:T(8,128)(2,1)S(1)} %get-tuple-element.59), channel_id=1, source_target_pairs={{0,16},{4,20},{8,24},{12,28},{16,0},{20,4},{24,8},{28,12},{32,48},... | collective-permute-start | bytes 196616 | tf_op jit(solution)/shard_map/ppermute | solution.py:453
  22.7 8.0 %collective-permute-start.10 = (bf16[256,128]{1,0:T(8,128)(2,1)S(1)}, bf16[256,128]{1,0:T(8,128)(2,1)S(1)}, u32[]{:S(2)}, u32[]{:S(2)}) collective-permute-start(bf16[256,128]{1,0:T(8,128)(2,1)S(1)} %get-tuple-element.58), channel_id=1, source_target_pairs={{0,8},{4,12},{8,16},{12,20},{16,24},{20,28},{24,0},{28,4},{32,40},... | collective-permute-start | bytes 196616 | tf_op jit(solution)/shard_map/ppermute | solution.py:453
  30.8 17.9 %collective-permute-start.13 = (bf16[4,256,128]{2,1,0:T(8,128)(2,1)S(1)}, bf16[4,256,128]{2,1,0:T(8,128)(2,1)S(1)}, u32[]{:S(2)}, u32[]{:S(2)}) collective-permute-start(bf16[4,256,128]{2,1,0:T(8,128)(2,1)S(1)} %pad_maximum_fusion.refs_4_), channel_id=1, source_target_pairs={{0,1},{1,2},{2,3},{3,128},{4,5},{5,6},{6,7},{7,132},{8,9},{9,10},{... | collective-permute-start | bytes 786440 | tf_op jit(solution)/shard_map/ppermute | solution.py:444
  31.9 38.5 %collective-permute-start.17 = (bf16[4,256,128]{2,1,0:T(8,128)(2,1)S(1)}, bf16[4,256,128]{2,1,0:T(8,128)(2,1)S(1)}, u32[]{:S(2)}, u32[]{:S(2)}) collective-permute-start(bf16[4,256,128]{2,1,0:T(8,128)(2,1)S(1)} %pad_maximum_fusion.refs_4_), channel_id=1, source_target_pairs={{0,131},{1,0},{2,1},{3,2},{4,135},{5,4},{6,5},{7,6},{8,139},{9,8},... | collective-permute-start | bytes 786440 | tf_op jit(solution)/shard_map/ppermute | solution.py:444
  48.7 22.4 %collective-permute-start.14 = (bf16[4,256,128]{2,1,0:T(8,128)(2,1)S(1)}, bf16[4,256,128]{2,1,0:T(8,128)(2,1)S(1)}, u32[]{:S(2)}, u32[]{:S(2)}) collective-permute-start(bf16[4,256,128]{2,1,0:T(8,128)(2,1)S(1)} %collective-permute-done.13.refs_5_), channel_id=1, source_target_pairs={{0,1},{1,2},{2,3},{3,128},{4,5},{5,6},{6,7},{7,132},{8,9},{9,10},{... | collective-permute-start | bytes 786440 | tf_op jit(solution)/shard_map/ppermute | solution.py:444
  58.9 89.9 %all-to-all-start.1 = ((bf16[64,48,128]{2,1,0:T(8,128)(2,1)}), bf16[64,48,128]{2,1,0:T(8,128)(2,1)S(1)}, u32[]{:S(2)}, u32[]{:S(2)}) async-start(bf16[64,48,128]{2,1,0:T(8,128)(2,1)} %complete.1), calls=%async_computation.1 | async-start | bytes 1572864 | tf_op jit(solution)/shard_map/all_to_all | solution.py:440
  70.4 25.2 %collective-permute-start.18 = (bf16[4,256,128]{2,1,0:T(8,128)(2,1)S(1)}, bf16[4,256,128]{2,1,0:T(8,128)(2,1)S(1)}, u32[]{:S(2)}, u32[]{:S(2)}) collective-permute-start(bf16[4,256,128]{2,1,0:T(8,128)(2,1)S(1)} %collective-permute-done.17.refs_11_), channel_id=1, source_target_pairs={{0,131},{1,0},{2,1},{3,2},{4,135},{5,4},{6,5},{7,6},{8,139},{9,8},... | collective-permute-start | bytes 786440 | tf_op jit(solution)/shard_map/ppermute | solution.py:444
  71.0 39.3 %collective-permute-start.15 = (bf16[4,256,128]{2,1,0:T(8,128)(2,1)S(1)}, bf16[4,256,128]{2,1,0:T(8,128)(2,1)S(1)}, u32[]{:S(2)}, u32[]{:S(2)}) collective-permute-start(bf16[4,256,128]{2,1,0:T(8,128)(2,1)S(1)} %collective-permute-done.14.refs_6_), channel_id=1, source_target_pairs={{0,1},{1,2},{2,3},{3,128},{4,5},{5,6},{6,7},{7,132},{8,9},{9,10},{... | collective-permute-start | bytes 786440 | tf_op jit(solution)/shard_map/ppermute | solution.py:444
  72.5 26.2 %collective-permute-start = (bf16[8,16,128]{2,1,0:T(8,128)(2,1)S(1)}, bf16[8,16,128]{2,1,0:T(8,128)(2,1)S(1)}, u32[]{:S(2)}, u32[]{:S(2)}) collective-permute-start(bf16[8,16,128]{2,1,0:T(8,128)(2,1)S(1)} %get-tuple-element.50), channel_id=1, source_target_pairs={{0,4},{4,0},{8,12},{12,8},{16,20},{20,16},{24,28},{28,24},{32,36},... | collective-permute-start | bytes 98312 | tf_op jit(solution)/shard_map/ppermute | solution.py:461
  72.5 26.2 %collective-permute-start.1 = (bf16[8,16,128]{2,1,0:T(8,128)(2,1)S(1)}, bf16[8,16,128]{2,1,0:T(8,128)(2,1)S(1)}, u32[]{:S(2)}, u32[]{:S(2)}) collective-permute-start(bf16[8,16,128]{2,1,0:T(8,128)(2,1)S(1)} %get-tuple-element.51), channel_id=1, source_target_pairs={{0,32},{4,36},{8,40},{12,44},{16,48},{20,52},{24,56},{28,60},{32,0... | collective-permute-start | bytes 98312 | tf_op jit(solution)/shard_map/ppermute | solution.py:461
  74.1 26.5 %collective-permute-start.2 = (bf16[8,16,128]{2,1,0:T(8,128)(2,1)S(1)}, bf16[8,16,128]{2,1,0:T(8,128)(2,1)S(1)}, u32[]{:S(2)}, u32[]{:S(2)}) collective-permute-start(bf16[8,16,128]{2,1,0:T(8,128)(2,1)S(1)} %get-tuple-element.52), channel_id=1, source_target_pairs={{0,36},{4,32},{8,44},{12,40},{16,52},{20,48},{24,60},{28,56},{32,4... | collective-permute-start | bytes 98312 | tf_op jit(solution)/shard_map/ppermute | solution.py:461
  95.6 6.3 %collective-permute-start.3 = (bf16[8,16,128]{2,1,0:T(8,128)(2,1)S(1)}, bf16[8,16,128]{2,1,0:T(8,128)(2,1)S(1)}, u32[]{:S(2)}, u32[]{:S(2)}) collective-permute-start(bf16[8,16,128]{2,1,0:T(8,128)(2,1)S(1)} %get-tuple-element.53), channel_id=1, source_target_pairs={{0,64},{4,68},{8,72},{12,76},{16,80},{20,84},{24,88},{28,92},{32,9... | collective-permute-start | bytes 98312 | tf_op jit(solution)/shard_map/ppermute | solution.py:461
  98.7 7.3 %collective-permute-start.4 = (bf16[8,16,128]{2,1,0:T(8,128)(2,1)S(1)}, bf16[8,16,128]{2,1,0:T(8,128)(2,1)S(1)}, u32[]{:S(2)}, u32[]{:S(2)}) collective-permute-start(bf16[8,16,128]{2,1,0:T(8,128)(2,1)S(1)} %get-tuple-element.54), channel_id=1, source_target_pairs={{0,68},{4,64},{8,76},{12,72},{16,84},{20,80},{24,92},{28,88},{32,1... | collective-permute-start | bytes 98312 | tf_op jit(solution)/shard_map/ppermute | solution.py:461
  98.7 7.3 %collective-permute-start.5 = (bf16[8,16,128]{2,1,0:T(8,128)(2,1)S(1)}, bf16[8,16,128]{2,1,0:T(8,128)(2,1)S(1)}, u32[]{:S(2)}, u32[]{:S(2)}) collective-permute-start(bf16[8,16,128]{2,1,0:T(8,128)(2,1)S(1)} %get-tuple-element.55), channel_id=1, source_target_pairs={{0,96},{4,100},{8,104},{12,108},{16,112},{20,116},{24,120},{28,124... | collective-permute-start | bytes 98312 | tf_op jit(solution)/shard_map/ppermute | solution.py:461
  100.6 5.4 %collective-permute-start.6 = (bf16[8,16,128]{2,1,0:T(8,128)(2,1)S(1)}, bf16[8,16,128]{2,1,0:T(8,128)(2,1)S(1)}, u32[]{:S(2)}, u32[]{:S(2)}) collective-permute-start(bf16[8,16,128]{2,1,0:T(8,128)(2,1)S(1)} %get-tuple-element.56), channel_id=1, source_target_pairs={{0,100},{4,96},{8,108},{12,104},{16,116},{20,112},{24,124},{28,120... | collective-permute-start | bytes 98312 | tf_op jit(solution)/shard_map/ppermute | solution.py:461
  101.8 15.9 %collective-permute-start.16 = (bf16[4,256,128]{2,1,0:T(8,128)(2,1)S(1)}, bf16[4,256,128]{2,1,0:T(8,128)(2,1)S(1)}, u32[]{:S(2)}, u32[]{:S(2)}) collective-permute-start(bf16[4,256,128]{2,1,0:T(8,128)(2,1)S(1)} %collective-permute-done.14.refs_6_), channel_id=1, source_target_pairs={{0,2},{1,3},{2,128},{3,129},{4,6},{5,7},{6,132},{7,133},{8,10},{9,... | collective-permute-start | bytes 786440 | tf_op jit(solution)/shard_map/ppermute | solution.py:444
  106.0 11.7 %collective-permute-start.19 = (bf16[4,256,128]{2,1,0:T(8,128)(2,1)S(1)}, bf16[4,256,128]{2,1,0:T(8,128)(2,1)S(1)}, u32[]{:S(2)}, u32[]{:S(2)}) collective-permute-start(bf16[4,256,128]{2,1,0:T(8,128)(2,1)S(1)} %collective-permute-done.18.refs_10_), channel_id=1, source_target_pairs={{0,131},{1,0},{2,1},{3,2},{4,135},{5,4},{6,5},{7,6},{8,139},{9,8},... | collective-permute-start | bytes 786440 | tf_op jit(solution)/shard_map/ppermute | solution.py:444
  106.1 11.7 %collective-permute-start.7 = (bf16[8,8,16,128]{3,2,1,0:T(8,128)(2,1)S(1)}, bf16[8,8,16,128]{3,2,1,0:T(8,128)(2,1)S(1)}, u32[]{:S(2)}, u32[]{:S(2)}) collective-permute-start(bf16[8,8,16,128]{3,2,1,0:T(8,128)(2,1)S(1)} %bundle.1.refs_0_), channel_id=1, source_target_pairs={{0,8},{4,12},{8,16},{12,20},{16,24},{20,28},{24,0},{28,4},{32,40},... | collective-permute-start | bytes 786440 | tf_op jit(solution)/shard_map/ppermute | solution.py:465
  107.6 14.9 %collective-permute-start.8 = (bf16[8,8,16,128]{3,2,1,0:T(8,128)(2,1)S(1)}, bf16[8,8,16,128]{3,2,1,0:T(8,128)(2,1)S(1)}, u32[]{:S(2)}, u32[]{:S(2)}) collective-permute-start(bf16[8,8,16,128]{3,2,1,0:T(8,128)(2,1)S(1)} %bundle.1.refs_0_), channel_id=1, source_target_pairs={{0,16},{4,20},{8,24},{12,28},{16,0},{20,4},{24,8},{28,12},{32,48},... | collective-permute-start | bytes 786440 | tf_op jit(solution)/shard_map/ppermute | solution.py:465
  110.3 12.2 %collective-permute-start.9 = (bf16[8,8,16,128]{3,2,1,0:T(8,128)(2,1)S(1)}, bf16[8,8,16,128]{3,2,1,0:T(8,128)(2,1)S(1)}, u32[]{:S(2)}, u32[]{:S(2)}) collective-permute-start(bf16[8,8,16,128]{3,2,1,0:T(8,128)(2,1)S(1)} %bundle.1.refs_0_), channel_id=1, source_target_pairs={{0,24},{4,28},{8,0},{12,4},{16,8},{20,12},{24,16},{28,20},{32,56},... | collective-permute-start | bytes 786440 | tf_op jit(solution)/shard_map/ppermute | solution.py:465
  124.6 24.2 %copy-start = (bf16[128,1024]{1,0:T(8,128)(2,1)S(1)}, bf16[128,1024]{1,0:T(8,128)(2,1)}, u32[]{:S(2)}) copy-start(bf16[128,1024]{1,0:T(8,128)(2,1)} %key_ref.3) | copy-start | bytes 786436
  124.6 24.2 %copy-start.1 = (bf16[128,1024]{1,0:T(8,128)(2,1)S(1)}, bf16[128,1024]{1,0:T(8,128)(2,1)}, u32[]{:S(2)}) copy-start(bf16[128,1024]{1,0:T(8,128)(2,1)} %value_ref.3) | copy-start | bytes 786436
  124.6 24.2 %copy-start.2 = (bf16[128,1024]{1,0:T(8,128)(2,1)S(1)}, bf16[128,1024]{1,0:T(8,128)(2,1)}, u32[]{:S(2)}) copy-start(bf16[128,1024]{1,0:T(8,128)(2,1)} %grad_ref.3) | copy-start | bytes 786436
  124.6 2.0 %collective-permute-start.20 = (bf16[4,2,64,512]{3,2,1,0:T(8,128)(2,1)S(1)}, bf16[4,2,64,512]{3,2,1,0:T(8,128)(2,1)S(1)}, u32[]{:S(2)}, u32[]{:S(2)}) collective-permute-start(bf16[4,2,64,512]{3,2,1,0:T(8,128)(2,1)S(1)} %get-tuple-element.62), channel_id=1, source_target_pairs={{0,4},{4,0},{8,12},{12,8},{16,20},{20,16},{24,28},{28,24},{32,36},... | collective-permute-start | bytes 1572872 | tf_op jit(solution)/shard_map/ppermute | solution.py:468
  126.8 6.5 %collective-permute-start.21 = (bf16[2,64,512]{2,1,0:T(8,128)(2,1)S(1)}, bf16[2,64,512]{2,1,0:T(8,128)(2,1)S(1)}, u32[]{:S(2)}, u32[]{:S(2)}) collective-permute-start(bf16[2,64,512]{2,1,0:T(8,128)(2,1)S(1)} %get-tuple-element.64), channel_id=1, source_target_pairs={{0,32},{4,36},{8,40},{12,44},{16,48},{20,52},{24,56},{28,60},{32,0... | collective-permute-start | bytes 393224 | tf_op jit(solution)/shard_map/ppermute | solution.py:470
  126.9 10.1 %collective-permute-start.22 = (bf16[2,64,512]{2,1,0:T(8,128)(2,1)S(1)}, bf16[2,64,512]{2,1,0:T(8,128)(2,1)S(1)}, u32[]{:S(2)}, u32[]{:S(2)}) collective-permute-start(bf16[2,64,512]{2,1,0:T(8,128)(2,1)S(1)} %get-tuple-element.65), channel_id=1, source_target_pairs={{0,64},{4,68},{8,72},{12,76},{16,80},{20,84},{24,88},{28,92},{32,9... | collective-permute-start | bytes 393224 | tf_op jit(solution)/shard_map/ppermute | solution.py:470
  130.5 8.6 %collective-permute-start.23 = (bf16[2,64,512]{2,1,0:T(8,128)(2,1)S(1)}, bf16[2,64,512]{2,1,0:T(8,128)(2,1)S(1)}, u32[]{:S(2)}, u32[]{:S(2)}) collective-permute-start(bf16[2,64,512]{2,1,0:T(8,128)(2,1)S(1)} %get-tuple-element.66), channel_id=1, source_target_pairs={{0,96},{4,100},{8,104},{12,108},{16,112},{20,116},{24,120},{28,124... | collective-permute-start | bytes 393224 | tf_op jit(solution)/shard_map/ppermute | solution.py:470
  139.8 8.3 %collective-permute-start.24 = (bf16[64,512]{1,0:T(8,128)(2,1)S(1)}, bf16[64,512]{1,0:T(8,128)(2,1)S(1)}, u32[]{:S(2)}, u32[]{:S(2)}) collective-permute-start(bf16[64,512]{1,0:T(8,128)(2,1)S(1)} %get-tuple-element.68), channel_id=1, source_target_pairs={{0,128},{4,132},{8,136},{12,140},{16,144},{20,148},{24,152},{28,15... | collective-permute-start | bytes 196616 | tf_op jit(solution)/shard_map/ppermute | solution.py:472

commit v6 on v5

--- a/solution.py
+++ b/solution.py
@@ -344,8 +344,8 @@
 
 
 def weight_body(where_ref, *refs):
-    values, features = refs[:4], refs[4:12]
-    kept_ref, sent_ref, aligned, pieces = refs[12:]
+    values, features, far_rest = refs[:4], refs[4:12], refs[12]
+    kept_ref, sent_ref, aligned, pieces = refs[13:]
     x, ring, place = where_ref[0], where_ref[1], where_ref[2]
     for apart, value_ref in enumerate(values):
         column = (x - apart + 4) % 4
@@ -362,7 +362,11 @@
         for half in range(2):
             source = (ring - apart - 4 * half + 8) % 8
             rows = features[apart + 4 * half]
-            rows = jnp.concatenate([rows[back] for back in range(4)], axis=1)
+            if apart + 4 * half == 4:
+                rows = [rows[0], rows[1], far_rest[0], far_rest[1]]
+            else:
+                rows = [rows[back] for back in range(4)]
+            rows = jnp.concatenate(rows, axis=1)
             term = lax.dot_general(
                 rows,
                 aligned[source // 4].reshape(512, 512),
@@ -388,7 +392,7 @@
         weight_body,
         out_shape=(jax.ShapeDtypeStruct((4, 2, 64, 512), jnp.bfloat16),) * 2,
         in_specs=[pl.BlockSpec(memory_space=pltpu.SMEM)]
-        + [pl.BlockSpec(memory_space=pltpu.VMEM)] * 12,
+        + [pl.BlockSpec(memory_space=pltpu.VMEM)] * 13,
         scratch_shapes=[
             pltpu.VMEM((2, 32, CHANNELS, 512), jnp.bfloat16),
             pltpu.VMEM((16, 64, 512), jnp.bfloat16),
@@ -459,12 +463,13 @@
     up2, down2 = ring_step(up, 1), ring_step(down, -1)
     back_grad, rest, *pieces = convolve(where, signals, tables)
     pieces = pieces[:1] + [lax.ppermute(pieces[n], "seq", across(n)) for n in range(1, 8)]
-    up3, down3, far = ring_step(up2, 1), ring_step(down2, -1), ring_step(up2, 2)
+    up3, down3 = ring_step(up2, 1), ring_step(down2, -1)
+    far, far_rest = ring_step(up2[:2], 2), ring_step(down2[2:], -2)
     results = complete(back_grad, rest, tables)
     value = bundle(pieces)
     values = [value] + [lax.ppermute(value, "seq", along_x(n)) for n in range(1, 4)]
     results = exchange(results)
-    kept, sent = weight_parts(where, values, (own, up, up2, up3, far, down3, down2, down))
+    kept, sent = weight_parts(where, values, (own, up, up2, up3, far, down3, down2, down, far_rest))
     received = lax.ppermute(sent, "seq", across(1))
     parts = join_cores(kept, received)
     parts = [parts[0]] + [lax.ppermute(parts[n], "seq", across(2 * n)) for n in range(1, 4)]

time: 151 us -> 153 us (1.013)
  the two profiles are of different devices: /device:TPU:32 before, /device:TPU:2 now
where the time goes in v6:
time: 153 us
  starting transfers between devices  70.8 us (46%)
  waiting for transfers between devices  62.6 us (41%)
  Pallas kernels  17.4 us (11%)
    all_to_all x2, starting transfers between devices, exchange(): return lax.all_to_all(array, 'seq', split_axis=0, concat_axis=0, tiled=True)  27.2 us
    ppermute x8, waiting for transfers between devices, ring_step(): return lax.ppermute(array, ('seq', 'chan'), along_z(shift))  25.2 us
    ppermute x8, starting transfers between devices, ring_step(): return lax.ppermute(array, ('seq', 'chan'), along_z(shift))  18.1 us
    ppermute x7, starting transfers between devices, shards(): lax.ppermute(pieces[n], 'seq', across(n))  9.66 us
    ppermute x3, waiting for transfers between devices, shards(): lax.ppermute(value, 'seq', along_x(n))  9.09 us
    ppermute x3, waiting for transfers between devices, shards(): own = [lax.ppermute(pieces[n], 'seq', along_x(n)) for n in range(1, 4)]  7.79 us
    ppermute x1, waiting for transfers between devices, shards(): received = lax.ppermute(sent, 'seq', opposite()).astype(jnp.float32)  7.54 us
    ppermute x3, waiting for transfers between devices, shards(): lax.ppermute(parts[n], 'seq', across(2 * n))  7.49 us
  transfers between devices with their start and end apart: 28, of which 16 were waited for; matrix products, arithmetic and copies ran while one was open for 1% of the time, Pallas kernels for 8%

profile of v6, /device:TPU:2, one launch (start us, length us, event | category | flops | bytes accessed | tf_op | source)
XLA Modules:
  0.0 152.7 jit_solution(3696896060669955792)
XLA Ops:
  0.6 3.7 %gather_signals.1 = bf16[64,64,128]{2,1,0:T(8,128)(2,1)} custom-call(bf16[128,1024]{1,0:T(8,128)(2,1)} %key_ref.3, bf16[128,1024]{1,0:T(8,128)(2,1)} %value_ref.3, bf16[128,1024]{1,0:T(8,128)(2,1)} %grad_ref.3, bf16[128,1024]{1,0:T(8,128)(2,1)} %query_ref.1, bf16[128,1024]{1,0:T(8,128)(2,1)} %taps_ref.1), custom_call_target="tpu_custom_call" | custom-call | tf_op jit(solution)/shard_map/gather_signals/pallas_call | solution.py:100
  4.4 14.8 %all-to-all-start = ((bf16[64,64,128]{2,1,0:T(8,128)(2,1)}), bf16[64,64,128]{2,1,0:T(8,128)(2,1)S(1)}, u32[]{:S(2)}, u32[]{:S(2)}) async-start(bf16[64,64,128]{2,1,0:T(8,128)(2,1)} %gather_signals.1), calls=%async_computation | async-start | bytes 2097152 | tf_op jit(solution)/shard_map/all_to_all | solution.py:444
  19.3 0.7 split_features.1
  20.0 0.5 collective-permute-start.12
  20.6 2.5 %collective-permute-start.11 = (bf16[256,128]{1,0:T(8,128)(2,1)S(1)}, bf16[256,128]{1,0:T(8,128)(2,1)S(1)}, u32[]{:S(2)}, u32[]{:S(2)}) collective-permute-start(bf16[256,128]{1,0:T(8,128)(2,1)S(1)} %get-tuple-element.59), channel_id=1, source_target_pairs={{0,16},{4,20},{8,24},{12,28},{16,0},{20,4},{24,8},{28,12},{32,48},... | collective-permute-start | bytes 196616 | tf_op jit(solution)/shard_map/ppermute | solution.py:457
  23.0 1.8 %collective-permute-start.10 = (bf16[256,128]{1,0:T(8,128)(2,1)S(1)}, bf16[256,128]{1,0:T(8,128)(2,1)S(1)}, u32[]{:S(2)}, u32[]{:S(2)}) collective-permute-start(bf16[256,128]{1,0:T(8,128)(2,1)S(1)} %get-tuple-element.58), channel_id=1, source_target_pairs={{0,8},{4,12},{8,16},{12,20},{16,24},{20,28},{24,0},{28,4},{32,40},... | collective-permute-start | bytes 196616 | tf_op jit(solution)/shard_map/ppermute | solution.py:457
  24.8 5.1 %collective-permute-done.12 = bf16[256,128]{1,0:T(8,128)(2,1)S(1)} collective-permute-done((bf16[256,128]{1,0:T(8,128)(2,1)S(1)}, bf16[256,128]{1,0:T(8,128)(2,1)S(1)}, u32[]{:S(2)}, u32[]{:S(2)}) %collective-permute-start.12) | collective-permute-done | bytes 65568 | tf_op jit(solution)/shard_map/ppermute | solution.py:457
  29.9 2.7 %collective-permute-done.11 = bf16[256,128]{1,0:T(8,128)(2,1)S(1)} collective-permute-done((bf16[256,128]{1,0:T(8,128)(2,1)S(1)}, bf16[256,128]{1,0:T(8,128)(2,1)S(1)}, u32[]{:S(2)}, u32[]{:S(2)}) %collective-permute-start.11) | collective-permute-done | bytes 65568 | tf_op jit(solution)/shard_map/ppermute | solution.py:457
  32.7 7.7 %collective-permute-start.17 = (bf16[4,256,128]{2,1,0:T(8,128)(2,1)S(1)}, bf16[4,256,128]{2,1,0:T(8,128)(2,1)S(1)}, u32[]{:S(2)}, u32[]{:S(2)}) collective-permute-start(bf16[4,256,128]{2,1,0:T(8,128)(2,1)S(1)} %pad_maximum_fusion.refs_4_), channel_id=1, source_target_pairs={{0,131},{1,0},{2,1},{3,2},{4,135},{5,4},{6,5},{7,6},{8,139},{9,8},... | collective-permute-start | bytes 786440 | tf_op jit(solution)/shard_map/ppermute | solution.py:448
  40.5 1.7 %all-to-all-done.signals_ref = bf16[64,64,128]{2,1,0:T(8,128)(2,1)S(1)} async-done(((bf16[64,64,128]{2,1,0:T(8,128)(2,1)}), bf16[64,64,128]{2,1,0:T(8,128)(2,1)S(1)}, u32[]{:S(2)}, u32[]{:S(2)}) %all-to-all-start) | async-done | bytes 1048608 | tf_op jit(solution)/shard_map/all_to_all | solution.py:444
  42.3 5.4 %convolve.1 = (bf16[64,16,128]{2,1,0:T(8,128)(2,1)S(1)}, bf16[4,576,256]{2,1,0:T(8,128)(2,1)S(1)}, bf16[8,16,128]{2,1,0:T(8,128)(2,1)S(1)}, bf16[8,16,128]{2,1,0...) custom-call(s32[4]{0:T(128)S(1)} %pad_add_fusion.where_ref, ...), custom_call_target="tpu_custom_call" | custom-call | tf_op jit(solution)/shard_map/convolve/pallas_call | solution.py:261
  47.7 3.3 %complete.1 = bf16[64,48,128]{2,1,0:T(8,128)(2,1)} custom-call(bf16[64,16,128]{2,1,0:T(8,128)(2,1)S(1)} %get-tuple-element.43.back_grad_ref, bf16[4,576,256]{2,1,0:T(8,128)(2,1)S(1)} %get-tuple-element.44.rest_ref, f32[72,128]{1,0:T(8,128)S(1)} %get-tuple-element.38.cos_ref, f32[72,128]{1,0:T(8,128)S(1)} %get-tuple-element.39.sin_ref, ...), custom_call_target="tpu_custom_call" | custom-call | tf_op jit(solution)/shard_map/complete/pallas_call | solution.py:301
  51.0 12.4 %all-to-all-start.1 = ((bf16[64,48,128]{2,1,0:T(8,128)(2,1)}), bf16[64,48,128]{2,1,0:T(8,128)(2,1)S(1)}, u32[]{:S(2)}, u32[]{:S(2)}) async-start(bf16[64,48,128]{2,1,0:T(8,128)(2,1)} %complete.1), calls=%async_computation.1 | async-start | bytes 1572864 | tf_op jit(solution)/shard_map/all_to_all | solution.py:444
  63.4 3.1 %collective-permute-start.14 = (bf16[4,256,128]{2,1,0:T(8,128)(2,1)S(1)}, bf16[4,256,128]{2,1,0:T(8,128)(2,1)S(1)}, u32[]{:S(2)}, u32[]{:S(2)}) collective-permute-start(bf16[4,256,128]{2,1,0:T(8,128)(2,1)S(1)} %collective-permute-done.13.refs_5_), channel_id=1, source_target_pairs={{0,1},{1,2},{2,3},{3,128},{4,5},{5,6},{6,7},{7,132},{8,9},{9,10},{... | collective-permute-start | bytes 786440 | tf_op jit(solution)/shard_map/ppermute | solution.py:448
  66.6 1.4 collective-permute-start.18
  67.9 23.3 %collective-permute-done.14.refs_6_ = bf16[4,256,128]{2,1,0:T(8,128)(2,1)S(1)} collective-permute-done((bf16[4,256,128]{2,1,0:T(8,128)(2,1)S(1)}, bf16[4,256,128]{2,1,0:T(8,128)(2,1)S(1)}, u32[]{:S(2)}, u32[]{:S(2)}) %collective-permute-start.14) | collective-permute-done | bytes 262176 | tf_op jit(solution)/shard_map/ppermute | solution.py:448
  91.4 4.2 %collective-permute-start.20 = (bf16[2,256,128]{2,1,0:T(8,128)(2,1)S(1)}, bf16[2,256,128]{2,1,0:T(8,128)(2,1)S(1)}, u32[]{:S(2)}, u32[]{:S(2)}) collective-permute-start(bf16[2,256,128]{2,1,0:T(8,128)(2,1)S(1)} %slice.9), channel_id=1, source_target_pairs={{0,130},{1,131},{2,0},{3,1},{4,134},{5,135},{6,4},{7,5},{8,138},{9... | collective-permute-start | bytes 393224 | tf_op jit(solution)/shard_map/ppermute | solution.py:448
  95.6 1.5 collective-permute-start.1
  97.1 0.3 collective-permute-start.2
  97.5 3.1 %collective-permute-start.3 = (bf16[8,16,128]{2,1,0:T(8,128)(2,1)S(1)}, bf16[8,16,128]{2,1,0:T(8,128)(2,1)S(1)}, u32[]{:S(2)}, u32[]{:S(2)}) collective-permute-start(bf16[8,16,128]{2,1,0:T(8,128)(2,1)S(1)} %get-tuple-element.53), channel_id=1, source_target_pairs={{0,64},{4,68},{8,72},{12,76},{16,80},{20,84},{24,88},{28,92},{32,9... | collective-permute-start | bytes 98312 | tf_op jit(solution)/shard_map/ppermute | solution.py:465
  100.5 1.3 collective-permute-start.4
  101.9 1.6 %collective-permute-start.5 = (bf16[8,16,128]{2,1,0:T(8,128)(2,1)S(1)}, bf16[8,16,128]{2,1,0:T(8,128)(2,1)S(1)}, u32[]{:S(2)}, u32[]{:S(2)}) collective-permute-start(bf16[8,16,128]{2,1,0:T(8,128)(2,1)S(1)} %get-tuple-element.55), channel_id=1, source_target_pairs={{0,96},{4,100},{8,104},{12,108},{16,112},{20,116},{24,120},{28,124... | collective-permute-start | bytes 98312 | tf_op jit(solution)/shard_map/ppermute | solution.py:465
  103.5 1.8 %collective-permute-start.6 = (bf16[8,16,128]{2,1,0:T(8,128)(2,1)S(1)}, bf16[8,16,128]{2,1,0:T(8,128)(2,1)S(1)}, u32[]{:S(2)}, u32[]{:S(2)}) collective-permute-start(bf16[8,16,128]{2,1,0:T(8,128)(2,1)S(1)} %get-tuple-element.56), channel_id=1, source_target_pairs={{0,100},{4,96},{8,108},{12,104},{16,116},{20,112},{24,124},{28,120... | collective-permute-start | bytes 98312 | tf_op jit(solution)/shard_map/ppermute | solution.py:465
  105.3 0.3 collective-permute-done.4.refs_5_
  105.6 1.7 %collective-permute-done.5.refs_6_ = bf16[8,16,128]{2,1,0:T(8,128)(2,1)S(1)} collective-permute-done((bf16[8,16,128]{2,1,0:T(8,128)(2,1)S(1)}, bf16[8,16,128]{2,1,0:T(8,128)(2,1)S(1)}, u32[]{:S(2)}, u32[]{:S(2)}) %collective-permute-start.5) | collective-permute-done | bytes 32800 | tf_op jit(solution)/shard_map/ppermute | solution.py:465
  107.2 1.6 %collective-permute-start.19 = (bf16[4,256,128]{2,1,0:T(8,128)(2,1)S(1)}, bf16[4,256,128]{2,1,0:T(8,128)(2,1)S(1)}, u32[]{:S(2)}, u32[]{:S(2)}) collective-permute-start(bf16[4,256,128]{2,1,0:T(8,128)(2,1)S(1)} %collective-permute-done.18.refs_10_), channel_id=1, source_target_pairs={{0,131},{1,0},{2,1},{3,2},{4,135},{5,4},{6,5},{7,6},{8,139},{9,8},... | collective-permute-start | bytes 786440 | tf_op jit(solution)/shard_map/ppermute | solution.py:448
  108.8 1.6 %collective-permute-start.7 = (bf16[8,8,16,128]{3,2,1,0:T(8,128)(2,1)S(1)}, bf16[8,8,16,128]{3,2,1,0:T(8,128)(2,1)S(1)}, u32[]{:S(2)}, u32[]{:S(2)}) collective-permute-start(bf16[8,8,16,128]{3,2,1,0:T(8,128)(2,1)S(1)} %bundle.1.refs_0_), channel_id=1, source_target_pairs={{0,8},{4,12},{8,16},{12,20},{16,24},{20,28},{24,0},{28,4},{32,40},... | collective-permute-start | bytes 786440 | tf_op jit(solution)/shard_map/ppermute | solution.py:470
  110.4 1.1 collective-permute-start.8
  111.5 2.1 %collective-permute-start.9 = (bf16[8,8,16,128]{3,2,1,0:T(8,128)(2,1)S(1)}, bf16[8,8,16,128]{3,2,1,0:T(8,128)(2,1)S(1)}, u32[]{:S(2)}, u32[]{:S(2)}) collective-permute-start(bf16[8,8,16,128]{3,2,1,0:T(8,128)(2,1)S(1)} %bundle.1.refs_0_), channel_id=1, source_target_pairs={{0,24},{4,28},{8,0},{12,4},{16,8},{20,12},{24,16},{28,20},{32,56},... | collective-permute-start | bytes 786440 | tf_op jit(solution)/shard_map/ppermute | solution.py:470
  113.6 1.6 %collective-permute-done.15.refs_7_ = bf16[4,256,128]{2,1,0:T(8,128)(2,1)S(1)} collective-permute-done((bf16[4,256,128]{2,1,0:T(8,128)(2,1)S(1)}, bf16[4,256,128]{2,1,0:T(8,128)(2,1)S(1)}, u32[]{:S(2)}, u32[]{:S(2)}) %collective-permute-start.15) | collective-permute-done | bytes 262176 | tf_op jit(solution)/shard_map/ppermute | solution.py:448
  115.3 0.2 collective-permute-done.19.refs_9_
  115.4 2.6 %collective-permute-done.7.refs_1_ = bf16[8,8,16,128]{3,2,1,0:T(8,128)(2,1)S(1)} collective-permute-done((bf16[8,8,16,128]{3,2,1,0:T(8,128)(2,1)S(1)}, bf16[8,8,16,128]{3,2,1,0:T(8,128)(2,1)S(1)}, u32[]{:S(2)}, u32[]{:S(2)}) %collective-permute-start.7) | collective-permute-done | bytes 262176 | tf_op jit(solution)/shard_map/ppermute | solution.py:470
  118.1 3.0 %collective-permute-done.8.refs_2_ = bf16[8,8,16,128]{3,2,1,0:T(8,128)(2,1)S(1)} collective-permute-done((bf16[8,8,16,128]{3,2,1,0:T(8,128)(2,1)S(1)}, bf16[8,8,16,128]{3,2,1,0:T(8,128)(2,1)S(1)}, u32[]{:S(2)}, u32[]{:S(2)}) %collective-permute-start.8) | collective-permute-done | bytes 262176 | tf_op jit(solution)/shard_map/ppermute | solution.py:470
  121.1 3.5 %collective-permute-done.9.refs_3_ = bf16[8,8,16,128]{3,2,1,0:T(8,128)(2,1)S(1)} collective-permute-done((bf16[8,8,16,128]{3,2,1,0:T(8,128)(2,1)S(1)}, bf16[8,8,16,128]{3,2,1,0:T(8,128)(2,1)S(1)}, u32[]{:S(2)}, u32[]{:S(2)}) %collective-permute-start.9) | collective-permute-done | bytes 262176 | tf_op jit(solution)/shard_map/ppermute | solution.py:470
  124.5 2.1 %weight_parts.1 = (bf16[4,2,64,512]{3,2,1,0:T(8,128)(2,1)S(1)}, bf16[4,2,64,512]{3,2,1,0:T(8,128)(2,1)S(1)}) custom-call(s32[4]{0:T(128)S(1)} %pad_add_fusion.where_ref, bf16[8,8,16,128]{3,2,1,0:T(8,128)(2,1)S(1)} %bundle.1.refs_0_, bf16[8,8,16,128]{3,2,1,0:T(8,128)(2,1)S(1)} %collective-permute-done.7.refs_1_, ...), custom_call_target="tpu_custom_call" | custom-call | tf_op jit(solution)/shard_map/weight_parts/pallas_call | solution.py:391
  126.8 1.9 %collective-permute-done.21.received_ref = bf16[4,2,64,512]{3,2,1,0:T(8,128)(2,1)S(1)} collective-permute-done((bf16[4,2,64,512]{3,2,1,0:T(8,128)(2,1)S(1)}, bf16[4,2,64,512]{3,2,1,0:T(8,128)(2,1)S(1)}, u32[]{:S(2)}, u32[]{:S(2)}) %collective-permute-start.21) | collective-permute-done | bytes 524320 | tf_op jit(solution)/shard_map/ppermute | solution.py:473
  128.7 0.1 join_cores.1
  128.8 0.8 collective-permute-start.22
  129.7 2.8 %collective-permute-start.23 = (bf16[2,64,512]{2,1,0:T(8,128)(2,1)S(1)}, bf16[2,64,512]{2,1,0:T(8,128)(2,1)S(1)}, u32[]{:S(2)}, u32[]{:S(2)}) collective-permute-start(bf16[2,64,512]{2,1,0:T(8,128)(2,1)S(1)} %get-tuple-element.65), channel_id=1, source_target_pairs={{0,64},{4,68},{8,72},{12,76},{16,80},{20,84},{24,88},{28,92},{32,9... | collective-permute-start | bytes 393224 | tf_op jit(solution)/shard_map/ppermute | solution.py:475
  132.4 1.2 collective-permute-start.24
  133.6 1.7 %collective-permute-done.22.refs_1_ = bf16[2,64,512]{2,1,0:T(8,128)(2,1)S(1)} collective-permute-done((bf16[2,64,512]{2,1,0:T(8,128)(2,1)S(1)}, bf16[2,64,512]{2,1,0:T(8,128)(2,1)S(1)}, u32[]{:S(2)}, u32[]{:S(2)}) %collective-permute-start.22) | collective-permute-done | bytes 131104 | tf_op jit(solution)/shard_map/ppermute | solution.py:475
  135.3 3.6 %collective-permute-done.23.refs_2_ = bf16[2,64,512]{2,1,0:T(8,128)(2,1)S(1)} collective-permute-done((bf16[2,64,512]{2,1,0:T(8,128)(2,1)S(1)}, bf16[2,64,512]{2,1,0:T(8,128)(2,1)S(1)}, u32[]{:S(2)}, u32[]{:S(2)}) %collective-permute-start.23) | collective-permute-done | bytes 131104 | tf_op jit(solution)/shard_map/ppermute | solution.py:475
  138.9 2.2 %collective-permute-done.24.refs_3_ = bf16[2,64,512]{2,1,0:T(8,128)(2,1)S(1)} collective-permute-done((bf16[2,64,512]{2,1,0:T(8,128)(2,1)S(1)}, bf16[2,64,512]{2,1,0:T(8,128)(2,1)S(1)}, u32[]{:S(2)}, u32[]{:S(2)}) %collective-permute-start.24) | collective-permute-done | bytes 131104 | tf_op jit(solution)/shard_map/ppermute | solution.py:475
  141.1 0.6 weight_total.1
  141.7 1.3 collective-permute-start.25
  143.0 7.5 %collective-permute-done.25 = bf16[64,512]{1,0:T(8,128)(2,1)S(1)} collective-permute-done((bf16[64,512]{1,0:T(8,128)(2,1)S(1)}, bf16[64,512]{1,0:T(8,128)(2,1)S(1)}, u32[]{:S(2)}, u32[]{:S(2)}) %collective-permute-start.25) | collective-permute-done | bytes 65568 | tf_op jit(solution)/shard_map/ppermute | solution.py:477
  150.6 0.7 maximum_select_fusion
  151.4 1.3 finish.1
  (44 shorter events, 0.6 us)
Async XLA Ops:
  4.3 15.0 %copy-start.3 = (bf16[128,1024]{1,0:T(8,128)(2,1)S(1)}, bf16[128,1024]{1,0:T(8,128)(2,1)}, u32[]{:S(2)}) copy-start(bf16[128,1024]{1,0:T(8,128)(2,1)} %input_ref.1) | copy-start | bytes 786436
  4.3 36.1 %copy-start.4 = (bf16[512,256]{1,0:T(8,128)(2,1)S(1)}, bf16[512,256]{1,0:T(8,128)(2,1)}, u32[]{:S(2)}) copy-start(bf16[512,256]{1,0:T(8,128)(2,1)} %constant.84.clone.refs_3_) | copy-start | bytes 786436
  4.3 36.1 %copy-start.5 = (bf16[512,256]{1,0:T(8,128)(2,1)S(1)}, bf16[512,256]{1,0:T(8,128)(2,1)}, u32[]{:S(2)}) copy-start(bf16[512,256]{1,0:T(8,128)(2,1)} %constant.85.clone.refs_4_) | copy-start | bytes 786436
  4.3 36.1 %copy-start.6 = (bf16[128,144]{1,0:T(8,128)(2,1)S(1)}, bf16[128,144]{1,0:T(8,128)(2,1)}, u32[]{:S(2)}) copy-start(bf16[128,144]{1,0:T(8,128)(2,1)} %constant.86.clone.refs_5_) | copy-start | bytes 110596
  4.3 36.1 %copy-start.7 = (bf16[144,128]{1,0:T(8,128)(2,1)S(1)}, bf16[144,128]{1,0:T(8,128)(2,1)}, u32[]{:S(2)}) copy-start(bf16[144,128]{1,0:T(8,128)(2,1)} %constant.81.clone.refs_0_) | copy-start | bytes 110596
  4.4 36.1 %copy-start.8 = (f32[72,128]{1,0:T(8,128)S(1)}, f32[72,128]{1,0:T(8,128)}, u32[]{:S(2)}) copy-start(f32[72,128]{1,0:T(8,128)} %constant.82.clone.refs_1_) | copy-start | bytes 110596
  4.4 36.1 %copy-start.9 = (f32[72,128]{1,0:T(8,128)S(1)}, f32[72,128]{1,0:T(8,128)}, u32[]{:S(2)}) copy-start(f32[72,128]{1,0:T(8,128)} %constant.83.clone.refs_2_) | copy-start | bytes 110596
  4.4 37.9 %all-to-all-start = ((bf16[64,64,128]{2,1,0:T(8,128)(2,1)}), bf16[64,64,128]{2,1,0:T(8,128)(2,1)S(1)}, u32[]{:S(2)}, u32[]{:S(2)}) async-start(bf16[64,64,128]{2,1,0:T(8,128)(2,1)} %gather_signals.1), calls=%async_computation | async-start | bytes 2097152 | tf_op jit(solution)/shard_map/all_to_all | solution.py:444
  20.0 9.9 %collective-permute-start.12 = (bf16[256,128]{1,0:T(8,128)(2,1)S(1)}, bf16[256,128]{1,0:T(8,128)(2,1)S(1)}, u32[]{:S(2)}, u32[]{:S(2)}) collective-permute-start(bf16[256,128]{1,0:T(8,128)(2,1)S(1)} %get-tuple-element.60), channel_id=1, source_target_pairs={{0,24},{4,28},{8,0},{12,4},{16,8},{20,12},{24,16},{28,20},{32,56},... | collective-permute-start | bytes 196616 | tf_op jit(solution)/shard_map/ppermute | solution.py:457
  20.6 12.0 %collective-permute-start.11 = (bf16[256,128]{1,0:T(8,128)(2,1)S(1)}, bf16[256,128]{1,0:T(8,128)(2,1)S(1)}, u32[]{:S(2)}, u32[]{:S(2)}) collective-permute-start(bf16[256,128]{1,0:T(8,128)(2,1)S(1)} %get-tuple-element.59), channel_id=1, source_target_pairs={{0,16},{4,20},{8,24},{12,28},{16,0},{20,4},{24,8},{28,12},{32,48},... | collective-permute-start | bytes 196616 | tf_op jit(solution)/shard_map/ppermute | solution.py:457
  23.0 9.6 %collective-permute-start.10 = (bf16[256,128]{1,0:T(8,128)(2,1)S(1)}, bf16[256,128]{1,0:T(8,128)(2,1)S(1)}, u32[]{:S(2)}, u32[]{:S(2)}) collective-permute-start(bf16[256,128]{1,0:T(8,128)(2,1)S(1)} %get-tuple-element.58), channel_id=1, source_target_pairs={{0,8},{4,12},{8,16},{12,20},{16,24},{20,28},{24,0},{28,4},{32,40},... | collective-permute-start | bytes 196616 | tf_op jit(solution)/shard_map/ppermute | solution.py:457
  32.6 30.8 %collective-permute-start.13 = (bf16[4,256,128]{2,1,0:T(8,128)(2,1)S(1)}, bf16[4,256,128]{2,1,0:T(8,128)(2,1)S(1)}, u32[]{:S(2)}, u32[]{:S(2)}) collective-permute-start(bf16[4,256,128]{2,1,0:T(8,128)(2,1)S(1)} %pad_maximum_fusion.refs_4_), channel_id=1, source_target_pairs={{0,1},{1,2},{2,3},{3,128},{4,5},{5,6},{6,7},{7,132},{8,9},{9,10},{... | collective-permute-start | bytes 786440 | tf_op jit(solution)/shard_map/ppermute | solution.py:448
  32.7 33.8 %collective-permute-start.17 = (bf16[4,256,128]{2,1,0:T(8,128)(2,1)S(1)}, bf16[4,256,128]{2,1,0:T(8,128)(2,1)S(1)}, u32[]{:S(2)}, u32[]{:S(2)}) collective-permute-start(bf16[4,256,128]{2,1,0:T(8,128)(2,1)S(1)} %pad_maximum_fusion.refs_4_), channel_id=1, source_target_pairs={{0,131},{1,0},{2,1},{3,2},{4,135},{5,4},{6,5},{7,6},{8,139},{9,8},... | collective-permute-start | bytes 786440 | tf_op jit(solution)/shard_map/ppermute | solution.py:448
  51.0 100.3 %all-to-all-start.1 = ((bf16[64,48,128]{2,1,0:T(8,128)(2,1)}), bf16[64,48,128]{2,1,0:T(8,128)(2,1)S(1)}, u32[]{:S(2)}, u32[]{:S(2)}) async-start(bf16[64,48,128]{2,1,0:T(8,128)(2,1)} %complete.1), calls=%async_computation.1 | async-start | bytes 1572864 | tf_op jit(solution)/shard_map/all_to_all | solution.py:444
  63.4 27.8 %collective-permute-start.14 = (bf16[4,256,128]{2,1,0:T(8,128)(2,1)S(1)}, bf16[4,256,128]{2,1,0:T(8,128)(2,1)S(1)}, u32[]{:S(2)}, u32[]{:S(2)}) collective-permute-start(bf16[4,256,128]{2,1,0:T(8,128)(2,1)S(1)} %collective-permute-done.13.refs_5_), channel_id=1, source_target_pairs={{0,1},{1,2},{2,3},{3,128},{4,5},{5,6},{6,7},{7,132},{8,9},{9,10},{... | collective-permute-start | bytes 786440 | tf_op jit(solution)/shard_map/ppermute | solution.py:448
  66.6 24.8 %collective-permute-start.18 = (bf16[4,256,128]{2,1,0:T(8,128)(2,1)S(1)}, bf16[4,256,128]{2,1,0:T(8,128)(2,1)S(1)}, u32[]{:S(2)}, u32[]{:S(2)}) collective-permute-start(bf16[4,256,128]{2,1,0:T(8,128)(2,1)S(1)} %collective-permute-done.17.refs_11_), channel_id=1, source_target_pairs={{0,131},{1,0},{2,1},{3,2},{4,135},{5,4},{6,5},{7,6},{8,139},{9,8},... | collective-permute-start | bytes 786440 | tf_op jit(solution)/shard_map/ppermute | solution.py:448
  91.3 19.1 %collective-permute-start.16 = (bf16[2,256,128]{2,1,0:T(8,128)(2,1)S(1)}, bf16[2,256,128]{2,1,0:T(8,128)(2,1)S(1)}, u32[]{:S(2)}, u32[]{:S(2)}) collective-permute-start(bf16[2,256,128]{2,1,0:T(8,128)(2,1)S(1)} %slice.8), channel_id=1, source_target_pairs={{0,2},{1,3},{2,128},{3,129},{4,6},{5,7},{6,132},{7,133},{8,10},{9,... | collective-permute-start | bytes 393224 | tf_op jit(solution)/shard_map/ppermute | solution.py:448
  91.4 20.1 %collective-permute-start.20 = (bf16[2,256,128]{2,1,0:T(8,128)(2,1)S(1)}, bf16[2,256,128]{2,1,0:T(8,128)(2,1)S(1)}, u32[]{:S(2)}, u32[]{:S(2)}) collective-permute-start(bf16[2,256,128]{2,1,0:T(8,128)(2,1)S(1)} %slice.9), channel_id=1, source_target_pairs={{0,130},{1,131},{2,0},{3,1},{4,134},{5,135},{6,4},{7,5},{8,138},{9... | collective-permute-start | bytes 393224 | tf_op jit(solution)/shard_map/ppermute | solution.py:448
  95.6 1.9 %collective-permute-start = (bf16[8,16,128]{2,1,0:T(8,128)(2,1)S(1)}, bf16[8,16,128]{2,1,0:T(8,128)(2,1)S(1)}, u32[]{:S(2)}, u32[]{:S(2)}) collective-permute-start(bf16[8,16,128]{2,1,0:T(8,128)(2,1)S(1)} %get-tuple-element.50), channel_id=1, source_target_pairs={{0,4},{4,0},{8,12},{12,8},{16,20},{20,16},{24,28},{28,24},{32,36},... | collective-permute-start | bytes 98312 | tf_op jit(solution)/shard_map/ppermute | solution.py:465
  95.6 4.9 %collective-permute-start.1 = (bf16[8,16,128]{2,1,0:T(8,128)(2,1)S(1)}, bf16[8,16,128]{2,1,0:T(8,128)(2,1)S(1)}, u32[]{:S(2)}, u32[]{:S(2)}) collective-permute-start(bf16[8,16,128]{2,1,0:T(8,128)(2,1)S(1)} %get-tuple-element.51), channel_id=1, source_target_pairs={{0,32},{4,36},{8,40},{12,44},{16,48},{20,52},{24,56},{28,60},{32,0... | collective-permute-start | bytes 98312 | tf_op jit(solution)/shard_map/ppermute | solution.py:465
  97.1 4.7 %collective-permute-start.2 = (bf16[8,16,128]{2,1,0:T(8,128)(2,1)S(1)}, bf16[8,16,128]{2,1,0:T(8,128)(2,1)S(1)}, u32[]{:S(2)}, u32[]{:S(2)}) collective-permute-start(bf16[8,16,128]{2,1,0:T(8,128)(2,1)S(1)} %get-tuple-element.52), channel_id=1, source_target_pairs={{0,36},{4,32},{8,44},{12,40},{16,52},{20,48},{24,60},{28,56},{32,4... | collective-permute-start | bytes 98312 | tf_op jit(solution)/shard_map/ppermute | solution.py:465
  97.5 6.0 %collective-permute-start.3 = (bf16[8,16,128]{2,1,0:T(8,128)(2,1)S(1)}, bf16[8,16,128]{2,1,0:T(8,128)(2,1)S(1)}, u32[]{:S(2)}, u32[]{:S(2)}) collective-permute-start(bf16[8,16,128]{2,1,0:T(8,128)(2,1)S(1)} %get-tuple-element.53), channel_id=1, source_target_pairs={{0,64},{4,68},{8,72},{12,76},{16,80},{20,84},{24,88},{28,92},{32,9... | collective-permute-start | bytes 98312 | tf_op jit(solution)/shard_map/ppermute | solution.py:465
  100.5 5.0 %collective-permute-start.4 = (bf16[8,16,128]{2,1,0:T(8,128)(2,1)S(1)}, bf16[8,16,128]{2,1,0:T(8,128)(2,1)S(1)}, u32[]{:S(2)}, u32[]{:S(2)}) collective-permute-start(bf16[8,16,128]{2,1,0:T(8,128)(2,1)S(1)} %get-tuple-element.54), channel_id=1, source_target_pairs={{0,68},{4,64},{8,76},{12,72},{16,84},{20,80},{24,92},{28,88},{32,1... | collective-permute-start | bytes 98312 | tf_op jit(solution)/shard_map/ppermute | solution.py:465
  101.9 5.4 %collective-permute-start.5 = (bf16[8,16,128]{2,1,0:T(8,128)(2,1)S(1)}, bf16[8,16,128]{2,1,0:T(8,128)(2,1)S(1)}, u32[]{:S(2)}, u32[]{:S(2)}) collective-permute-start(bf16[8,16,128]{2,1,0:T(8,128)(2,1)S(1)} %get-tuple-element.55), channel_id=1, source_target_pairs={{0,96},{4,100},{8,104},{12,108},{16,112},{20,116},{24,120},{28,124... | collective-permute-start | bytes 98312 | tf_op jit(solution)/shard_map/ppermute | solution.py:465
  103.5 5.3 %collective-permute-start.6 = (bf16[8,16,128]{2,1,0:T(8,128)(2,1)S(1)}, bf16[8,16,128]{2,1,0:T(8,128)(2,1)S(1)}, u32[]{:S(2)}, u32[]{:S(2)}) collective-permute-start(bf16[8,16,128]{2,1,0:T(8,128)(2,1)S(1)} %get-tuple-element.56), channel_id=1, source_target_pairs={{0,100},{4,96},{8,108},{12,104},{16,116},{20,112},{24,124},{28,120... | collective-permute-start | bytes 98312 | tf_op jit(solution)/shard_map/ppermute | solution.py:465
  105.6 9.7 %collective-permute-start.15 = (bf16[4,256,128]{2,1,0:T(8,128)(2,1)S(1)}, bf16[4,256,128]{2,1,0:T(8,128)(2,1)S(1)}, u32[]{:S(2)}, u32[]{:S(2)}) collective-permute-start(bf16[4,256,128]{2,1,0:T(8,128)(2,1)S(1)} %collective-permute-done.14.refs_6_), channel_id=1, source_target_pairs={{0,1},{1,2},{2,3},{3,128},{4,5},{5,6},{6,7},{7,132},{8,9},{9,10},{... | collective-permute-start | bytes 786440 | tf_op jit(solution)/shard_map/ppermute | solution.py:448
  107.2 8.2 %collective-permute-start.19 = (bf16[4,256,128]{2,1,0:T(8,128)(2,1)S(1)}, bf16[4,256,128]{2,1,0:T(8,128)(2,1)S(1)}, u32[]{:S(2)}, u32[]{:S(2)}) collective-permute-start(bf16[4,256,128]{2,1,0:T(8,128)(2,1)S(1)} %collective-permute-done.18.refs_10_), channel_id=1, source_target_pairs={{0,131},{1,0},{2,1},{3,2},{4,135},{5,4},{6,5},{7,6},{8,139},{9,8},... | collective-permute-start | bytes 786440 | tf_op jit(solution)/shard_map/ppermute | solution.py:448
  108.8 9.3 %collective-permute-start.7 = (bf16[8,8,16,128]{3,2,1,0:T(8,128)(2,1)S(1)}, bf16[8,8,16,128]{3,2,1,0:T(8,128)(2,1)S(1)}, u32[]{:S(2)}, u32[]{:S(2)}) collective-permute-start(bf16[8,8,16,128]{3,2,1,0:T(8,128)(2,1)S(1)} %bundle.1.refs_0_), channel_id=1, source_target_pairs={{0,8},{4,12},{8,16},{12,20},{16,24},{20,28},{24,0},{28,4},{32,40},... | collective-permute-start | bytes 786440 | tf_op jit(solution)/shard_map/ppermute | solution.py:470
  110.4 10.7 %collective-permute-start.8 = (bf16[8,8,16,128]{3,2,1,0:T(8,128)(2,1)S(1)}, bf16[8,8,16,128]{3,2,1,0:T(8,128)(2,1)S(1)}, u32[]{:S(2)}, u32[]{:S(2)}) collective-permute-start(bf16[8,8,16,128]{3,2,1,0:T(8,128)(2,1)S(1)} %bundle.1.refs_0_), channel_id=1, source_target_pairs={{0,16},{4,20},{8,24},{12,28},{16,0},{20,4},{24,8},{28,12},{32,48},... | collective-permute-start | bytes 786440 | tf_op jit(solution)/shard_map/ppermute | solution.py:470
  111.5 13.0 %collective-permute-start.9 = (bf16[8,8,16,128]{3,2,1,0:T(8,128)(2,1)S(1)}, bf16[8,8,16,128]{3,2,1,0:T(8,128)(2,1)S(1)}, u32[]{:S(2)}, u32[]{:S(2)}) collective-permute-start(bf16[8,8,16,128]{3,2,1,0:T(8,128)(2,1)S(1)} %bundle.1.refs_0_), channel_id=1, source_target_pairs={{0,24},{4,28},{8,0},{12,4},{16,8},{20,12},{24,16},{28,20},{32,56},... | collective-permute-start | bytes 786440 | tf_op jit(solution)/shard_map/ppermute | solution.py:470
  126.6 24.7 %copy-start = (bf16[128,1024]{1,0:T(8,128)(2,1)S(1)}, bf16[128,1024]{1,0:T(8,128)(2,1)}, u32[]{:S(2)}) copy-start(bf16[128,1024]{1,0:T(8,128)(2,1)} %key_ref.3) | copy-start | bytes 786436
  126.7 24.7 %copy-start.1 = (bf16[128,1024]{1,0:T(8,128)(2,1)S(1)}, bf16[128,1024]{1,0:T(8,128)(2,1)}, u32[]{:S(2)}) copy-start(bf16[128,1024]{1,0:T(8,128)(2,1)} %value_ref.3) | copy-start | bytes 786436
  126.7 24.7 %copy-start.2 = (bf16[128,1024]{1,0:T(8,128)(2,1)S(1)}, bf16[128,1024]{1,0:T(8,128)(2,1)}, u32[]{:S(2)}) copy-start(bf16[128,1024]{1,0:T(8,128)(2,1)} %grad_ref.3) | copy-start | bytes 786436
  126.7 2.0 %collective-permute-start.21 = (bf16[4,2,64,512]{3,2,1,0:T(8,128)(2,1)S(1)}, bf16[4,2,64,512]{3,2,1,0:T(8,128)(2,1)S(1)}, u32[]{:S(2)}, u32[]{:S(2)}) collective-permute-start(bf16[4,2,64,512]{3,2,1,0:T(8,128)(2,1)S(1)} %get-tuple-element.62), channel_id=1, source_target_pairs={{0,4},{4,0},{8,12},{12,8},{16,20},{20,16},{24,28},{28,24},{32,36},... | collective-permute-start | bytes 1572872 | tf_op jit(solution)/shard_map/ppermute | solution.py:473
  128.8 6.5 %collective-permute-start.22 = (bf16[2,64,512]{2,1,0:T(8,128)(2,1)S(1)}, bf16[2,64,512]{2,1,0:T(8,128)(2,1)S(1)}, u32[]{:S(2)}, u32[]{:S(2)}) collective-permute-start(bf16[2,64,512]{2,1,0:T(8,128)(2,1)S(1)} %get-tuple-element.64), channel_id=1, source_target_pairs={{0,32},{4,36},{8,40},{12,44},{16,48},{20,52},{24,56},{28,60},{32,0... | collective-permute-start | bytes 393224 | tf_op jit(solution)/shard_map/ppermute | solution.py:475
  129.7 9.2 %collective-permute-start.23 = (bf16[2,64,512]{2,1,0:T(8,128)(2,1)S(1)}, bf16[2,64,512]{2,1,0:T(8,128)(2,1)S(1)}, u32[]{:S(2)}, u32[]{:S(2)}) collective-permute-start(bf16[2,64,512]{2,1,0:T(8,128)(2,1)S(1)} %get-tuple-element.65), channel_id=1, source_target_pairs={{0,64},{4,68},{8,72},{12,76},{16,80},{20,84},{24,88},{28,92},{32,9... | collective-permute-start | bytes 393224 | tf_op jit(solution)/shard_map/ppermute | solution.py:475
  132.4 8.6 %collective-permute-start.24 = (bf16[2,64,512]{2,1,0:T(8,128)(2,1)S(1)}, bf16[2,64,512]{2,1,0:T(8,128)(2,1)S(1)}, u32[]{:S(2)}, u32[]{:S(2)}) collective-permute-start(bf16[2,64,512]{2,1,0:T(8,128)(2,1)S(1)} %get-tuple-element.66), channel_id=1, source_target_pairs={{0,96},{4,100},{8,104},{12,108},{16,112},{20,116},{24,120},{28,124... | collective-permute-start | bytes 393224 | tf_op jit(solution)/shard_map/ppermute | solution.py:475
  141.7 8.9 %collective-permute-start.25 = (bf16[64,512]{1,0:T(8,128)(2,1)S(1)}, bf16[64,512]{1,0:T(8,128)(2,1)S(1)}, u32[]{:S(2)}, u32[]{:S(2)}) collective-permute-start(bf16[64,512]{1,0:T(8,128)(2,1)S(1)} %get-tuple-element.68), channel_id=1, source_target_pairs={{0,128},{4,132},{8,136},{12,140},{16,144},{20,148},{24,152},{28,15... | collective-permute-start | bytes 196616 | tf_op jit(solution)/shard_map/ppermute | solution.py:477

commit v7 on v6

--- a/solution.py
+++ b/solution.py
@@ -82,11 +82,10 @@
 
 
 WHOLE_GRANT = 60 << 20
-STEPS = 4
 
 
 def gather_body(key_ref, value_ref, grad_ref, query_ref, taps_ref, sent_ref):
-    for part in range(8 // STEPS):
+    for part in range(8):
         cols = pl.ds(part * 128, 128)
         key = key_ref[:, cols].astype(jnp.float32)
         mixed = key * value_ref[:, cols].astype(jnp.float32)
@@ -99,10 +98,7 @@
 def gather_signals(gate_key, value_proj, grad_out, gate_query, filter_taps):
     return pl.pallas_call(
         gather_body,
-        grid=(STEPS,),
         out_shape=jax.ShapeDtypeStruct((BLOCKS, SENT, ROWS), jnp.bfloat16),
-        in_specs=[pl.BlockSpec((ROWS, 1024 // STEPS), lambda i: (0, i))] * 5,
-        out_specs=pl.BlockSpec((BLOCKS // STEPS, SENT, ROWS), lambda i: (i, 0, 0)),
         name="gather_signals",
         compiler_params=pltpu.CompilerParams(vmem_limit_bytes=WHOLE_GRANT),
     )(gate_key, value_proj, grad_out, gate_query, filter_taps)

time: 153 us -> 152 us (level)
  no operation moved by 1% of the time
where the time goes in v7:
time: 152 us
  starting transfers between devices  70.8 us (47%)
  waiting for transfers between devices  62.6 us (41%)
  Pallas kernels  16.4 us (11%)
    all_to_all x2, starting transfers between devices, exchange(): return lax.all_to_all(array, 'seq', split_axis=0, concat_axis=0, tiled=True)  27.2 us
    ppermute x8, waiting for transfers between devices, ring_step(): return lax.ppermute(array, ('seq', 'chan'), along_z(shift))  25.2 us
    ppermute x8, starting transfers between devices, ring_step(): return lax.ppermute(array, ('seq', 'chan'), along_z(shift))  18.1 us
    ppermute x7, starting transfers between devices, shards(): lax.ppermute(pieces[n], 'seq', across(n))  9.66 us
    ppermute x3, waiting for transfers between devices, shards(): lax.ppermute(value, 'seq', along_x(n))  9.09 us
    ppermute x3, waiting for transfers between devices, shards(): own = [lax.ppermute(pieces[n], 'seq', along_x(n)) for n in range(1, 4)]  7.79 us
    ppermute x1, waiting for transfers between devices, shards(): received = lax.ppermute(sent, 'seq', opposite()).astype(jnp.float32)  7.55 us
    ppermute x3, waiting for transfers between devices, shards(): lax.ppermute(parts[n], 'seq', across(2 * n))  7.49 us
  transfers between devices with their start and end apart: 28, of which 16 were waited for; matrix products, arithmetic and copies ran while one was open for 1% of the time, Pallas kernels for 8%

profile of v7, /device:TPU:2, one launch (start us, length us, event | category | flops | bytes accessed | tf_op | source)
XLA Modules:
  0.0 151.6 jit_solution(17025300247133740674)
XLA Ops:
  0.6 2.7 %gather_signals.1 = bf16[64,64,128]{2,1,0:T(8,128)(2,1)} custom-call(bf16[128,1024]{1,0:T(8,128)(2,1)} %key_ref.3, bf16[128,1024]{1,0:T(8,128)(2,1)} %value_ref.3, bf16[128,1024]{1,0:T(8,128)(2,1)} %grad_ref.3, bf16[128,1024]{1,0:T(8,128)(2,1)} %query_ref.1, bf16[128,1024]{1,0:T(8,128)(2,1)} %taps_ref.1), custom_call_target="tpu_custom_call" | custom-call | tf_op jit(solution)/shard_map/gather_signals/pallas_call | solution.py:99
  3.3 14.8 %all-to-all-start = ((bf16[64,64,128]{2,1,0:T(8,128)(2,1)}), bf16[64,64,128]{2,1,0:T(8,128)(2,1)S(1)}, u32[]{:S(2)}, u32[]{:S(2)}) async-start(bf16[64,64,128]{2,1,0:T(8,128)(2,1)} %gather_signals.1), calls=%async_computation | async-start | bytes 2097152 | tf_op jit(solution)/shard_map/all_to_all | solution.py:440
  18.3 0.7 split_features.1
  19.0 0.5 collective-permute-start.12
  19.5 2.5 %collective-permute-start.11 = (bf16[256,128]{1,0:T(8,128)(2,1)S(1)}, bf16[256,128]{1,0:T(8,128)(2,1)S(1)}, u32[]{:S(2)}, u32[]{:S(2)}) collective-permute-start(bf16[256,128]{1,0:T(8,128)(2,1)S(1)} %get-tuple-element.59), channel_id=1, source_target_pairs={{0,16},{4,20},{8,24},{12,28},{16,0},{20,4},{24,8},{28,12},{32,48},... | collective-permute-start | bytes 196616 | tf_op jit(solution)/shard_map/ppermute | solution.py:453
  22.0 1.8 %collective-permute-start.10 = (bf16[256,128]{1,0:T(8,128)(2,1)S(1)}, bf16[256,128]{1,0:T(8,128)(2,1)S(1)}, u32[]{:S(2)}, u32[]{:S(2)}) collective-permute-start(bf16[256,128]{1,0:T(8,128)(2,1)S(1)} %get-tuple-element.58), channel_id=1, source_target_pairs={{0,8},{4,12},{8,16},{12,20},{16,24},{20,28},{24,0},{28,4},{32,40},... | collective-permute-start | bytes 196616 | tf_op jit(solution)/shard_map/ppermute | solution.py:453
  23.8 5.1 %collective-permute-done.12 = bf16[256,128]{1,0:T(8,128)(2,1)S(1)} collective-permute-done((bf16[256,128]{1,0:T(8,128)(2,1)S(1)}, bf16[256,128]{1,0:T(8,128)(2,1)S(1)}, u32[]{:S(2)}, u32[]{:S(2)}) %collective-permute-start.12) | collective-permute-done | bytes 65568 | tf_op jit(solution)/shard_map/ppermute | solution.py:453
  28.9 2.7 %collective-permute-done.11 = bf16[256,128]{1,0:T(8,128)(2,1)S(1)} collective-permute-done((bf16[256,128]{1,0:T(8,128)(2,1)S(1)}, bf16[256,128]{1,0:T(8,128)(2,1)S(1)}, u32[]{:S(2)}, u32[]{:S(2)}) %collective-permute-start.11) | collective-permute-done | bytes 65568 | tf_op jit(solution)/shard_map/ppermute | solution.py:453
  31.7 7.7 %collective-permute-start.17 = (bf16[4,256,128]{2,1,0:T(8,128)(2,1)S(1)}, bf16[4,256,128]{2,1,0:T(8,128)(2,1)S(1)}, u32[]{:S(2)}, u32[]{:S(2)}) collective-permute-start(bf16[4,256,128]{2,1,0:T(8,128)(2,1)S(1)} %pad_maximum_fusion.refs_4_), channel_id=1, source_target_pairs={{0,131},{1,0},{2,1},{3,2},{4,135},{5,4},{6,5},{7,6},{8,139},{9,8},... | collective-permute-start | bytes 786440 | tf_op jit(solution)/shard_map/ppermute | solution.py:444
  39.5 1.7 %all-to-all-done.signals_ref = bf16[64,64,128]{2,1,0:T(8,128)(2,1)S(1)} async-done(((bf16[64,64,128]{2,1,0:T(8,128)(2,1)}), bf16[64,64,128]{2,1,0:T(8,128)(2,1)S(1)}, u32[]{:S(2)}, u32[]{:S(2)}) %all-to-all-start) | async-done | bytes 1048608 | tf_op jit(solution)/shard_map/all_to_all | solution.py:440
  41.2 5.4 %convolve.1 = (bf16[64,16,128]{2,1,0:T(8,128)(2,1)S(1)}, bf16[4,576,256]{2,1,0:T(8,128)(2,1)S(1)}, bf16[8,16,128]{2,1,0:T(8,128)(2,1)S(1)}, bf16[8,16,128]{2,1,0...) custom-call(s32[4]{0:T(128)S(1)} %pad_add_fusion.where_ref, ...), custom_call_target="tpu_custom_call" | custom-call | tf_op jit(solution)/shard_map/convolve/pallas_call | solution.py:257
  46.7 3.3 %complete.1 = bf16[64,48,128]{2,1,0:T(8,128)(2,1)} custom-call(bf16[64,16,128]{2,1,0:T(8,128)(2,1)S(1)} %get-tuple-element.43.back_grad_ref, bf16[4,576,256]{2,1,0:T(8,128)(2,1)S(1)} %get-tuple-element.44.rest_ref, f32[72,128]{1,0:T(8,128)S(1)} %get-tuple-element.38.cos_ref, f32[72,128]{1,0:T(8,128)S(1)} %get-tuple-element.39.sin_ref, ...), custom_call_target="tpu_custom_call" | custom-call | tf_op jit(solution)/shard_map/complete/pallas_call | solution.py:297
  50.0 12.4 %all-to-all-start.1 = ((bf16[64,48,128]{2,1,0:T(8,128)(2,1)}), bf16[64,48,128]{2,1,0:T(8,128)(2,1)S(1)}, u32[]{:S(2)}, u32[]{:S(2)}) async-start(bf16[64,48,128]{2,1,0:T(8,128)(2,1)} %complete.1), calls=%async_computation.1 | async-start | bytes 1572864 | tf_op jit(solution)/shard_map/all_to_all | solution.py:440
  62.4 3.1 %collective-permute-start.14 = (bf16[4,256,128]{2,1,0:T(8,128)(2,1)S(1)}, bf16[4,256,128]{2,1,0:T(8,128)(2,1)S(1)}, u32[]{:S(2)}, u32[]{:S(2)}) collective-permute-start(bf16[4,256,128]{2,1,0:T(8,128)(2,1)S(1)} %collective-permute-done.13.refs_5_), channel_id=1, source_target_pairs={{0,1},{1,2},{2,3},{3,128},{4,5},{5,6},{6,7},{7,132},{8,9},{9,10},{... | collective-permute-start | bytes 786440 | tf_op jit(solution)/shard_map/ppermute | solution.py:444
  65.5 1.4 collective-permute-start.18
  66.9 23.3 %collective-permute-done.14.refs_6_ = bf16[4,256,128]{2,1,0:T(8,128)(2,1)S(1)} collective-permute-done((bf16[4,256,128]{2,1,0:T(8,128)(2,1)S(1)}, bf16[4,256,128]{2,1,0:T(8,128)(2,1)S(1)}, u32[]{:S(2)}, u32[]{:S(2)}) %collective-permute-start.14) | collective-permute-done | bytes 262176 | tf_op jit(solution)/shard_map/ppermute | solution.py:444
  90.4 4.2 %collective-permute-start.20 = (bf16[2,256,128]{2,1,0:T(8,128)(2,1)S(1)}, bf16[2,256,128]{2,1,0:T(8,128)(2,1)S(1)}, u32[]{:S(2)}, u32[]{:S(2)}) collective-permute-start(bf16[2,256,128]{2,1,0:T(8,128)(2,1)S(1)} %slice.9), channel_id=1, source_target_pairs={{0,130},{1,131},{2,0},{3,1},{4,134},{5,135},{6,4},{7,5},{8,138},{9... | collective-permute-start | bytes 393224 | tf_op jit(solution)/shard_map/ppermute | solution.py:444
  94.6 1.5 %collective-permute-start.1 = (bf16[8,16,128]{2,1,0:T(8,128)(2,1)S(1)}, bf16[8,16,128]{2,1,0:T(8,128)(2,1)S(1)}, u32[]{:S(2)}, u32[]{:S(2)}) collective-permute-start(bf16[8,16,128]{2,1,0:T(8,128)(2,1)S(1)} %get-tuple-element.51), channel_id=1, source_target_pairs={{0,32},{4,36},{8,40},{12,44},{16,48},{20,52},{24,56},{28,60},{32,0... | collective-permute-start | bytes 98312 | tf_op jit(solution)/shard_map/ppermute | solution.py:461
  96.1 0.3 collective-permute-start.2
  96.4 3.1 %collective-permute-start.3 = (bf16[8,16,128]{2,1,0:T(8,128)(2,1)S(1)}, bf16[8,16,128]{2,1,0:T(8,128)(2,1)S(1)}, u32[]{:S(2)}, u32[]{:S(2)}) collective-permute-start(bf16[8,16,128]{2,1,0:T(8,128)(2,1)S(1)} %get-tuple-element.53), channel_id=1, source_target_pairs={{0,64},{4,68},{8,72},{12,76},{16,80},{20,84},{24,88},{28,92},{32,9... | collective-permute-start | bytes 98312 | tf_op jit(solution)/shard_map/ppermute | solution.py:461
  99.5 1.3 collective-permute-start.4
  100.8 1.6 %collective-permute-start.5 = (bf16[8,16,128]{2,1,0:T(8,128)(2,1)S(1)}, bf16[8,16,128]{2,1,0:T(8,128)(2,1)S(1)}, u32[]{:S(2)}, u32[]{:S(2)}) collective-permute-start(bf16[8,16,128]{2,1,0:T(8,128)(2,1)S(1)} %get-tuple-element.55), channel_id=1, source_target_pairs={{0,96},{4,100},{8,104},{12,108},{16,112},{20,116},{24,120},{28,124... | collective-permute-start | bytes 98312 | tf_op jit(solution)/shard_map/ppermute | solution.py:461
  102.4 1.8 %collective-permute-start.6 = (bf16[8,16,128]{2,1,0:T(8,128)(2,1)S(1)}, bf16[8,16,128]{2,1,0:T(8,128)(2,1)S(1)}, u32[]{:S(2)}, u32[]{:S(2)}) collective-permute-start(bf16[8,16,128]{2,1,0:T(8,128)(2,1)S(1)} %get-tuple-element.56), channel_id=1, source_target_pairs={{0,100},{4,96},{8,108},{12,104},{16,116},{20,112},{24,124},{28,120... | collective-permute-start | bytes 98312 | tf_op jit(solution)/shard_map/ppermute | solution.py:461
  104.2 0.3 collective-permute-done.4.refs_5_
  104.5 1.7 %collective-permute-done.5.refs_6_ = bf16[8,16,128]{2,1,0:T(8,128)(2,1)S(1)} collective-permute-done((bf16[8,16,128]{2,1,0:T(8,128)(2,1)S(1)}, bf16[8,16,128]{2,1,0:T(8,128)(2,1)S(1)}, u32[]{:S(2)}, u32[]{:S(2)}) %collective-permute-start.5) | collective-permute-done | bytes 32800 | tf_op jit(solution)/shard_map/ppermute | solution.py:461
  106.2 1.6 %collective-permute-start.19 = (bf16[4,256,128]{2,1,0:T(8,128)(2,1)S(1)}, bf16[4,256,128]{2,1,0:T(8,128)(2,1)S(1)}, u32[]{:S(2)}, u32[]{:S(2)}) collective-permute-start(bf16[4,256,128]{2,1,0:T(8,128)(2,1)S(1)} %collective-permute-done.18.refs_10_), channel_id=1, source_target_pairs={{0,131},{1,0},{2,1},{3,2},{4,135},{5,4},{6,5},{7,6},{8,139},{9,8},... | collective-permute-start | bytes 786440 | tf_op jit(solution)/shard_map/ppermute | solution.py:444
  107.8 1.6 %collective-permute-start.7 = (bf16[8,8,16,128]{3,2,1,0:T(8,128)(2,1)S(1)}, bf16[8,8,16,128]{3,2,1,0:T(8,128)(2,1)S(1)}, u32[]{:S(2)}, u32[]{:S(2)}) collective-permute-start(bf16[8,8,16,128]{3,2,1,0:T(8,128)(2,1)S(1)} %bundle.1.refs_0_), channel_id=1, source_target_pairs={{0,8},{4,12},{8,16},{12,20},{16,24},{20,28},{24,0},{28,4},{32,40},... | collective-permute-start | bytes 786440 | tf_op jit(solution)/shard_map/ppermute | solution.py:466
  109.3 1.1 collective-permute-start.8
  110.5 2.1 %collective-permute-start.9 = (bf16[8,8,16,128]{3,2,1,0:T(8,128)(2,1)S(1)}, bf16[8,8,16,128]{3,2,1,0:T(8,128)(2,1)S(1)}, u32[]{:S(2)}, u32[]{:S(2)}) collective-permute-start(bf16[8,8,16,128]{3,2,1,0:T(8,128)(2,1)S(1)} %bundle.1.refs_0_), channel_id=1, source_target_pairs={{0,24},{4,28},{8,0},{12,4},{16,8},{20,12},{24,16},{28,20},{32,56},... | collective-permute-start | bytes 786440 | tf_op jit(solution)/shard_map/ppermute | solution.py:466
  112.6 1.6 %collective-permute-done.15.refs_7_ = bf16[4,256,128]{2,1,0:T(8,128)(2,1)S(1)} collective-permute-done((bf16[4,256,128]{2,1,0:T(8,128)(2,1)S(1)}, bf16[4,256,128]{2,1,0:T(8,128)(2,1)S(1)}, u32[]{:S(2)}, u32[]{:S(2)}) %collective-permute-start.15) | collective-permute-done | bytes 262176 | tf_op jit(solution)/shard_map/ppermute | solution.py:444
  114.2 0.2 collective-permute-done.19.refs_9_
  114.4 2.6 %collective-permute-done.7.refs_1_ = bf16[8,8,16,128]{3,2,1,0:T(8,128)(2,1)S(1)} collective-permute-done((bf16[8,8,16,128]{3,2,1,0:T(8,128)(2,1)S(1)}, bf16[8,8,16,128]{3,2,1,0:T(8,128)(2,1)S(1)}, u32[]{:S(2)}, u32[]{:S(2)}) %collective-permute-start.7) | collective-permute-done | bytes 262176 | tf_op jit(solution)/shard_map/ppermute | solution.py:466
  117.0 3.0 %collective-permute-done.8.refs_2_ = bf16[8,8,16,128]{3,2,1,0:T(8,128)(2,1)S(1)} collective-permute-done((bf16[8,8,16,128]{3,2,1,0:T(8,128)(2,1)S(1)}, bf16[8,8,16,128]{3,2,1,0:T(8,128)(2,1)S(1)}, u32[]{:S(2)}, u32[]{:S(2)}) %collective-permute-start.8) | collective-permute-done | bytes 262176 | tf_op jit(solution)/shard_map/ppermute | solution.py:466
  120.0 3.5 %collective-permute-done.9.refs_3_ = bf16[8,8,16,128]{3,2,1,0:T(8,128)(2,1)S(1)} collective-permute-done((bf16[8,8,16,128]{3,2,1,0:T(8,128)(2,1)S(1)}, bf16[8,8,16,128]{3,2,1,0:T(8,128)(2,1)S(1)}, u32[]{:S(2)}, u32[]{:S(2)}) %collective-permute-start.9) | collective-permute-done | bytes 262176 | tf_op jit(solution)/shard_map/ppermute | solution.py:466
  123.5 2.1 %weight_parts.1 = (bf16[4,2,64,512]{3,2,1,0:T(8,128)(2,1)S(1)}, bf16[4,2,64,512]{3,2,1,0:T(8,128)(2,1)S(1)}) custom-call(s32[4]{0:T(128)S(1)} %pad_add_fusion.where_ref, bf16[8,8,16,128]{3,2,1,0:T(8,128)(2,1)S(1)} %bundle.1.refs_0_, bf16[8,8,16,128]{3,2,1,0:T(8,128)(2,1)S(1)} %collective-permute-done.7.refs_1_, ...), custom_call_target="tpu_custom_call" | custom-call | tf_op jit(solution)/shard_map/weight_parts/pallas_call | solution.py:387
  125.7 1.9 %collective-permute-done.21.received_ref = bf16[4,2,64,512]{3,2,1,0:T(8,128)(2,1)S(1)} collective-permute-done((bf16[4,2,64,512]{3,2,1,0:T(8,128)(2,1)S(1)}, bf16[4,2,64,512]{3,2,1,0:T(8,128)(2,1)S(1)}, u32[]{:S(2)}, u32[]{:S(2)}) %collective-permute-start.21) | collective-permute-done | bytes 524320 | tf_op jit(solution)/shard_map/ppermute | solution.py:469
  127.6 0.1 join_cores.1
  127.8 0.8 collective-permute-start.22
  128.6 2.8 %collective-permute-start.23 = (bf16[2,64,512]{2,1,0:T(8,128)(2,1)S(1)}, bf16[2,64,512]{2,1,0:T(8,128)(2,1)S(1)}, u32[]{:S(2)}, u32[]{:S(2)}) collective-permute-start(bf16[2,64,512]{2,1,0:T(8,128)(2,1)S(1)} %get-tuple-element.65), channel_id=1, source_target_pairs={{0,64},{4,68},{8,72},{12,76},{16,80},{20,84},{24,88},{28,92},{32,9... | collective-permute-start | bytes 393224 | tf_op jit(solution)/shard_map/ppermute | solution.py:471
  131.4 1.2 collective-permute-start.24
  132.6 1.7 %collective-permute-done.22.refs_1_ = bf16[2,64,512]{2,1,0:T(8,128)(2,1)S(1)} collective-permute-done((bf16[2,64,512]{2,1,0:T(8,128)(2,1)S(1)}, bf16[2,64,512]{2,1,0:T(8,128)(2,1)S(1)}, u32[]{:S(2)}, u32[]{:S(2)}) %collective-permute-start.22) | collective-permute-done | bytes 131104 | tf_op jit(solution)/shard_map/ppermute | solution.py:471
  134.2 3.6 %collective-permute-done.23.refs_2_ = bf16[2,64,512]{2,1,0:T(8,128)(2,1)S(1)} collective-permute-done((bf16[2,64,512]{2,1,0:T(8,128)(2,1)S(1)}, bf16[2,64,512]{2,1,0:T(8,128)(2,1)S(1)}, u32[]{:S(2)}, u32[]{:S(2)}) %collective-permute-start.23) | collective-permute-done | bytes 131104 | tf_op jit(solution)/shard_map/ppermute | solution.py:471
  137.8 2.2 %collective-permute-done.24.refs_3_ = bf16[2,64,512]{2,1,0:T(8,128)(2,1)S(1)} collective-permute-done((bf16[2,64,512]{2,1,0:T(8,128)(2,1)S(1)}, bf16[2,64,512]{2,1,0:T(8,128)(2,1)S(1)}, u32[]{:S(2)}, u32[]{:S(2)}) %collective-permute-start.24) | collective-permute-done | bytes 131104 | tf_op jit(solution)/shard_map/ppermute | solution.py:471
  140.0 0.6 weight_total.1
  140.7 1.3 collective-permute-start.25
  142.0 7.5 %collective-permute-done.25 = bf16[64,512]{1,0:T(8,128)(2,1)S(1)} collective-permute-done((bf16[64,512]{1,0:T(8,128)(2,1)S(1)}, bf16[64,512]{1,0:T(8,128)(2,1)S(1)}, u32[]{:S(2)}, u32[]{:S(2)}) %collective-permute-start.25) | collective-permute-done | bytes 65568 | tf_op jit(solution)/shard_map/ppermute | solution.py:473
  149.6 0.7 maximum_select_fusion
  150.3 1.3 finish.1
  (44 shorter events, 0.6 us)
Async XLA Ops:
  3.3 15.0 %copy-start.3 = (bf16[128,1024]{1,0:T(8,128)(2,1)S(1)}, bf16[128,1024]{1,0:T(8,128)(2,1)}, u32[]{:S(2)}) copy-start(bf16[128,1024]{1,0:T(8,128)(2,1)} %input_ref.1) | copy-start | bytes 786436
  3.3 36.1 %copy-start.4 = (bf16[512,256]{1,0:T(8,128)(2,1)S(1)}, bf16[512,256]{1,0:T(8,128)(2,1)}, u32[]{:S(2)}) copy-start(bf16[512,256]{1,0:T(8,128)(2,1)} %constant.84.clone.refs_3_) | copy-start | bytes 786436
  3.3 36.1 %copy-start.5 = (bf16[512,256]{1,0:T(8,128)(2,1)S(1)}, bf16[512,256]{1,0:T(8,128)(2,1)}, u32[]{:S(2)}) copy-start(bf16[512,256]{1,0:T(8,128)(2,1)} %constant.85.clone.refs_4_) | copy-start | bytes 786436
  3.3 36.1 %copy-start.6 = (bf16[128,144]{1,0:T(8,128)(2,1)S(1)}, bf16[128,144]{1,0:T(8,128)(2,1)}, u32[]{:S(2)}) copy-start(bf16[128,144]{1,0:T(8,128)(2,1)} %constant.86.clone.refs_5_) | copy-start | bytes 110596
  3.3 36.1 %copy-start.7 = (bf16[144,128]{1,0:T(8,128)(2,1)S(1)}, bf16[144,128]{1,0:T(8,128)(2,1)}, u32[]{:S(2)}) copy-start(bf16[144,128]{1,0:T(8,128)(2,1)} %constant.81.clone.refs_0_) | copy-start | bytes 110596
  3.3 36.1 %copy-start.8 = (f32[72,128]{1,0:T(8,128)S(1)}, f32[72,128]{1,0:T(8,128)}, u32[]{:S(2)}) copy-start(f32[72,128]{1,0:T(8,128)} %constant.82.clone.refs_1_) | copy-start | bytes 110596
  3.3 36.1 %copy-start.9 = (f32[72,128]{1,0:T(8,128)S(1)}, f32[72,128]{1,0:T(8,128)}, u32[]{:S(2)}) copy-start(f32[72,128]{1,0:T(8,128)} %constant.83.clone.refs_2_) | copy-start | bytes 110596
  3.3 37.9 %all-to-all-start = ((bf16[64,64,128]{2,1,0:T(8,128)(2,1)}), bf16[64,64,128]{2,1,0:T(8,128)(2,1)S(1)}, u32[]{:S(2)}, u32[]{:S(2)}) async-start(bf16[64,64,128]{2,1,0:T(8,128)(2,1)} %gather_signals.1), calls=%async_computation | async-start | bytes 2097152 | tf_op jit(solution)/shard_map/all_to_all | solution.py:440
  19.0 9.9 %collective-permute-start.12 = (bf16[256,128]{1,0:T(8,128)(2,1)S(1)}, bf16[256,128]{1,0:T(8,128)(2,1)S(1)}, u32[]{:S(2)}, u32[]{:S(2)}) collective-permute-start(bf16[256,128]{1,0:T(8,128)(2,1)S(1)} %get-tuple-element.60), channel_id=1, source_target_pairs={{0,24},{4,28},{8,0},{12,4},{16,8},{20,12},{24,16},{28,20},{32,56},... | collective-permute-start | bytes 196616 | tf_op jit(solution)/shard_map/ppermute | solution.py:453
  19.5 12.0 %collective-permute-start.11 = (bf16[256,128]{1,0:T(8,128)(2,1)S(1)}, bf16[256,128]{1,0:T(8,128)(2,1)S(1)}, u32[]{:S(2)}, u32[]{:S(2)}) collective-permute-start(bf16[256,128]{1,0:T(8,128)(2,1)S(1)} %get-tuple-element.59), channel_id=1, source_target_pairs={{0,16},{4,20},{8,24},{12,28},{16,0},{20,4},{24,8},{28,12},{32,48},... | collective-permute-start | bytes 196616 | tf_op jit(solution)/shard_map/ppermute | solution.py:453
  22.0 9.6 %collective-permute-start.10 = (bf16[256,128]{1,0:T(8,128)(2,1)S(1)}, bf16[256,128]{1,0:T(8,128)(2,1)S(1)}, u32[]{:S(2)}, u32[]{:S(2)}) collective-permute-start(bf16[256,128]{1,0:T(8,128)(2,1)S(1)} %get-tuple-element.58), channel_id=1, source_target_pairs={{0,8},{4,12},{8,16},{12,20},{16,24},{20,28},{24,0},{28,4},{32,40},... | collective-permute-start | bytes 196616 | tf_op jit(solution)/shard_map/ppermute | solution.py:453
  31.6 30.8 %collective-permute-start.13 = (bf16[4,256,128]{2,1,0:T(8,128)(2,1)S(1)}, bf16[4,256,128]{2,1,0:T(8,128)(2,1)S(1)}, u32[]{:S(2)}, u32[]{:S(2)}) collective-permute-start(bf16[4,256,128]{2,1,0:T(8,128)(2,1)S(1)} %pad_maximum_fusion.refs_4_), channel_id=1, source_target_pairs={{0,1},{1,2},{2,3},{3,128},{4,5},{5,6},{6,7},{7,132},{8,9},{9,10},{... | collective-permute-start | bytes 786440 | tf_op jit(solution)/shard_map/ppermute | solution.py:444
  31.7 33.8 %collective-permute-start.17 = (bf16[4,256,128]{2,1,0:T(8,128)(2,1)S(1)}, bf16[4,256,128]{2,1,0:T(8,128)(2,1)S(1)}, u32[]{:S(2)}, u32[]{:S(2)}) collective-permute-start(bf16[4,256,128]{2,1,0:T(8,128)(2,1)S(1)} %pad_maximum_fusion.refs_4_), channel_id=1, source_target_pairs={{0,131},{1,0},{2,1},{3,2},{4,135},{5,4},{6,5},{7,6},{8,139},{9,8},... | collective-permute-start | bytes 786440 | tf_op jit(solution)/shard_map/ppermute | solution.py:444
  50.0 100.3 %all-to-all-start.1 = ((bf16[64,48,128]{2,1,0:T(8,128)(2,1)}), bf16[64,48,128]{2,1,0:T(8,128)(2,1)S(1)}, u32[]{:S(2)}, u32[]{:S(2)}) async-start(bf16[64,48,128]{2,1,0:T(8,128)(2,1)} %complete.1), calls=%async_computation.1 | async-start | bytes 1572864 | tf_op jit(solution)/shard_map/all_to_all | solution.py:440
  62.4 27.8 %collective-permute-start.14 = (bf16[4,256,128]{2,1,0:T(8,128)(2,1)S(1)}, bf16[4,256,128]{2,1,0:T(8,128)(2,1)S(1)}, u32[]{:S(2)}, u32[]{:S(2)}) collective-permute-start(bf16[4,256,128]{2,1,0:T(8,128)(2,1)S(1)} %collective-permute-done.13.refs_5_), channel_id=1, source_target_pairs={{0,1},{1,2},{2,3},{3,128},{4,5},{5,6},{6,7},{7,132},{8,9},{9,10},{... | collective-permute-start | bytes 786440 | tf_op jit(solution)/shard_map/ppermute | solution.py:444
  65.5 24.8 %collective-permute-start.18 = (bf16[4,256,128]{2,1,0:T(8,128)(2,1)S(1)}, bf16[4,256,128]{2,1,0:T(8,128)(2,1)S(1)}, u32[]{:S(2)}, u32[]{:S(2)}) collective-permute-start(bf16[4,256,128]{2,1,0:T(8,128)(2,1)S(1)} %collective-permute-done.17.refs_11_), channel_id=1, source_target_pairs={{0,131},{1,0},{2,1},{3,2},{4,135},{5,4},{6,5},{7,6},{8,139},{9,8},... | collective-permute-start | bytes 786440 | tf_op jit(solution)/shard_map/ppermute | solution.py:444
  90.3 19.1 %collective-permute-start.16 = (bf16[2,256,128]{2,1,0:T(8,128)(2,1)S(1)}, bf16[2,256,128]{2,1,0:T(8,128)(2,1)S(1)}, u32[]{:S(2)}, u32[]{:S(2)}) collective-permute-start(bf16[2,256,128]{2,1,0:T(8,128)(2,1)S(1)} %slice.8), channel_id=1, source_target_pairs={{0,2},{1,3},{2,128},{3,129},{4,6},{5,7},{6,132},{7,133},{8,10},{9,... | collective-permute-start | bytes 393224 | tf_op jit(solution)/shard_map/ppermute | solution.py:444
  90.4 20.1 %collective-permute-start.20 = (bf16[2,256,128]{2,1,0:T(8,128)(2,1)S(1)}, bf16[2,256,128]{2,1,0:T(8,128)(2,1)S(1)}, u32[]{:S(2)}, u32[]{:S(2)}) collective-permute-start(bf16[2,256,128]{2,1,0:T(8,128)(2,1)S(1)} %slice.9), channel_id=1, source_target_pairs={{0,130},{1,131},{2,0},{3,1},{4,134},{5,135},{6,4},{7,5},{8,138},{9... | collective-permute-start | bytes 393224 | tf_op jit(solution)/shard_map/ppermute | solution.py:444
  94.6 1.9 %collective-permute-start = (bf16[8,16,128]{2,1,0:T(8,128)(2,1)S(1)}, bf16[8,16,128]{2,1,0:T(8,128)(2,1)S(1)}, u32[]{:S(2)}, u32[]{:S(2)}) collective-permute-start(bf16[8,16,128]{2,1,0:T(8,128)(2,1)S(1)} %get-tuple-element.50), channel_id=1, source_target_pairs={{0,4},{4,0},{8,12},{12,8},{16,20},{20,16},{24,28},{28,24},{32,36},... | collective-permute-start | bytes 98312 | tf_op jit(solution)/shard_map/ppermute | solution.py:461
  94.6 4.9 %collective-permute-start.1 = (bf16[8,16,128]{2,1,0:T(8,128)(2,1)S(1)}, bf16[8,16,128]{2,1,0:T(8,128)(2,1)S(1)}, u32[]{:S(2)}, u32[]{:S(2)}) collective-permute-start(bf16[8,16,128]{2,1,0:T(8,128)(2,1)S(1)} %get-tuple-element.51), channel_id=1, source_target_pairs={{0,32},{4,36},{8,40},{12,44},{16,48},{20,52},{24,56},{28,60},{32,0... | collective-permute-start | bytes 98312 | tf_op jit(solution)/shard_map/ppermute | solution.py:461
  96.1 4.7 %collective-permute-start.2 = (bf16[8,16,128]{2,1,0:T(8,128)(2,1)S(1)}, bf16[8,16,128]{2,1,0:T(8,128)(2,1)S(1)}, u32[]{:S(2)}, u32[]{:S(2)}) collective-permute-start(bf16[8,16,128]{2,1,0:T(8,128)(2,1)S(1)} %get-tuple-element.52), channel_id=1, source_target_pairs={{0,36},{4,32},{8,44},{12,40},{16,52},{20,48},{24,60},{28,56},{32,4... | collective-permute-start | bytes 98312 | tf_op jit(solution)/shard_map/ppermute | solution.py:461
  96.4 6.0 %collective-permute-start.3 = (bf16[8,16,128]{2,1,0:T(8,128)(2,1)S(1)}, bf16[8,16,128]{2,1,0:T(8,128)(2,1)S(1)}, u32[]{:S(2)}, u32[]{:S(2)}) collective-permute-start(bf16[8,16,128]{2,1,0:T(8,128)(2,1)S(1)} %get-tuple-element.53), channel_id=1, source_target_pairs={{0,64},{4,68},{8,72},{12,76},{16,80},{20,84},{24,88},{28,92},{32,9... | collective-permute-start | bytes 98312 | tf_op jit(solution)/shard_map/ppermute | solution.py:461
  99.5 5.0 %collective-permute-start.4 = (bf16[8,16,128]{2,1,0:T(8,128)(2,1)S(1)}, bf16[8,16,128]{2,1,0:T(8,128)(2,1)S(1)}, u32[]{:S(2)}, u32[]{:S(2)}) collective-permute-start(bf16[8,16,128]{2,1,0:T(8,128)(2,1)S(1)} %get-tuple-element.54), channel_id=1, source_target_pairs={{0,68},{4,64},{8,76},{12,72},{16,84},{20,80},{24,92},{28,88},{32,1... | collective-permute-start | bytes 98312 | tf_op jit(solution)/shard_map/ppermute | solution.py:461
  100.8 5.4 %collective-permute-start.5 = (bf16[8,16,128]{2,1,0:T(8,128)(2,1)S(1)}, bf16[8,16,128]{2,1,0:T(8,128)(2,1)S(1)}, u32[]{:S(2)}, u32[]{:S(2)}) collective-permute-start(bf16[8,16,128]{2,1,0:T(8,128)(2,1)S(1)} %get-tuple-element.55), channel_id=1, source_target_pairs={{0,96},{4,100},{8,104},{12,108},{16,112},{20,116},{24,120},{28,124... | collective-permute-start | bytes 98312 | tf_op jit(solution)/shard_map/ppermute | solution.py:461
  102.4 5.3 %collective-permute-start.6 = (bf16[8,16,128]{2,1,0:T(8,128)(2,1)S(1)}, bf16[8,16,128]{2,1,0:T(8,128)(2,1)S(1)}, u32[]{:S(2)}, u32[]{:S(2)}) collective-permute-start(bf16[8,16,128]{2,1,0:T(8,128)(2,1)S(1)} %get-tuple-element.56), channel_id=1, source_target_pairs={{0,100},{4,96},{8,108},{12,104},{16,116},{20,112},{24,124},{28,120... | collective-permute-start | bytes 98312 | tf_op jit(solution)/shard_map/ppermute | solution.py:461
  104.5 9.7 %collective-permute-start.15 = (bf16[4,256,128]{2,1,0:T(8,128)(2,1)S(1)}, bf16[4,256,128]{2,1,0:T(8,128)(2,1)S(1)}, u32[]{:S(2)}, u32[]{:S(2)}) collective-permute-start(bf16[4,256,128]{2,1,0:T(8,128)(2,1)S(1)} %collective-permute-done.14.refs_6_), channel_id=1, source_target_pairs={{0,1},{1,2},{2,3},{3,128},{4,5},{5,6},{6,7},{7,132},{8,9},{9,10},{... | collective-permute-start | bytes 786440 | tf_op jit(solution)/shard_map/ppermute | solution.py:444
  106.2 8.2 %collective-permute-start.19 = (bf16[4,256,128]{2,1,0:T(8,128)(2,1)S(1)}, bf16[4,256,128]{2,1,0:T(8,128)(2,1)S(1)}, u32[]{:S(2)}, u32[]{:S(2)}) collective-permute-start(bf16[4,256,128]{2,1,0:T(8,128)(2,1)S(1)} %collective-permute-done.18.refs_10_), channel_id=1, source_target_pairs={{0,131},{1,0},{2,1},{3,2},{4,135},{5,4},{6,5},{7,6},{8,139},{9,8},... | collective-permute-start | bytes 786440 | tf_op jit(solution)/shard_map/ppermute | solution.py:444
  107.8 9.3 %collective-permute-start.7 = (bf16[8,8,16,128]{3,2,1,0:T(8,128)(2,1)S(1)}, bf16[8,8,16,128]{3,2,1,0:T(8,128)(2,1)S(1)}, u32[]{:S(2)}, u32[]{:S(2)}) collective-permute-start(bf16[8,8,16,128]{3,2,1,0:T(8,128)(2,1)S(1)} %bundle.1.refs_0_), channel_id=1, source_target_pairs={{0,8},{4,12},{8,16},{12,20},{16,24},{20,28},{24,0},{28,4},{32,40},... | collective-permute-start | bytes 786440 | tf_op jit(solution)/shard_map/ppermute | solution.py:466
  109.3 10.7 %collective-permute-start.8 = (bf16[8,8,16,128]{3,2,1,0:T(8,128)(2,1)S(1)}, bf16[8,8,16,128]{3,2,1,0:T(8,128)(2,1)S(1)}, u32[]{:S(2)}, u32[]{:S(2)}) collective-permute-start(bf16[8,8,16,128]{3,2,1,0:T(8,128)(2,1)S(1)} %bundle.1.refs_0_), channel_id=1, source_target_pairs={{0,16},{4,20},{8,24},{12,28},{16,0},{20,4},{24,8},{28,12},{32,48},... | collective-permute-start | bytes 786440 | tf_op jit(solution)/shard_map/ppermute | solution.py:466
  110.5 13.0 %collective-permute-start.9 = (bf16[8,8,16,128]{3,2,1,0:T(8,128)(2,1)S(1)}, bf16[8,8,16,128]{3,2,1,0:T(8,128)(2,1)S(1)}, u32[]{:S(2)}, u32[]{:S(2)}) collective-permute-start(bf16[8,8,16,128]{3,2,1,0:T(8,128)(2,1)S(1)} %bundle.1.refs_0_), channel_id=1, source_target_pairs={{0,24},{4,28},{8,0},{12,4},{16,8},{20,12},{24,16},{28,20},{32,56},... | collective-permute-start | bytes 786440 | tf_op jit(solution)/shard_map/ppermute | solution.py:466
  125.6 24.7 %copy-start = (bf16[128,1024]{1,0:T(8,128)(2,1)S(1)}, bf16[128,1024]{1,0:T(8,128)(2,1)}, u32[]{:S(2)}) copy-start(bf16[128,1024]{1,0:T(8,128)(2,1)} %key_ref.3) | copy-start | bytes 786436
  125.6 24.7 %copy-start.1 = (bf16[128,1024]{1,0:T(8,128)(2,1)S(1)}, bf16[128,1024]{1,0:T(8,128)(2,1)}, u32[]{:S(2)}) copy-start(bf16[128,1024]{1,0:T(8,128)(2,1)} %value_ref.3) | copy-start | bytes 786436
  125.6 24.7 %copy-start.2 = (bf16[128,1024]{1,0:T(8,128)(2,1)S(1)}, bf16[128,1024]{1,0:T(8,128)(2,1)}, u32[]{:S(2)}) copy-start(bf16[128,1024]{1,0:T(8,128)(2,1)} %grad_ref.3) | copy-start | bytes 786436
  125.6 2.0 %collective-permute-start.21 = (bf16[4,2,64,512]{3,2,1,0:T(8,128)(2,1)S(1)}, bf16[4,2,64,512]{3,2,1,0:T(8,128)(2,1)S(1)}, u32[]{:S(2)}, u32[]{:S(2)}) collective-permute-start(bf16[4,2,64,512]{3,2,1,0:T(8,128)(2,1)S(1)} %get-tuple-element.62), channel_id=1, source_target_pairs={{0,4},{4,0},{8,12},{12,8},{16,20},{20,16},{24,28},{28,24},{32,36},... | collective-permute-start | bytes 1572872 | tf_op jit(solution)/shard_map/ppermute | solution.py:469
  127.8 6.5 %collective-permute-start.22 = (bf16[2,64,512]{2,1,0:T(8,128)(2,1)S(1)}, bf16[2,64,512]{2,1,0:T(8,128)(2,1)S(1)}, u32[]{:S(2)}, u32[]{:S(2)}) collective-permute-start(bf16[2,64,512]{2,1,0:T(8,128)(2,1)S(1)} %get-tuple-element.64), channel_id=1, source_target_pairs={{0,32},{4,36},{8,40},{12,44},{16,48},{20,52},{24,56},{28,60},{32,0... | collective-permute-start | bytes 393224 | tf_op jit(solution)/shard_map/ppermute | solution.py:471
  128.6 9.2 %collective-permute-start.23 = (bf16[2,64,512]{2,1,0:T(8,128)(2,1)S(1)}, bf16[2,64,512]{2,1,0:T(8,128)(2,1)S(1)}, u32[]{:S(2)}, u32[]{:S(2)}) collective-permute-start(bf16[2,64,512]{2,1,0:T(8,128)(2,1)S(1)} %get-tuple-element.65), channel_id=1, source_target_pairs={{0,64},{4,68},{8,72},{12,76},{16,80},{20,84},{24,88},{28,92},{32,9... | collective-permute-start | bytes 393224 | tf_op jit(solution)/shard_map/ppermute | solution.py:471
  131.4 8.6 %collective-permute-start.24 = (bf16[2,64,512]{2,1,0:T(8,128)(2,1)S(1)}, bf16[2,64,512]{2,1,0:T(8,128)(2,1)S(1)}, u32[]{:S(2)}, u32[]{:S(2)}) collective-permute-start(bf16[2,64,512]{2,1,0:T(8,128)(2,1)S(1)} %get-tuple-element.66), channel_id=1, source_target_pairs={{0,96},{4,100},{8,104},{12,108},{16,112},{20,116},{24,120},{28,124... | collective-permute-start | bytes 393224 | tf_op jit(solution)/shard_map/ppermute | solution.py:471
  140.7 8.9 %collective-permute-start.25 = (bf16[64,512]{1,0:T(8,128)(2,1)S(1)}, bf16[64,512]{1,0:T(8,128)(2,1)S(1)}, u32[]{:S(2)}, u32[]{:S(2)}) collective-permute-start(bf16[64,512]{1,0:T(8,128)(2,1)S(1)} %get-tuple-element.68), channel_id=1, source_target_pairs={{0,128},{4,132},{8,136},{12,140},{16,144},{20,148},{24,152},{28,15... | collective-permute-start | bytes 196616 | tf_op jit(solution)/shard_map/ppermute | solution.py:473

commit v8 on v5

--- a/solution.py
+++ b/solution.py
@@ -38,7 +38,7 @@
     pairs = []
     for flat in range(256):
         s, c = divmod(flat, 4)
-        place = (s // 32 * 4 + c + shift) % 8
+        place = (s // 32 * 4 + c + (-shift if s % 2 else shift)) % 8
         pairs.append((flat, (place // 4 * 32 + s % 32) * 4 + place % 4))
     return pairs
 
@@ -82,11 +82,10 @@
 
 
 WHOLE_GRANT = 60 << 20
-STEPS = 4
 
 
 def gather_body(key_ref, value_ref, grad_ref, query_ref, taps_ref, sent_ref):
-    for part in range(8 // STEPS):
+    for part in range(8):
         cols = pl.ds(part * 128, 128)
         key = key_ref[:, cols].astype(jnp.float32)
         mixed = key * value_ref[:, cols].astype(jnp.float32)
@@ -99,10 +98,7 @@
 def gather_signals(gate_key, value_proj, grad_out, gate_query, filter_taps):
     return pl.pallas_call(
         gather_body,
-        grid=(STEPS,),
         out_shape=jax.ShapeDtypeStruct((BLOCKS, SENT, ROWS), jnp.bfloat16),
-        in_specs=[pl.BlockSpec((ROWS, 1024 // STEPS), lambda i: (0, i))] * 5,
-        out_specs=pl.BlockSpec((BLOCKS // STEPS, SENT, ROWS), lambda i: (i, 0, 0)),
         name="gather_signals",
         compiler_params=pltpu.CompilerParams(vmem_limit_bytes=WHOLE_GRANT),
     )(gate_key, value_proj, grad_out, gate_query, filter_taps)
@@ -347,6 +343,7 @@
     values, features = refs[:4], refs[4:12]
     kept_ref, sent_ref, aligned, pieces = refs[12:]
     x, ring, place = where_ref[0], where_ref[1], where_ref[2]
+    turn = 1 - 2 * (place % 2)
     for apart, value_ref in enumerate(values):
         column = (x - apart + 4) % 4
         for flip in range(8):
@@ -360,7 +357,7 @@
     for apart in range(4):
         total = None
         for half in range(2):
-            source = (ring - apart - 4 * half + 8) % 8
+            source = (ring - turn * (apart + 4 * half) + 8) % 8
             rows = features[apart + 4 * half]
             rows = jnp.concatenate([rows[back] for back in range(4)], axis=1)
             term = lax.dot_general(
@@ -370,7 +367,7 @@
                 preferred_element_type=jnp.float32,
             )
             total = term if total is None else total + term
-        group = (ring - apart + 8) % 4
+        group = (ring - turn * apart + 8) % 4
         for side in range(2):
             for core in range(2):
                 target = ((group % 2) * 2 + side) * 2 + core

time: 151 us -> 152 us (level)
    ppermute x7, waiting for transfers between devices: 41.7 us -> 38 us  [ring_step(): return lax.ppermute(array, ('seq', 'chan'), along_z(shift))]
    ppermute x3, waiting for transfers between devices: 4.74 us -> 7.59 us  [shards(): lax.ppermute(value, 'seq', along_x(n))]
    ppermute x7, starting transfers between devices: 10.6 us -> 12.4 us  [ring_step(): return lax.ppermute(array, ('seq', 'chan'), along_z(shift))]
    ppermute x1, waiting for transfers between devices: 5.64 us -> 7.37 us  [shards(): received = lax.ppermute(sent, 'seq', opposite()).astype(jnp.float32)]
  transfers between devices with their start and end apart: 27 -> 27, of which waited for: 13 -> 15; matrix products, arithmetic and copies ran while one was open for 1% -> 1% of each run, Pallas kernels for 8% -> 8%
where the time goes in v8:
time: 152 us; the launch traced here: 151 us
  waiting for transfers between devices  70.1 us (46%)
  starting transfers between devices  62.5 us (41%)
  Pallas kernels  16.4 us (11%)
    ppermute x7, waiting for transfers between devices, ring_step(): return lax.ppermute(array, ('seq', 'chan'), along_z(shift))  38 us
    all_to_all x2, starting transfers between devices, exchange(): return lax.all_to_all(array, 'seq', split_axis=0, concat_axis=0, tiled=True)  25.2 us
    ppermute x7, starting transfers between devices, ring_step(): return lax.ppermute(array, ('seq', 'chan'), along_z(shift))  12.4 us
    ppermute x7, starting transfers between devices, shards(): lax.ppermute(pieces[n], 'seq', across(n))  8.06 us
    ppermute x3, waiting for transfers between devices, shards(): lax.ppermute(parts[n], 'seq', across(2 * n))  8.02 us
    ppermute x3, waiting for transfers between devices, shards(): lax.ppermute(value, 'seq', along_x(n))  7.59 us
    ppermute x1, waiting for transfers between devices, shards(): received = lax.ppermute(sent, 'seq', opposite()).astype(jnp.float32)  7.37 us
    ppermute x3, waiting for transfers between devices, shards(): own = [lax.ppermute(pieces[n], 'seq', along_x(n)) for n in range(1, 4)]  7.12 us
  transfers between devices with their start and end apart: 27, of which 15 were waited for; matrix products, arithmetic and copies ran while one was open for 1% of the time, Pallas kernels for 8%

profile of v8, /device:TPU:32, one launch (start us, length us, event | category | flops | bytes accessed | tf_op | source)
XLA Modules:
  0.0 150.8 jit_solution(12597393801683061797)
XLA Ops:
  0.6 2.7 %gather_signals.1 = bf16[64,64,128]{2,1,0:T(8,128)(2,1)} custom-call(bf16[128,1024]{1,0:T(8,128)(2,1)} %key_ref.3, bf16[128,1024]{1,0:T(8,128)(2,1)} %value_ref.3, bf16[128,1024]{1,0:T(8,128)(2,1)} %grad_ref.3, bf16[128,1024]{1,0:T(8,128)(2,1)} %query_ref.1, bf16[128,1024]{1,0:T(8,128)(2,1)} %taps_ref.1), custom_call_target="tpu_custom_call" | custom-call | tf_op jit(solution)/shard_map/gather_signals/pallas_call | solution.py:99
  3.3 13.8 %all-to-all-start = ((bf16[64,64,128]{2,1,0:T(8,128)(2,1)}), bf16[64,64,128]{2,1,0:T(8,128)(2,1)S(1)}, u32[]{:S(2)}, u32[]{:S(2)}) async-start(bf16[64,64,128]{2,1,0:T(8,128)(2,1)} %gather_signals.1), calls=%async_computation | async-start | bytes 2097152 | tf_op jit(solution)/shard_map/all_to_all | solution.py:437
  17.2 0.1 pad_add_fusion.where_ref
  17.3 0.7 split_features.1
  18.0 2.9 %collective-permute-start.12 = (bf16[256,128]{1,0:T(8,128)(2,1)S(1)}, bf16[256,128]{1,0:T(8,128)(2,1)S(1)}, u32[]{:S(2)}, u32[]{:S(2)}) collective-permute-start(bf16[256,128]{1,0:T(8,128)(2,1)S(1)} %get-tuple-element.60), channel_id=1, source_target_pairs={{0,24},{4,28},{8,0},{12,4},{16,8},{20,12},{24,16},{28,20},{32,56},... | collective-permute-start | bytes 196616 | tf_op jit(solution)/shard_map/ppermute | solution.py:450
  20.9 0.9 collective-permute-start.11
  21.7 0.9 collective-permute-start.10
  22.6 5.2 %collective-permute-done.12 = bf16[256,128]{1,0:T(8,128)(2,1)S(1)} collective-permute-done((bf16[256,128]{1,0:T(8,128)(2,1)S(1)}, bf16[256,128]{1,0:T(8,128)(2,1)S(1)}, u32[]{:S(2)}, u32[]{:S(2)}) %collective-permute-start.12) | collective-permute-done | bytes 65568 | tf_op jit(solution)/shard_map/ppermute | solution.py:450
  27.7 1.6 %collective-permute-done.11 = bf16[256,128]{1,0:T(8,128)(2,1)S(1)} collective-permute-done((bf16[256,128]{1,0:T(8,128)(2,1)S(1)}, bf16[256,128]{1,0:T(8,128)(2,1)S(1)}, u32[]{:S(2)}, u32[]{:S(2)}) %collective-permute-start.11) | collective-permute-done | bytes 65568 | tf_op jit(solution)/shard_map/ppermute | solution.py:450
  29.3 0.4 collective-permute-done.10
  29.7 1.1 collective-permute-start.13
  30.8 2.3 %collective-permute-start.17 = (bf16[4,256,128]{2,1,0:T(8,128)(2,1)S(1)}, bf16[4,256,128]{2,1,0:T(8,128)(2,1)S(1)}, u32[]{:S(2)}, u32[]{:S(2)}) collective-permute-start(bf16[4,256,128]{2,1,0:T(8,128)(2,1)S(1)} %pad_maximum_fusion.refs_4_), channel_id=1, source_target_pairs={{0,131},{1,0},{2,1},{3,2},{4,5},{5,6},{6,7},{7,132},{8,139},{9,8},... | collective-permute-start | bytes 786440 | tf_op jit(solution)/shard_map/ppermute | solution.py:441
  33.1 13.4 %collective-permute-done.13.refs_5_ = bf16[4,256,128]{2,1,0:T(8,128)(2,1)S(1)} collective-permute-done((bf16[4,256,128]{2,1,0:T(8,128)(2,1)S(1)}, bf16[4,256,128]{2,1,0:T(8,128)(2,1)S(1)}, u32[]{:S(2)}, u32[]{:S(2)}) %collective-permute-start.13) | collective-permute-done | bytes 262176 | tf_op jit(solution)/shard_map/ppermute | solution.py:441
  46.5 2.5 %collective-permute-start.14 = (bf16[4,256,128]{2,1,0:T(8,128)(2,1)S(1)}, bf16[4,256,128]{2,1,0:T(8,128)(2,1)S(1)}, u32[]{:S(2)}, u32[]{:S(2)}) collective-permute-start(bf16[4,256,128]{2,1,0:T(8,128)(2,1)S(1)} %collective-permute-done.13.refs_5_), channel_id=1, source_target_pairs={{0,1},{1,2},{2,3},{3,128},{4,135},{5,4},{6,5},{7,6},{8,9},{9,10},{... | collective-permute-start | bytes 786440 | tf_op jit(solution)/shard_map/ppermute | solution.py:441
  49.1 5.4 %convolve.1 = (bf16[64,16,128]{2,1,0:T(8,128)(2,1)S(1)}, bf16[4,576,256]{2,1,0:T(8,128)(2,1)S(1)}, bf16[8,16,128]{2,1,0:T(8,128)(2,1)S(1)}, bf16[8,16,128]{2,1,0...) custom-call(s32[4]{0:T(128)S(1)} %pad_add_fusion.where_ref, ...), custom_call_target="tpu_custom_call" | custom-call | tf_op jit(solution)/shard_map/convolve/pallas_call | solution.py:257
  54.5 3.4 %complete.1 = bf16[64,48,128]{2,1,0:T(8,128)(2,1)} custom-call(bf16[64,16,128]{2,1,0:T(8,128)(2,1)S(1)} %get-tuple-element.43.back_grad_ref, bf16[4,576,256]{2,1,0:T(8,128)(2,1)S(1)} %get-tuple-element.44.rest_ref, f32[72,128]{1,0:T(8,128)S(1)} %get-tuple-element.38.cos_ref, f32[72,128]{1,0:T(8,128)S(1)} %get-tuple-element.39.sin_ref, ...), custom_call_target="tpu_custom_call" | custom-call | tf_op jit(solution)/shard_map/complete/pallas_call | solution.py:297
  57.9 11.4 %all-to-all-start.1 = ((bf16[64,48,128]{2,1,0:T(8,128)(2,1)}), bf16[64,48,128]{2,1,0:T(8,128)(2,1)S(1)}, u32[]{:S(2)}, u32[]{:S(2)}) async-start(bf16[64,48,128]{2,1,0:T(8,128)(2,1)} %complete.1), calls=%async_computation.1 | async-start | bytes 1572864 | tf_op jit(solution)/shard_map/all_to_all | solution.py:437
  69.3 2.6 %collective-permute-start.18 = (bf16[4,256,128]{2,1,0:T(8,128)(2,1)S(1)}, bf16[4,256,128]{2,1,0:T(8,128)(2,1)S(1)}, u32[]{:S(2)}, u32[]{:S(2)}) collective-permute-start(bf16[4,256,128]{2,1,0:T(8,128)(2,1)S(1)} %collective-permute-done.17.refs_11_), channel_id=1, source_target_pairs={{0,131},{1,0},{2,1},{3,2},{4,5},{5,6},{6,7},{7,132},{8,139},{9,8},... | collective-permute-start | bytes 786440 | tf_op jit(solution)/shard_map/ppermute | solution.py:441
  71.9 1.7 %collective-permute-start.1 = (bf16[8,16,128]{2,1,0:T(8,128)(2,1)S(1)}, bf16[8,16,128]{2,1,0:T(8,128)(2,1)S(1)}, u32[]{:S(2)}, u32[]{:S(2)}) collective-permute-start(bf16[8,16,128]{2,1,0:T(8,128)(2,1)S(1)} %get-tuple-element.51), channel_id=1, source_target_pairs={{0,32},{4,36},{8,40},{12,44},{16,48},{20,52},{24,56},{28,60},{32,0... | collective-permute-start | bytes 98312 | tf_op jit(solution)/shard_map/ppermute | solution.py:458
  73.6 0.2 collective-permute-start.2
  73.8 20.9 %collective-permute-done.18.refs_10_ = bf16[4,256,128]{2,1,0:T(8,128)(2,1)S(1)} collective-permute-done((bf16[4,256,128]{2,1,0:T(8,128)(2,1)S(1)}, bf16[4,256,128]{2,1,0:T(8,128)(2,1)S(1)}, u32[]{:S(2)}, u32[]{:S(2)}) %collective-permute-start.18) | collective-permute-done | bytes 262176 | tf_op jit(solution)/shard_map/ppermute | solution.py:441
  94.7 3.0 %collective-permute-start.3 = (bf16[8,16,128]{2,1,0:T(8,128)(2,1)S(1)}, bf16[8,16,128]{2,1,0:T(8,128)(2,1)S(1)}, u32[]{:S(2)}, u32[]{:S(2)}) collective-permute-start(bf16[8,16,128]{2,1,0:T(8,128)(2,1)S(1)} %get-tuple-element.53), channel_id=1, source_target_pairs={{0,64},{4,68},{8,72},{12,76},{16,80},{20,84},{24,88},{28,92},{32,9... | collective-permute-start | bytes 98312 | tf_op jit(solution)/shard_map/ppermute | solution.py:458
  97.7 2.7 %collective-permute-start.5 = (bf16[8,16,128]{2,1,0:T(8,128)(2,1)S(1)}, bf16[8,16,128]{2,1,0:T(8,128)(2,1)S(1)}, u32[]{:S(2)}, u32[]{:S(2)}) collective-permute-start(bf16[8,16,128]{2,1,0:T(8,128)(2,1)S(1)} %get-tuple-element.55), channel_id=1, source_target_pairs={{0,96},{4,100},{8,104},{12,108},{16,112},{20,116},{24,120},{28,124... | collective-permute-start | bytes 98312 | tf_op jit(solution)/shard_map/ppermute | solution.py:458
  100.4 0.5 collective-permute-start.6
  100.9 3.9 %collective-permute-start.16 = (bf16[4,256,128]{2,1,0:T(8,128)(2,1)S(1)}, bf16[4,256,128]{2,1,0:T(8,128)(2,1)S(1)}, u32[]{:S(2)}, u32[]{:S(2)}) collective-permute-start(bf16[4,256,128]{2,1,0:T(8,128)(2,1)S(1)} %collective-permute-done.14.refs_6_), channel_id=1, source_target_pairs={{0,2},{1,3},{2,128},{3,129},{4,134},{5,135},{6,4},{7,5},{8,10},{9,... | collective-permute-start | bytes 786440 | tf_op jit(solution)/shard_map/ppermute | solution.py:441
  104.8 0.1 collective-permute-done.6.refs_7_
  105.0 1.6 %collective-permute-start.7 = (bf16[8,8,16,128]{3,2,1,0:T(8,128)(2,1)S(1)}, bf16[8,8,16,128]{3,2,1,0:T(8,128)(2,1)S(1)}, u32[]{:S(2)}, u32[]{:S(2)}) collective-permute-start(bf16[8,8,16,128]{3,2,1,0:T(8,128)(2,1)S(1)} %bundle.1.refs_0_), channel_id=1, source_target_pairs={{0,8},{4,12},{8,16},{12,20},{16,24},{20,28},{24,0},{28,4},{32,40},... | collective-permute-start | bytes 786440 | tf_op jit(solution)/shard_map/ppermute | solution.py:462
  106.6 2.7 %collective-permute-start.8 = (bf16[8,8,16,128]{3,2,1,0:T(8,128)(2,1)S(1)}, bf16[8,8,16,128]{3,2,1,0:T(8,128)(2,1)S(1)}, u32[]{:S(2)}, u32[]{:S(2)}) collective-permute-start(bf16[8,8,16,128]{3,2,1,0:T(8,128)(2,1)S(1)} %bundle.1.refs_0_), channel_id=1, source_target_pairs={{0,16},{4,20},{8,24},{12,28},{16,0},{20,4},{24,8},{28,12},{32,48},... | collective-permute-start | bytes 786440 | tf_op jit(solution)/shard_map/ppermute | solution.py:462
  109.3 1.4 collective-permute-start.9
  110.7 2.5 %collective-permute-done.16.refs_8_ = bf16[4,256,128]{2,1,0:T(8,128)(2,1)S(1)} collective-permute-done((bf16[4,256,128]{2,1,0:T(8,128)(2,1)S(1)}, bf16[4,256,128]{2,1,0:T(8,128)(2,1)S(1)}, u32[]{:S(2)}, u32[]{:S(2)}) %collective-permute-start.16) | collective-permute-done | bytes 262176 | tf_op jit(solution)/shard_map/ppermute | solution.py:441
  113.2 1.2 collective-permute-done.19.refs_9_
  114.4 1.0 collective-permute-done.7.refs_1_
  115.5 6.6 %collective-permute-done.8.refs_2_ = bf16[8,8,16,128]{3,2,1,0:T(8,128)(2,1)S(1)} collective-permute-done((bf16[8,8,16,128]{3,2,1,0:T(8,128)(2,1)S(1)}, bf16[8,8,16,128]{3,2,1,0:T(8,128)(2,1)S(1)}, u32[]{:S(2)}, u32[]{:S(2)}) %collective-permute-start.8) | collective-permute-done | bytes 262176 | tf_op jit(solution)/shard_map/ppermute | solution.py:462
  122.0 2.1 %weight_parts.1 = (bf16[4,2,64,512]{3,2,1,0:T(8,128)(2,1)S(1)}, bf16[4,2,64,512]{3,2,1,0:T(8,128)(2,1)S(1)}) custom-call(s32[4]{0:T(128)S(1)} %pad_add_fusion.where_ref, bf16[8,8,16,128]{3,2,1,0:T(8,128)(2,1)S(1)} %bundle.1.refs_0_, bf16[8,8,16,128]{3,2,1,0:T(8,128)(2,1)S(1)} %collective-permute-done.7.refs_1_, ...), custom_call_target="tpu_custom_call" | custom-call | tf_op jit(solution)/shard_map/weight_parts/pallas_call | solution.py:384
  124.2 0.2 collective-permute-start.20
  124.4 1.8 %collective-permute-done.20.received_ref = bf16[4,2,64,512]{3,2,1,0:T(8,128)(2,1)S(1)} collective-permute-done((bf16[4,2,64,512]{3,2,1,0:T(8,128)(2,1)S(1)}, bf16[4,2,64,512]{3,2,1,0:T(8,128)(2,1)S(1)}, u32[]{:S(2)}, u32[]{:S(2)}) %collective-permute-start.20) | collective-permute-done | bytes 524320 | tf_op jit(solution)/shard_map/ppermute | solution.py:465
  126.2 0.1 join_cores.1
  126.3 0.4 collective-permute-start.21
  126.7 3.7 %collective-permute-start.22 = (bf16[2,64,512]{2,1,0:T(8,128)(2,1)S(1)}, bf16[2,64,512]{2,1,0:T(8,128)(2,1)S(1)}, u32[]{:S(2)}, u32[]{:S(2)}) collective-permute-start(bf16[2,64,512]{2,1,0:T(8,128)(2,1)S(1)} %get-tuple-element.65), channel_id=1, source_target_pairs={{0,64},{4,68},{8,72},{12,76},{16,80},{20,84},{24,88},{28,92},{32,9... | collective-permute-start | bytes 393224 | tf_op jit(solution)/shard_map/ppermute | solution.py:467
  130.5 0.6 collective-permute-start.23
  131.1 1.7 %collective-permute-done.21.refs_1_ = bf16[2,64,512]{2,1,0:T(8,128)(2,1)S(1)} collective-permute-done((bf16[2,64,512]{2,1,0:T(8,128)(2,1)S(1)}, bf16[2,64,512]{2,1,0:T(8,128)(2,1)S(1)}, u32[]{:S(2)}, u32[]{:S(2)}) %collective-permute-start.21) | collective-permute-done | bytes 131104 | tf_op jit(solution)/shard_map/ppermute | solution.py:467
  132.8 4.1 %collective-permute-done.22.refs_2_ = bf16[2,64,512]{2,1,0:T(8,128)(2,1)S(1)} collective-permute-done((bf16[2,64,512]{2,1,0:T(8,128)(2,1)S(1)}, bf16[2,64,512]{2,1,0:T(8,128)(2,1)S(1)}, u32[]{:S(2)}, u32[]{:S(2)}) %collective-permute-start.22) | collective-permute-done | bytes 131104 | tf_op jit(solution)/shard_map/ppermute | solution.py:467
  136.9 2.2 %collective-permute-done.23.refs_3_ = bf16[2,64,512]{2,1,0:T(8,128)(2,1)S(1)} collective-permute-done((bf16[2,64,512]{2,1,0:T(8,128)(2,1)S(1)}, bf16[2,64,512]{2,1,0:T(8,128)(2,1)S(1)}, u32[]{:S(2)}, u32[]{:S(2)}) %collective-permute-start.23) | collective-permute-done | bytes 131104 | tf_op jit(solution)/shard_map/ppermute | solution.py:467
  139.1 0.6 weight_total.1
  139.7 1.6 %collective-permute-start.24 = (bf16[64,512]{1,0:T(8,128)(2,1)S(1)}, bf16[64,512]{1,0:T(8,128)(2,1)S(1)}, u32[]{:S(2)}, u32[]{:S(2)}) collective-permute-start(bf16[64,512]{1,0:T(8,128)(2,1)S(1)} %get-tuple-element.68), channel_id=1, source_target_pairs={{0,128},{4,132},{8,136},{12,140},{16,144},{20,148},{24,152},{28,15... | collective-permute-start | bytes 196616 | tf_op jit(solution)/shard_map/ppermute | solution.py:469
  141.3 7.4 %collective-permute-done.24 = bf16[64,512]{1,0:T(8,128)(2,1)S(1)} collective-permute-done((bf16[64,512]{1,0:T(8,128)(2,1)S(1)}, bf16[64,512]{1,0:T(8,128)(2,1)S(1)}, u32[]{:S(2)}, u32[]{:S(2)}) %collective-permute-start.24) | collective-permute-done | bytes 65568 | tf_op jit(solution)/shard_map/ppermute | solution.py:469
  148.7 0.7 maximum_select_fusion
  149.5 1.3 finish.1
  (40 shorter events, 0.2 us)
Async XLA Ops:
  3.3 14.0 %copy-start.3 = (bf16[128,1024]{1,0:T(8,128)(2,1)S(1)}, bf16[128,1024]{1,0:T(8,128)(2,1)}, u32[]{:S(2)}) copy-start(bf16[128,1024]{1,0:T(8,128)(2,1)} %input_ref.1) | copy-start | bytes 786436
  3.3 45.7 %copy-start.4 = (bf16[512,256]{1,0:T(8,128)(2,1)S(1)}, bf16[512,256]{1,0:T(8,128)(2,1)}, u32[]{:S(2)}) copy-start(bf16[512,256]{1,0:T(8,128)(2,1)} %constant.84.clone.refs_3_) | copy-start | bytes 786436
  3.3 45.7 %copy-start.5 = (bf16[512,256]{1,0:T(8,128)(2,1)S(1)}, bf16[512,256]{1,0:T(8,128)(2,1)}, u32[]{:S(2)}) copy-start(bf16[512,256]{1,0:T(8,128)(2,1)} %constant.85.clone.refs_4_) | copy-start | bytes 786436
  3.3 45.7 %copy-start.6 = (bf16[128,144]{1,0:T(8,128)(2,1)S(1)}, bf16[128,144]{1,0:T(8,128)(2,1)}, u32[]{:S(2)}) copy-start(bf16[128,144]{1,0:T(8,128)(2,1)} %constant.86.clone.refs_5_) | copy-start | bytes 110596
  3.3 45.7 %copy-start.7 = (bf16[144,128]{1,0:T(8,128)(2,1)S(1)}, bf16[144,128]{1,0:T(8,128)(2,1)}, u32[]{:S(2)}) copy-start(bf16[144,128]{1,0:T(8,128)(2,1)} %constant.81.clone.refs_0_) | copy-start | bytes 110596
  3.3 45.7 %copy-start.8 = (f32[72,128]{1,0:T(8,128)S(1)}, f32[72,128]{1,0:T(8,128)}, u32[]{:S(2)}) copy-start(f32[72,128]{1,0:T(8,128)} %constant.82.clone.refs_1_) | copy-start | bytes 110596
  3.3 45.7 %copy-start.9 = (f32[72,128]{1,0:T(8,128)S(1)}, f32[72,128]{1,0:T(8,128)}, u32[]{:S(2)}) copy-start(f32[72,128]{1,0:T(8,128)} %constant.83.clone.refs_2_) | copy-start | bytes 110596
  3.3 45.8 %all-to-all-start = ((bf16[64,64,128]{2,1,0:T(8,128)(2,1)}), bf16[64,64,128]{2,1,0:T(8,128)(2,1)S(1)}, u32[]{:S(2)}, u32[]{:S(2)}) async-start(bf16[64,64,128]{2,1,0:T(8,128)(2,1)} %gather_signals.1), calls=%async_computation | async-start | bytes 2097152 | tf_op jit(solution)/shard_map/all_to_all | solution.py:437
  18.0 9.7 %collective-permute-start.12 = (bf16[256,128]{1,0:T(8,128)(2,1)S(1)}, bf16[256,128]{1,0:T(8,128)(2,1)S(1)}, u32[]{:S(2)}, u32[]{:S(2)}) collective-permute-start(bf16[256,128]{1,0:T(8,128)(2,1)S(1)} %get-tuple-element.60), channel_id=1, source_target_pairs={{0,24},{4,28},{8,0},{12,4},{16,8},{20,12},{24,16},{28,20},{32,56},... | collective-permute-start | bytes 196616 | tf_op jit(solution)/shard_map/ppermute | solution.py:450
  20.9 8.4 %collective-permute-start.11 = (bf16[256,128]{1,0:T(8,128)(2,1)S(1)}, bf16[256,128]{1,0:T(8,128)(2,1)S(1)}, u32[]{:S(2)}, u32[]{:S(2)}) collective-permute-start(bf16[256,128]{1,0:T(8,128)(2,1)S(1)} %get-tuple-element.59), channel_id=1, source_target_pairs={{0,16},{4,20},{8,24},{12,28},{16,0},{20,4},{24,8},{28,12},{32,48},... | collective-permute-start | bytes 196616 | tf_op jit(solution)/shard_map/ppermute | solution.py:450
  21.7 8.0 %collective-permute-start.10 = (bf16[256,128]{1,0:T(8,128)(2,1)S(1)}, bf16[256,128]{1,0:T(8,128)(2,1)S(1)}, u32[]{:S(2)}, u32[]{:S(2)}) collective-permute-start(bf16[256,128]{1,0:T(8,128)(2,1)S(1)} %get-tuple-element.58), channel_id=1, source_target_pairs={{0,8},{4,12},{8,16},{12,20},{16,24},{20,28},{24,0},{28,4},{32,40},... | collective-permute-start | bytes 196616 | tf_op jit(solution)/shard_map/ppermute | solution.py:450
  29.7 16.8 %collective-permute-start.13 = (bf16[4,256,128]{2,1,0:T(8,128)(2,1)S(1)}, bf16[4,256,128]{2,1,0:T(8,128)(2,1)S(1)}, u32[]{:S(2)}, u32[]{:S(2)}) collective-permute-start(bf16[4,256,128]{2,1,0:T(8,128)(2,1)S(1)} %pad_maximum_fusion.refs_4_), channel_id=1, source_target_pairs={{0,1},{1,2},{2,3},{3,128},{4,135},{5,4},{6,5},{7,6},{8,9},{9,10},{... | collective-permute-start | bytes 786440 | tf_op jit(solution)/shard_map/ppermute | solution.py:441
  30.8 38.5 %collective-permute-start.17 = (bf16[4,256,128]{2,1,0:T(8,128)(2,1)S(1)}, bf16[4,256,128]{2,1,0:T(8,128)(2,1)S(1)}, u32[]{:S(2)}, u32[]{:S(2)}) collective-permute-start(bf16[4,256,128]{2,1,0:T(8,128)(2,1)S(1)} %pad_maximum_fusion.refs_4_), channel_id=1, source_target_pairs={{0,131},{1,0},{2,1},{3,2},{4,5},{5,6},{6,7},{7,132},{8,139},{9,8},... | collective-permute-start | bytes 786440 | tf_op jit(solution)/shard_map/ppermute | solution.py:441
  46.5 25.4 %collective-permute-start.14 = (bf16[4,256,128]{2,1,0:T(8,128)(2,1)S(1)}, bf16[4,256,128]{2,1,0:T(8,128)(2,1)S(1)}, u32[]{:S(2)}, u32[]{:S(2)}) collective-permute-start(bf16[4,256,128]{2,1,0:T(8,128)(2,1)S(1)} %collective-permute-done.13.refs_5_), channel_id=1, source_target_pairs={{0,1},{1,2},{2,3},{3,128},{4,135},{5,4},{6,5},{7,6},{8,9},{9,10},{... | collective-permute-start | bytes 786440 | tf_op jit(solution)/shard_map/ppermute | solution.py:441
  57.9 91.5 %all-to-all-start.1 = ((bf16[64,48,128]{2,1,0:T(8,128)(2,1)}), bf16[64,48,128]{2,1,0:T(8,128)(2,1)S(1)}, u32[]{:S(2)}, u32[]{:S(2)}) async-start(bf16[64,48,128]{2,1,0:T(8,128)(2,1)} %complete.1), calls=%async_computation.1 | async-start | bytes 1572864 | tf_op jit(solution)/shard_map/all_to_all | solution.py:437
  69.3 25.4 %collective-permute-start.18 = (bf16[4,256,128]{2,1,0:T(8,128)(2,1)S(1)}, bf16[4,256,128]{2,1,0:T(8,128)(2,1)S(1)}, u32[]{:S(2)}, u32[]{:S(2)}) collective-permute-start(bf16[4,256,128]{2,1,0:T(8,128)(2,1)S(1)} %collective-permute-done.17.refs_11_), channel_id=1, source_target_pairs={{0,131},{1,0},{2,1},{3,2},{4,5},{5,6},{6,7},{7,132},{8,139},{9,8},... | collective-permute-start | bytes 786440 | tf_op jit(solution)/shard_map/ppermute | solution.py:441
  71.9 37.4 %collective-permute-start.15 = (bf16[4,256,128]{2,1,0:T(8,128)(2,1)S(1)}, bf16[4,256,128]{2,1,0:T(8,128)(2,1)S(1)}, u32[]{:S(2)}, u32[]{:S(2)}) collective-permute-start(bf16[4,256,128]{2,1,0:T(8,128)(2,1)S(1)} %collective-permute-done.14.refs_6_), channel_id=1, source_target_pairs={{0,1},{1,2},{2,3},{3,128},{4,135},{5,4},{6,5},{7,6},{8,9},{9,10},{... | collective-permute-start | bytes 786440 | tf_op jit(solution)/shard_map/ppermute | solution.py:441
  71.9 25.8 %collective-permute-start = (bf16[8,16,128]{2,1,0:T(8,128)(2,1)S(1)}, bf16[8,16,128]{2,1,0:T(8,128)(2,1)S(1)}, u32[]{:S(2)}, u32[]{:S(2)}) collective-permute-start(bf16[8,16,128]{2,1,0:T(8,128)(2,1)S(1)} %get-tuple-element.50), channel_id=1, source_target_pairs={{0,4},{4,0},{8,12},{12,8},{16,20},{20,16},{24,28},{28,24},{32,36},... | collective-permute-start | bytes 98312 | tf_op jit(solution)/shard_map/ppermute | solution.py:458
  71.9 25.8 %collective-permute-start.1 = (bf16[8,16,128]{2,1,0:T(8,128)(2,1)S(1)}, bf16[8,16,128]{2,1,0:T(8,128)(2,1)S(1)}, u32[]{:S(2)}, u32[]{:S(2)}) collective-permute-start(bf16[8,16,128]{2,1,0:T(8,128)(2,1)S(1)} %get-tuple-element.51), channel_id=1, source_target_pairs={{0,32},{4,36},{8,40},{12,44},{16,48},{20,52},{24,56},{28,60},{32,0... | collective-permute-start | bytes 98312 | tf_op jit(solution)/shard_map/ppermute | solution.py:458
  73.6 26.9 %collective-permute-start.2 = (bf16[8,16,128]{2,1,0:T(8,128)(2,1)S(1)}, bf16[8,16,128]{2,1,0:T(8,128)(2,1)S(1)}, u32[]{:S(2)}, u32[]{:S(2)}) collective-permute-start(bf16[8,16,128]{2,1,0:T(8,128)(2,1)S(1)} %get-tuple-element.52), channel_id=1, source_target_pairs={{0,36},{4,32},{8,44},{12,40},{16,52},{20,48},{24,60},{28,56},{32,4... | collective-permute-start | bytes 98312 | tf_op jit(solution)/shard_map/ppermute | solution.py:458
  94.7 6.2 %collective-permute-start.3 = (bf16[8,16,128]{2,1,0:T(8,128)(2,1)S(1)}, bf16[8,16,128]{2,1,0:T(8,128)(2,1)S(1)}, u32[]{:S(2)}, u32[]{:S(2)}) collective-permute-start(bf16[8,16,128]{2,1,0:T(8,128)(2,1)S(1)} %get-tuple-element.53), channel_id=1, source_target_pairs={{0,64},{4,68},{8,72},{12,76},{16,80},{20,84},{24,88},{28,92},{32,9... | collective-permute-start | bytes 98312 | tf_op jit(solution)/shard_map/ppermute | solution.py:458
  97.7 7.1 %collective-permute-start.4 = (bf16[8,16,128]{2,1,0:T(8,128)(2,1)S(1)}, bf16[8,16,128]{2,1,0:T(8,128)(2,1)S(1)}, u32[]{:S(2)}, u32[]{:S(2)}) collective-permute-start(bf16[8,16,128]{2,1,0:T(8,128)(2,1)S(1)} %get-tuple-element.54), channel_id=1, source_target_pairs={{0,68},{4,64},{8,76},{12,72},{16,84},{20,80},{24,92},{28,88},{32,1... | collective-permute-start | bytes 98312 | tf_op jit(solution)/shard_map/ppermute | solution.py:458
  97.7 7.1 %collective-permute-start.5 = (bf16[8,16,128]{2,1,0:T(8,128)(2,1)S(1)}, bf16[8,16,128]{2,1,0:T(8,128)(2,1)S(1)}, u32[]{:S(2)}, u32[]{:S(2)}) collective-permute-start(bf16[8,16,128]{2,1,0:T(8,128)(2,1)S(1)} %get-tuple-element.55), channel_id=1, source_target_pairs={{0,96},{4,100},{8,104},{12,108},{16,112},{20,116},{24,120},{28,124... | collective-permute-start | bytes 98312 | tf_op jit(solution)/shard_map/ppermute | solution.py:458
  100.4 4.6 %collective-permute-start.6 = (bf16[8,16,128]{2,1,0:T(8,128)(2,1)S(1)}, bf16[8,16,128]{2,1,0:T(8,128)(2,1)S(1)}, u32[]{:S(2)}, u32[]{:S(2)}) collective-permute-start(bf16[8,16,128]{2,1,0:T(8,128)(2,1)S(1)} %get-tuple-element.56), channel_id=1, source_target_pairs={{0,100},{4,96},{8,108},{12,104},{16,116},{20,112},{24,124},{28,120... | collective-permute-start | bytes 98312 | tf_op jit(solution)/shard_map/ppermute | solution.py:458
  100.9 12.3 %collective-permute-start.16 = (bf16[4,256,128]{2,1,0:T(8,128)(2,1)S(1)}, bf16[4,256,128]{2,1,0:T(8,128)(2,1)S(1)}, u32[]{:S(2)}, u32[]{:S(2)}) collective-permute-start(bf16[4,256,128]{2,1,0:T(8,128)(2,1)S(1)} %collective-permute-done.14.refs_6_), channel_id=1, source_target_pairs={{0,2},{1,3},{2,128},{3,129},{4,134},{5,135},{6,4},{7,5},{8,10},{9,... | collective-permute-start | bytes 786440 | tf_op jit(solution)/shard_map/ppermute | solution.py:441
  104.8 9.6 %collective-permute-start.19 = (bf16[4,256,128]{2,1,0:T(8,128)(2,1)S(1)}, bf16[4,256,128]{2,1,0:T(8,128)(2,1)S(1)}, u32[]{:S(2)}, u32[]{:S(2)}) collective-permute-start(bf16[4,256,128]{2,1,0:T(8,128)(2,1)S(1)} %collective-permute-done.18.refs_10_), channel_id=1, source_target_pairs={{0,131},{1,0},{2,1},{3,2},{4,5},{5,6},{6,7},{7,132},{8,139},{9,8},... | collective-permute-start | bytes 786440 | tf_op jit(solution)/shard_map/ppermute | solution.py:441
  105.0 10.5 %collective-permute-start.7 = (bf16[8,8,16,128]{3,2,1,0:T(8,128)(2,1)S(1)}, bf16[8,8,16,128]{3,2,1,0:T(8,128)(2,1)S(1)}, u32[]{:S(2)}, u32[]{:S(2)}) collective-permute-start(bf16[8,8,16,128]{3,2,1,0:T(8,128)(2,1)S(1)} %bundle.1.refs_0_), channel_id=1, source_target_pairs={{0,8},{4,12},{8,16},{12,20},{16,24},{20,28},{24,0},{28,4},{32,40},... | collective-permute-start | bytes 786440 | tf_op jit(solution)/shard_map/ppermute | solution.py:462
  106.6 15.5 %collective-permute-start.8 = (bf16[8,8,16,128]{3,2,1,0:T(8,128)(2,1)S(1)}, bf16[8,8,16,128]{3,2,1,0:T(8,128)(2,1)S(1)}, u32[]{:S(2)}, u32[]{:S(2)}) collective-permute-start(bf16[8,8,16,128]{3,2,1,0:T(8,128)(2,1)S(1)} %bundle.1.refs_0_), channel_id=1, source_target_pairs={{0,16},{4,20},{8,24},{12,28},{16,0},{20,4},{24,8},{28,12},{32,48},... | collective-permute-start | bytes 786440 | tf_op jit(solution)/shard_map/ppermute | solution.py:462
  109.3 12.8 %collective-permute-start.9 = (bf16[8,8,16,128]{3,2,1,0:T(8,128)(2,1)S(1)}, bf16[8,8,16,128]{3,2,1,0:T(8,128)(2,1)S(1)}, u32[]{:S(2)}, u32[]{:S(2)}) collective-permute-start(bf16[8,8,16,128]{3,2,1,0:T(8,128)(2,1)S(1)} %bundle.1.refs_0_), channel_id=1, source_target_pairs={{0,24},{4,28},{8,0},{12,4},{16,8},{20,12},{24,16},{28,20},{32,56},... | collective-permute-start | bytes 786440 | tf_op jit(solution)/shard_map/ppermute | solution.py:462
  124.2 25.3 %copy-start = (bf16[128,1024]{1,0:T(8,128)(2,1)S(1)}, bf16[128,1024]{1,0:T(8,128)(2,1)}, u32[]{:S(2)}) copy-start(bf16[128,1024]{1,0:T(8,128)(2,1)} %key_ref.3) | copy-start | bytes 786436
  124.2 25.3 %copy-start.1 = (bf16[128,1024]{1,0:T(8,128)(2,1)S(1)}, bf16[128,1024]{1,0:T(8,128)(2,1)}, u32[]{:S(2)}) copy-start(bf16[128,1024]{1,0:T(8,128)(2,1)} %value_ref.3) | copy-start | bytes 786436
  124.2 25.3 %copy-start.2 = (bf16[128,1024]{1,0:T(8,128)(2,1)S(1)}, bf16[128,1024]{1,0:T(8,128)(2,1)}, u32[]{:S(2)}) copy-start(bf16[128,1024]{1,0:T(8,128)(2,1)} %grad_ref.3) | copy-start | bytes 786436
  124.2 2.0 %collective-permute-start.20 = (bf16[4,2,64,512]{3,2,1,0:T(8,128)(2,1)S(1)}, bf16[4,2,64,512]{3,2,1,0:T(8,128)(2,1)S(1)}, u32[]{:S(2)}, u32[]{:S(2)}) collective-permute-start(bf16[4,2,64,512]{3,2,1,0:T(8,128)(2,1)S(1)} %get-tuple-element.62), channel_id=1, source_target_pairs={{0,4},{4,0},{8,12},{12,8},{16,20},{20,16},{24,28},{28,24},{32,36},... | collective-permute-start | bytes 1572872 | tf_op jit(solution)/shard_map/ppermute | solution.py:465
  126.3 6.5 %collective-permute-start.21 = (bf16[2,64,512]{2,1,0:T(8,128)(2,1)S(1)}, bf16[2,64,512]{2,1,0:T(8,128)(2,1)S(1)}, u32[]{:S(2)}, u32[]{:S(2)}) collective-permute-start(bf16[2,64,512]{2,1,0:T(8,128)(2,1)S(1)} %get-tuple-element.64), channel_id=1, source_target_pairs={{0,32},{4,36},{8,40},{12,44},{16,48},{20,52},{24,56},{28,60},{32,0... | collective-permute-start | bytes 393224 | tf_op jit(solution)/shard_map/ppermute | solution.py:467
  126.7 10.2 %collective-permute-start.22 = (bf16[2,64,512]{2,1,0:T(8,128)(2,1)S(1)}, bf16[2,64,512]{2,1,0:T(8,128)(2,1)S(1)}, u32[]{:S(2)}, u32[]{:S(2)}) collective-permute-start(bf16[2,64,512]{2,1,0:T(8,128)(2,1)S(1)} %get-tuple-element.65), channel_id=1, source_target_pairs={{0,64},{4,68},{8,72},{12,76},{16,80},{20,84},{24,88},{28,92},{32,9... | collective-permute-start | bytes 393224 | tf_op jit(solution)/shard_map/ppermute | solution.py:467
  130.5 8.6 %collective-permute-start.23 = (bf16[2,64,512]{2,1,0:T(8,128)(2,1)S(1)}, bf16[2,64,512]{2,1,0:T(8,128)(2,1)S(1)}, u32[]{:S(2)}, u32[]{:S(2)}) collective-permute-start(bf16[2,64,512]{2,1,0:T(8,128)(2,1)S(1)} %get-tuple-element.66), channel_id=1, source_target_pairs={{0,96},{4,100},{8,104},{12,108},{16,112},{20,116},{24,120},{28,124... | collective-permute-start | bytes 393224 | tf_op jit(solution)/shard_map/ppermute | solution.py:467
  139.7 9.0 %collective-permute-start.24 = (bf16[64,512]{1,0:T(8,128)(2,1)S(1)}, bf16[64,512]{1,0:T(8,128)(2,1)S(1)}, u32[]{:S(2)}, u32[]{:S(2)}) collective-permute-start(bf16[64,512]{1,0:T(8,128)(2,1)S(1)} %get-tuple-element.68), channel_id=1, source_target_pairs={{0,128},{4,132},{8,136},{12,140},{16,144},{20,148},{24,152},{28,15... | collective-permute-start | bytes 196616 | tf_op jit(solution)/shard_map/ppermute | solution.py:469

commit v9 on v8

--- a/solution.py
+++ b/solution.py
@@ -166,7 +166,7 @@
     where_ref, signals_ref, first_ref, cos_ref, sin_ref, ahead_ref, back_ref, last_ref,
     out_ref, rest_ref, *refs,
 ):
-    pieces, (wide_in, wide_out, wide_value, sorted_value) = refs[:8], refs[8:]
+    pieces, (wide_in, wide_out, wide_value, sorted_value) = refs[:4], refs[4:]
     wide_in[...] = signals_ref[...].astype(jnp.float32).reshape(BLOCKS * SENT, ROWS)
 
     def step(index, carry):
@@ -250,7 +250,8 @@
         z, y, x, core = block // 32, block // 8 % 4, block // 2 % 4, block % 2
         sorted_value[y * 2 + core, z * 4 + x] = tile
     for flip, piece in enumerate(pieces):
-        piece[...] = sorted_value[where_ref[2] ^ flip]
+        for other in range(2):
+            piece[other] = sorted_value[where_ref[2] ^ (2 * flip + other)]
 
 
 def convolve(where, signals, tables):
@@ -260,7 +261,7 @@
             jax.ShapeDtypeStruct((BLOCKS, CHANNELS, ROWS), jnp.bfloat16),
             jax.ShapeDtypeStruct((CHANNELS // UNROLL, 2 * UNROLL * KEPT, 256), jnp.bfloat16),
         )
-        + (jax.ShapeDtypeStruct((8, CHANNELS, ROWS), jnp.bfloat16),) * 8,
+        + (jax.ShapeDtypeStruct((2, 8, CHANNELS, ROWS), jnp.bfloat16),) * 4,
         in_specs=[pl.BlockSpec(memory_space=pltpu.SMEM)] + [pl.BlockSpec(memory_space=pltpu.VMEM)] * 7,
         scratch_shapes=[
             pltpu.VMEM((BLOCKS * SENT, ROWS), jnp.float32),
@@ -325,18 +326,35 @@
     )
 
 
-def bundle_body(*refs):
-    for n, piece in enumerate(refs[:8]):
-        refs[8][n] = piece[...]
-
-
-def bundle(pieces):
+def sort_body(*refs):
+    pieces, (kept_ref, sent_ref) = refs[:4], refs[4:]
+    for n, piece in enumerate(pieces):
+        kept_ref[n] = piece[0]
+        sent_ref[n] = piece[1]
+
+
+def sort_cores(pieces):
+    return pl.pallas_call(
+        sort_body,
+        out_shape=(jax.ShapeDtypeStruct((4, 8, CHANNELS, ROWS), jnp.bfloat16),) * 2,
+        name="sort_cores",
+        compiler_params=pltpu.CompilerParams(vmem_limit_bytes=VMEM_GRANT),
+    )(*pieces)
+
+
+def bundle_body(kept_ref, received_ref, out_ref):
+    for n in range(4):
+        out_ref[2 * n] = kept_ref[n]
+        out_ref[2 * n + 1] = received_ref[n]
+
+
+def bundle(kept, received):
     return pl.pallas_call(
         bundle_body,
         out_shape=jax.ShapeDtypeStruct((8, 8, CHANNELS, ROWS), jnp.bfloat16),
         name="bundle",
         compiler_params=pltpu.CompilerParams(vmem_limit_bytes=VMEM_GRANT),
-    )(*pieces)
+    )(kept, received)
 
 
 def weight_body(where_ref, *refs):
@@ -455,10 +473,12 @@
     signals = exchange(sent)
     up2, down2 = ring_step(up, 1), ring_step(down, -1)
     back_grad, rest, *pieces = convolve(where, signals, tables)
-    pieces = pieces[:1] + [lax.ppermute(pieces[n], "seq", across(n)) for n in range(1, 8)]
+    pieces = pieces[:1] + [lax.ppermute(pieces[n], "seq", across(2 * n)) for n in range(1, 4)]
+    kept, sent = sort_cores(pieces)
+    received = lax.ppermute(sent, "seq", across(1))
     up3, down3, far = ring_step(up2, 1), ring_step(down2, -1), ring_step(up2, 2)
     results = complete(back_grad, rest, tables)
-    value = bundle(pieces)
+    value = bundle(kept, received)
     values = [value] + [lax.ppermute(value, "seq", along_x(n)) for n in range(1, 4)]
     results = exchange(results)
     kept, sent = weight_parts(where, values, (own, up, up2, up3, far, down3, down2, down))

time: 152 us -> 143 us (0.941)
  the two profiles are of different devices: /device:TPU:32 before, /device:TPU:2 now
where the time goes in v9:
time: 143 us
  waiting for transfers between devices  62.7 us (44%)
  starting transfers between devices  62.2 us (43%)
  Pallas kernels  16.4 us (11%)
    all_to_all x2, starting transfers between devices, exchange(): return lax.all_to_all(array, 'seq', split_axis=0, concat_axis=0, tiled=True)  26.1 us
    ppermute x7, waiting for transfers between devices, ring_step(): return lax.ppermute(array, ('seq', 'chan'), along_z(shift))  23.7 us
    ppermute x7, starting transfers between devices, ring_step(): return lax.ppermute(array, ('seq', 'chan'), along_z(shift))  15.4 us
    ppermute x3, waiting for transfers between devices, shards(): lax.ppermute(value, 'seq', along_x(n))  8.76 us
    ppermute x3, waiting for transfers between devices, shards(): lax.ppermute(parts[n], 'seq', across(2 * n))  8.25 us
    ppermute x3, waiting for transfers between devices, shards(): own = [lax.ppermute(pieces[n], 'seq', along_x(n)) for n in range(1, 4)]  7.79 us
    ppermute x1, waiting for transfers between devices, shards(): received = lax.ppermute(sent, 'seq', opposite()).astype(jnp.float32)  7.08 us
    pallas_call x1, Pallas kernels, convolve(): pl.pallas_call(convolve_body, out_shape=(jax.ShapeDtypeStruct((BLOCKS, CH...  5.44 us
  transfers between devices with their start and end apart: 24, of which 16 were waited for; matrix products, arithmetic and copies ran while one was open for 1% of the time, Pallas kernels for 9%

profile of v9, /device:TPU:2, one launch (start us, length us, event | category | flops | bytes accessed | tf_op | source)
XLA Modules:
  0.0 143.1 jit_solution(4893337554357269898)
XLA Ops:
  0.6 2.6 %gather_signals.1 = bf16[64,64,128]{2,1,0:T(8,128)(2,1)} custom-call(bf16[128,1024]{1,0:T(8,128)(2,1)} %key_ref.3, bf16[128,1024]{1,0:T(8,128)(2,1)} %value_ref.3, bf16[128,1024]{1,0:T(8,128)(2,1)} %grad_ref.3, bf16[128,1024]{1,0:T(8,128)(2,1)} %query_ref.1, bf16[128,1024]{1,0:T(8,128)(2,1)} %taps_ref.1), custom_call_target="tpu_custom_call" | custom-call | tf_op jit(solution)/shard_map/gather_signals/pallas_call | solution.py:99
  3.3 14.8 %all-to-all-start = ((bf16[64,64,128]{2,1,0:T(8,128)(2,1)}), bf16[64,64,128]{2,1,0:T(8,128)(2,1)S(1)}, u32[]{:S(2)}, u32[]{:S(2)}) async-start(bf16[64,64,128]{2,1,0:T(8,128)(2,1)} %gather_signals.1), calls=%async_computation | async-start | bytes 2097152 | tf_op jit(solution)/shard_map/all_to_all | solution.py:455
  18.2 0.1 pad_add_fusion.where_ref
  18.3 0.7 split_features.1
  19.0 0.5 collective-permute-start.9
  19.5 2.5 %collective-permute-start.8 = (bf16[256,128]{1,0:T(8,128)(2,1)S(1)}, bf16[256,128]{1,0:T(8,128)(2,1)S(1)}, u32[]{:S(2)}, u32[]{:S(2)}) collective-permute-start(bf16[256,128]{1,0:T(8,128)(2,1)S(1)} %get-tuple-element.55), channel_id=1, source_target_pairs={{0,16},{4,20},{8,24},{12,28},{16,0},{20,4},{24,8},{28,12},{32,48},... | collective-permute-start | bytes 196616 | tf_op jit(solution)/shard_map/ppermute | solution.py:468
  22.0 1.8 %collective-permute-start.7 = (bf16[256,128]{1,0:T(8,128)(2,1)S(1)}, bf16[256,128]{1,0:T(8,128)(2,1)S(1)}, u32[]{:S(2)}, u32[]{:S(2)}) collective-permute-start(bf16[256,128]{1,0:T(8,128)(2,1)S(1)} %get-tuple-element.54), channel_id=1, source_target_pairs={{0,8},{4,12},{8,16},{12,20},{16,24},{20,28},{24,0},{28,4},{32,40},... | collective-permute-start | bytes 196616 | tf_op jit(solution)/shard_map/ppermute | solution.py:468
  23.8 5.1 %collective-permute-done.9 = bf16[256,128]{1,0:T(8,128)(2,1)S(1)} collective-permute-done((bf16[256,128]{1,0:T(8,128)(2,1)S(1)}, bf16[256,128]{1,0:T(8,128)(2,1)S(1)}, u32[]{:S(2)}, u32[]{:S(2)}) %collective-permute-start.9) | collective-permute-done | bytes 65568 | tf_op jit(solution)/shard_map/ppermute | solution.py:468
  28.9 2.7 %collective-permute-done.8 = bf16[256,128]{1,0:T(8,128)(2,1)S(1)} collective-permute-done((bf16[256,128]{1,0:T(8,128)(2,1)S(1)}, bf16[256,128]{1,0:T(8,128)(2,1)S(1)}, u32[]{:S(2)}, u32[]{:S(2)}) %collective-permute-start.8) | collective-permute-done | bytes 65568 | tf_op jit(solution)/shard_map/ppermute | solution.py:468
  31.6 0.1 collective-permute-start.10
  31.7 7.7 %collective-permute-start.14 = (bf16[4,256,128]{2,1,0:T(8,128)(2,1)S(1)}, bf16[4,256,128]{2,1,0:T(8,128)(2,1)S(1)}, u32[]{:S(2)}, u32[]{:S(2)}) collective-permute-start(bf16[4,256,128]{2,1,0:T(8,128)(2,1)S(1)} %pad_maximum_fusion.refs_4_), channel_id=1, source_target_pairs={{0,131},{1,0},{2,1},{3,2},{4,5},{5,6},{6,7},{7,132},{8,139},{9,8},... | collective-permute-start | bytes 786440 | tf_op jit(solution)/shard_map/ppermute | solution.py:459
  39.4 12.1 %collective-permute-done.10.refs_5_ = bf16[4,256,128]{2,1,0:T(8,128)(2,1)S(1)} collective-permute-done((bf16[4,256,128]{2,1,0:T(8,128)(2,1)S(1)}, bf16[4,256,128]{2,1,0:T(8,128)(2,1)S(1)}, u32[]{:S(2)}, u32[]{:S(2)}) %collective-permute-start.10) | collective-permute-done | bytes 262176 | tf_op jit(solution)/shard_map/ppermute | solution.py:459
  51.6 5.4 %convolve.1 = (bf16[64,16,128]{2,1,0:T(8,128)(2,1)S(1)}, bf16[4,576,256]{2,1,0:T(8,128)(2,1)S(1)}, bf16[2,8,16,128]{3,2,1,0:T(8,128)(2,1)S(1)}, bf16[2,8,16,128]...) custom-call(s32[4]{0:T(128)S(1)} %pad_add_fusion.where_ref, ...), custom_call_target="tpu_custom_call" | custom-call | tf_op jit(solution)/shard_map/convolve/pallas_call | solution.py:258
  57.1 3.4 %complete.1 = bf16[64,48,128]{2,1,0:T(8,128)(2,1)} custom-call(bf16[64,16,128]{2,1,0:T(8,128)(2,1)S(1)} %get-tuple-element.41.back_grad_ref, bf16[4,576,256]{2,1,0:T(8,128)(2,1)S(1)} %get-tuple-element.42.rest_ref, f32[72,128]{1,0:T(8,128)S(1)} %get-tuple-element.36.cos_ref, f32[72,128]{1,0:T(8,128)S(1)} %get-tuple-element.37.sin_ref, ...), custom_call_target="tpu_custom_call" | custom-call | tf_op jit(solution)/shard_map/complete/pallas_call | solution.py:298
  60.4 11.3 %all-to-all-start.1 = ((bf16[64,48,128]{2,1,0:T(8,128)(2,1)}), bf16[64,48,128]{2,1,0:T(8,128)(2,1)S(1)}, u32[]{:S(2)}, u32[]{:S(2)}) async-start(bf16[64,48,128]{2,1,0:T(8,128)(2,1)} %complete.1), calls=%async_computation.1 | async-start | bytes 1572864 | tf_op jit(solution)/shard_map/all_to_all | solution.py:455
  71.8 4.8 %collective-permute-start.15 = (bf16[4,256,128]{2,1,0:T(8,128)(2,1)S(1)}, bf16[4,256,128]{2,1,0:T(8,128)(2,1)S(1)}, u32[]{:S(2)}, u32[]{:S(2)}) collective-permute-start(bf16[4,256,128]{2,1,0:T(8,128)(2,1)S(1)} %collective-permute-done.14.refs_11_), channel_id=1, source_target_pairs={{0,131},{1,0},{2,1},{3,2},{4,5},{5,6},{6,7},{7,132},{8,139},{9,8},... | collective-permute-start | bytes 786440 | tf_op jit(solution)/shard_map/ppermute | solution.py:459
  76.6 1.5 %collective-permute-start = (bf16[2,8,16,128]{3,2,1,0:T(8,128)(2,1)S(1)}, bf16[2,8,16,128]{3,2,1,0:T(8,128)(2,1)S(1)}, u32[]{:S(2)}, u32[]{:S(2)}) collective-permute-start(bf16[2,8,16,128]{3,2,1,0:T(8,128)(2,1)S(1)} %get-tuple-element.48), channel_id=1, source_target_pairs={{0,32},{4,36},{8,40},{12,44},{16,48},{20,52},{24,56},{28,60},{32,0... | collective-permute-start | bytes 196616 | tf_op jit(solution)/shard_map/ppermute | solution.py:476
  78.1 2.8 %collective-permute-start.1 = (bf16[2,8,16,128]{3,2,1,0:T(8,128)(2,1)S(1)}, bf16[2,8,16,128]{3,2,1,0:T(8,128)(2,1)S(1)}, u32[]{:S(2)}, u32[]{:S(2)}) collective-permute-start(bf16[2,8,16,128]{3,2,1,0:T(8,128)(2,1)S(1)} %get-tuple-element.49), channel_id=1, source_target_pairs={{0,64},{4,68},{8,72},{12,76},{16,80},{20,84},{24,88},{28,92},{32,9... | collective-permute-start | bytes 196616 | tf_op jit(solution)/shard_map/ppermute | solution.py:476
  80.9 0.4 collective-permute-start.2
  81.3 2.4 %collective-permute-done.refs_1_ = bf16[2,8,16,128]{3,2,1,0:T(8,128)(2,1)S(1)} collective-permute-done((bf16[2,8,16,128]{3,2,1,0:T(8,128)(2,1)S(1)}, bf16[2,8,16,128]{3,2,1,0:T(8,128)(2,1)S(1)}, u32[]{:S(2)}, u32[]{:S(2)}) %collective-permute-start) | collective-permute-done | bytes 65568 | tf_op jit(solution)/shard_map/ppermute | solution.py:476
  83.7 1.2 collective-permute-done.1.refs_2_
  84.9 1.6 %collective-permute-done.2.refs_3_ = bf16[2,8,16,128]{3,2,1,0:T(8,128)(2,1)S(1)} collective-permute-done((bf16[2,8,16,128]{3,2,1,0:T(8,128)(2,1)S(1)}, bf16[2,8,16,128]{3,2,1,0:T(8,128)(2,1)S(1)}, u32[]{:S(2)}, u32[]{:S(2)}) %collective-permute-start.2) | collective-permute-done | bytes 65568 | tf_op jit(solution)/shard_map/ppermute | solution.py:476
  86.5 0.3 collective-permute-start.3
  86.8 0.1 collective-permute-start.13
  86.9 8.3 %collective-permute-done.15.refs_10_ = bf16[4,256,128]{2,1,0:T(8,128)(2,1)S(1)} collective-permute-done((bf16[4,256,128]{2,1,0:T(8,128)(2,1)S(1)}, bf16[4,256,128]{2,1,0:T(8,128)(2,1)S(1)}, u32[]{:S(2)}, u32[]{:S(2)}) %collective-permute-start.15) | collective-permute-done | bytes 262176 | tf_op jit(solution)/shard_map/ppermute | solution.py:459
  95.2 2.7 %collective-permute-start.16 = (bf16[4,256,128]{2,1,0:T(8,128)(2,1)S(1)}, bf16[4,256,128]{2,1,0:T(8,128)(2,1)S(1)}, u32[]{:S(2)}, u32[]{:S(2)}) collective-permute-start(bf16[4,256,128]{2,1,0:T(8,128)(2,1)S(1)} %collective-permute-done.15.refs_10_), channel_id=1, source_target_pairs={{0,131},{1,0},{2,1},{3,2},{4,5},{5,6},{6,7},{7,132},{8,139},{9,8},... | collective-permute-start | bytes 786440 | tf_op jit(solution)/shard_map/ppermute | solution.py:459
  97.9 1.5 %collective-permute-start.4 = (bf16[8,8,16,128]{3,2,1,0:T(8,128)(2,1)S(1)}, bf16[8,8,16,128]{3,2,1,0:T(8,128)(2,1)S(1)}, u32[]{:S(2)}, u32[]{:S(2)}) collective-permute-start(bf16[8,8,16,128]{3,2,1,0:T(8,128)(2,1)S(1)} %bundle.1.refs_0_), channel_id=1, source_target_pairs={{0,8},{4,12},{8,16},{12,20},{16,24},{20,28},{24,0},{28,4},{32,40},... | collective-permute-start | bytes 786440 | tf_op jit(solution)/shard_map/ppermute | solution.py:482
  99.4 0.7 collective-permute-start.5
  100.1 2.5 %collective-permute-start.6 = (bf16[8,8,16,128]{3,2,1,0:T(8,128)(2,1)S(1)}, bf16[8,8,16,128]{3,2,1,0:T(8,128)(2,1)S(1)}, u32[]{:S(2)}, u32[]{:S(2)}) collective-permute-start(bf16[8,8,16,128]{3,2,1,0:T(8,128)(2,1)S(1)} %bundle.1.refs_0_), channel_id=1, source_target_pairs={{0,24},{4,28},{8,0},{12,4},{16,8},{20,12},{24,16},{28,20},{32,56},... | collective-permute-start | bytes 786440 | tf_op jit(solution)/shard_map/ppermute | solution.py:482
  102.7 3.3 %collective-permute-done.13.refs_8_ = bf16[4,256,128]{2,1,0:T(8,128)(2,1)S(1)} collective-permute-done((bf16[4,256,128]{2,1,0:T(8,128)(2,1)S(1)}, bf16[4,256,128]{2,1,0:T(8,128)(2,1)S(1)}, u32[]{:S(2)}, u32[]{:S(2)}) %collective-permute-start.13) | collective-permute-done | bytes 262176 | tf_op jit(solution)/shard_map/ppermute | solution.py:459
  105.9 1.2 collective-permute-done.4.refs_1_
  107.1 3.0 %collective-permute-done.5.refs_2_ = bf16[8,8,16,128]{3,2,1,0:T(8,128)(2,1)S(1)} collective-permute-done((bf16[8,8,16,128]{3,2,1,0:T(8,128)(2,1)S(1)}, bf16[8,8,16,128]{3,2,1,0:T(8,128)(2,1)S(1)}, u32[]{:S(2)}, u32[]{:S(2)}) %collective-permute-start.5) | collective-permute-done | bytes 262176 | tf_op jit(solution)/shard_map/ppermute | solution.py:482
  110.2 4.5 %collective-permute-done.6.refs_3_ = bf16[8,8,16,128]{3,2,1,0:T(8,128)(2,1)S(1)} collective-permute-done((bf16[8,8,16,128]{3,2,1,0:T(8,128)(2,1)S(1)}, bf16[8,8,16,128]{3,2,1,0:T(8,128)(2,1)S(1)}, u32[]{:S(2)}, u32[]{:S(2)}) %collective-permute-start.6) | collective-permute-done | bytes 262176 | tf_op jit(solution)/shard_map/ppermute | solution.py:482
  114.7 2.1 %weight_parts.1 = (bf16[4,2,64,512]{3,2,1,0:T(8,128)(2,1)S(1)}, bf16[4,2,64,512]{3,2,1,0:T(8,128)(2,1)S(1)}) custom-call(s32[4]{0:T(128)S(1)} %pad_add_fusion.where_ref, bf16[8,8,16,128]{3,2,1,0:T(8,128)(2,1)S(1)} %bundle.1.refs_0_, bf16[8,8,16,128]{3,2,1,0:T(8,128)(2,1)S(1)} %collective-permute-done.4.refs_1_, ...), custom_call_target="tpu_custom_call" | custom-call | tf_op jit(solution)/shard_map/weight_parts/pallas_call | solution.py:402
  116.9 0.1 collective-permute-start.17
  117.0 1.9 %collective-permute-done.17.received_ref = bf16[4,2,64,512]{3,2,1,0:T(8,128)(2,1)S(1)} collective-permute-done((bf16[4,2,64,512]{3,2,1,0:T(8,128)(2,1)S(1)}, bf16[4,2,64,512]{3,2,1,0:T(8,128)(2,1)S(1)}, u32[]{:S(2)}, u32[]{:S(2)}) %collective-permute-start.17) | collective-permute-done | bytes 524320 | tf_op jit(solution)/shard_map/ppermute | solution.py:485
  118.9 0.1 join_cores.1
  119.0 1.6 %collective-permute-start.18 = (bf16[2,64,512]{2,1,0:T(8,128)(2,1)S(1)}, bf16[2,64,512]{2,1,0:T(8,128)(2,1)S(1)}, u32[]{:S(2)}, u32[]{:S(2)}) collective-permute-start(bf16[2,64,512]{2,1,0:T(8,128)(2,1)S(1)} %get-tuple-element.60), channel_id=1, source_target_pairs={{0,32},{4,36},{8,40},{12,44},{16,48},{20,52},{24,56},{28,60},{32,0... | collective-permute-start | bytes 393224 | tf_op jit(solution)/shard_map/ppermute | solution.py:487
  120.6 2.8 %collective-permute-start.19 = (bf16[2,64,512]{2,1,0:T(8,128)(2,1)S(1)}, bf16[2,64,512]{2,1,0:T(8,128)(2,1)S(1)}, u32[]{:S(2)}, u32[]{:S(2)}) collective-permute-start(bf16[2,64,512]{2,1,0:T(8,128)(2,1)S(1)} %get-tuple-element.61), channel_id=1, source_target_pairs={{0,64},{4,68},{8,72},{12,76},{16,80},{20,84},{24,88},{28,92},{32,9... | collective-permute-start | bytes 393224 | tf_op jit(solution)/shard_map/ppermute | solution.py:487
  123.4 0.4 collective-permute-start.20
  123.8 1.5 %collective-permute-done.18.refs_1_ = bf16[2,64,512]{2,1,0:T(8,128)(2,1)S(1)} collective-permute-done((bf16[2,64,512]{2,1,0:T(8,128)(2,1)S(1)}, bf16[2,64,512]{2,1,0:T(8,128)(2,1)S(1)}, u32[]{:S(2)}, u32[]{:S(2)}) %collective-permute-start.18) | collective-permute-done | bytes 131104 | tf_op jit(solution)/shard_map/ppermute | solution.py:487
  125.2 4.6 %collective-permute-done.19.refs_2_ = bf16[2,64,512]{2,1,0:T(8,128)(2,1)S(1)} collective-permute-done((bf16[2,64,512]{2,1,0:T(8,128)(2,1)S(1)}, bf16[2,64,512]{2,1,0:T(8,128)(2,1)S(1)}, u32[]{:S(2)}, u32[]{:S(2)}) %collective-permute-start.19) | collective-permute-done | bytes 131104 | tf_op jit(solution)/shard_map/ppermute | solution.py:487
  129.8 2.2 %collective-permute-done.20.refs_3_ = bf16[2,64,512]{2,1,0:T(8,128)(2,1)S(1)} collective-permute-done((bf16[2,64,512]{2,1,0:T(8,128)(2,1)S(1)}, bf16[2,64,512]{2,1,0:T(8,128)(2,1)S(1)}, u32[]{:S(2)}, u32[]{:S(2)}) %collective-permute-start.20) | collective-permute-done | bytes 131104 | tf_op jit(solution)/shard_map/ppermute | solution.py:487
  132.0 0.6 weight_total.1
  132.7 1.3 collective-permute-start.21
  134.0 7.1 %collective-permute-done.21 = bf16[64,512]{1,0:T(8,128)(2,1)S(1)} collective-permute-done((bf16[64,512]{1,0:T(8,128)(2,1)S(1)}, bf16[64,512]{1,0:T(8,128)(2,1)S(1)}, u32[]{:S(2)}, u32[]{:S(2)}) %collective-permute-start.21) | collective-permute-done | bytes 65568 | tf_op jit(solution)/shard_map/ppermute | solution.py:489
  141.1 0.7 maximum_select_fusion
  141.8 1.3 finish.1
  (35 shorter events, 0.2 us)
Async XLA Ops:
  3.3 15.0 %copy-start.3 = (bf16[128,1024]{1,0:T(8,128)(2,1)S(1)}, bf16[128,1024]{1,0:T(8,128)(2,1)}, u32[]{:S(2)}) copy-start(bf16[128,1024]{1,0:T(8,128)(2,1)} %input_ref.1) | copy-start | bytes 786436
  3.3 48.2 %copy-start.4 = (bf16[512,256]{1,0:T(8,128)(2,1)S(1)}, bf16[512,256]{1,0:T(8,128)(2,1)}, u32[]{:S(2)}) copy-start(bf16[512,256]{1,0:T(8,128)(2,1)} %constant.84.clone.refs_3_) | copy-start | bytes 786436
  3.3 48.3 %copy-start.5 = (bf16[512,256]{1,0:T(8,128)(2,1)S(1)}, bf16[512,256]{1,0:T(8,128)(2,1)}, u32[]{:S(2)}) copy-start(bf16[512,256]{1,0:T(8,128)(2,1)} %constant.85.clone.refs_4_) | copy-start | bytes 786436
  3.3 48.3 %copy-start.6 = (bf16[128,144]{1,0:T(8,128)(2,1)S(1)}, bf16[128,144]{1,0:T(8,128)(2,1)}, u32[]{:S(2)}) copy-start(bf16[128,144]{1,0:T(8,128)(2,1)} %constant.86.clone.refs_5_) | copy-start | bytes 110596
  3.3 48.3 %copy-start.7 = (bf16[144,128]{1,0:T(8,128)(2,1)S(1)}, bf16[144,128]{1,0:T(8,128)(2,1)}, u32[]{:S(2)}) copy-start(bf16[144,128]{1,0:T(8,128)(2,1)} %constant.81.clone.refs_0_) | copy-start | bytes 110596
  3.3 48.3 %copy-start.8 = (f32[72,128]{1,0:T(8,128)S(1)}, f32[72,128]{1,0:T(8,128)}, u32[]{:S(2)}) copy-start(f32[72,128]{1,0:T(8,128)} %constant.82.clone.refs_1_) | copy-start | bytes 110596
  3.3 48.3 %copy-start.9 = (f32[72,128]{1,0:T(8,128)S(1)}, f32[72,128]{1,0:T(8,128)}, u32[]{:S(2)}) copy-start(f32[72,128]{1,0:T(8,128)} %constant.83.clone.refs_2_) | copy-start | bytes 110596
  3.3 48.3 %all-to-all-start = ((bf16[64,64,128]{2,1,0:T(8,128)(2,1)}), bf16[64,64,128]{2,1,0:T(8,128)(2,1)S(1)}, u32[]{:S(2)}, u32[]{:S(2)}) async-start(bf16[64,64,128]{2,1,0:T(8,128)(2,1)} %gather_signals.1), calls=%async_computation | async-start | bytes 2097152 | tf_op jit(solution)/shard_map/all_to_all | solution.py:455
  19.0 9.9 %collective-permute-start.9 = (bf16[256,128]{1,0:T(8,128)(2,1)S(1)}, bf16[256,128]{1,0:T(8,128)(2,1)S(1)}, u32[]{:S(2)}, u32[]{:S(2)}) collective-permute-start(bf16[256,128]{1,0:T(8,128)(2,1)S(1)} %get-tuple-element.56), channel_id=1, source_target_pairs={{0,24},{4,28},{8,0},{12,4},{16,8},{20,12},{24,16},{28,20},{32,56},... | collective-permute-start | bytes 196616 | tf_op jit(solution)/shard_map/ppermute | solution.py:468
  19.5 12.0 %collective-permute-start.8 = (bf16[256,128]{1,0:T(8,128)(2,1)S(1)}, bf16[256,128]{1,0:T(8,128)(2,1)S(1)}, u32[]{:S(2)}, u32[]{:S(2)}) collective-permute-start(bf16[256,128]{1,0:T(8,128)(2,1)S(1)} %get-tuple-element.55), channel_id=1, source_target_pairs={{0,16},{4,20},{8,24},{12,28},{16,0},{20,4},{24,8},{28,12},{32,48},... | collective-permute-start | bytes 196616 | tf_op jit(solution)/shard_map/ppermute | solution.py:468
  22.0 9.6 %collective-permute-start.7 = (bf16[256,128]{1,0:T(8,128)(2,1)S(1)}, bf16[256,128]{1,0:T(8,128)(2,1)S(1)}, u32[]{:S(2)}, u32[]{:S(2)}) collective-permute-start(bf16[256,128]{1,0:T(8,128)(2,1)S(1)} %get-tuple-element.54), channel_id=1, source_target_pairs={{0,8},{4,12},{8,16},{12,20},{16,24},{20,28},{24,0},{28,4},{32,40},... | collective-permute-start | bytes 196616 | tf_op jit(solution)/shard_map/ppermute | solution.py:468
  31.6 19.9 %collective-permute-start.10 = (bf16[4,256,128]{2,1,0:T(8,128)(2,1)S(1)}, bf16[4,256,128]{2,1,0:T(8,128)(2,1)S(1)}, u32[]{:S(2)}, u32[]{:S(2)}) collective-permute-start(bf16[4,256,128]{2,1,0:T(8,128)(2,1)S(1)} %pad_maximum_fusion.refs_4_), channel_id=1, source_target_pairs={{0,1},{1,2},{2,3},{3,128},{4,135},{5,4},{6,5},{7,6},{8,9},{9,10},{... | collective-permute-start | bytes 786440 | tf_op jit(solution)/shard_map/ppermute | solution.py:459
  31.7 40.1 %collective-permute-start.14 = (bf16[4,256,128]{2,1,0:T(8,128)(2,1)S(1)}, bf16[4,256,128]{2,1,0:T(8,128)(2,1)S(1)}, u32[]{:S(2)}, u32[]{:S(2)}) collective-permute-start(bf16[4,256,128]{2,1,0:T(8,128)(2,1)S(1)} %pad_maximum_fusion.refs_4_), channel_id=1, source_target_pairs={{0,131},{1,0},{2,1},{3,2},{4,5},{5,6},{6,7},{7,132},{8,139},{9,8},... | collective-permute-start | bytes 786440 | tf_op jit(solution)/shard_map/ppermute | solution.py:459
  51.5 25.0 %collective-permute-start.11 = (bf16[4,256,128]{2,1,0:T(8,128)(2,1)S(1)}, bf16[4,256,128]{2,1,0:T(8,128)(2,1)S(1)}, u32[]{:S(2)}, u32[]{:S(2)}) collective-permute-start(bf16[4,256,128]{2,1,0:T(8,128)(2,1)S(1)} %collective-permute-done.10.refs_5_), channel_id=1, source_target_pairs={{0,1},{1,2},{2,3},{3,128},{4,135},{5,4},{6,5},{7,6},{8,9},{9,10},{... | collective-permute-start | bytes 786440 | tf_op jit(solution)/shard_map/ppermute | solution.py:459
  60.4 81.4 %all-to-all-start.1 = ((bf16[64,48,128]{2,1,0:T(8,128)(2,1)}), bf16[64,48,128]{2,1,0:T(8,128)(2,1)S(1)}, u32[]{:S(2)}, u32[]{:S(2)}) async-start(bf16[64,48,128]{2,1,0:T(8,128)(2,1)} %complete.1), calls=%async_computation.1 | async-start | bytes 1572864 | tf_op jit(solution)/shard_map/all_to_all | solution.py:455
  71.8 23.4 %collective-permute-start.15 = (bf16[4,256,128]{2,1,0:T(8,128)(2,1)S(1)}, bf16[4,256,128]{2,1,0:T(8,128)(2,1)S(1)}, u32[]{:S(2)}, u32[]{:S(2)}) collective-permute-start(bf16[4,256,128]{2,1,0:T(8,128)(2,1)S(1)} %collective-permute-done.14.refs_11_), channel_id=1, source_target_pairs={{0,131},{1,0},{2,1},{3,2},{4,5},{5,6},{6,7},{7,132},{8,139},{9,8},... | collective-permute-start | bytes 786440 | tf_op jit(solution)/shard_map/ppermute | solution.py:459
  76.6 23.6 %collective-permute-start.12 = (bf16[4,256,128]{2,1,0:T(8,128)(2,1)S(1)}, bf16[4,256,128]{2,1,0:T(8,128)(2,1)S(1)}, u32[]{:S(2)}, u32[]{:S(2)}) collective-permute-start(bf16[4,256,128]{2,1,0:T(8,128)(2,1)S(1)} %collective-permute-done.11.refs_6_), channel_id=1, source_target_pairs={{0,1},{1,2},{2,3},{3,128},{4,135},{5,4},{6,5},{7,6},{8,9},{9,10},{... | collective-permute-start | bytes 786440 | tf_op jit(solution)/shard_map/ppermute | solution.py:459
  76.6 7.1 %collective-permute-start = (bf16[2,8,16,128]{3,2,1,0:T(8,128)(2,1)S(1)}, bf16[2,8,16,128]{3,2,1,0:T(8,128)(2,1)S(1)}, u32[]{:S(2)}, u32[]{:S(2)}) collective-permute-start(bf16[2,8,16,128]{3,2,1,0:T(8,128)(2,1)S(1)} %get-tuple-element.48), channel_id=1, source_target_pairs={{0,32},{4,36},{8,40},{12,44},{16,48},{20,52},{24,56},{28,60},{32,0... | collective-permute-start | bytes 196616 | tf_op jit(solution)/shard_map/ppermute | solution.py:476
  78.1 6.8 %collective-permute-start.1 = (bf16[2,8,16,128]{3,2,1,0:T(8,128)(2,1)S(1)}, bf16[2,8,16,128]{3,2,1,0:T(8,128)(2,1)S(1)}, u32[]{:S(2)}, u32[]{:S(2)}) collective-permute-start(bf16[2,8,16,128]{3,2,1,0:T(8,128)(2,1)S(1)} %get-tuple-element.49), channel_id=1, source_target_pairs={{0,64},{4,68},{8,72},{12,76},{16,80},{20,84},{24,88},{28,92},{32,9... | collective-permute-start | bytes 196616 | tf_op jit(solution)/shard_map/ppermute | solution.py:476
  80.9 5.6 %collective-permute-start.2 = (bf16[2,8,16,128]{3,2,1,0:T(8,128)(2,1)S(1)}, bf16[2,8,16,128]{3,2,1,0:T(8,128)(2,1)S(1)}, u32[]{:S(2)}, u32[]{:S(2)}) collective-permute-start(bf16[2,8,16,128]{3,2,1,0:T(8,128)(2,1)S(1)} %get-tuple-element.50), channel_id=1, source_target_pairs={{0,96},{4,100},{8,104},{12,108},{16,112},{20,116},{24,120},{28,124... | collective-permute-start | bytes 196616 | tf_op jit(solution)/shard_map/ppermute | solution.py:476
  86.5 11.4 %collective-permute-start.3 = (bf16[4,8,16,128]{3,2,1,0:T(8,128)(2,1)S(1)}, bf16[4,8,16,128]{3,2,1,0:T(8,128)(2,1)S(1)}, u32[]{:S(2)}, u32[]{:S(2)}) collective-permute-start(bf16[4,8,16,128]{3,2,1,0:T(8,128)(2,1)S(1)} %get-tuple-element.52), channel_id=1, source_target_pairs={{0,4},{4,0},{8,12},{12,8},{16,20},{20,16},{24,28},{28,24},{32,36},... | collective-permute-start | bytes 393224 | tf_op jit(solution)/shard_map/ppermute | solution.py:478
  86.8 19.1 %collective-permute-start.13 = (bf16[4,256,128]{2,1,0:T(8,128)(2,1)S(1)}, bf16[4,256,128]{2,1,0:T(8,128)(2,1)S(1)}, u32[]{:S(2)}, u32[]{:S(2)}) collective-permute-start(bf16[4,256,128]{2,1,0:T(8,128)(2,1)S(1)} %collective-permute-done.11.refs_6_), channel_id=1, source_target_pairs={{0,2},{1,3},{2,128},{3,129},{4,134},{5,135},{6,4},{7,5},{8,10},{9,... | collective-permute-start | bytes 786440 | tf_op jit(solution)/shard_map/ppermute | solution.py:459
  95.2 10.8 %collective-permute-start.16 = (bf16[4,256,128]{2,1,0:T(8,128)(2,1)S(1)}, bf16[4,256,128]{2,1,0:T(8,128)(2,1)S(1)}, u32[]{:S(2)}, u32[]{:S(2)}) collective-permute-start(bf16[4,256,128]{2,1,0:T(8,128)(2,1)S(1)} %collective-permute-done.15.refs_10_), channel_id=1, source_target_pairs={{0,131},{1,0},{2,1},{3,2},{4,5},{5,6},{6,7},{7,132},{8,139},{9,8},... | collective-permute-start | bytes 786440 | tf_op jit(solution)/shard_map/ppermute | solution.py:459
  97.9 9.3 %collective-permute-start.4 = (bf16[8,8,16,128]{3,2,1,0:T(8,128)(2,1)S(1)}, bf16[8,8,16,128]{3,2,1,0:T(8,128)(2,1)S(1)}, u32[]{:S(2)}, u32[]{:S(2)}) collective-permute-start(bf16[8,8,16,128]{3,2,1,0:T(8,128)(2,1)S(1)} %bundle.1.refs_0_), channel_id=1, source_target_pairs={{0,8},{4,12},{8,16},{12,20},{16,24},{20,28},{24,0},{28,4},{32,40},... | collective-permute-start | bytes 786440 | tf_op jit(solution)/shard_map/ppermute | solution.py:482
  99.4 10.7 %collective-permute-start.5 = (bf16[8,8,16,128]{3,2,1,0:T(8,128)(2,1)S(1)}, bf16[8,8,16,128]{3,2,1,0:T(8,128)(2,1)S(1)}, u32[]{:S(2)}, u32[]{:S(2)}) collective-permute-start(bf16[8,8,16,128]{3,2,1,0:T(8,128)(2,1)S(1)} %bundle.1.refs_0_), channel_id=1, source_target_pairs={{0,16},{4,20},{8,24},{12,28},{16,0},{20,4},{24,8},{28,12},{32,48},... | collective-permute-start | bytes 786440 | tf_op jit(solution)/shard_map/ppermute | solution.py:482
  100.1 14.6 %collective-permute-start.6 = (bf16[8,8,16,128]{3,2,1,0:T(8,128)(2,1)S(1)}, bf16[8,8,16,128]{3,2,1,0:T(8,128)(2,1)S(1)}, u32[]{:S(2)}, u32[]{:S(2)}) collective-permute-start(bf16[8,8,16,128]{3,2,1,0:T(8,128)(2,1)S(1)} %bundle.1.refs_0_), channel_id=1, source_target_pairs={{0,24},{4,28},{8,0},{12,4},{16,8},{20,12},{24,16},{28,20},{32,56},... | collective-permute-start | bytes 786440 | tf_op jit(solution)/shard_map/ppermute | solution.py:482
  116.8 25.0 %copy-start = (bf16[128,1024]{1,0:T(8,128)(2,1)S(1)}, bf16[128,1024]{1,0:T(8,128)(2,1)}, u32[]{:S(2)}) copy-start(bf16[128,1024]{1,0:T(8,128)(2,1)} %key_ref.3) | copy-start | bytes 786436
  116.8 25.0 %copy-start.1 = (bf16[128,1024]{1,0:T(8,128)(2,1)S(1)}, bf16[128,1024]{1,0:T(8,128)(2,1)}, u32[]{:S(2)}) copy-start(bf16[128,1024]{1,0:T(8,128)(2,1)} %value_ref.3) | copy-start | bytes 786436
  116.9 25.0 %copy-start.2 = (bf16[128,1024]{1,0:T(8,128)(2,1)S(1)}, bf16[128,1024]{1,0:T(8,128)(2,1)}, u32[]{:S(2)}) copy-start(bf16[128,1024]{1,0:T(8,128)(2,1)} %grad_ref.3) | copy-start | bytes 786436
  116.9 2.0 %collective-permute-start.17 = (bf16[4,2,64,512]{3,2,1,0:T(8,128)(2,1)S(1)}, bf16[4,2,64,512]{3,2,1,0:T(8,128)(2,1)S(1)}, u32[]{:S(2)}, u32[]{:S(2)}) collective-permute-start(bf16[4,2,64,512]{3,2,1,0:T(8,128)(2,1)S(1)} %get-tuple-element.58), channel_id=1, source_target_pairs={{0,4},{4,0},{8,12},{12,8},{16,20},{20,16},{24,28},{28,24},{32,36},... | collective-permute-start | bytes 1572872 | tf_op jit(solution)/shard_map/ppermute | solution.py:485
  119.0 6.2 %collective-permute-start.18 = (bf16[2,64,512]{2,1,0:T(8,128)(2,1)S(1)}, bf16[2,64,512]{2,1,0:T(8,128)(2,1)S(1)}, u32[]{:S(2)}, u32[]{:S(2)}) collective-permute-start(bf16[2,64,512]{2,1,0:T(8,128)(2,1)S(1)} %get-tuple-element.60), channel_id=1, source_target_pairs={{0,32},{4,36},{8,40},{12,44},{16,48},{20,52},{24,56},{28,60},{32,0... | collective-permute-start | bytes 393224 | tf_op jit(solution)/shard_map/ppermute | solution.py:487
  120.6 9.2 %collective-permute-start.19 = (bf16[2,64,512]{2,1,0:T(8,128)(2,1)S(1)}, bf16[2,64,512]{2,1,0:T(8,128)(2,1)S(1)}, u32[]{:S(2)}, u32[]{:S(2)}) collective-permute-start(bf16[2,64,512]{2,1,0:T(8,128)(2,1)S(1)} %get-tuple-element.61), channel_id=1, source_target_pairs={{0,64},{4,68},{8,72},{12,76},{16,80},{20,84},{24,88},{28,92},{32,9... | collective-permute-start | bytes 393224 | tf_op jit(solution)/shard_map/ppermute | solution.py:487
  123.4 8.6 %collective-permute-start.20 = (bf16[2,64,512]{2,1,0:T(8,128)(2,1)S(1)}, bf16[2,64,512]{2,1,0:T(8,128)(2,1)S(1)}, u32[]{:S(2)}, u32[]{:S(2)}) collective-permute-start(bf16[2,64,512]{2,1,0:T(8,128)(2,1)S(1)} %get-tuple-element.62), channel_id=1, source_target_pairs={{0,96},{4,100},{8,104},{12,108},{16,112},{20,116},{24,120},{28,124... | collective-permute-start | bytes 393224 | tf_op jit(solution)/shard_map/ppermute | solution.py:487
  132.7 8.4 %collective-permute-start.21 = (bf16[64,512]{1,0:T(8,128)(2,1)S(1)}, bf16[64,512]{1,0:T(8,128)(2,1)S(1)}, u32[]{:S(2)}, u32[]{:S(2)}) collective-permute-start(bf16[64,512]{1,0:T(8,128)(2,1)S(1)} %get-tuple-element.64), channel_id=1, source_target_pairs={{0,128},{4,132},{8,136},{12,140},{16,144},{20,148},{24,152},{28,15... | collective-permute-start | bytes 196616 | tf_op jit(solution)/shard_map/ppermute | solution.py:489

commit v10 on v9

--- a/solution.py
+++ b/solution.py
@@ -140,7 +140,7 @@
     )(where, layer_input)
 
 
-UNROLL = 4
+UNROLL = 8
 
 
 def invert(pairs, number, cosine, sine, back_ref, last_ref):
@@ -476,15 +476,18 @@
     pieces = pieces[:1] + [lax.ppermute(pieces[n], "seq", across(2 * n)) for n in range(1, 4)]
     kept, sent = sort_cores(pieces)
     received = lax.ppermute(sent, "seq", across(1))
-    up3, down3, far = ring_step(up2, 1), ring_step(down2, -1), ring_step(up2, 2)
+    up3, down3 = ring_step(up2, 1), ring_step(down2, -1)
+    far = ring_step(up2, 2)
     results = complete(back_grad, rest, tables)
     value = bundle(kept, received)
-    values = [value] + [lax.ppermute(value, "seq", along_x(n)) for n in range(1, 4)]
+    right, left = (lax.ppermute(value, "seq", along_x(n)) for n in (1, 3))
+    values = [value, right, lax.ppermute(value, "seq", along_x(2)), left]
     results = exchange(results)
     kept, sent = weight_parts(where, values, (own, up, up2, up3, far, down3, down2, down))
     received = lax.ppermute(sent, "seq", across(1))
     parts = join_cores(kept, received)
-    parts = [parts[0]] + [lax.ppermute(parts[n], "seq", across(2 * n)) for n in range(1, 4)]
+    near = [lax.ppermute(parts[n], "seq", across(2 * n)) for n in (1, 3)]
+    parts = [parts[0], lax.ppermute(parts[2], "seq", across(4)), *near]
     kept, sent = weight_total(where, parts)
     received = lax.ppermute(sent, "seq", opposite()).astype(jnp.float32)
     grad_query, grad_key, grad_value, grad_filter = finish(results, grad_out, value_proj, gate_key)

time: 143 us -> 140 us (0.979)
  the two profiles are of different devices: /device:TPU:2 before, /device:TPU:16 now
where the time goes in v10:
time: 140 us
  waiting for transfers between devices  63.8 us (46%)
  starting transfers between devices  59.2 us (42%)
  Pallas kernels  15.1 us (11%)
    all_to_all x2, starting transfers between devices, exchange(): return lax.all_to_all(array, 'seq', split_axis=0, concat_axis=0, tiled=True)  25.8 us
    ppermute x7, waiting for transfers between devices, ring_step(): return lax.ppermute(array, ('seq', 'chan'), along_z(shift))  23.7 us
    ppermute x7, starting transfers between devices, ring_step(): return lax.ppermute(array, ('seq', 'chan'), along_z(shift))  14 us
    ppermute x3, waiting for transfers between devices, shards(): own = [lax.ppermute(pieces[n], 'seq', along_x(n)) for n in range(1, 4)]  10.3 us
    ppermute x1, waiting for transfers between devices, shards(): received = lax.ppermute(sent, 'seq', opposite()).astype(jnp.float32)  8.24 us
    ppermute x1, waiting for transfers between devices, shards(): values = [value, right, lax.ppermute(value, 'seq', along_x(2)), left]  6.56 us
    ppermute x3, waiting for transfers between devices, shards(): lax.ppermute(pieces[n], 'seq', across(2 * n))  5.27 us
    pallas_call x1, Pallas kernels, convolve(): pl.pallas_call(convolve_body, out_shape=(jax.ShapeDtypeStruct((BLOCKS, CH...  4.68 us
  transfers between devices with their start and end apart: 24, of which 16 were waited for; matrix products, arithmetic and copies ran while one was open for 1% of the time, Pallas kernels for 8%

profile of v10, /device:TPU:16, one launch (start us, length us, event | category | flops | bytes accessed | tf_op | source)
XLA Modules:
  0.0 139.9 jit_solution(3730094928879464554)
XLA Ops:
  0.6 2.6 %gather_signals.1 = bf16[64,64,128]{2,1,0:T(8,128)(2,1)} custom-call(bf16[128,1024]{1,0:T(8,128)(2,1)} %key_ref.3, bf16[128,1024]{1,0:T(8,128)(2,1)} %value_ref.3, bf16[128,1024]{1,0:T(8,128)(2,1)} %grad_ref.3, bf16[128,1024]{1,0:T(8,128)(2,1)} %query_ref.1, bf16[128,1024]{1,0:T(8,128)(2,1)} %taps_ref.1), custom_call_target="tpu_custom_call" | custom-call | tf_op jit(solution)/shard_map/gather_signals/pallas_call | solution.py:99
  3.3 14.6 %all-to-all-start = ((bf16[64,64,128]{2,1,0:T(8,128)(2,1)}), bf16[64,64,128]{2,1,0:T(8,128)(2,1)S(1)}, u32[]{:S(2)}, u32[]{:S(2)}) async-start(bf16[64,64,128]{2,1,0:T(8,128)(2,1)} %gather_signals.1), calls=%async_computation | async-start | bytes 2097152 | tf_op jit(solution)/shard_map/all_to_all | solution.py:455
  18.0 0.1 pad_add_fusion.where_ref
  18.1 0.7 split_features.1
  18.8 2.8 %collective-permute-start.9 = (bf16[256,128]{1,0:T(8,128)(2,1)S(1)}, bf16[256,128]{1,0:T(8,128)(2,1)S(1)}, u32[]{:S(2)}, u32[]{:S(2)}) collective-permute-start(bf16[256,128]{1,0:T(8,128)(2,1)S(1)} %get-tuple-element.56), channel_id=1, source_target_pairs={{0,24},{4,28},{8,0},{12,4},{16,8},{20,12},{24,16},{28,20},{32,56},... | collective-permute-start | bytes 196616 | tf_op jit(solution)/shard_map/ppermute | solution.py:468
  21.6 0.8 collective-permute-start.8
  22.4 0.9 collective-permute-start.7
  23.3 7.1 %collective-permute-done.9 = bf16[256,128]{1,0:T(8,128)(2,1)S(1)} collective-permute-done((bf16[256,128]{1,0:T(8,128)(2,1)S(1)}, bf16[256,128]{1,0:T(8,128)(2,1)S(1)}, u32[]{:S(2)}, u32[]{:S(2)}) %collective-permute-start.9) | collective-permute-done | bytes 65568 | tf_op jit(solution)/shard_map/ppermute | solution.py:468
  30.3 1.7 %collective-permute-done.8 = bf16[256,128]{1,0:T(8,128)(2,1)S(1)} collective-permute-done((bf16[256,128]{1,0:T(8,128)(2,1)S(1)}, bf16[256,128]{1,0:T(8,128)(2,1)S(1)}, u32[]{:S(2)}, u32[]{:S(2)}) %collective-permute-start.8) | collective-permute-done | bytes 65568 | tf_op jit(solution)/shard_map/ppermute | solution.py:468
  32.0 1.5 %collective-permute-done.7 = bf16[256,128]{1,0:T(8,128)(2,1)S(1)} collective-permute-done((bf16[256,128]{1,0:T(8,128)(2,1)S(1)}, bf16[256,128]{1,0:T(8,128)(2,1)S(1)}, u32[]{:S(2)}, u32[]{:S(2)}) %collective-permute-start.7) | collective-permute-done | bytes 65568 | tf_op jit(solution)/shard_map/ppermute | solution.py:468
  33.6 0.1 collective-permute-start.10
  33.7 6.3 %collective-permute-start.14 = (bf16[4,256,128]{2,1,0:T(8,128)(2,1)S(1)}, bf16[4,256,128]{2,1,0:T(8,128)(2,1)S(1)}, u32[]{:S(2)}, u32[]{:S(2)}) collective-permute-start(bf16[4,256,128]{2,1,0:T(8,128)(2,1)S(1)} %pad_maximum_fusion.refs_4_), channel_id=1, source_target_pairs={{0,131},{1,0},{2,1},{3,2},{4,5},{5,6},{6,7},{7,132},{8,139},{9,8},... | collective-permute-start | bytes 786440 | tf_op jit(solution)/shard_map/ppermute | solution.py:459
  40.0 11.5 %collective-permute-done.10.refs_5_ = bf16[4,256,128]{2,1,0:T(8,128)(2,1)S(1)} collective-permute-done((bf16[4,256,128]{2,1,0:T(8,128)(2,1)S(1)}, bf16[4,256,128]{2,1,0:T(8,128)(2,1)S(1)}, u32[]{:S(2)}, u32[]{:S(2)}) %collective-permute-start.10) | collective-permute-done | bytes 262176 | tf_op jit(solution)/shard_map/ppermute | solution.py:459
  51.6 4.7 %convolve.1 = (bf16[64,16,128]{2,1,0:T(8,128)(2,1)S(1)}, bf16[2,1152,256]{2,1,0:T(8,128)(2,1)S(1)}, bf16[2,8,16,128]{3,2,1,0:T(8,128)(2,1)S(1)}, bf16[2,8,16,128...) custom-call(s32[4]{0:T(128)S(1)} %pad_add_fusion.where_ref, ...), custom_call_target="tpu_custom_call" | custom-call | tf_op jit(solution)/shard_map/convolve/pallas_call | solution.py:258
  56.3 2.8 %complete.1 = bf16[64,48,128]{2,1,0:T(8,128)(2,1)} custom-call(bf16[64,16,128]{2,1,0:T(8,128)(2,1)S(1)} %get-tuple-element.41.back_grad_ref, bf16[2,1152,256]{2,1,0:T(8,128)(2,1)S(1)} %get-tuple-element.42.rest_ref, f32[72,128]{1,0:T(8,128)S(1)} %get-tuple-element.36.cos_ref, f32[72,128]{1,0:T(8,128)S(1)} %get-tuple-element.37.sin_ref, ...), custom_call_target="tpu_custom_call" | custom-call | tf_op jit(solution)/shard_map/complete/pallas_call | solution.py:298
  59.1 11.2 %all-to-all-start.1 = ((bf16[64,48,128]{2,1,0:T(8,128)(2,1)}), bf16[64,48,128]{2,1,0:T(8,128)(2,1)S(1)}, u32[]{:S(2)}, u32[]{:S(2)}) async-start(bf16[64,48,128]{2,1,0:T(8,128)(2,1)} %complete.1), calls=%async_computation.1 | async-start | bytes 1572864 | tf_op jit(solution)/shard_map/all_to_all | solution.py:455
  70.3 4.9 %collective-permute-start.15 = (bf16[4,256,128]{2,1,0:T(8,128)(2,1)S(1)}, bf16[4,256,128]{2,1,0:T(8,128)(2,1)S(1)}, u32[]{:S(2)}, u32[]{:S(2)}) collective-permute-start(bf16[4,256,128]{2,1,0:T(8,128)(2,1)S(1)} %collective-permute-done.14.refs_11_), channel_id=1, source_target_pairs={{0,131},{1,0},{2,1},{3,2},{4,5},{5,6},{6,7},{7,132},{8,139},{9,8},... | collective-permute-start | bytes 786440 | tf_op jit(solution)/shard_map/ppermute | solution.py:459
  75.2 1.2 collective-permute-start
  76.4 0.7 collective-permute-start.1
  77.1 1.5 %collective-permute-start.2 = (bf16[2,8,16,128]{3,2,1,0:T(8,128)(2,1)S(1)}, bf16[2,8,16,128]{3,2,1,0:T(8,128)(2,1)S(1)}, u32[]{:S(2)}, u32[]{:S(2)}) collective-permute-start(bf16[2,8,16,128]{3,2,1,0:T(8,128)(2,1)S(1)} %get-tuple-element.50), channel_id=1, source_target_pairs={{0,96},{4,100},{8,104},{12,108},{16,112},{20,116},{24,120},{28,124... | collective-permute-start | bytes 196616 | tf_op jit(solution)/shard_map/ppermute | solution.py:476
  78.7 2.8 %collective-permute-done.refs_1_ = bf16[2,8,16,128]{3,2,1,0:T(8,128)(2,1)S(1)} collective-permute-done((bf16[2,8,16,128]{3,2,1,0:T(8,128)(2,1)S(1)}, bf16[2,8,16,128]{3,2,1,0:T(8,128)(2,1)S(1)}, u32[]{:S(2)}, u32[]{:S(2)}) %collective-permute-start) | collective-permute-done | bytes 65568 | tf_op jit(solution)/shard_map/ppermute | solution.py:476
  81.5 1.8 %collective-permute-done.1.refs_2_ = bf16[2,8,16,128]{3,2,1,0:T(8,128)(2,1)S(1)} collective-permute-done((bf16[2,8,16,128]{3,2,1,0:T(8,128)(2,1)S(1)}, bf16[2,8,16,128]{3,2,1,0:T(8,128)(2,1)S(1)}, u32[]{:S(2)}, u32[]{:S(2)}) %collective-permute-start.1) | collective-permute-done | bytes 65568 | tf_op jit(solution)/shard_map/ppermute | solution.py:476
  83.2 0.7 collective-permute-done.2.refs_3_
  84.0 0.1 collective-permute-start.3
  84.1 0.1 collective-permute-start.13
  84.1 9.5 %collective-permute-done.15.refs_10_ = bf16[4,256,128]{2,1,0:T(8,128)(2,1)S(1)} collective-permute-done((bf16[4,256,128]{2,1,0:T(8,128)(2,1)S(1)}, bf16[4,256,128]{2,1,0:T(8,128)(2,1)S(1)}, u32[]{:S(2)}, u32[]{:S(2)}) %collective-permute-start.15) | collective-permute-done | bytes 262176 | tf_op jit(solution)/shard_map/ppermute | solution.py:459
  93.7 2.7 %collective-permute-start.16 = (bf16[4,256,128]{2,1,0:T(8,128)(2,1)S(1)}, bf16[4,256,128]{2,1,0:T(8,128)(2,1)S(1)}, u32[]{:S(2)}, u32[]{:S(2)}) collective-permute-start(bf16[4,256,128]{2,1,0:T(8,128)(2,1)S(1)} %collective-permute-done.15.refs_10_), channel_id=1, source_target_pairs={{0,131},{1,0},{2,1},{3,2},{4,5},{5,6},{6,7},{7,132},{8,139},{9,8},... | collective-permute-start | bytes 786440 | tf_op jit(solution)/shard_map/ppermute | solution.py:459
  96.4 1.5 %collective-permute-start.4 = (bf16[8,8,16,128]{3,2,1,0:T(8,128)(2,1)S(1)}, bf16[8,8,16,128]{3,2,1,0:T(8,128)(2,1)S(1)}, u32[]{:S(2)}, u32[]{:S(2)}) collective-permute-start(bf16[8,8,16,128]{3,2,1,0:T(8,128)(2,1)S(1)} %bundle.1.refs_0_), channel_id=1, source_target_pairs={{0,8},{4,12},{8,16},{12,20},{16,24},{20,28},{24,0},{28,4},{32,40},... | collective-permute-start | bytes 786440 | tf_op jit(solution)/shard_map/ppermute | solution.py:483
  98.0 2.7 %collective-permute-start.5 = (bf16[8,8,16,128]{3,2,1,0:T(8,128)(2,1)S(1)}, bf16[8,8,16,128]{3,2,1,0:T(8,128)(2,1)S(1)}, u32[]{:S(2)}, u32[]{:S(2)}) collective-permute-start(bf16[8,8,16,128]{3,2,1,0:T(8,128)(2,1)S(1)} %bundle.1.refs_0_), channel_id=1, source_target_pairs={{0,16},{4,20},{8,24},{12,28},{16,0},{20,4},{24,8},{28,12},{32,48},... | collective-permute-start | bytes 786440 | tf_op jit(solution)/shard_map/ppermute | solution.py:484
  100.7 1.4 %collective-permute-start.6 = (bf16[8,8,16,128]{3,2,1,0:T(8,128)(2,1)S(1)}, bf16[8,8,16,128]{3,2,1,0:T(8,128)(2,1)S(1)}, u32[]{:S(2)}, u32[]{:S(2)}) collective-permute-start(bf16[8,8,16,128]{3,2,1,0:T(8,128)(2,1)S(1)} %bundle.1.refs_0_), channel_id=1, source_target_pairs={{0,24},{4,28},{8,0},{12,4},{16,8},{20,12},{24,16},{28,20},{32,56},... | collective-permute-start | bytes 786440 | tf_op jit(solution)/shard_map/ppermute | solution.py:483
  102.1 2.6 %collective-permute-done.13.refs_8_ = bf16[4,256,128]{2,1,0:T(8,128)(2,1)S(1)} collective-permute-done((bf16[4,256,128]{2,1,0:T(8,128)(2,1)S(1)}, bf16[4,256,128]{2,1,0:T(8,128)(2,1)S(1)}, u32[]{:S(2)}, u32[]{:S(2)}) %collective-permute-start.13) | collective-permute-done | bytes 262176 | tf_op jit(solution)/shard_map/ppermute | solution.py:459
  104.7 2.1 %collective-permute-done.4.refs_1_ = bf16[8,8,16,128]{3,2,1,0:T(8,128)(2,1)S(1)} collective-permute-done((bf16[8,8,16,128]{3,2,1,0:T(8,128)(2,1)S(1)}, bf16[8,8,16,128]{3,2,1,0:T(8,128)(2,1)S(1)}, u32[]{:S(2)}, u32[]{:S(2)}) %collective-permute-start.4) | collective-permute-done | bytes 262176 | tf_op jit(solution)/shard_map/ppermute | solution.py:483
  106.8 6.6 %collective-permute-done.5.refs_2_ = bf16[8,8,16,128]{3,2,1,0:T(8,128)(2,1)S(1)} collective-permute-done((bf16[8,8,16,128]{3,2,1,0:T(8,128)(2,1)S(1)}, bf16[8,8,16,128]{3,2,1,0:T(8,128)(2,1)S(1)}, u32[]{:S(2)}, u32[]{:S(2)}) %collective-permute-start.5) | collective-permute-done | bytes 262176 | tf_op jit(solution)/shard_map/ppermute | solution.py:484
  113.4 2.1 %weight_parts.1 = (bf16[4,2,64,512]{3,2,1,0:T(8,128)(2,1)S(1)}, bf16[4,2,64,512]{3,2,1,0:T(8,128)(2,1)S(1)}) custom-call(s32[4]{0:T(128)S(1)} %pad_add_fusion.where_ref, bf16[8,8,16,128]{3,2,1,0:T(8,128)(2,1)S(1)} %bundle.1.refs_0_, bf16[8,8,16,128]{3,2,1,0:T(8,128)(2,1)S(1)} %collective-permute-done.4.refs_1_, ...), custom_call_target="tpu_custom_call" | custom-call | tf_op jit(solution)/shard_map/weight_parts/pallas_call | solution.py:402
  115.6 0.2 collective-permute-start.17
  115.7 1.8 %collective-permute-done.17.received_ref = bf16[4,2,64,512]{3,2,1,0:T(8,128)(2,1)S(1)} collective-permute-done((bf16[4,2,64,512]{3,2,1,0:T(8,128)(2,1)S(1)}, bf16[4,2,64,512]{3,2,1,0:T(8,128)(2,1)S(1)}, u32[]{:S(2)}, u32[]{:S(2)}) %collective-permute-start.17) | collective-permute-done | bytes 524320 | tf_op jit(solution)/shard_map/ppermute | solution.py:487
  117.6 0.1 join_cores.1
  117.7 0.5 collective-permute-start.18
  118.2 2.1 %collective-permute-start.19 = (bf16[2,64,512]{2,1,0:T(8,128)(2,1)S(1)}, bf16[2,64,512]{2,1,0:T(8,128)(2,1)S(1)}, u32[]{:S(2)}, u32[]{:S(2)}) collective-permute-start(bf16[2,64,512]{2,1,0:T(8,128)(2,1)S(1)} %get-tuple-element.61), channel_id=1, source_target_pairs={{0,32},{4,36},{8,40},{12,44},{16,48},{20,52},{24,56},{28,60},{32,0... | collective-permute-start | bytes 393224 | tf_op jit(solution)/shard_map/ppermute | solution.py:489
  120.4 1.5 %collective-permute-start.20 = (bf16[2,64,512]{2,1,0:T(8,128)(2,1)S(1)}, bf16[2,64,512]{2,1,0:T(8,128)(2,1)S(1)}, u32[]{:S(2)}, u32[]{:S(2)}) collective-permute-start(bf16[2,64,512]{2,1,0:T(8,128)(2,1)S(1)} %get-tuple-element.62), channel_id=1, source_target_pairs={{0,96},{4,100},{8,104},{12,108},{16,112},{20,116},{24,120},{28,124... | collective-permute-start | bytes 393224 | tf_op jit(solution)/shard_map/ppermute | solution.py:489
  121.9 3.8 %collective-permute-done.18.refs_1_ = bf16[2,64,512]{2,1,0:T(8,128)(2,1)S(1)} collective-permute-done((bf16[2,64,512]{2,1,0:T(8,128)(2,1)S(1)}, bf16[2,64,512]{2,1,0:T(8,128)(2,1)S(1)}, u32[]{:S(2)}, u32[]{:S(2)}) %collective-permute-start.18) | collective-permute-done | bytes 131104 | tf_op jit(solution)/shard_map/ppermute | solution.py:490
  125.7 1.0 collective-permute-done.19.refs_2_
  126.7 1.0 collective-permute-done.20.refs_3_
  127.6 0.6 weight_total.1
  128.3 1.3 collective-permute-start.21
  129.6 8.2 %collective-permute-done.21 = bf16[64,512]{1,0:T(8,128)(2,1)S(1)} collective-permute-done((bf16[64,512]{1,0:T(8,128)(2,1)S(1)}, bf16[64,512]{1,0:T(8,128)(2,1)S(1)}, u32[]{:S(2)}, u32[]{:S(2)}) %collective-permute-start.21) | collective-permute-done | bytes 65568 | tf_op jit(solution)/shard_map/ppermute | solution.py:492
  137.9 0.7 maximum_select_fusion
  138.6 1.3 finish.1
  (35 shorter events, 0.2 us)
Async XLA Ops:
  3.3 14.8 %copy-start.3 = (bf16[128,1024]{1,0:T(8,128)(2,1)S(1)}, bf16[128,1024]{1,0:T(8,128)(2,1)}, u32[]{:S(2)}) copy-start(bf16[128,1024]{1,0:T(8,128)(2,1)} %input_ref.1) | copy-start | bytes 786436
  3.3 48.2 %copy-start.4 = (bf16[512,256]{1,0:T(8,128)(2,1)S(1)}, bf16[512,256]{1,0:T(8,128)(2,1)}, u32[]{:S(2)}) copy-start(bf16[512,256]{1,0:T(8,128)(2,1)} %constant.84.clone.refs_3_) | copy-start | bytes 786436
  3.3 48.2 %copy-start.5 = (bf16[512,256]{1,0:T(8,128)(2,1)S(1)}, bf16[512,256]{1,0:T(8,128)(2,1)}, u32[]{:S(2)}) copy-start(bf16[512,256]{1,0:T(8,128)(2,1)} %constant.85.clone.refs_4_) | copy-start | bytes 786436
  3.3 48.2 %copy-start.6 = (bf16[128,144]{1,0:T(8,128)(2,1)S(1)}, bf16[128,144]{1,0:T(8,128)(2,1)}, u32[]{:S(2)}) copy-start(bf16[128,144]{1,0:T(8,128)(2,1)} %constant.86.clone.refs_5_) | copy-start | bytes 110596
  3.3 48.2 %copy-start.7 = (bf16[144,128]{1,0:T(8,128)(2,1)S(1)}, bf16[144,128]{1,0:T(8,128)(2,1)}, u32[]{:S(2)}) copy-start(bf16[144,128]{1,0:T(8,128)(2,1)} %constant.81.clone.refs_0_) | copy-start | bytes 110596
  3.3 48.2 %copy-start.8 = (f32[72,128]{1,0:T(8,128)S(1)}, f32[72,128]{1,0:T(8,128)}, u32[]{:S(2)}) copy-start(f32[72,128]{1,0:T(8,128)} %constant.82.clone.refs_1_) | copy-start | bytes 110596
  3.3 48.2 %copy-start.9 = (f32[72,128]{1,0:T(8,128)S(1)}, f32[72,128]{1,0:T(8,128)}, u32[]{:S(2)}) copy-start(f32[72,128]{1,0:T(8,128)} %constant.83.clone.refs_2_) | copy-start | bytes 110596
  3.3 48.2 %all-to-all-start = ((bf16[64,64,128]{2,1,0:T(8,128)(2,1)}), bf16[64,64,128]{2,1,0:T(8,128)(2,1)S(1)}, u32[]{:S(2)}, u32[]{:S(2)}) async-start(bf16[64,64,128]{2,1,0:T(8,128)(2,1)} %gather_signals.1), calls=%async_computation | async-start | bytes 2097152 | tf_op jit(solution)/shard_map/all_to_all | solution.py:455
  18.8 11.5 %collective-permute-start.9 = (bf16[256,128]{1,0:T(8,128)(2,1)S(1)}, bf16[256,128]{1,0:T(8,128)(2,1)S(1)}, u32[]{:S(2)}, u32[]{:S(2)}) collective-permute-start(bf16[256,128]{1,0:T(8,128)(2,1)S(1)} %get-tuple-element.56), channel_id=1, source_target_pairs={{0,24},{4,28},{8,0},{12,4},{16,8},{20,12},{24,16},{28,20},{32,56},... | collective-permute-start | bytes 196616 | tf_op jit(solution)/shard_map/ppermute | solution.py:468
  21.6 10.5 %collective-permute-start.8 = (bf16[256,128]{1,0:T(8,128)(2,1)S(1)}, bf16[256,128]{1,0:T(8,128)(2,1)S(1)}, u32[]{:S(2)}, u32[]{:S(2)}) collective-permute-start(bf16[256,128]{1,0:T(8,128)(2,1)S(1)} %get-tuple-element.55), channel_id=1, source_target_pairs={{0,16},{4,20},{8,24},{12,28},{16,0},{20,4},{24,8},{28,12},{32,48},... | collective-permute-start | bytes 196616 | tf_op jit(solution)/shard_map/ppermute | solution.py:468
  22.4 11.2 %collective-permute-start.7 = (bf16[256,128]{1,0:T(8,128)(2,1)S(1)}, bf16[256,128]{1,0:T(8,128)(2,1)S(1)}, u32[]{:S(2)}, u32[]{:S(2)}) collective-permute-start(bf16[256,128]{1,0:T(8,128)(2,1)S(1)} %get-tuple-element.54), channel_id=1, source_target_pairs={{0,8},{4,12},{8,16},{12,20},{16,24},{20,28},{24,0},{28,4},{32,40},... | collective-permute-start | bytes 196616 | tf_op jit(solution)/shard_map/ppermute | solution.py:468
  33.6 17.9 %collective-permute-start.10 = (bf16[4,256,128]{2,1,0:T(8,128)(2,1)S(1)}, bf16[4,256,128]{2,1,0:T(8,128)(2,1)S(1)}, u32[]{:S(2)}, u32[]{:S(2)}) collective-permute-start(bf16[4,256,128]{2,1,0:T(8,128)(2,1)S(1)} %pad_maximum_fusion.refs_4_), channel_id=1, source_target_pairs={{0,1},{1,2},{2,3},{3,128},{4,135},{5,4},{6,5},{7,6},{8,9},{9,10},{... | collective-permute-start | bytes 786440 | tf_op jit(solution)/shard_map/ppermute | solution.py:459
  33.7 36.6 %collective-permute-start.14 = (bf16[4,256,128]{2,1,0:T(8,128)(2,1)S(1)}, bf16[4,256,128]{2,1,0:T(8,128)(2,1)S(1)}, u32[]{:S(2)}, u32[]{:S(2)}) collective-permute-start(bf16[4,256,128]{2,1,0:T(8,128)(2,1)S(1)} %pad_maximum_fusion.refs_4_), channel_id=1, source_target_pairs={{0,131},{1,0},{2,1},{3,2},{4,5},{5,6},{6,7},{7,132},{8,139},{9,8},... | collective-permute-start | bytes 786440 | tf_op jit(solution)/shard_map/ppermute | solution.py:459
  51.5 23.7 %collective-permute-start.11 = (bf16[4,256,128]{2,1,0:T(8,128)(2,1)S(1)}, bf16[4,256,128]{2,1,0:T(8,128)(2,1)S(1)}, u32[]{:S(2)}, u32[]{:S(2)}) collective-permute-start(bf16[4,256,128]{2,1,0:T(8,128)(2,1)S(1)} %collective-permute-done.10.refs_5_), channel_id=1, source_target_pairs={{0,1},{1,2},{2,3},{3,128},{4,135},{5,4},{6,5},{7,6},{8,9},{9,10},{... | collective-permute-start | bytes 786440 | tf_op jit(solution)/shard_map/ppermute | solution.py:459
  59.1 79.5 %all-to-all-start.1 = ((bf16[64,48,128]{2,1,0:T(8,128)(2,1)}), bf16[64,48,128]{2,1,0:T(8,128)(2,1)S(1)}, u32[]{:S(2)}, u32[]{:S(2)}) async-start(bf16[64,48,128]{2,1,0:T(8,128)(2,1)} %complete.1), calls=%async_computation.1 | async-start | bytes 1572864 | tf_op jit(solution)/shard_map/all_to_all | solution.py:455
  70.3 23.4 %collective-permute-start.15 = (bf16[4,256,128]{2,1,0:T(8,128)(2,1)S(1)}, bf16[4,256,128]{2,1,0:T(8,128)(2,1)S(1)}, u32[]{:S(2)}, u32[]{:S(2)}) collective-permute-start(bf16[4,256,128]{2,1,0:T(8,128)(2,1)S(1)} %collective-permute-done.14.refs_11_), channel_id=1, source_target_pairs={{0,131},{1,0},{2,1},{3,2},{4,5},{5,6},{6,7},{7,132},{8,139},{9,8},... | collective-permute-start | bytes 786440 | tf_op jit(solution)/shard_map/ppermute | solution.py:459
  75.2 25.5 %collective-permute-start.12 = (bf16[4,256,128]{2,1,0:T(8,128)(2,1)S(1)}, bf16[4,256,128]{2,1,0:T(8,128)(2,1)S(1)}, u32[]{:S(2)}, u32[]{:S(2)}) collective-permute-start(bf16[4,256,128]{2,1,0:T(8,128)(2,1)S(1)} %collective-permute-done.11.refs_6_), channel_id=1, source_target_pairs={{0,1},{1,2},{2,3},{3,128},{4,135},{5,4},{6,5},{7,6},{8,9},{9,10},{... | collective-permute-start | bytes 786440 | tf_op jit(solution)/shard_map/ppermute | solution.py:459
  75.2 6.3 %collective-permute-start = (bf16[2,8,16,128]{3,2,1,0:T(8,128)(2,1)S(1)}, bf16[2,8,16,128]{3,2,1,0:T(8,128)(2,1)S(1)}, u32[]{:S(2)}, u32[]{:S(2)}) collective-permute-start(bf16[2,8,16,128]{3,2,1,0:T(8,128)(2,1)S(1)} %get-tuple-element.48), channel_id=1, source_target_pairs={{0,32},{4,36},{8,40},{12,44},{16,48},{20,52},{24,56},{28,60},{32,0... | collective-permute-start | bytes 196616 | tf_op jit(solution)/shard_map/ppermute | solution.py:476
  76.4 6.8 %collective-permute-start.1 = (bf16[2,8,16,128]{3,2,1,0:T(8,128)(2,1)S(1)}, bf16[2,8,16,128]{3,2,1,0:T(8,128)(2,1)S(1)}, u32[]{:S(2)}, u32[]{:S(2)}) collective-permute-start(bf16[2,8,16,128]{3,2,1,0:T(8,128)(2,1)S(1)} %get-tuple-element.49), channel_id=1, source_target_pairs={{0,64},{4,68},{8,72},{12,76},{16,80},{20,84},{24,88},{28,92},{32,9... | collective-permute-start | bytes 196616 | tf_op jit(solution)/shard_map/ppermute | solution.py:476
  77.1 6.8 %collective-permute-start.2 = (bf16[2,8,16,128]{3,2,1,0:T(8,128)(2,1)S(1)}, bf16[2,8,16,128]{3,2,1,0:T(8,128)(2,1)S(1)}, u32[]{:S(2)}, u32[]{:S(2)}) collective-permute-start(bf16[2,8,16,128]{3,2,1,0:T(8,128)(2,1)S(1)} %get-tuple-element.50), channel_id=1, source_target_pairs={{0,96},{4,100},{8,104},{12,108},{16,112},{20,116},{24,120},{28,124... | collective-permute-start | bytes 196616 | tf_op jit(solution)/shard_map/ppermute | solution.py:476
  84.0 12.4 %collective-permute-start.3 = (bf16[4,8,16,128]{3,2,1,0:T(8,128)(2,1)S(1)}, bf16[4,8,16,128]{3,2,1,0:T(8,128)(2,1)S(1)}, u32[]{:S(2)}, u32[]{:S(2)}) collective-permute-start(bf16[4,8,16,128]{3,2,1,0:T(8,128)(2,1)S(1)} %get-tuple-element.52), channel_id=1, source_target_pairs={{0,4},{4,0},{8,12},{12,8},{16,20},{20,16},{24,28},{28,24},{32,36},... | collective-permute-start | bytes 393224 | tf_op jit(solution)/shard_map/ppermute | solution.py:478
  84.1 20.6 %collective-permute-start.13 = (bf16[4,256,128]{2,1,0:T(8,128)(2,1)S(1)}, bf16[4,256,128]{2,1,0:T(8,128)(2,1)S(1)}, u32[]{:S(2)}, u32[]{:S(2)}) collective-permute-start(bf16[4,256,128]{2,1,0:T(8,128)(2,1)S(1)} %collective-permute-done.11.refs_6_), channel_id=1, source_target_pairs={{0,2},{1,3},{2,128},{3,129},{4,134},{5,135},{6,4},{7,5},{8,10},{9,... | collective-permute-start | bytes 786440 | tf_op jit(solution)/shard_map/ppermute | solution.py:459
  93.7 11.0 %collective-permute-start.16 = (bf16[4,256,128]{2,1,0:T(8,128)(2,1)S(1)}, bf16[4,256,128]{2,1,0:T(8,128)(2,1)S(1)}, u32[]{:S(2)}, u32[]{:S(2)}) collective-permute-start(bf16[4,256,128]{2,1,0:T(8,128)(2,1)S(1)} %collective-permute-done.15.refs_10_), channel_id=1, source_target_pairs={{0,131},{1,0},{2,1},{3,2},{4,5},{5,6},{6,7},{7,132},{8,139},{9,8},... | collective-permute-start | bytes 786440 | tf_op jit(solution)/shard_map/ppermute | solution.py:459
  96.4 10.4 %collective-permute-start.4 = (bf16[8,8,16,128]{3,2,1,0:T(8,128)(2,1)S(1)}, bf16[8,8,16,128]{3,2,1,0:T(8,128)(2,1)S(1)}, u32[]{:S(2)}, u32[]{:S(2)}) collective-permute-start(bf16[8,8,16,128]{3,2,1,0:T(8,128)(2,1)S(1)} %bundle.1.refs_0_), channel_id=1, source_target_pairs={{0,8},{4,12},{8,16},{12,20},{16,24},{20,28},{24,0},{28,4},{32,40},... | collective-permute-start | bytes 786440 | tf_op jit(solution)/shard_map/ppermute | solution.py:483
  98.0 15.4 %collective-permute-start.5 = (bf16[8,8,16,128]{3,2,1,0:T(8,128)(2,1)S(1)}, bf16[8,8,16,128]{3,2,1,0:T(8,128)(2,1)S(1)}, u32[]{:S(2)}, u32[]{:S(2)}) collective-permute-start(bf16[8,8,16,128]{3,2,1,0:T(8,128)(2,1)S(1)} %bundle.1.refs_0_), channel_id=1, source_target_pairs={{0,16},{4,20},{8,24},{12,28},{16,0},{20,4},{24,8},{28,12},{32,48},... | collective-permute-start | bytes 786440 | tf_op jit(solution)/shard_map/ppermute | solution.py:484
  100.7 12.7 %collective-permute-start.6 = (bf16[8,8,16,128]{3,2,1,0:T(8,128)(2,1)S(1)}, bf16[8,8,16,128]{3,2,1,0:T(8,128)(2,1)S(1)}, u32[]{:S(2)}, u32[]{:S(2)}) collective-permute-start(bf16[8,8,16,128]{3,2,1,0:T(8,128)(2,1)S(1)} %bundle.1.refs_0_), channel_id=1, source_target_pairs={{0,24},{4,28},{8,0},{12,4},{16,8},{20,12},{24,16},{28,20},{32,56},... | collective-permute-start | bytes 786440 | tf_op jit(solution)/shard_map/ppermute | solution.py:483
  115.5 23.1 %copy-start = (bf16[128,1024]{1,0:T(8,128)(2,1)S(1)}, bf16[128,1024]{1,0:T(8,128)(2,1)}, u32[]{:S(2)}) copy-start(bf16[128,1024]{1,0:T(8,128)(2,1)} %key_ref.3) | copy-start | bytes 786436
  115.6 23.0 %copy-start.1 = (bf16[128,1024]{1,0:T(8,128)(2,1)S(1)}, bf16[128,1024]{1,0:T(8,128)(2,1)}, u32[]{:S(2)}) copy-start(bf16[128,1024]{1,0:T(8,128)(2,1)} %value_ref.3) | copy-start | bytes 786436
  115.6 23.0 %copy-start.2 = (bf16[128,1024]{1,0:T(8,128)(2,1)S(1)}, bf16[128,1024]{1,0:T(8,128)(2,1)}, u32[]{:S(2)}) copy-start(bf16[128,1024]{1,0:T(8,128)(2,1)} %grad_ref.3) | copy-start | bytes 786436
  115.6 2.0 %collective-permute-start.17 = (bf16[4,2,64,512]{3,2,1,0:T(8,128)(2,1)S(1)}, bf16[4,2,64,512]{3,2,1,0:T(8,128)(2,1)S(1)}, u32[]{:S(2)}, u32[]{:S(2)}) collective-permute-start(bf16[4,2,64,512]{3,2,1,0:T(8,128)(2,1)S(1)} %get-tuple-element.58), channel_id=1, source_target_pairs={{0,4},{4,0},{8,12},{12,8},{16,20},{20,16},{24,28},{28,24},{32,36},... | collective-permute-start | bytes 1572872 | tf_op jit(solution)/shard_map/ppermute | solution.py:487
  117.7 8.0 %collective-permute-start.18 = (bf16[2,64,512]{2,1,0:T(8,128)(2,1)S(1)}, bf16[2,64,512]{2,1,0:T(8,128)(2,1)S(1)}, u32[]{:S(2)}, u32[]{:S(2)}) collective-permute-start(bf16[2,64,512]{2,1,0:T(8,128)(2,1)S(1)} %get-tuple-element.60), channel_id=1, source_target_pairs={{0,64},{4,68},{8,72},{12,76},{16,80},{20,84},{24,88},{28,92},{32,9... | collective-permute-start | bytes 393224 | tf_op jit(solution)/shard_map/ppermute | solution.py:490
  118.2 8.4 %collective-permute-start.19 = (bf16[2,64,512]{2,1,0:T(8,128)(2,1)S(1)}, bf16[2,64,512]{2,1,0:T(8,128)(2,1)S(1)}, u32[]{:S(2)}, u32[]{:S(2)}) collective-permute-start(bf16[2,64,512]{2,1,0:T(8,128)(2,1)S(1)} %get-tuple-element.61), channel_id=1, source_target_pairs={{0,32},{4,36},{8,40},{12,44},{16,48},{20,52},{24,56},{28,60},{32,0... | collective-permute-start | bytes 393224 | tf_op jit(solution)/shard_map/ppermute | solution.py:489
  120.4 7.3 %collective-permute-start.20 = (bf16[2,64,512]{2,1,0:T(8,128)(2,1)S(1)}, bf16[2,64,512]{2,1,0:T(8,128)(2,1)S(1)}, u32[]{:S(2)}, u32[]{:S(2)}) collective-permute-start(bf16[2,64,512]{2,1,0:T(8,128)(2,1)S(1)} %get-tuple-element.62), channel_id=1, source_target_pairs={{0,96},{4,100},{8,104},{12,108},{16,112},{20,116},{24,120},{28,124... | collective-permute-start | bytes 393224 | tf_op jit(solution)/shard_map/ppermute | solution.py:489
  128.3 9.6 %collective-permute-start.21 = (bf16[64,512]{1,0:T(8,128)(2,1)S(1)}, bf16[64,512]{1,0:T(8,128)(2,1)S(1)}, u32[]{:S(2)}, u32[]{:S(2)}) collective-permute-start(bf16[64,512]{1,0:T(8,128)(2,1)S(1)} %get-tuple-element.64), channel_id=1, source_target_pairs={{0,128},{4,132},{8,136},{12,140},{16,144},{20,148},{24,152},{28,15... | collective-permute-start | bytes 196616 | tf_op jit(solution)/shard_map/ppermute | solution.py:492
